TPU v7x, 256 devices: a whole 4x4x8 slice. The times are simulated.
256 devices in a mesh: scen: 64 (over y, x, z_hi), rootr: 2 (over core), rootc: 2 (over z_lo).
Axes of the slice: x: 4, y: 4, z: 8 (z_hi: 4, z_lo: 2; z = z_hi * 2 + z_lo), core: 2. Of those that a mesh axis runs over, the one named last changes fastest.
Arguments:
- start_guess: float32 [8192, 256], P(('scen', 'rootr'), 'rootc'), may hold values from -6 to 6
- right_side: float32 [8192, 256], P(('scen', 'rootr'), 'rootc'), may hold values from -6 to 6
- root_diagonal: float32 [8192], P(('scen', 'rootr')), may hold values from 1 to 4
- preconditioner: bfloat16 [8192, 8192], P(('scen', 'rootr')), may hold values from -0.015625 to 0.015625
- border_block: bfloat16 [128, 512, 768], P(('scen', 'rootr'), 'rootc'), may hold values from -0.21875 to 0.21875
- coupling_inverse: bfloat16 [128, 512, 512], P(('scen', 'rootr'), 'rootc'), may hold values from -0.25 to 0.25
- border_count: int32 [128], P(('scen', 'rootr')), may hold values from 64 to 512, as said below
- column_tiles: int32 [128, 6], P(('scen', 'rootr')), may hold values from 0 to 63, as said below
Outputs:
- final_iterate: float32 [8192, 256], P(('scen', 'rootr'), 'rootc')
Inputs may be any that keep to these rules, and one draw needn't show every extreme that they name: A scenario's live border rows are its first border_count rows; some scenario has exactly 512. `column_tiles`: each row names 6 different tiles in rising order.
All inputs are finite; a program needn't handle non-finite values.
Results may differ from a plain program's by a relative error of at most 0.0022.
Values may be sent and summed in bfloat16 or wider, within the bound.
No kernel may reach another device: no remote copies, remote signals or barrier semaphores. Data moves between devices by JAX's collectives and lax.ppermute only.
A program may use at most 64 MiB of HBM per device.

v0:
```python
import jax
import jax.numpy as jnp
from jax import lax
from jax.sharding import Mesh
from jax.sharding import PartitionSpec as P

TILE = 128
SCEN_ROOTR = ("scen_0", "scen_1", "scen_2", "rootr")


def joined_along(pieces, dim):
    pieces = jnp.moveaxis(pieces, 0, dim)
    shape = pieces.shape
    return pieces.reshape(*shape[:dim], shape[dim] * shape[dim + 1], *shape[dim + 2 :])


def from_everyone(shard, axis):
    copies = jnp.broadcast_to(shard, (lax.axis_size(axis), *shard.shape))
    return lax.all_to_all(copies, axis, split_axis=0, concat_axis=0, tiled=True)


def gather_directly(shard, axis, dim):
    return joined_along(from_everyone(shard, axis), dim)


def gather_axes(shard, axes, dim):
    far, near = axes
    pieces = from_everyone(from_everyone(shard, far), near)
    return joined_along(pieces.swapaxes(0, 1).reshape(-1, *shard.shape), dim)


def cut_along(shard, dim, length):
    before, after = (shard.shape[:dim], shard.shape[dim + 1 :])
    return jnp.moveaxis(shard.reshape(*before, length, -1, *after), dim, 0)


def summed_on_arrival(shard, axis, dim):
    pieces = cut_along(shard, dim, lax.axis_size(axis))
    arrived = lax.all_to_all(pieces, axis, split_axis=0, concat_axis=0, tiled=True)
    return arrived.sum(axis=0)


def sum_by_axis(shard, axes, dim):
    far, near = axes
    pieces = cut_along(shard, dim, lax.axis_size(far))
    nearer = summed_on_arrival(pieces, near, dim + 1)
    arrived = lax.all_to_all(nearer, far, split_axis=0, concat_axis=0, tiled=True)
    return arrived.sum(axis=0)


def rows_for(lines, length):
    spare = -len(lines) % length
    return jnp.pad(lines, [(0, spare)] + [(0, 0)] * (lines.ndim - 1))


def nested_sum(shard, axes):
    lines = shard.reshape(-1, shard.shape[-1])
    own = sum_by_axis(rows_for(lines, lax.axis_size(axes[0]) * lax.axis_size(axes[1])), axes, 0)
    whole = gather_axes(own, axes, 0)
    return whole[: len(lines)].reshape(shard.shape)


def border_product(matrix, operand, live_here):
    half_rows = matrix.shape[0]
    live_mask = (jnp.arange(half_rows) < live_here)[:, None]
    product = jnp.dot(matrix, operand, preferred_element_type=jnp.float32)
    return jnp.where(live_mask, product, 0.0).astype(jnp.bfloat16)


def border_transpose(border, solved):
    numbers = (((0,), (0,)), ((), ()))
    return lax.dot_general(border, solved, numbers, preferred_element_type=jnp.float32)


def local(
    start_guess,
    right_side,
    root_diagonal,
    preconditioner,
    border_block,
    coupling_inverse,
    border_count,
    column_tiles,
):
    own_rows = start_guess.shape[0]
    half_rhs = start_guess.shape[1]
    half_rows = border_block.shape[1]
    coupled_cols = border_block.shape[2]
    order_rows = preconditioner.shape[1]
    border = border_block[0]
    inverse_rows = coupling_inverse[0]
    tile_ids = column_tiles[0]
    offset = lax.axis_index("rootc") * half_rows
    live_here = jnp.clip(border_count[0] - offset, 0, half_rows)
    iterate = start_guess
    own_low = iterate.astype(jnp.bfloat16)
    both_halves = gather_directly(own_low, "rootc", 1)
    gathered = gather_axes(both_halves, (("scen_0", "scen_1", "scen_2"), "rootr"), 0)
    all_rhs = gathered.shape[1]
    picked = gathered.reshape(order_rows // TILE, TILE, all_rhs)[tile_ids].reshape(
        coupled_cols, all_rhs
    )
    values_local = border_product(border, picked, live_here)
    values_whole = gather_directly(values_local, "rootc", 0)
    solved = border_product(inverse_rows, values_whole, live_here)
    term_part = border_transpose(border, solved)
    term_half = summed_on_arrival(term_part, "rootc", 1)
    spread_terms = jnp.zeros((order_rows // TILE, TILE, half_rhs), jnp.float32)
    spread_terms = (
        spread_terms.at[tile_ids]
        .add(term_half.reshape(-1, TILE, half_rhs))
        .reshape(order_rows, half_rhs)
    )
    own_terms = right_side - root_diagonal[:, None] * iterate
    first_row = lax.axis_index(SCEN_ROOTR) * own_rows
    current = lax.dynamic_slice_in_dim(spread_terms, first_row, own_rows, 0)
    spread_terms = lax.dynamic_update_slice_in_dim(spread_terms, current + own_terms, first_row, 0)
    residual = nested_sum(spread_terms, (("scen_0", "scen_1", "scen_2"), "rootr"))
    update = jnp.dot(
        preconditioner, residual.astype(jnp.bfloat16), preferred_element_type=jnp.float32
    )
    iterate = iterate + update
    return iterate


def solution(mesh):
    torus = Mesh(
        mesh.devices.reshape(4, 4, 4, mesh.shape["rootr"], mesh.shape["rootc"]),
        ("scen_0", "scen_1", "scen_2", "rootr", "rootc"),
    )
    in_specs = (
        P(SCEN_ROOTR, "rootc"),
        P(SCEN_ROOTR, "rootc"),
        P(SCEN_ROOTR),
        P(SCEN_ROOTR, None),
        P(SCEN_ROOTR, "rootc", None),
        P(SCEN_ROOTR, "rootc", None),
        P(SCEN_ROOTR),
        P(SCEN_ROOTR, None),
    )
    out_specs = P(SCEN_ROOTR, "rootc")
    return jax.shard_map(local, mesh=torus, in_specs=in_specs, out_specs=out_specs, check_vma=False)
```

profile of v0, /device:TPU:1, one launch (start us, length us, event | category | flops | bytes accessed | tf_op | source)
XLA Modules:
  0.0 236.2 jit_solution(12804651503025404459)
XLA Ops:
  0.0 0.0 copy-start
  0.0 0.0 copy-start.6
  0.0 0.9 convert_element_type.22
  0.9 6.3 %all_to_all.45 = bf16[2,64,128]{2,1,0:T(8,128)(2,1)S(1)} all-to-all(bf16[2,64,128]{2,1,0:T(8,128)(2,1)S(1)} %broadcast_in_dim.44), channel_id=1, replica_groups=mesh['scen_0'=4,'scen_1'=4,'scen_2'=4,'rootr'=2,'rootc'=2] {'rootc'}, dimensions={0} | all-to-all | bytes 65536 | tf_op jit(solution)/shard_map/all_to_all | solution.py:19
  7.2 1.6 broadcast_in_dim.45
  8.8 13.9 %all-to-all-start.1 = ((bf16[64,64,256]{2,1,0:T(8,128)(2,1)}), bf16[64,64,256]{2,1,0:T(8,128)(2,1)S(1)}, u32[]{:S(2)}, u32[]{:S(2)}) async-start(bf16[64,64,256]{2,1,0:T(8,128)(2,1)} %broadcast_in_dim.45), calls=%async_computation.1 | async-start | bytes 4194304 | tf_op jit(solution)/shard_map/all_to_all | solution.py:19
  23.4 0.0 copy-done.6
  23.5 51.7 %all-to-all-done.1 = bf16[64,64,256]{2,1,0:T(8,128)(2,1)S(1)} async-done(((bf16[64,64,256]{2,1,0:T(8,128)(2,1)}), bf16[64,64,256]{2,1,0:T(8,128)(2,1)S(1)}, u32[]{:S(2)}, u32[]{:S(2)}) %all-to-all-start.1) | async-done | bytes 2097184 | tf_op jit(solution)/shard_map/all_to_all | solution.py:19
  75.2 0.5 broadcast_in_dim.46
  75.7 8.6 %all_to_all.46 = bf16[2,64,64,256]{3,2,1,0:T(8,128)(2,1)S(1)} all-to-all(bf16[2,64,64,256]{3,2,1,0:T(8,128)(2,1)S(1)} %broadcast_in_dim.46), channel_id=1, replica_groups=mesh['scen_0'=4,'scen_1'=4,'scen_2'=4,'rootr'=2,'rootc'=2] {'rootr'}, dimensions={0} | all-to-all | bytes 8388608 | tf_op jit(solution)/shard_map/all_to_all | solution.py:19
  84.2 0.0 copy-start.1
  84.2 0.0 copy-start.3
  84.2 2.2 copy.22
  86.5 2.8 %gather_fusion = bf16[6,128,256]{2,1,0:T(8,128)(2,1)S(1)} fusion(bf16[64,128,256]{2,1,0:T(8,128)(2,1)} %bitcast.52, s32[1024]{0:T(1024)S(1)} %pad_clamp_fusion), kind=kCustom, calls=%fused_computation | custom fusion | bytes 786456 | tf_op jit(solution)/shard_map/gather | solution.py:100
  89.2 0.0 copy-done.1
  89.3 0.3 fusion.2
  89.6 0.1 copy.23
  89.7 7.3 %all_to_all.47 = bf16[2,256,256]{2,1,0:T(8,128)(2,1)S(1)} all-to-all(bf16[2,256,256]{2,1,0:T(8,128)(2,1)S(1)} %broadcast_in_dim.48), channel_id=1, replica_groups=mesh['scen_0'=4,'scen_1'=4,'scen_2'=4,'rootr'=2,'rootc'=2] {'rootc'}, dimensions={0} | all-to-all | bytes 524288 | tf_op jit(solution)/shard_map/all_to_all | solution.py:19
  97.0 0.0 copy-done.3
  97.0 1.4 fusion.3
  98.5 0.0 copy-start.2
  98.5 0.0 copy-start.4
  98.5 0.0 copy-start.5
  98.5 3.7 %all-to-all-start.4 = ((f32[2,768,128]{1,2,0:T(8,128)}), f32[2,768,128]{1,2,0:T(8,128)S(1)}, u32[]{:S(2)}, u32[]{:S(2)}) async-start(f32[2,768,128]{1,2,0:T(8,128)} %bitcast.13), calls=%async_computation.4 | async-start | bytes 1572864 | tf_op jit(solution)/shard_map/all_to_all | solution.py:39
  102.2 9.6 %all-to-all-done.4 = f32[2,768,128]{1,2,0:T(8,128)S(1)} async-done(((f32[2,768,128]{1,2,0:T(8,128)}), f32[2,768,128]{1,2,0:T(8,128)S(1)}, u32[]{:S(2)}, u32[]{:S(2)}) %all-to-all-start.4) | async-done | bytes 786464 | tf_op jit(solution)/shard_map/all_to_all | solution.py:39
  111.7 0.1 reduce_sum.27
  111.8 0.2 copy.24
  112.0 2.4 %broadcast_in_dim.42 = f32[64,128,128]{2,1,0:T(8,128)} broadcast(f32[]{:T(128)} %constant.13.clone.1), dimensions={} | broadcast | bytes 4194308 | tf_op jit(solution)/shard_map/broadcast_in_dim | solution.py:108
  114.4 2.6 %scatter_fusion = f32[64,128,128]{2,1,0:T(8,128)} fusion(f32[64,128,128]{2,1,0:T(8,128)} %broadcast_in_dim.42, s32[6]{0:T(128)S(1)} %fusion.11, f32[6,128,128]{2,1,0:T(8,128)S(1)} %bitcast.53), kind=kCustom, calls=%fused_computation.1 | custom fusion | flops 98304 | bytes 1179672 | tf_op jit(solution)/shard_map/scatter-add | solution.py:111
  117.0 0.0 copy-done.2
  117.0 0.0 copy-done.4
  117.0 0.0 copy-done.5
  117.0 1.4 add_dynamic-update-slice_fusion
  118.4 2.5 %copy.25 = f32[2,64,64,128]{3,2,1,0:T(8,128)S(1)} copy(f32[2,64,64,128]{3,2,0,1:T(8,128)} %bitcast.50) | data formatting | bytes 8388608 | tf_op jit(solution)/shard_map/transpose | solution.py:34
  120.9 9.9 %all_to_all.48 = f32[2,64,64,128]{3,2,1,0:T(8,128)} all-to-all(f32[2,64,64,128]{3,2,1,0:T(8,128)S(1)} %copy.25), channel_id=1, replica_groups=mesh['scen_0'=4,'scen_1'=4,'scen_2'=4,'rootr'=2,'rootc'=2] {'rootr'}, dimensions={0} | all-to-all | bytes 8388608 | tf_op jit(solution)/shard_map/all_to_all | solution.py:39
  130.9 2.8 %reduce_sum.28 = f32[64,64,128]{2,1,0:T(8,128)S(1)} reduce(f32[2,64,64,128]{3,2,1,0:T(8,128)} %all_to_all.48, f32[]{:T(128)} %constant.13.clone.1), dimensions={0}, to_apply=%region_2.3 | reduce | flops 524288 | bytes 6291460 | tf_op jit(solution)/shard_map/reduce_sum | solution.py:40
  133.6 57.7 %all_to_all.49 = f32[64,64,128]{2,1,0:T(8,128)} all-to-all(f32[64,64,128]{2,1,0:T(8,128)S(1)} %reduce_sum.28), channel_id=1, replica_groups=mesh['scen_0'=4,'scen_1'=4,'scen_2'=4,'rootr'=2,'rootc'=2] {'scen_0','sc..., dimensions={0} | all-to-all | bytes 4194304 | tf_op jit(solution)/shard_map/all_to_all | solution.py:47
  191.4 1.7 reduce_sum.29
  193.1 0.2 broadcast_in_dim.49
  193.4 33.0 %all_to_all.50 = bf16[64,64,128]{2,1,0:T(8,128)(2,1)S(1)} all-to-all(bf16[64,64,128]{2,1,0:T(8,128)(2,1)S(1)} %broadcast_in_dim.49), channel_id=1, replica_groups=mesh['scen_0'=4,'scen_1'=4,'scen_2'=4,'rootr'=2,'rootc'=2] {'scen_0','sc..., dimensions={0} | all-to-all | bytes 2097152 | tf_op jit(solution)/shard_map/all_to_all | solution.py:19
  226.4 0.6 broadcast_in_dim.50
  227.0 7.9 %all_to_all.51 = bf16[2,64,64,128]{3,2,1,0:T(8,128)(2,1)S(1)} all-to-all(bf16[2,64,64,128]{3,2,1,0:T(8,128)(2,1)S(1)} %broadcast_in_dim.50), channel_id=1, replica_groups=mesh['scen_0'=4,'scen_1'=4,'scen_2'=4,'rootr'=2,'rootc'=2] {'rootr'}, dimensions={0} | all-to-all | bytes 4194304 | tf_op jit(solution)/shard_map/all_to_all | solution.py:19
  234.9 0.2 copy.30
  235.1 0.0 copy-done
  235.1 1.1 fusion.4
  (6 shorter events, 0.0 us)
Async XLA Ops:
  0.0 235.1 %copy-start = (bf16[64,8192]{1,0:T(8,128)(2,1)S(1)}, bf16[64,8192]{1,0:T(8,128)(2,1)}, u32[]{:S(2)}) copy-start(bf16[64,8192]{1,0:T(8,128)(2,1)} %param.11) | copy-start | bytes 3145732
  0.0 23.4 %copy-start.6 = (s32[1,6]{1,0:T(1,128)S(1)}, s32[1,6]{1,0:T(1,128)}, u32[]{:S(2)}) copy-start(s32[1,6]{1,0:T(1,128)} %param.15) | copy-start | bytes 76
  8.8 66.4 %all-to-all-start.1 = ((bf16[64,64,256]{2,1,0:T(8,128)(2,1)}), bf16[64,64,256]{2,1,0:T(8,128)(2,1)S(1)}, u32[]{:S(2)}, u32[]{:S(2)}) async-start(bf16[64,64,256]{2,1,0:T(8,128)(2,1)} %broadcast_in_dim.45), calls=%async_computation.1 | async-start | bytes 4194304 | tf_op jit(solution)/shard_map/all_to_all | solution.py:19
  84.2 5.0 %copy-start.1 = (bf16[1,256,768]{2,1,0:T(8,128)(2,1)S(1)}, bf16[1,256,768]{2,1,0:T(8,128)(2,1)}, u32[]{:S(2)}) copy-start(bf16[1,256,768]{2,1,0:T(8,128)(2,1)} %param.12) | copy-start | bytes 1179652
  84.2 12.8 %copy-start.3 = (bf16[1,256,512]{2,1,0:T(8,128)(2,1)S(1)}, bf16[1,256,512]{2,1,0:T(8,128)(2,1)}, u32[]{:S(2)}) copy-start(bf16[1,256,512]{2,1,0:T(8,128)(2,1)} %param.13) | copy-start | bytes 786436
  98.5 18.5 %copy-start.2 = (f32[64,128]{1,0:T(8,128)S(1)}, f32[64,128]{1,0:T(8,128)}, u32[]{:S(2)}) copy-start(f32[64,128]{1,0:T(8,128)} %param.8) | copy-start | bytes 98308
  98.5 18.5 %copy-start.4 = (f32[64,128]{1,0:T(8,128)S(1)}, f32[64,128]{1,0:T(8,128)}, u32[]{:S(2)}) copy-start(f32[64,128]{1,0:T(8,128)} %param.9) | copy-start | bytes 98308
  98.5 18.5 %copy-start.5 = (f32[64]{0:T(128)S(1)}, f32[64]{0:T(128)}, u32[]{:S(2)}) copy-start(f32[64]{0:T(128)} %param.10) | copy-start | bytes 772
  98.5 13.3 %all-to-all-start.4 = ((f32[2,768,128]{1,2,0:T(8,128)}), f32[2,768,128]{1,2,0:T(8,128)S(1)}, u32[]{:S(2)}, u32[]{:S(2)}) async-start(f32[2,768,128]{1,2,0:T(8,128)} %bitcast.13), calls=%async_computation.4 | async-start | bytes 1572864 | tf_op jit(solution)/shard_map/all_to_all | solution.py:39
where the time goes:
time: 237 us; the launch traced here: 236 us
  blocking collectives  131 us (55%)
  waiting for transfers between devices  61.3 us (26%)
  starting transfers between devices  17.6 us (7%)
  local copies, waits for them, and re-layouts  13.4 us (6%)
  other arithmetic  9.45 us (4%)
  matrix products  2.88 us (1%)
    all_to_all x5, blocking collectives, from_everyone(): return lax.all_to_all(copies, axis, split_axis=0, concat_axis=0, tiled=True)  63.1 us
    all_to_all x1, blocking collectives, sum_by_axis(): lax.all_to_all(nearer, far, split_axis=0, concat_axis=0, tiled=True)  57.7 us
    all_to_all x1, waiting for transfers between devices, from_everyone(): return lax.all_to_all(copies, axis, split_axis=0, concat_axis=0, tiled=True)  51.7 us
    all_to_all x1, starting transfers between devices, from_everyone(): return lax.all_to_all(copies, axis, split_axis=0, concat_axis=0, tiled=True)  13.9 us
    all_to_all x1, blocking collectives, summed_on_arrival(): lax.all_to_all(pieces, axis, split_axis=0, concat_axis=0, tiled=True)  9.94 us
    all_to_all x1, waiting for transfers between devices, summed_on_arrival(): lax.all_to_all(pieces, axis, split_axis=0, concat_axis=0, tiled=True)  9.58 us
  transfers between devices with their start and end apart: 2, of which 2 were waited for; matrix products, arithmetic and copies ran while one was open for 0% of the time, Pallas kernels for 0%

commit v1 on v0

v1 whole, which is shorter than its diff:
```python
import functools

import jax
import jax.numpy as jnp
from jax import lax
from jax.experimental import pallas as pl
from jax.experimental.pallas import tpu as pltpu
from jax.sharding import Mesh
from jax.sharding import PartitionSpec as P

TILE = 128
HALF = 64
RING = 4
Y, X, Z, CORE, SIDE = "scen_0", "scen_1", "scen_2", "rootr", "rootc"
SCEN_ROOTR = (Y, X, Z, CORE)
SWAP = [(0, 1), (1, 0)]
F32 = jnp.float32
BF16 = jnp.bfloat16

VMEM = pl.BlockSpec(memory_space=pltpu.VMEM)
SMEM = pl.BlockSpec(memory_space=pltpu.SMEM)


def swap(value, axis):
    return lax.ppermute(value, axis, SWAP)


def from_ahead(value, axis, distance):
    return lax.ppermute(value, axis, [(i, (i - distance) % RING) for i in range(RING)])


def to_ahead(value, axis, distance):
    return lax.ppermute(value, axis, [(i, (i + distance) % RING) for i in range(RING)])


def ring_pieces(value, axis):
    return [value] + [from_ahead(value, axis, k) for k in range(1, RING)]


def ring_gather(value):
    line = jnp.stack(ring_pieces(value, Z))
    plane = jnp.concatenate(ring_pieces(line, X))
    return ring_pieces(plane, Y)


def place(tile, where):
    dy = (tile // 16 - where[0]) % RING
    dx = ((tile // 4) % 4 - where[1]) % RING
    dz = (tile % 4 - where[2]) % RING
    return dy, dx * 4 + dz


def pick_kernel(where, own_ids, other_ids, p0, p1, p2, p3, own_ref, other_ref):
    pieces = (p0, p1, p2, p3)
    for ids, out in ((other_ids, other_ref), (own_ids, own_ref)):
        for j in range(ids.shape[1]):
            dy, rest = place(ids[0, j], where)
            for k, piece in enumerate(pieces):

                @pl.when(dy == k)
                def _():
                    out[j] = piece[rest]


def scenario_kernel(
    where, count, own_picked, other_picked, border_own, border_other, inverse_own, inverse_other,
    keep_ref, send_ref, picked, values,
):
    core, side = where[3], where[4]
    half_rows = border_own.shape[0]
    tiles = own_picked.shape[0]
    for j in range(tiles):
        picked[pl.ds(pl.multiple_of(j * TILE + core * HALF, HALF), HALF), :] = own_picked[j]
        picked[pl.ds(pl.multiple_of(j * TILE + (1 - core) * HALF, HALF), HALF), :] = other_picked[j]
    rows = lax.broadcasted_iota(jnp.int32, (half_rows, values.shape[1]), 0)
    own_start = pl.multiple_of(side * half_rows, half_rows)
    other_start = pl.multiple_of((1 - side) * half_rows, half_rows)
    live = count[0]

    def masked(product, start):
        return jnp.where(rows + start < live, product, 0.0).astype(BF16)

    whole = picked[...]
    values[pl.ds(own_start, half_rows), :] = masked(
        jnp.dot(border_own[...], whole, preferred_element_type=F32), own_start
    )
    values[pl.ds(other_start, half_rows), :] = masked(
        jnp.dot(border_other[...], whole, preferred_element_type=F32), other_start
    )
    operand = values[...]
    solved_own = masked(jnp.dot(inverse_own[...], operand, preferred_element_type=F32), own_start)
    solved_other = masked(jnp.dot(inverse_other[...], operand, preferred_element_type=F32), other_start)
    numbers = (((0,), (0,)), ((), ()))
    term = lax.dot_general(border_own[...], solved_own, numbers, preferred_element_type=F32)
    term += lax.dot_general(border_other[...], solved_other, numbers, preferred_element_type=F32)
    term = term.reshape(tiles, 2, HALF, term.shape[1])

    @pl.when(core == 0)
    def _():
        keep_ref[...] = term[:, 0]
        send_ref[...] = term[:, 1]

    @pl.when(core == 1)
    def _():
        keep_ref[...] = term[:, 1]
        send_ref[...] = term[:, 0]


def scatter_kernel(where, own_ids, other_ids, keep, arrived, near, c1, c2, c3, total):
    total[...] = jnp.zeros_like(total)
    for ids, terms in ((own_ids, keep), (other_ids, arrived)):
        for j in range(ids.shape[1]):
            dy, rest = place(ids[0, j], where)
            total[dy * 16 + rest] += terms[j]
    near[...] = total[0:16]
    for k, chunk in enumerate((c1, c2, c3)):
        chunk[...] = total[16 * (k + 1) : 16 * (k + 2)].astype(BF16)


def update_kernel(where, start, precond, *refs):
    pieces, (out_ref, whole) = refs[:8], refs[8:]
    y, x, z, core = where[0], where[1], where[2], where[3]
    for side in range(2):
        half = core if side == 0 else 1 - core
        for k in range(RING):
            piece = pieces[side * RING + k]
            base_y = ((y + k) % RING) * 16
            for i in range(RING):
                base_x = base_y + ((x + i) % RING) * 4
                for j in range(RING):
                    tile = base_x + (z + j) % RING
                    at = pl.multiple_of(tile * TILE + half * HALF, HALF)
                    whole[pl.ds(at, HALF), :] = piece[i * RING + j]
    out_ref[...] = start[...] + jnp.dot(precond[...], whole[...], preferred_element_type=F32)


def call(kernel, specs, outs, scratch=(), flops=0, moved=0):
    return pl.pallas_call(
        kernel,
        out_shape=outs,
        in_specs=specs,
        out_specs=jax.tree.map(lambda _: VMEM, outs),
        scratch_shapes=scratch,
        cost_estimate=pl.CostEstimate(flops=flops, bytes_accessed=moved, transcendentals=0),
        compiler_params=pltpu.CompilerParams(vmem_limit_bytes=32 * 1024 * 1024),
    )


def local(
    start_guess,
    right_side,
    root_diagonal,
    preconditioner,
    border_block,
    coupling_inverse,
    border_count,
    column_tiles,
):
    rows, cols = start_guess.shape
    shape = jax.ShapeDtypeStruct
    where = jnp.stack([lax.axis_index(a) for a in (Y, X, Z, CORE, SIDE)]).astype(jnp.int32)
    border, inverse = border_block[0], coupling_inverse[0]
    tiles = column_tiles.shape[1]

    pieces = ring_gather(start_guess.astype(BF16))
    other_tiles = swap(column_tiles, CORE)
    border_other = swap(border, SIDE)
    inverse_other = swap(inverse, SIDE)

    own_half, for_other = call(
        pick_kernel,
        [SMEM] * 3 + [VMEM] * 4,
        [shape((tiles, HALF, cols), BF16)] * 2,
    )(where, column_tiles, other_tiles, *pieces)
    other_half = swap(for_other, CORE)
    keep, send = call(
        scenario_kernel,
        [SMEM] * 2 + [VMEM] * 6,
        [shape((tiles, HALF, cols), F32)] * 2,
        [pltpu.VMEM((tiles * TILE, cols), BF16), pltpu.VMEM((2 * border.shape[0], cols), BF16)],
    )(where, border_count, own_half, other_half, border, border_other, inverse, inverse_other)
    arrived = swap(send, CORE)
    chunk = (16, HALF, cols)
    near, c1, c2, c3 = call(
        scatter_kernel,
        [SMEM] * 3 + [VMEM] * 2,
        [shape(chunk, F32)] + [shape(chunk, BF16)] * 3,
        [pltpu.VMEM((64, HALF, cols), F32)],
    )(where, column_tiles, other_tiles, keep, arrived)

    plane = near
    for k, c in enumerate((c1, c2, c3)):
        plane = plane + to_ahead(c, Y, k + 1).astype(F32)
    plane = plane.reshape(RING, RING, HALF, cols)
    line = plane[0]
    for k in range(1, RING):
        line = line + to_ahead(plane[k].astype(BF16), X, k).astype(F32)
    total = line[0]
    for k in range(1, RING):
        total = total + to_ahead(line[k].astype(BF16), Z, k).astype(F32)
    residual = right_side - root_diagonal[:, None] * start_guess + total

    mine = ring_gather(residual.astype(BF16))
    partners = [swap(piece, CORE) for piece in mine]
    return call(
        update_kernel,
        [SMEM] + [VMEM] * 10,
        shape((rows, cols), F32),
        [pltpu.VMEM((preconditioner.shape[1], cols), BF16)],
    )(where, start_guess, preconditioner, *mine, *partners)


def solution(mesh):
    torus = Mesh(
        mesh.devices.reshape(RING, RING, RING, mesh.shape["rootr"], mesh.shape["rootc"]),
        (Y, X, Z, CORE, SIDE),
    )
    in_specs = (
        P(SCEN_ROOTR, SIDE),
        P(SCEN_ROOTR, SIDE),
        P(SCEN_ROOTR),
        P(SCEN_ROOTR, None),
        P(SCEN_ROOTR, SIDE, None),
        P(SCEN_ROOTR, SIDE, None),
        P(SCEN_ROOTR),
        P(SCEN_ROOTR, None),
    )
    return jax.shard_map(
        local, mesh=torus, in_specs=in_specs, out_specs=P(SCEN_ROOTR, SIDE), check_vma=False
    )
```

time: 237 us -> 113 us (0.48)
  blocking collectives: 131 us -> 0 us
  starting transfers between devices: 17.6 us -> 75.5 us
  waiting for transfers between devices: 61.3 us -> 29.7 us
  local copies, waits for them, and re-layouts: 13.4 us -> 0.27 us
  other arithmetic: 9.45 us -> 1.07 us
  Pallas kernels: 0 us -> 5.5 us
  matrix products: 2.88 us -> 0 us
    all_to_all x7 -> x0, blocking collectives: 131 us -> none  [the longest x5 63.1 us: from_everyone(): return lax.all_to_all(copies, axis, split_axis=0, concat_axis=0, tiled=True)]
    ppermute x0 -> x36, starting transfers between devices: none -> 75.5 us  [the longest x18 34.7 us: from_ahead(): lax.ppermute(value, axis, [(i, (i - distance) % RING) for i in range(RING)])]
    all_to_all x2 -> x0, waiting for transfers between devices: 61.3 us -> none  [the longest x1 51.7 us: from_everyone(): return lax.all_to_all(copies, axis, split_axis=0, concat_axis=0, tiled=True)]
    ppermute x0 -> x36, waiting for transfers between devices: none -> 29.7 us  [the longest x9 18.6 us: to_ahead(): lax.ppermute(value, axis, [(i, (i + distance) % RING) for i in range(RING)])]
    all_to_all x2 -> x0, starting transfers between devices: 17.6 us -> none  [the longest x1 13.9 us: from_everyone(): return lax.all_to_all(copies, axis, split_axis=0, concat_axis=0, tiled=True)]
    pallas_call x0 -> x4, Pallas kernels: none -> 5.5 us  [the longest x1 1.9 us: local(): call(update_kernel, [SMEM] + [VMEM] * 10, shape((rows, cols), F32), [pltp...]
    broadcast_in_dim x7 -> x0, local copies, waits for them, and re-layouts: 5.41 us -> none  [the longest x6 2.97 us: from_everyone(): copies = jnp.broadcast_to(shard, (lax.axis_size(axis), *shard.shape))]
    reduce_sum x3 -> x0, other arithmetic: 4.56 us -> none  [the longest x2 2.83 us: summed_on_arrival(): return arrived.sum(axis=0)]
  transfers between devices with their start and end apart: 2 -> 36, of which waited for: 2 -> 16; matrix products, arithmetic and copies ran while one was open for 0% -> 0% of each run, Pallas kernels for 0% -> 1%
where the time goes in v1:
time: 113 us
  starting transfers between devices  75.5 us (67%)
  waiting for transfers between devices  29.7 us (26%)
  Pallas kernels  5.5 us (5%)
    ppermute x18, starting transfers between devices, from_ahead(): lax.ppermute(value, axis, [(i, (i - distance) % RING) for i in range(RING)])  34.7 us
    ppermute x9, starting transfers between devices, swap(): return lax.ppermute(value, axis, SWAP)  26.5 us
    ppermute x9, waiting for transfers between devices, to_ahead(): lax.ppermute(value, axis, [(i, (i + distance) % RING) for i in range(RING)])  18.6 us
    ppermute x9, starting transfers between devices, to_ahead(): lax.ppermute(value, axis, [(i, (i + distance) % RING) for i in range(RING)])  14.4 us
    ppermute x18, waiting for transfers between devices, from_ahead(): lax.ppermute(value, axis, [(i, (i - distance) % RING) for i in range(RING)])  7.4 us
    ppermute x9, waiting for transfers between devices, swap(): return lax.ppermute(value, axis, SWAP)  3.69 us
  transfers between devices with their start and end apart: 36, of which 16 were waited for; matrix products, arithmetic and copies ran while one was open for 0% of the time, Pallas kernels for 1%

profile of v1, /device:TPU:1, one launch (start us, length us, event | category | flops | bytes accessed | tf_op | source)
XLA Modules:
  0.0 112.9 jit_solution(8281424237502203479)
XLA Ops:
  0.0 0.8 constant_dynamic-update-slice_fusion.6
  0.8 3.8 %collective-permute-start.3 = (bf16[64,128]{1,0:T(8,128)(2,1)S(1)}, bf16[64,128]{1,0:T(8,128)(2,1)S(1)}, u32[]{:S(2)}, u32[]{:S(2)}) collective-permute-start(bf16[64,128]{1,0:T(8,128)(2,1)S(1)} %get-tuple-element.28), channel_id=1, source_target_pairs={{0,4},{4,8},{8,12},{12,0},{1,5},{5,9},{9,13},{13,1},{2,6},{6,10},{... | collective-permute-start | bytes 49160 | tf_op jit(solution)/shard_map/ppermute | solution.py:29
  4.6 5.1 %collective-permute-start.2 = (bf16[64,128]{1,0:T(8,128)(2,1)S(1)}, bf16[64,128]{1,0:T(8,128)(2,1)S(1)}, u32[]{:S(2)}, u32[]{:S(2)}) collective-permute-start(bf16[64,128]{1,0:T(8,128)(2,1)S(1)} %get-tuple-element.28), channel_id=1, source_target_pairs={{0,8},{4,12},{8,0},{12,4},{1,9},{5,13},{9,1},{13,5},{2,10},{6,14},... | collective-permute-start | bytes 49160 | tf_op jit(solution)/shard_map/ppermute | solution.py:29
  9.7 2.4 %collective-permute-start.1 = (bf16[64,128]{1,0:T(8,128)(2,1)S(1)}, bf16[64,128]{1,0:T(8,128)(2,1)S(1)}, u32[]{:S(2)}, u32[]{:S(2)}) collective-permute-start(bf16[64,128]{1,0:T(8,128)(2,1)S(1)} %get-tuple-element.28), channel_id=1, source_target_pairs={{0,12},{4,0},{8,4},{12,8},{1,13},{5,1},{9,5},{13,9},{2,14},{6,2},{... | collective-permute-start | bytes 49160 | tf_op jit(solution)/shard_map/ppermute | solution.py:29
  12.1 0.7 collective-permute-start.11
  13.2 1.3 %collective-permute-start.6 = (bf16[4,64,128]{2,1,0:T(8,128)(2,1)S(1)}, bf16[4,64,128]{2,1,0:T(8,128)(2,1)S(1)}, u32[]{:S(2)}, u32[]{:S(2)}) collective-permute-start(bf16[4,64,128]{2,1,0:T(8,128)(2,1)S(1)} %pad_maximum_fusion), channel_id=1, source_target_pairs={{0,16},{16,32},{32,48},{48,0},{1,17},{17,33},{33,49},{49,1},{2,18}... | collective-permute-start | bytes 196616 | tf_op jit(solution)/shard_map/ppermute | solution.py:29
  14.5 2.5 %collective-permute-start.5 = (bf16[4,64,128]{2,1,0:T(8,128)(2,1)S(1)}, bf16[4,64,128]{2,1,0:T(8,128)(2,1)S(1)}, u32[]{:S(2)}, u32[]{:S(2)}) collective-permute-start(bf16[4,64,128]{2,1,0:T(8,128)(2,1)S(1)} %pad_maximum_fusion), channel_id=1, source_target_pairs={{0,32},{16,48},{32,0},{48,16},{1,33},{17,49},{33,1},{49,17},{2,34}... | collective-permute-start | bytes 196616 | tf_op jit(solution)/shard_map/ppermute | solution.py:29
  17.0 1.2 %collective-permute-start.4 = (bf16[4,64,128]{2,1,0:T(8,128)(2,1)S(1)}, bf16[4,64,128]{2,1,0:T(8,128)(2,1)S(1)}, u32[]{:S(2)}, u32[]{:S(2)}) collective-permute-start(bf16[4,64,128]{2,1,0:T(8,128)(2,1)S(1)} %pad_maximum_fusion), channel_id=1, source_target_pairs={{0,48},{16,0},{32,16},{48,32},{1,49},{17,1},{33,17},{49,33},{2,50}... | collective-permute-start | bytes 196616 | tf_op jit(solution)/shard_map/ppermute | solution.py:29
  18.1 2.2 %collective-permute-done.4 = bf16[4,64,128]{2,1,0:T(8,128)(2,1)S(1)} collective-permute-done((bf16[4,64,128]{2,1,0:T(8,128)(2,1)S(1)}, bf16[4,64,128]{2,1,0:T(8,128)(2,1)S(1)}, u32[]{:S(2)}, u32[]{:S(2)}) %collective-permute-start.4) | collective-permute-done | bytes 65568 | tf_op jit(solution)/shard_map/ppermute | solution.py:29
  20.4 1.4 %collective-permute-start.9 = (bf16[16,64,128]{2,1,0:T(8,128)(2,1)S(1)}, bf16[16,64,128]{2,1,0:T(8,128)(2,1)S(1)}, u32[]{:S(2)}, u32[]{:S(2)}) collective-permute-start(bf16[16,64,128]{2,1,0:T(8,128)(2,1)S(1)} %constant_dynamic-update-slice_fusion.p0), channel_id=1, source_target_pairs={{0,64},{64,128},{128,192},{192,0},{1,65},{65,129},{129,193},{193,1... | collective-permute-start | bytes 786440 | tf_op jit(solution)/shard_map/ppermute | solution.py:29
  21.8 2.6 %collective-permute-start.8 = (bf16[16,64,128]{2,1,0:T(8,128)(2,1)S(1)}, bf16[16,64,128]{2,1,0:T(8,128)(2,1)S(1)}, u32[]{:S(2)}, u32[]{:S(2)}) collective-permute-start(bf16[16,64,128]{2,1,0:T(8,128)(2,1)S(1)} %constant_dynamic-update-slice_fusion.p0), channel_id=1, source_target_pairs={{0,128},{64,192},{128,0},{192,64},{1,129},{65,193},{129,1},{193,65... | collective-permute-start | bytes 786440 | tf_op jit(solution)/shard_map/ppermute | solution.py:29
  24.4 1.1 collective-permute-start.7
  25.5 4.7 %collective-permute-start = (s32[1,6]{1,0:T(1,128)S(1)}, s32[1,6]{1,0:T(1,128)S(1)}, u32[]{:S(2)}, u32[]{:S(2)}) collective-permute-start(s32[1,6]{1,0:T(1,128)S(1)} %copy-done.4), channel_id=1, source_target_pairs={{0,2},{2,0},{1,3},{3,1},{4,6},{6,4},{5,7},{7,5},{8,10},{10,8},{9,1... | collective-permute-start | bytes 80 | tf_op jit(solution)/shard_map/ppermute | solution.py:25
  30.3 0.8 collective-permute-done.other_ids
  31.1 0.8 collective-permute-start.12
  32.2 1.0 shard_map.82
  33.2 5.2 %collective-permute-start.10 = (bf16[6,64,128]{2,1,0:T(8,128)(2,1)S(1)}, bf16[6,64,128]{2,1,0:T(8,128)(2,1)S(1)}, u32[]{:S(2)}, u32[]{:S(2)}) collective-permute-start(bf16[6,64,128]{2,1,0:T(8,128)(2,1)S(1)} %get-tuple-element.14), channel_id=1, source_target_pairs={{0,2},{2,0},{1,3},{3,1},{4,6},{6,4},{5,7},{7,5},{8,10},{10,8},{9,1... | collective-permute-start | bytes 294920 | tf_op jit(solution)/shard_map/ppermute | solution.py:25
  39.4 1.6 %shard_map.83 = (f32[6,64,128]{2,1,0:T(8,128)S(1)}, f32[6,64,128]{2,1,0:T(8,128)S(1)}) custom-call(s32[5]{0:T(128)S(1)} %stack.53.where, s32[1]{0:T(128)S(6)} %copy.21.count, bf16[6,64,128]{2,1,0:T(8,128)(2,1)S(1)} %get-tuple-element.13.own_picked, bf16[6,64,128]{2,1,0:T(8,128)(2,1)S(1)} %collective-permute-done.10.other_picked, ...), custom_call_target="tpu_custom_call" | custom-call | tf_op jit(solution)/shard_map/pallas_call | solution.py:176
  41.5 1.1 collective-permute-done.13.arrived
  42.5 1.0 shard_map.84
  43.5 1.0 collective-permute-start.14
  44.5 2.1 %collective-permute-start.15 = (bf16[16,64,128]{2,1,0:T(8,128)(2,1)S(1)}, bf16[16,64,128]{2,1,0:T(8,128)(2,1)S(1)}, u32[]{:S(2)}, u32[]{:S(2)}) collective-permute-start(bf16[16,64,128]{2,1,0:T(8,128)(2,1)S(1)} %get-tuple-element.19), channel_id=1, source_target_pairs={{0,128},{64,192},{128,0},{192,64},{1,129},{65,193},{129,1},{193,65... | collective-permute-start | bytes 786440 | tf_op jit(solution)/shard_map/ppermute | solution.py:33
  46.7 1.3 %collective-permute-start.16 = (bf16[16,64,128]{2,1,0:T(8,128)(2,1)S(1)}, bf16[16,64,128]{2,1,0:T(8,128)(2,1)S(1)}, u32[]{:S(2)}, u32[]{:S(2)}) collective-permute-start(bf16[16,64,128]{2,1,0:T(8,128)(2,1)S(1)} %get-tuple-element.20), channel_id=1, source_target_pairs={{0,192},{64,0},{128,64},{192,128},{1,193},{65,1},{129,65},{193,129... | collective-permute-start | bytes 786440 | tf_op jit(solution)/shard_map/ppermute | solution.py:33
  48.0 4.4 %collective-permute-done.14 = bf16[16,64,128]{2,1,0:T(8,128)(2,1)S(1)} collective-permute-done((bf16[16,64,128]{2,1,0:T(8,128)(2,1)S(1)}, bf16[16,64,128]{2,1,0:T(8,128)(2,1)S(1)}, u32[]{:S(2)}, u32[]{:S(2)}) %collective-permute-start.14) | collective-permute-done | bytes 262176 | tf_op jit(solution)/shard_map/ppermute | solution.py:33
  52.4 6.0 %collective-permute-done.15 = bf16[16,64,128]{2,1,0:T(8,128)(2,1)S(1)} collective-permute-done((bf16[16,64,128]{2,1,0:T(8,128)(2,1)S(1)}, bf16[16,64,128]{2,1,0:T(8,128)(2,1)S(1)}, u32[]{:S(2)}, u32[]{:S(2)}) %collective-permute-start.15) | collective-permute-done | bytes 262176 | tf_op jit(solution)/shard_map/ppermute | solution.py:33
  58.8 2.5 %collective-permute-start.19 = (bf16[4,64,128]{2,1,0:T(8,128)(2,1)S(1)}, bf16[4,64,128]{2,1,0:T(8,128)(2,1)S(1)}, u32[]{:S(2)}, u32[]{:S(2)}) collective-permute-start(bf16[4,64,128]{2,1,0:T(8,128)(2,1)S(1)} %get-tuple-element.30), channel_id=1, source_target_pairs={{0,48},{16,0},{32,16},{48,32},{1,49},{17,1},{33,17},{49,33},{2,50}... | collective-permute-start | bytes 196616 | tf_op jit(solution)/shard_map/ppermute | solution.py:33
  61.3 0.8 collective-permute-start.18
  62.1 0.9 collective-permute-done.17
  63.0 3.5 %collective-permute-done.18 = bf16[4,64,128]{2,1,0:T(8,128)(2,1)S(1)} collective-permute-done((bf16[4,64,128]{2,1,0:T(8,128)(2,1)S(1)}, bf16[4,64,128]{2,1,0:T(8,128)(2,1)S(1)}, u32[]{:S(2)}, u32[]{:S(2)}) %collective-permute-start.18) | collective-permute-done | bytes 65568 | tf_op jit(solution)/shard_map/ppermute | solution.py:33
  66.5 1.9 %collective-permute-start.20 = (bf16[64,128]{1,0:T(8,128)(2,1)S(1)}, bf16[64,128]{1,0:T(8,128)(2,1)S(1)}, u32[]{:S(2)}, u32[]{:S(2)}) collective-permute-start(bf16[64,128]{1,0:T(8,128)(2,1)S(1)} %get-tuple-element.32), channel_id=1, source_target_pairs={{0,4},{4,8},{8,12},{12,0},{1,5},{5,9},{9,13},{13,1},{2,6},{6,10},{... | collective-permute-start | bytes 49160 | tf_op jit(solution)/shard_map/ppermute | solution.py:33
  68.4 1.9 %collective-permute-start.22 = (bf16[64,128]{1,0:T(8,128)(2,1)S(1)}, bf16[64,128]{1,0:T(8,128)(2,1)S(1)}, u32[]{:S(2)}, u32[]{:S(2)}) collective-permute-start(bf16[64,128]{1,0:T(8,128)(2,1)S(1)} %get-tuple-element.33), channel_id=1, source_target_pairs={{0,12},{4,0},{8,4},{12,8},{1,13},{5,1},{9,5},{13,9},{2,14},{6,2},{... | collective-permute-start | bytes 49160 | tf_op jit(solution)/shard_map/ppermute | solution.py:33
  70.2 2.6 %collective-permute-start.21 = (bf16[64,128]{1,0:T(8,128)(2,1)S(1)}, bf16[64,128]{1,0:T(8,128)(2,1)S(1)}, u32[]{:S(2)}, u32[]{:S(2)}) collective-permute-start(bf16[64,128]{1,0:T(8,128)(2,1)S(1)} %get-tuple-element.34), channel_id=1, source_target_pairs={{0,8},{4,12},{8,0},{12,4},{1,9},{5,13},{9,1},{13,5},{2,10},{6,14},... | collective-permute-start | bytes 49160 | tf_op jit(solution)/shard_map/ppermute | solution.py:33
  72.9 3.9 %collective-permute-done.21 = bf16[64,128]{1,0:T(8,128)(2,1)S(1)} collective-permute-done((bf16[64,128]{1,0:T(8,128)(2,1)S(1)}, bf16[64,128]{1,0:T(8,128)(2,1)S(1)}, u32[]{:S(2)}, u32[]{:S(2)}) %collective-permute-start.21) | collective-permute-done | bytes 16416 | tf_op jit(solution)/shard_map/ppermute | solution.py:33
  76.9 0.5 collective-permute-start.25
  77.4 3.9 %collective-permute-start.24 = (bf16[64,128]{1,0:T(8,128)(2,1)S(1)}, bf16[64,128]{1,0:T(8,128)(2,1)S(1)}, u32[]{:S(2)}, u32[]{:S(2)}) collective-permute-start(bf16[64,128]{1,0:T(8,128)(2,1)S(1)} %get-tuple-element.22), channel_id=1, source_target_pairs={{0,8},{4,12},{8,0},{12,4},{1,9},{5,13},{9,1},{13,5},{2,10},{6,14},... | collective-permute-start | bytes 49160 | tf_op jit(solution)/shard_map/ppermute | solution.py:29
  81.3 1.9 %collective-permute-start.23 = (bf16[64,128]{1,0:T(8,128)(2,1)S(1)}, bf16[64,128]{1,0:T(8,128)(2,1)S(1)}, u32[]{:S(2)}, u32[]{:S(2)}) collective-permute-start(bf16[64,128]{1,0:T(8,128)(2,1)S(1)} %get-tuple-element.22), channel_id=1, source_target_pairs={{0,12},{4,0},{8,4},{12,8},{1,13},{5,1},{9,5},{13,9},{2,14},{6,2},{... | collective-permute-start | bytes 49160 | tf_op jit(solution)/shard_map/ppermute | solution.py:29
  83.2 0.7 collective-permute-done.24
  83.9 0.8 collective-permute-done.23
  84.9 2.1 %collective-permute-start.27 = (bf16[4,64,128]{2,1,0:T(8,128)(2,1)S(1)}, bf16[4,64,128]{2,1,0:T(8,128)(2,1)S(1)}, u32[]{:S(2)}, u32[]{:S(2)}) collective-permute-start(bf16[4,64,128]{2,1,0:T(8,128)(2,1)S(1)} %pad_maximum_fusion.1), channel_id=1, source_target_pairs={{0,32},{16,48},{32,0},{48,16},{1,33},{17,49},{33,1},{49,17},{2,34}... | collective-permute-start | bytes 196616 | tf_op jit(solution)/shard_map/ppermute | solution.py:29
  86.9 0.6 collective-permute-start.26
  87.6 3.0 %collective-permute-done.26 = bf16[4,64,128]{2,1,0:T(8,128)(2,1)S(1)} collective-permute-done((bf16[4,64,128]{2,1,0:T(8,128)(2,1)S(1)}, bf16[4,64,128]{2,1,0:T(8,128)(2,1)S(1)}, u32[]{:S(2)}, u32[]{:S(2)}) %collective-permute-start.26) | collective-permute-done | bytes 65568 | tf_op jit(solution)/shard_map/ppermute | solution.py:29
  90.6 1.8 %collective-permute-start.31 = (bf16[16,64,128]{2,1,0:T(8,128)(2,1)S(1)}, bf16[16,64,128]{2,1,0:T(8,128)(2,1)S(1)}, u32[]{:S(2)}, u32[]{:S(2)}) collective-permute-start(bf16[16,64,128]{2,1,0:T(8,128)(2,1)S(1)} %constant_dynamic-update-slice_fusion.7.refs_0_), channel_id=1, source_target_pairs={{0,64},{64,128},{128,192},{192,0},{1,65},{65,129},{129,193},{193,1... | collective-permute-start | bytes 786440 | tf_op jit(solution)/shard_map/ppermute | solution.py:29
  92.4 2.3 %collective-permute-start.30 = (bf16[16,64,128]{2,1,0:T(8,128)(2,1)S(1)}, bf16[16,64,128]{2,1,0:T(8,128)(2,1)S(1)}, u32[]{:S(2)}, u32[]{:S(2)}) collective-permute-start(bf16[16,64,128]{2,1,0:T(8,128)(2,1)S(1)} %constant_dynamic-update-slice_fusion.7.refs_0_), channel_id=1, source_target_pairs={{0,128},{64,192},{128,0},{192,64},{1,129},{65,193},{129,1},{193,65... | collective-permute-start | bytes 786440 | tf_op jit(solution)/shard_map/ppermute | solution.py:29
  95.0 8.4 %collective-permute-start.32 = (bf16[16,64,128]{2,1,0:T(8,128)(2,1)S(1)}, bf16[16,64,128]{2,1,0:T(8,128)(2,1)S(1)}, u32[]{:S(2)}, u32[]{:S(2)}) collective-permute-start(bf16[16,64,128]{2,1,0:T(8,128)(2,1)S(1)} %constant_dynamic-update-slice_fusion.7.refs_0_), channel_id=1, source_target_pairs={{0,2},{2,0},{1,3},{3,1},{4,6},{6,4},{5,7},{7,5},{8,10},{10,8},{9,1... | collective-permute-start | bytes 786440 | tf_op jit(solution)/shard_map/ppermute | solution.py:25
  103.3 2.5 %collective-permute-start.35 = (bf16[16,64,128]{2,1,0:T(8,128)(2,1)S(1)}, bf16[16,64,128]{2,1,0:T(8,128)(2,1)S(1)}, u32[]{:S(2)}, u32[]{:S(2)}) collective-permute-start(bf16[16,64,128]{2,1,0:T(8,128)(2,1)S(1)} %collective-permute-done.31.refs_3_), channel_id=1, source_target_pairs={{0,2},{2,0},{1,3},{3,1},{4,6},{6,4},{5,7},{7,5},{8,10},{10,8},{9,1... | collective-permute-start | bytes 786440 | tf_op jit(solution)/shard_map/ppermute | solution.py:25
  105.8 3.7 %collective-permute-start.34 = (bf16[16,64,128]{2,1,0:T(8,128)(2,1)S(1)}, bf16[16,64,128]{2,1,0:T(8,128)(2,1)S(1)}, u32[]{:S(2)}, u32[]{:S(2)}) collective-permute-start(bf16[16,64,128]{2,1,0:T(8,128)(2,1)S(1)} %collective-permute-done.30.refs_2_), channel_id=1, source_target_pairs={{0,2},{2,0},{1,3},{3,1},{4,6},{6,4},{5,7},{7,5},{8,10},{10,8},{9,1... | collective-permute-start | bytes 786440 | tf_op jit(solution)/shard_map/ppermute | solution.py:25
  109.5 1.1 %collective-permute-done.34.refs_6_ = bf16[16,64,128]{2,1,0:T(8,128)(2,1)S(1)} collective-permute-done((bf16[16,64,128]{2,1,0:T(8,128)(2,1)S(1)}, bf16[16,64,128]{2,1,0:T(8,128)(2,1)S(1)}, u32[]{:S(2)}, u32[]{:S(2)}) %collective-permute-start.34) | collective-permute-done | bytes 262176 | tf_op jit(solution)/shard_map/ppermute | solution.py:25
  111.0 1.9 %shard_map.85 = f32[64,128]{1,0:T(8,128)} custom-call(s32[5]{0:T(128)S(1)} %stack.53.where, f32[64,128]{1,0:T(8,128)S(1)} %copy-done.2, bf16[64,8192]{1,0:T(8,128)(2,1)S(1)} %copy-done, bf16[16,64,128]{2,1,0:T(8,128)(2,1)S(1)} %constant_dynamic-update-slice_fusion.7.refs_0_, bf16[16,64,128]{2,1,0:T(8,128)(2,1)S(1)} %collective-permute-done.29.refs_1_, ...), custom_call_target="tpu_custom_call" | custom-call | tf_op jit(solution)/shard_map/pallas_call | solution.py:205
  (63 shorter events, 3.0 us)
Async XLA Ops:
  0.8 12.1 %collective-permute-start.3 = (bf16[64,128]{1,0:T(8,128)(2,1)S(1)}, bf16[64,128]{1,0:T(8,128)(2,1)S(1)}, u32[]{:S(2)}, u32[]{:S(2)}) collective-permute-start(bf16[64,128]{1,0:T(8,128)(2,1)S(1)} %get-tuple-element.28), channel_id=1, source_target_pairs={{0,4},{4,8},{8,12},{12,0},{1,5},{5,9},{9,13},{13,1},{2,6},{6,10},{... | collective-permute-start | bytes 49160 | tf_op jit(solution)/shard_map/ppermute | solution.py:29
  4.6 8.2 %collective-permute-start.2 = (bf16[64,128]{1,0:T(8,128)(2,1)S(1)}, bf16[64,128]{1,0:T(8,128)(2,1)S(1)}, u32[]{:S(2)}, u32[]{:S(2)}) collective-permute-start(bf16[64,128]{1,0:T(8,128)(2,1)S(1)} %get-tuple-element.28), channel_id=1, source_target_pairs={{0,8},{4,12},{8,0},{12,4},{1,9},{5,13},{9,1},{13,5},{2,10},{6,14},... | collective-permute-start | bytes 49160 | tf_op jit(solution)/shard_map/ppermute | solution.py:29
  9.7 3.5 %collective-permute-start.1 = (bf16[64,128]{1,0:T(8,128)(2,1)S(1)}, bf16[64,128]{1,0:T(8,128)(2,1)S(1)}, u32[]{:S(2)}, u32[]{:S(2)}) collective-permute-start(bf16[64,128]{1,0:T(8,128)(2,1)S(1)} %get-tuple-element.28), channel_id=1, source_target_pairs={{0,12},{4,0},{8,4},{12,8},{1,13},{5,1},{9,5},{13,9},{2,14},{6,2},{... | collective-permute-start | bytes 49160 | tf_op jit(solution)/shard_map/ppermute | solution.py:29
  12.1 27.0 %collective-permute-start.11 = (bf16[256,768]{1,0:T(8,128)(2,1)}, bf16[256,768]{1,0:T(8,128)(2,1)S(1)}, u32[]{:S(2)}, u32[]{:S(2)}) collective-permute-start(bf16[256,768]{1,0:T(8,128)(2,1)} %bitcast.42), channel_id=1, source_target_pairs={{0,1},{1,0},{2,3},{3,2},{4,5},{5,4},{6,7},{7,6},{8,9},{9,8},{10,11... | collective-permute-start | bytes 1179656 | tf_op jit(solution)/shard_map/ppermute | solution.py:25
  13.2 17.9 %copy-start.3 = (bf16[1,256,512]{2,1,0:T(8,128)(2,1)S(1)}, bf16[1,256,512]{2,1,0:T(8,128)(2,1)}, u32[]{:S(2)}) copy-start(bf16[1,256,512]{2,1,0:T(8,128)(2,1)} %param.13) | copy-start | bytes 786436
  13.2 7.2 %collective-permute-start.6 = (bf16[4,64,128]{2,1,0:T(8,128)(2,1)S(1)}, bf16[4,64,128]{2,1,0:T(8,128)(2,1)S(1)}, u32[]{:S(2)}, u32[]{:S(2)}) collective-permute-start(bf16[4,64,128]{2,1,0:T(8,128)(2,1)S(1)} %pad_maximum_fusion), channel_id=1, source_target_pairs={{0,16},{16,32},{32,48},{48,0},{1,17},{17,33},{33,49},{49,1},{2,18}... | collective-permute-start | bytes 196616 | tf_op jit(solution)/shard_map/ppermute | solution.py:29
  14.5 5.9 %collective-permute-start.5 = (bf16[4,64,128]{2,1,0:T(8,128)(2,1)S(1)}, bf16[4,64,128]{2,1,0:T(8,128)(2,1)S(1)}, u32[]{:S(2)}, u32[]{:S(2)}) collective-permute-start(bf16[4,64,128]{2,1,0:T(8,128)(2,1)S(1)} %pad_maximum_fusion), channel_id=1, source_target_pairs={{0,32},{16,48},{32,0},{48,16},{1,33},{17,49},{33,1},{49,17},{2,34}... | collective-permute-start | bytes 196616 | tf_op jit(solution)/shard_map/ppermute | solution.py:29
  17.0 3.4 %collective-permute-start.4 = (bf16[4,64,128]{2,1,0:T(8,128)(2,1)S(1)}, bf16[4,64,128]{2,1,0:T(8,128)(2,1)S(1)}, u32[]{:S(2)}, u32[]{:S(2)}) collective-permute-start(bf16[4,64,128]{2,1,0:T(8,128)(2,1)S(1)} %pad_maximum_fusion), channel_id=1, source_target_pairs={{0,48},{16,0},{32,16},{48,32},{1,49},{17,1},{33,17},{49,33},{2,50}... | collective-permute-start | bytes 196616 | tf_op jit(solution)/shard_map/ppermute | solution.py:29
  20.4 5.1 %copy-start.4 = (s32[1,6]{1,0:T(1,128)S(1)}, s32[1,6]{1,0:T(1,128)}, u32[]{:S(2)}) copy-start(s32[1,6]{1,0:T(1,128)} %own_ids.3) | copy-start | bytes 76
  20.4 11.5 %collective-permute-start.9 = (bf16[16,64,128]{2,1,0:T(8,128)(2,1)S(1)}, bf16[16,64,128]{2,1,0:T(8,128)(2,1)S(1)}, u32[]{:S(2)}, u32[]{:S(2)}) collective-permute-start(bf16[16,64,128]{2,1,0:T(8,128)(2,1)S(1)} %constant_dynamic-update-slice_fusion.p0), channel_id=1, source_target_pairs={{0,64},{64,128},{128,192},{192,0},{1,65},{65,129},{129,193},{193,1... | collective-permute-start | bytes 786440 | tf_op jit(solution)/shard_map/ppermute | solution.py:29
  21.8 10.4 %collective-permute-start.8 = (bf16[16,64,128]{2,1,0:T(8,128)(2,1)S(1)}, bf16[16,64,128]{2,1,0:T(8,128)(2,1)S(1)}, u32[]{:S(2)}, u32[]{:S(2)}) collective-permute-start(bf16[16,64,128]{2,1,0:T(8,128)(2,1)S(1)} %constant_dynamic-update-slice_fusion.p0), channel_id=1, source_target_pairs={{0,128},{64,192},{128,0},{192,64},{1,129},{65,193},{129,1},{193,65... | collective-permute-start | bytes 786440 | tf_op jit(solution)/shard_map/ppermute | solution.py:29
  24.4 7.7 %collective-permute-start.7 = (bf16[16,64,128]{2,1,0:T(8,128)(2,1)S(1)}, bf16[16,64,128]{2,1,0:T(8,128)(2,1)S(1)}, u32[]{:S(2)}, u32[]{:S(2)}) collective-permute-start(bf16[16,64,128]{2,1,0:T(8,128)(2,1)S(1)} %constant_dynamic-update-slice_fusion.p0), channel_id=1, source_target_pairs={{0,192},{64,0},{128,64},{192,128},{1,193},{65,1},{129,65},{193,129... | collective-permute-start | bytes 786440 | tf_op jit(solution)/shard_map/ppermute | solution.py:29
  25.5 5.6 %collective-permute-start = (s32[1,6]{1,0:T(1,128)S(1)}, s32[1,6]{1,0:T(1,128)S(1)}, u32[]{:S(2)}, u32[]{:S(2)}) collective-permute-start(s32[1,6]{1,0:T(1,128)S(1)} %copy-done.4), channel_id=1, source_target_pairs={{0,2},{2,0},{1,3},{3,1},{4,6},{6,4},{5,7},{7,5},{8,10},{10,8},{9,1... | collective-permute-start | bytes 80 | tf_op jit(solution)/shard_map/ppermute | solution.py:25
  31.1 8.0 %collective-permute-start.12 = (bf16[256,512]{1,0:T(8,128)(2,1)S(1)}, bf16[256,512]{1,0:T(8,128)(2,1)S(1)}, u32[]{:S(2)}, u32[]{:S(2)}) collective-permute-start(bf16[256,512]{1,0:T(8,128)(2,1)S(1)} %bitcast.44), channel_id=1, source_target_pairs={{0,1},{1,0},{2,3},{3,2},{4,5},{5,4},{6,7},{7,6},{8,9},{9,8},{10,11... | collective-permute-start | bytes 786440 | tf_op jit(solution)/shard_map/ppermute | solution.py:25
  31.9 7.5 %copy-start.1 = (bf16[1,256,768]{2,1,0:T(8,128)(2,1)S(1)}, bf16[1,256,768]{2,1,0:T(8,128)(2,1)}, u32[]{:S(2)}) copy-start(bf16[1,256,768]{2,1,0:T(8,128)(2,1)} %param.12) | copy-start | bytes 1179652
  33.2 6.2 %collective-permute-start.10 = (bf16[6,64,128]{2,1,0:T(8,128)(2,1)S(1)}, bf16[6,64,128]{2,1,0:T(8,128)(2,1)S(1)}, u32[]{:S(2)}, u32[]{:S(2)}) collective-permute-start(bf16[6,64,128]{2,1,0:T(8,128)(2,1)S(1)} %get-tuple-element.14), channel_id=1, source_target_pairs={{0,2},{2,0},{1,3},{3,1},{4,6},{6,4},{5,7},{7,5},{8,10},{10,8},{9,1... | collective-permute-start | bytes 294920 | tf_op jit(solution)/shard_map/ppermute | solution.py:25
  41.0 1.6 %collective-permute-start.13 = (f32[6,64,128]{2,1,0:T(8,128)S(1)}, f32[6,64,128]{2,1,0:T(8,128)S(1)}, u32[]{:S(2)}, u32[]{:S(2)}) collective-permute-start(f32[6,64,128]{2,1,0:T(8,128)S(1)} %get-tuple-element.16), channel_id=1, source_target_pairs={{0,2},{2,0},{1,3},{3,1},{4,6},{6,4},{5,7},{7,5},{8,10},{10,8},{9,1... | collective-permute-start | bytes 589832 | tf_op jit(solution)/shard_map/ppermute | solution.py:25
  43.5 8.8 %collective-permute-start.14 = (bf16[16,64,128]{2,1,0:T(8,128)(2,1)S(1)}, bf16[16,64,128]{2,1,0:T(8,128)(2,1)S(1)}, u32[]{:S(2)}, u32[]{:S(2)}) collective-permute-start(bf16[16,64,128]{2,1,0:T(8,128)(2,1)S(1)} %get-tuple-element.18), channel_id=1, source_target_pairs={{0,64},{64,128},{128,192},{192,0},{1,65},{65,129},{129,193},{193,1... | collective-permute-start | bytes 786440 | tf_op jit(solution)/shard_map/ppermute | solution.py:33
  44.5 13.8 %collective-permute-start.15 = (bf16[16,64,128]{2,1,0:T(8,128)(2,1)S(1)}, bf16[16,64,128]{2,1,0:T(8,128)(2,1)S(1)}, u32[]{:S(2)}, u32[]{:S(2)}) collective-permute-start(bf16[16,64,128]{2,1,0:T(8,128)(2,1)S(1)} %get-tuple-element.19), channel_id=1, source_target_pairs={{0,128},{64,192},{128,0},{192,64},{1,129},{65,193},{129,1},{193,65... | collective-permute-start | bytes 786440 | tf_op jit(solution)/shard_map/ppermute | solution.py:33
  46.7 11.7 %collective-permute-start.16 = (bf16[16,64,128]{2,1,0:T(8,128)(2,1)S(1)}, bf16[16,64,128]{2,1,0:T(8,128)(2,1)S(1)}, u32[]{:S(2)}, u32[]{:S(2)}) collective-permute-start(bf16[16,64,128]{2,1,0:T(8,128)(2,1)S(1)} %get-tuple-element.20), channel_id=1, source_target_pairs={{0,192},{64,0},{128,64},{192,128},{1,193},{65,1},{129,65},{193,129... | collective-permute-start | bytes 786440 | tf_op jit(solution)/shard_map/ppermute | solution.py:33
  58.4 18.5 %copy-start.2 = (f32[64,128]{1,0:T(8,128)S(1)}, f32[64,128]{1,0:T(8,128)}, u32[]{:S(2)}) copy-start(f32[64,128]{1,0:T(8,128)} %start.1) | copy-start | bytes 98308
  58.4 18.5 %copy-start.5 = (f32[64,128]{1,0:T(8,128)S(1)}, f32[64,128]{1,0:T(8,128)}, u32[]{:S(2)}) copy-start(f32[64,128]{1,0:T(8,128)} %param.9) | copy-start | bytes 98308
  58.4 18.5 %copy-start.6 = (f32[64]{0:T(128)S(1)}, f32[64]{0:T(128)}, u32[]{:S(2)}) copy-start(f32[64]{0:T(128)} %param.10) | copy-start | bytes 772
  58.5 52.5 %copy-start = (bf16[64,8192]{1,0:T(8,128)(2,1)S(1)}, bf16[64,8192]{1,0:T(8,128)(2,1)}, u32[]{:S(2)}) copy-start(bf16[64,8192]{1,0:T(8,128)(2,1)} %precond.1) | copy-start | bytes 3145732
  58.6 4.4 %collective-permute-start.17 = (bf16[4,64,128]{2,1,0:T(8,128)(2,1)S(1)}, bf16[4,64,128]{2,1,0:T(8,128)(2,1)S(1)}, u32[]{:S(2)}, u32[]{:S(2)}) collective-permute-start(bf16[4,64,128]{2,1,0:T(8,128)(2,1)S(1)} %get-tuple-element.29), channel_id=1, source_target_pairs={{0,16},{16,32},{32,48},{48,0},{1,17},{17,33},{33,49},{49,1},{2,18}... | collective-permute-start | bytes 196616 | tf_op jit(solution)/shard_map/ppermute | solution.py:33
  58.8 4.1 %collective-permute-start.19 = (bf16[4,64,128]{2,1,0:T(8,128)(2,1)S(1)}, bf16[4,64,128]{2,1,0:T(8,128)(2,1)S(1)}, u32[]{:S(2)}, u32[]{:S(2)}) collective-permute-start(bf16[4,64,128]{2,1,0:T(8,128)(2,1)S(1)} %get-tuple-element.30), channel_id=1, source_target_pairs={{0,48},{16,0},{32,16},{48,32},{1,49},{17,1},{33,17},{49,33},{2,50}... | collective-permute-start | bytes 196616 | tf_op jit(solution)/shard_map/ppermute | solution.py:33
  61.3 5.1 %collective-permute-start.18 = (bf16[4,64,128]{2,1,0:T(8,128)(2,1)S(1)}, bf16[4,64,128]{2,1,0:T(8,128)(2,1)S(1)}, u32[]{:S(2)}, u32[]{:S(2)}) collective-permute-start(bf16[4,64,128]{2,1,0:T(8,128)(2,1)S(1)} %get-tuple-element.31), channel_id=1, source_target_pairs={{0,32},{16,48},{32,0},{48,16},{1,33},{17,49},{33,1},{49,17},{2,34}... | collective-permute-start | bytes 196616 | tf_op jit(solution)/shard_map/ppermute | solution.py:33
  66.5 6.4 %collective-permute-start.20 = (bf16[64,128]{1,0:T(8,128)(2,1)S(1)}, bf16[64,128]{1,0:T(8,128)(2,1)S(1)}, u32[]{:S(2)}, u32[]{:S(2)}) collective-permute-start(bf16[64,128]{1,0:T(8,128)(2,1)S(1)} %get-tuple-element.32), channel_id=1, source_target_pairs={{0,4},{4,8},{8,12},{12,0},{1,5},{5,9},{9,13},{13,1},{2,6},{6,10},{... | collective-permute-start | bytes 49160 | tf_op jit(solution)/shard_map/ppermute | solution.py:33
  68.4 4.5 %collective-permute-start.22 = (bf16[64,128]{1,0:T(8,128)(2,1)S(1)}, bf16[64,128]{1,0:T(8,128)(2,1)S(1)}, u32[]{:S(2)}, u32[]{:S(2)}) collective-permute-start(bf16[64,128]{1,0:T(8,128)(2,1)S(1)} %get-tuple-element.33), channel_id=1, source_target_pairs={{0,12},{4,0},{8,4},{12,8},{1,13},{5,1},{9,5},{13,9},{2,14},{6,2},{... | collective-permute-start | bytes 49160 | tf_op jit(solution)/shard_map/ppermute | solution.py:33
  70.2 6.6 %collective-permute-start.21 = (bf16[64,128]{1,0:T(8,128)(2,1)S(1)}, bf16[64,128]{1,0:T(8,128)(2,1)S(1)}, u32[]{:S(2)}, u32[]{:S(2)}) collective-permute-start(bf16[64,128]{1,0:T(8,128)(2,1)S(1)} %get-tuple-element.34), channel_id=1, source_target_pairs={{0,8},{4,12},{8,0},{12,4},{1,9},{5,13},{9,1},{13,5},{2,10},{6,14},... | collective-permute-start | bytes 49160 | tf_op jit(solution)/shard_map/ppermute | solution.py:33
  76.9 6.3 %collective-permute-start.25 = (bf16[64,128]{1,0:T(8,128)(2,1)S(1)}, bf16[64,128]{1,0:T(8,128)(2,1)S(1)}, u32[]{:S(2)}, u32[]{:S(2)}) collective-permute-start(bf16[64,128]{1,0:T(8,128)(2,1)S(1)} %get-tuple-element.22), channel_id=1, source_target_pairs={{0,4},{4,8},{8,12},{12,0},{1,5},{5,9},{9,13},{13,1},{2,6},{6,10},{... | collective-permute-start | bytes 49160 | tf_op jit(solution)/shard_map/ppermute | solution.py:29
  77.4 6.5 %collective-permute-start.24 = (bf16[64,128]{1,0:T(8,128)(2,1)S(1)}, bf16[64,128]{1,0:T(8,128)(2,1)S(1)}, u32[]{:S(2)}, u32[]{:S(2)}) collective-permute-start(bf16[64,128]{1,0:T(8,128)(2,1)S(1)} %get-tuple-element.22), channel_id=1, source_target_pairs={{0,8},{4,12},{8,0},{12,4},{1,9},{5,13},{9,1},{13,5},{2,10},{6,14},... | collective-permute-start | bytes 49160 | tf_op jit(solution)/shard_map/ppermute | solution.py:29
  81.3 3.5 %collective-permute-start.23 = (bf16[64,128]{1,0:T(8,128)(2,1)S(1)}, bf16[64,128]{1,0:T(8,128)(2,1)S(1)}, u32[]{:S(2)}, u32[]{:S(2)}) collective-permute-start(bf16[64,128]{1,0:T(8,128)(2,1)S(1)} %get-tuple-element.22), channel_id=1, source_target_pairs={{0,12},{4,0},{8,4},{12,8},{1,13},{5,1},{9,5},{13,9},{2,14},{6,2},{... | collective-permute-start | bytes 49160 | tf_op jit(solution)/shard_map/ppermute | solution.py:29
  84.8 5.8 %collective-permute-start.28 = (bf16[4,64,128]{2,1,0:T(8,128)(2,1)S(1)}, bf16[4,64,128]{2,1,0:T(8,128)(2,1)S(1)}, u32[]{:S(2)}, u32[]{:S(2)}) collective-permute-start(bf16[4,64,128]{2,1,0:T(8,128)(2,1)S(1)} %pad_maximum_fusion.1), channel_id=1, source_target_pairs={{0,16},{16,32},{32,48},{48,0},{1,17},{17,33},{33,49},{49,1},{2,18}... | collective-permute-start | bytes 196616 | tf_op jit(solution)/shard_map/ppermute | solution.py:29
  84.9 5.7 %collective-permute-start.27 = (bf16[4,64,128]{2,1,0:T(8,128)(2,1)S(1)}, bf16[4,64,128]{2,1,0:T(8,128)(2,1)S(1)}, u32[]{:S(2)}, u32[]{:S(2)}) collective-permute-start(bf16[4,64,128]{2,1,0:T(8,128)(2,1)S(1)} %pad_maximum_fusion.1), channel_id=1, source_target_pairs={{0,32},{16,48},{32,0},{48,16},{1,33},{17,49},{33,1},{49,17},{2,34}... | collective-permute-start | bytes 196616 | tf_op jit(solution)/shard_map/ppermute | solution.py:29
  86.9 3.6 %collective-permute-start.26 = (bf16[4,64,128]{2,1,0:T(8,128)(2,1)S(1)}, bf16[4,64,128]{2,1,0:T(8,128)(2,1)S(1)}, u32[]{:S(2)}, u32[]{:S(2)}) collective-permute-start(bf16[4,64,128]{2,1,0:T(8,128)(2,1)S(1)} %pad_maximum_fusion.1), channel_id=1, source_target_pairs={{0,48},{16,0},{32,16},{48,32},{1,49},{17,1},{33,17},{49,33},{2,50}... | collective-permute-start | bytes 196616 | tf_op jit(solution)/shard_map/ppermute | solution.py:29
  90.6 12.7 %collective-permute-start.31 = (bf16[16,64,128]{2,1,0:T(8,128)(2,1)S(1)}, bf16[16,64,128]{2,1,0:T(8,128)(2,1)S(1)}, u32[]{:S(2)}, u32[]{:S(2)}) collective-permute-start(bf16[16,64,128]{2,1,0:T(8,128)(2,1)S(1)} %constant_dynamic-update-slice_fusion.7.refs_0_), channel_id=1, source_target_pairs={{0,64},{64,128},{128,192},{192,0},{1,65},{65,129},{129,193},{193,1... | collective-permute-start | bytes 786440 | tf_op jit(solution)/shard_map/ppermute | solution.py:29
  92.4 13.4 %collective-permute-start.30 = (bf16[16,64,128]{2,1,0:T(8,128)(2,1)S(1)}, bf16[16,64,128]{2,1,0:T(8,128)(2,1)S(1)}, u32[]{:S(2)}, u32[]{:S(2)}) collective-permute-start(bf16[16,64,128]{2,1,0:T(8,128)(2,1)S(1)} %constant_dynamic-update-slice_fusion.7.refs_0_), channel_id=1, source_target_pairs={{0,128},{64,192},{128,0},{192,64},{1,129},{65,193},{129,1},{193,65... | collective-permute-start | bytes 786440 | tf_op jit(solution)/shard_map/ppermute | solution.py:29
  94.7 14.8 %collective-permute-start.29 = (bf16[16,64,128]{2,1,0:T(8,128)(2,1)S(1)}, bf16[16,64,128]{2,1,0:T(8,128)(2,1)S(1)}, u32[]{:S(2)}, u32[]{:S(2)}) collective-permute-start(bf16[16,64,128]{2,1,0:T(8,128)(2,1)S(1)} %constant_dynamic-update-slice_fusion.7.refs_0_), channel_id=1, source_target_pairs={{0,192},{64,0},{128,64},{192,128},{1,193},{65,1},{129,65},{193,129... | collective-permute-start | bytes 786440 | tf_op jit(solution)/shard_map/ppermute | solution.py:29
  95.0 14.5 %collective-permute-start.32 = (bf16[16,64,128]{2,1,0:T(8,128)(2,1)S(1)}, bf16[16,64,128]{2,1,0:T(8,128)(2,1)S(1)}, u32[]{:S(2)}, u32[]{:S(2)}) collective-permute-start(bf16[16,64,128]{2,1,0:T(8,128)(2,1)S(1)} %constant_dynamic-update-slice_fusion.7.refs_0_), channel_id=1, source_target_pairs={{0,2},{2,0},{1,3},{3,1},{4,6},{6,4},{5,7},{7,5},{8,10},{10,8},{9,1... | collective-permute-start | bytes 786440 | tf_op jit(solution)/shard_map/ppermute | solution.py:25
  103.3 6.2 %collective-permute-start.35 = (bf16[16,64,128]{2,1,0:T(8,128)(2,1)S(1)}, bf16[16,64,128]{2,1,0:T(8,128)(2,1)S(1)}, u32[]{:S(2)}, u32[]{:S(2)}) collective-permute-start(bf16[16,64,128]{2,1,0:T(8,128)(2,1)S(1)} %collective-permute-done.31.refs_3_), channel_id=1, source_target_pairs={{0,2},{2,0},{1,3},{3,1},{4,6},{6,4},{5,7},{7,5},{8,10},{10,8},{9,1... | collective-permute-start | bytes 786440 | tf_op jit(solution)/shard_map/ppermute | solution.py:25
  105.8 4.8 %collective-permute-start.34 = (bf16[16,64,128]{2,1,0:T(8,128)(2,1)S(1)}, bf16[16,64,128]{2,1,0:T(8,128)(2,1)S(1)}, u32[]{:S(2)}, u32[]{:S(2)}) collective-permute-start(bf16[16,64,128]{2,1,0:T(8,128)(2,1)S(1)} %collective-permute-done.30.refs_2_), channel_id=1, source_target_pairs={{0,2},{2,0},{1,3},{3,1},{4,6},{6,4},{5,7},{7,5},{8,10},{10,8},{9,1... | collective-permute-start | bytes 786440 | tf_op jit(solution)/shard_map/ppermute | solution.py:25
  109.5 1.5 %collective-permute-start.33 = (bf16[16,64,128]{2,1,0:T(8,128)(2,1)S(1)}, bf16[16,64,128]{2,1,0:T(8,128)(2,1)S(1)}, u32[]{:S(2)}, u32[]{:S(2)}) collective-permute-start(bf16[16,64,128]{2,1,0:T(8,128)(2,1)S(1)} %collective-permute-done.29.refs_1_), channel_id=1, source_target_pairs={{0,2},{2,0},{1,3},{3,1},{4,6},{6,4},{5,7},{7,5},{8,10},{10,8},{9,1... | collective-permute-start | bytes 786440 | tf_op jit(solution)/shard_map/ppermute | solution.py:25

commit v2 on v1

--- a/solution.py
+++ b/solution.py
@@ -37,17 +37,26 @@
     return [value] + [from_ahead(value, axis, k) for k in range(1, RING)]
 
 
-def ring_gather(value):
-    line = jnp.stack(ring_pieces(value, Z))
-    plane = jnp.concatenate(ring_pieces(line, X))
-    return ring_pieces(plane, Y)
+def pair(axis, value, first):
+    other = [1, 0, 3, 2] if first else [3, 2, 1, 0]
+    return lax.ppermute(value, axis, list(enumerate(other)))
+
+
+def line_gather(value):
+    two = jnp.stack([value, pair(Z, value, True)])
+    return jnp.concatenate([two, pair(Z, two, False)])
+
+
+def line_slot(tile_z, z):
+    return jnp.where(
+        tile_z == z, 0, jnp.where(tile_z == (z ^ 1), 1, jnp.where(tile_z == 3 - z, 2, 3))
+    )
 
 
 def place(tile, where):
     dy = (tile // 16 - where[0]) % RING
     dx = ((tile // 4) % 4 - where[1]) % RING
-    dz = (tile % 4 - where[2]) % RING
-    return dy, dx * 4 + dz
+    return dy, dx * 4 + line_slot(tile % 4, where[2])
 
 
 def pick_kernel(where, own_ids, other_ids, p0, p1, p2, p3, own_ref, other_ref):
@@ -117,21 +126,24 @@
         chunk[...] = total[16 * (k + 1) : 16 * (k + 2)].astype(BF16)
 
 
-def update_kernel(where, start, precond, *refs):
-    pieces, (out_ref, whole) = refs[:8], refs[8:]
+def update_kernel(where, start, precond, b1, b2, b3, *refs):
+    pieces, (o0, o1, o2, o3, whole) = refs[:8], refs[8:]
     y, x, z, core = where[0], where[1], where[2], where[3]
+    slots = (z, z ^ 1, 3 - z, (3 - z) ^ 1)
     for side in range(2):
         half = core if side == 0 else 1 - core
-        for k in range(RING):
-            piece = pieces[side * RING + k]
-            base_y = ((y + k) % RING) * 16
-            for i in range(RING):
-                base_x = base_y + ((x + i) % RING) * 4
-                for j in range(RING):
-                    tile = base_x + (z + j) % RING
-                    at = pl.multiple_of(tile * TILE + half * HALF, HALF)
-                    whole[pl.ds(at, HALF), :] = piece[i * RING + j]
-    out_ref[...] = start[...] + jnp.dot(precond[...], whole[...], preferred_element_type=F32)
+        for i in range(RING):
+            piece = pieces[side * RING + i]
+            base = ((x + i) % RING) * 4
+            for j in range(RING):
+                at = pl.multiple_of((base + slots[j]) * TILE + half * HALF, HALF)
+                whole[pl.ds(at, HALF), :] = piece[j]
+    operand = whole[...]
+    span = operand.shape[0]
+    own = precond[:, pl.ds(pl.multiple_of(y * span, span), span)]
+    o0[...] = start[...] + jnp.dot(own, operand, preferred_element_type=F32)
+    for block, out in ((b1, o1), (b2, o2), (b3, o3)):
+        out[...] = jnp.dot(block[...], operand, preferred_element_type=F32)
 
 
 def call(kernel, specs, outs, scratch=(), flops=0, moved=0):
@@ -162,7 +174,15 @@
     border, inverse = border_block[0], coupling_inverse[0]
     tiles = column_tiles.shape[1]
 
-    pieces = ring_gather(start_guess.astype(BF16))
+    line = line_gather(start_guess.astype(BF16))
+    plane = jnp.concatenate(ring_pieces(line, X))
+    pieces = ring_pieces(plane, Y)
+    span = preconditioner.shape[1] // RING
+    blocks = []
+    for k in range(1, RING):
+        first = ((where[0] + k) % RING) * span
+        columns = lax.dynamic_slice_in_dim(preconditioner, first, span, 1)
+        blocks.append(to_ahead(columns, Y, k))
     other_tiles = swap(column_tiles, CORE)
     border_other = swap(border, SIDE)
     inverse_other = swap(inverse, SIDE)
@@ -195,19 +215,25 @@
     line = plane[0]
     for k in range(1, RING):
         line = line + to_ahead(plane[k].astype(BF16), X, k).astype(F32)
-    total = line[0]
+    own_terms = right_side - root_diagonal[:, None] * start_guess
+    line = line + jnp.concatenate([own_terms[None], jnp.zeros_like(line[1:])])
+    met = pair(Z, line.astype(BF16), True).astype(F32)
+    line = line + jnp.stack([met[1], met[0], met[3], met[2]])
+    met = pair(Z, line.astype(BF16), False).astype(F32)
+    line = line + jnp.concatenate([met[2:], met[:2]])
+
+    mine = ring_pieces(line.astype(BF16), X)
+    partners = [swap(piece, CORE) for piece in mine]
+    parts = call(
+        update_kernel,
+        [SMEM] + [VMEM] * 13,
+        [shape((rows, cols), F32)] * RING,
+        [pltpu.VMEM((span, cols), BF16)],
+    )(where, start_guess, preconditioner, *blocks, *mine, *partners)
+    out = parts[0]
     for k in range(1, RING):
-        total = total + to_ahead(line[k].astype(BF16), Z, k).astype(F32)
-    residual = right_side - root_diagonal[:, None] * start_guess + total
-
-    mine = ring_gather(residual.astype(BF16))
-    partners = [swap(piece, CORE) for piece in mine]
-    return call(
-        update_kernel,
-        [SMEM] + [VMEM] * 10,
-        shape((rows, cols), F32),
-        [pltpu.VMEM((preconditioner.shape[1], cols), BF16)],
-    )(where, start_guess, preconditioner, *mine, *partners)
+        out = out + from_ahead(parts[k], Y, k)
+    return out
 
 
 def solution(mesh):

time: 113 us -> 104 us (0.920)
  starting transfers between devices: 75.5 us -> 51.7 us
  waiting for transfers between devices: 29.7 us -> 44.9 us
    ppermute x18 -> x12, starting transfers between devices: 34.7 us -> 14.7 us  [from_ahead(): lax.ppermute(value, axis, [(i, (i - distance) % RING) for i in range(RING)])]
    ppermute x0 -> x4, waiting for transfers between devices: none -> 12.2 us  [pair(): return lax.ppermute(value, axis, list(enumerate(other)))]
    ppermute x9, starting transfers between devices: 26.5 us -> 16.7 us  [swap(): return lax.ppermute(value, axis, SWAP)]
    ppermute x0 -> x4, starting transfers between devices: none -> 9.38 us  [pair(): return lax.ppermute(value, axis, list(enumerate(other)))]
    ppermute x9, starting transfers between devices: 14.4 us -> 10.9 us  [to_ahead(): lax.ppermute(value, axis, [(i, (i + distance) % RING) for i in range(RING)])]
    ppermute x18 -> x12, waiting for transfers between devices: 7.4 us -> 9.88 us  [from_ahead(): lax.ppermute(value, axis, [(i, (i - distance) % RING) for i in range(RING)])]
  transfers between devices with their start and end apart: 36 -> 34, of which waited for: 16 -> 20; matrix products, arithmetic and copies ran while one was open for 0% -> 0% of each run, Pallas kernels for 1% -> 1%
where the time goes in v2:
time: 104 us
  starting transfers between devices  51.7 us (50%)
  waiting for transfers between devices  44.9 us (43%)
  Pallas kernels  4.64 us (4%)
  other arithmetic  1.72 us (2%)
    ppermute x9, waiting for transfers between devices, to_ahead(): lax.ppermute(value, axis, [(i, (i + distance) % RING) for i in range(RING)])  19.7 us
    ppermute x9, starting transfers between devices, swap(): return lax.ppermute(value, axis, SWAP)  16.7 us
    ppermute x12, starting transfers between devices, from_ahead(): lax.ppermute(value, axis, [(i, (i - distance) % RING) for i in range(RING)])  14.7 us
    ppermute x4, waiting for transfers between devices, pair(): return lax.ppermute(value, axis, list(enumerate(other)))  12.2 us
    ppermute x9, starting transfers between devices, to_ahead(): lax.ppermute(value, axis, [(i, (i + distance) % RING) for i in range(RING)])  10.9 us
    ppermute x12, waiting for transfers between devices, from_ahead(): lax.ppermute(value, axis, [(i, (i - distance) % RING) for i in range(RING)])  9.88 us
    ppermute x4, starting transfers between devices, pair(): return lax.ppermute(value, axis, list(enumerate(other)))  9.38 us
    ppermute x9, waiting for transfers between devices, swap(): return lax.ppermute(value, axis, SWAP)  3.07 us
  transfers between devices with their start and end apart: 34, of which 20 were waited for; matrix products, arithmetic and copies ran while one was open for 0% of the time, Pallas kernels for 1%

profile of v2, /device:TPU:1, one launch (start us, length us, event | category | flops | bytes accessed | tf_op | source)
XLA Modules:
  0.0 104.0 jit_solution(17744846830774631333)
XLA Ops:
  0.0 0.8 constant_dynamic-update-slice_fusion.5
  0.8 3.8 %collective-permute-start.4 = (bf16[64,128]{1,0:T(8,128)(2,1)S(1)}, bf16[64,128]{1,0:T(8,128)(2,1)S(1)}, u32[]{:S(2)}, u32[]{:S(2)}) collective-permute-start(bf16[64,128]{1,0:T(8,128)(2,1)S(1)} %get-tuple-element.34), channel_id=1, source_target_pairs={{0,4},{4,0},{8,12},{12,8},{1,5},{5,1},{9,13},{13,9},{2,6},{6,2},{1... | collective-permute-start | bytes 49160 | tf_op jit(solution)/shard_map/ppermute | solution.py:42
  4.6 1.6 %collective-permute-start.13 = (bf16[256,768]{1,0:T(8,128)(2,1)}, bf16[256,768]{1,0:T(8,128)(2,1)S(1)}, u32[]{:S(2)}, u32[]{:S(2)}) collective-permute-start(bf16[256,768]{1,0:T(8,128)(2,1)} %bitcast.13), channel_id=1, source_target_pairs={{0,1},{1,0},{2,3},{3,2},{4,5},{5,4},{6,7},{7,6},{8,9},{9,8},{10,11... | collective-permute-start | bytes 1179656 | tf_op jit(solution)/shard_map/ppermute | solution.py:25
  6.2 4.9 %collective-permute-start.5 = (bf16[2,64,128]{2,1,0:T(8,128)(2,1)S(1)}, bf16[2,64,128]{2,1,0:T(8,128)(2,1)S(1)}, u32[]{:S(2)}, u32[]{:S(2)}) collective-permute-start(bf16[2,64,128]{2,1,0:T(8,128)(2,1)S(1)} %pad_maximum_fusion.1), channel_id=1, source_target_pairs={{0,12},{4,8},{8,4},{12,0},{1,13},{5,9},{9,5},{13,1},{2,14},{6,10},... | collective-permute-start | bytes 98312 | tf_op jit(solution)/shard_map/ppermute | solution.py:42
  11.1 7.6 %collective-permute-done.5 = bf16[2,64,128]{2,1,0:T(8,128)(2,1)S(1)} collective-permute-done((bf16[2,64,128]{2,1,0:T(8,128)(2,1)S(1)}, bf16[2,64,128]{2,1,0:T(8,128)(2,1)S(1)}, u32[]{:S(2)}, u32[]{:S(2)}) %collective-permute-start.5) | collective-permute-done | bytes 32800 | tf_op jit(solution)/shard_map/ppermute | solution.py:42
  18.7 2.6 %collective-permute-start.6 = (bf16[4,64,128]{2,1,0:T(8,128)(2,1)S(1)}, bf16[4,64,128]{2,1,0:T(8,128)(2,1)S(1)}, u32[]{:S(2)}, u32[]{:S(2)}) collective-permute-start(bf16[4,64,128]{2,1,0:T(8,128)(2,1)S(1)} %pad_maximum_fusion), channel_id=1, source_target_pairs={{0,48},{16,0},{32,16},{48,32},{1,49},{17,1},{33,17},{49,33},{2,50}... | collective-permute-start | bytes 196616 | tf_op jit(solution)/shard_map/ppermute | solution.py:29
  21.3 0.5 collective-permute-start.7
  21.8 0.6 collective-permute-start.8
  22.6 3.3 %collective-permute-done.7 = bf16[4,64,128]{2,1,0:T(8,128)(2,1)S(1)} collective-permute-done((bf16[4,64,128]{2,1,0:T(8,128)(2,1)S(1)}, bf16[4,64,128]{2,1,0:T(8,128)(2,1)S(1)}, u32[]{:S(2)}, u32[]{:S(2)}) %collective-permute-start.7) | collective-permute-done | bytes 65568 | tf_op jit(solution)/shard_map/ppermute | solution.py:29
  26.0 0.6 collective-permute-done.8
  26.6 3.0 %collective-permute-start.10 = (bf16[16,64,128]{2,1,0:T(8,128)(2,1)S(1)}, bf16[16,64,128]{2,1,0:T(8,128)(2,1)S(1)}, u32[]{:S(2)}, u32[]{:S(2)}) collective-permute-start(bf16[16,64,128]{2,1,0:T(8,128)(2,1)S(1)} %constant_dynamic-update-slice_fusion.p0), channel_id=1, source_target_pairs={{0,128},{64,192},{128,0},{192,64},{1,129},{65,193},{129,1},{193,65... | collective-permute-start | bytes 786440 | tf_op jit(solution)/shard_map/ppermute | solution.py:29
  29.6 0.4 collective-permute-start.11
  30.0 2.3 %collective-permute-start.9 = (bf16[16,64,128]{2,1,0:T(8,128)(2,1)S(1)}, bf16[16,64,128]{2,1,0:T(8,128)(2,1)S(1)}, u32[]{:S(2)}, u32[]{:S(2)}) collective-permute-start(bf16[16,64,128]{2,1,0:T(8,128)(2,1)S(1)} %constant_dynamic-update-slice_fusion.p0), channel_id=1, source_target_pairs={{0,192},{64,0},{128,64},{192,128},{1,193},{65,1},{129,65},{193,129... | collective-permute-start | bytes 786440 | tf_op jit(solution)/shard_map/ppermute | solution.py:29
  32.3 4.3 %collective-permute-start.3 = (s32[1,6]{1,0:T(1,128)S(1)}, s32[1,6]{1,0:T(1,128)S(1)}, u32[]{:S(2)}, u32[]{:S(2)}) collective-permute-start(s32[1,6]{1,0:T(1,128)S(1)} %copy-done.4), channel_id=1, source_target_pairs={{0,2},{2,0},{1,3},{3,1},{4,6},{6,4},{5,7},{7,5},{8,10},{10,8},{9,1... | collective-permute-start | bytes 80 | tf_op jit(solution)/shard_map/ppermute | solution.py:25
  36.5 0.8 collective-permute-done.3.other_ids
  37.5 2.1 %collective-permute-done.11.p3 = bf16[16,64,128]{2,1,0:T(8,128)(2,1)S(1)} collective-permute-done((bf16[16,64,128]{2,1,0:T(8,128)(2,1)S(1)}, bf16[16,64,128]{2,1,0:T(8,128)(2,1)S(1)}, u32[]{:S(2)}, u32[]{:S(2)}) %collective-permute-start.11) | collective-permute-done | bytes 262176 | tf_op jit(solution)/shard_map/ppermute | solution.py:29
  39.5 1.0 shard_map.82
  40.6 3.5 %collective-permute-start.12 = (bf16[6,64,128]{2,1,0:T(8,128)(2,1)S(1)}, bf16[6,64,128]{2,1,0:T(8,128)(2,1)S(1)}, u32[]{:S(2)}, u32[]{:S(2)}) collective-permute-start(bf16[6,64,128]{2,1,0:T(8,128)(2,1)S(1)} %get-tuple-element.18), channel_id=1, source_target_pairs={{0,2},{2,0},{1,3},{3,1},{4,6},{6,4},{5,7},{7,5},{8,10},{10,8},{9,1... | collective-permute-start | bytes 294920 | tf_op jit(solution)/shard_map/ppermute | solution.py:25
  45.0 1.6 %shard_map.83 = (f32[6,64,128]{2,1,0:T(8,128)S(1)}, f32[6,64,128]{2,1,0:T(8,128)S(1)}) custom-call(s32[5]{0:T(128)S(1)} %stack.35.where, s32[1]{0:T(128)S(6)} %copy.14.count, bf16[6,64,128]{2,1,0:T(8,128)(2,1)S(1)} %get-tuple-element.17.own_picked, bf16[6,64,128]{2,1,0:T(8,128)(2,1)S(1)} %collective-permute-done.12.other_picked, ...), custom_call_target="tpu_custom_call" | custom-call | tf_op jit(solution)/shard_map/pallas_call | solution.py:196
  46.6 1.2 %collective-permute-start.15 = (f32[6,64,128]{2,1,0:T(8,128)S(1)}, f32[6,64,128]{2,1,0:T(8,128)S(1)}, u32[]{:S(2)}, u32[]{:S(2)}) collective-permute-start(f32[6,64,128]{2,1,0:T(8,128)S(1)} %get-tuple-element.20), channel_id=1, source_target_pairs={{0,2},{2,0},{1,3},{3,1},{4,6},{6,4},{5,7},{7,5},{8,10},{10,8},{9,1... | collective-permute-start | bytes 589832 | tf_op jit(solution)/shard_map/ppermute | solution.py:25
  47.7 1.1 %collective-permute-done.15.arrived = f32[6,64,128]{2,1,0:T(8,128)S(1)} collective-permute-done((f32[6,64,128]{2,1,0:T(8,128)S(1)}, f32[6,64,128]{2,1,0:T(8,128)S(1)}, u32[]{:S(2)}, u32[]{:S(2)}) %collective-permute-start.15) | collective-permute-done | bytes 196640 | tf_op jit(solution)/shard_map/ppermute | solution.py:25
  48.8 1.0 shard_map.84
  49.8 0.5 collective-permute-start.16
  50.3 2.4 %collective-permute-start.17 = (bf16[16,64,128]{2,1,0:T(8,128)(2,1)S(1)}, bf16[16,64,128]{2,1,0:T(8,128)(2,1)S(1)}, u32[]{:S(2)}, u32[]{:S(2)}) collective-permute-start(bf16[16,64,128]{2,1,0:T(8,128)(2,1)S(1)} %get-tuple-element.23), channel_id=1, source_target_pairs={{0,128},{64,192},{128,0},{192,64},{1,129},{65,193},{129,1},{193,65... | collective-permute-start | bytes 786440 | tf_op jit(solution)/shard_map/ppermute | solution.py:33
  53.0 5.6 %collective-permute-done.16 = bf16[16,64,128]{2,1,0:T(8,128)(2,1)S(1)} collective-permute-done((bf16[16,64,128]{2,1,0:T(8,128)(2,1)S(1)}, bf16[16,64,128]{2,1,0:T(8,128)(2,1)S(1)}, u32[]{:S(2)}, u32[]{:S(2)}) %collective-permute-start.16) | collective-permute-done | bytes 262176 | tf_op jit(solution)/shard_map/ppermute | solution.py:33
  58.6 5.8 %collective-permute-done.17 = bf16[16,64,128]{2,1,0:T(8,128)(2,1)S(1)} collective-permute-done((bf16[16,64,128]{2,1,0:T(8,128)(2,1)S(1)}, bf16[16,64,128]{2,1,0:T(8,128)(2,1)S(1)}, u32[]{:S(2)}, u32[]{:S(2)}) %collective-permute-start.17) | collective-permute-done | bytes 262176 | tf_op jit(solution)/shard_map/ppermute | solution.py:33
  64.8 1.5 %collective-permute-start.20 = (bf16[4,64,128]{2,1,0:T(8,128)(2,1)S(1)}, bf16[4,64,128]{2,1,0:T(8,128)(2,1)S(1)}, u32[]{:S(2)}, u32[]{:S(2)}) collective-permute-start(bf16[4,64,128]{2,1,0:T(8,128)(2,1)S(1)} %get-tuple-element.40), channel_id=1, source_target_pairs={{0,32},{16,48},{32,0},{48,16},{1,33},{17,49},{33,1},{49,17},{2,34}... | collective-permute-start | bytes 196616 | tf_op jit(solution)/shard_map/ppermute | solution.py:33
  66.3 1.7 %collective-permute-start.21 = (bf16[4,64,128]{2,1,0:T(8,128)(2,1)S(1)}, bf16[4,64,128]{2,1,0:T(8,128)(2,1)S(1)}, u32[]{:S(2)}, u32[]{:S(2)}) collective-permute-start(bf16[4,64,128]{2,1,0:T(8,128)(2,1)S(1)} %get-tuple-element.39), channel_id=1, source_target_pairs={{0,48},{16,0},{32,16},{48,32},{1,49},{17,1},{33,17},{49,33},{2,50}... | collective-permute-start | bytes 196616 | tf_op jit(solution)/shard_map/ppermute | solution.py:33
  68.1 1.7 %collective-permute-done.19 = bf16[4,64,128]{2,1,0:T(8,128)(2,1)S(1)} collective-permute-done((bf16[4,64,128]{2,1,0:T(8,128)(2,1)S(1)}, bf16[4,64,128]{2,1,0:T(8,128)(2,1)S(1)}, u32[]{:S(2)}, u32[]{:S(2)}) %collective-permute-start.19) | collective-permute-done | bytes 65568 | tf_op jit(solution)/shard_map/ppermute | solution.py:33
  70.0 0.8 collective-permute-done.21
  70.8 0.6 collective-permute-start.22
  71.4 4.0 %collective-permute-done.22 = bf16[4,64,128]{2,1,0:T(8,128)(2,1)S(1)} collective-permute-done((bf16[4,64,128]{2,1,0:T(8,128)(2,1)S(1)}, bf16[4,64,128]{2,1,0:T(8,128)(2,1)S(1)}, u32[]{:S(2)}, u32[]{:S(2)}) %collective-permute-start.22) | collective-permute-done | bytes 65568 | tf_op jit(solution)/shard_map/ppermute | solution.py:42
  75.6 1.4 %collective-permute-start = (bf16[64,2048]{1,0:T(8,128)(2,1)S(1)}, bf16[64,2048]{1,0:T(8,128)(2,1)S(1)}, u32[]{:S(2)}, u32[]{:S(2)}) collective-permute-start(bf16[64,2048]{1,0:T(8,128)(2,1)S(1)} %get-tuple-element.37), channel_id=1, source_target_pairs={{0,64},{64,128},{128,192},{192,0},{1,65},{65,129},{129,193},{193,1... | collective-permute-start | bytes 786440 | tf_op jit(solution)/shard_map/ppermute | solution.py:33
  76.9 3.1 %collective-permute-start.1 = (bf16[64,2048]{1,0:T(8,128)(2,1)S(1)}, bf16[64,2048]{1,0:T(8,128)(2,1)S(1)}, u32[]{:S(2)}, u32[]{:S(2)}) collective-permute-start(bf16[64,2048]{1,0:T(8,128)(2,1)S(1)} %get-tuple-element.36), channel_id=1, source_target_pairs={{0,128},{64,192},{128,0},{192,64},{1,129},{65,193},{129,1},{193,65... | collective-permute-start | bytes 786440 | tf_op jit(solution)/shard_map/ppermute | solution.py:33
  80.1 0.6 collective-permute-done.23
  80.7 2.2 %collective-permute-start.24 = (bf16[4,64,128]{2,1,0:T(8,128)(2,1)S(1)}, bf16[4,64,128]{2,1,0:T(8,128)(2,1)S(1)}, u32[]{:S(2)}, u32[]{:S(2)}) collective-permute-start(bf16[4,64,128]{2,1,0:T(8,128)(2,1)S(1)} %fusion.3.refs_0_), channel_id=1, source_target_pairs={{0,48},{16,0},{32,16},{48,32},{1,49},{17,1},{33,17},{49,33},{2,50}... | collective-permute-start | bytes 196616 | tf_op jit(solution)/shard_map/ppermute | solution.py:29
  83.1 0.5 collective-permute-start.26
  83.6 5.5 %collective-permute-done.1.b2 = bf16[64,2048]{1,0:T(8,128)(2,1)S(1)} collective-permute-done((bf16[64,2048]{1,0:T(8,128)(2,1)S(1)}, bf16[64,2048]{1,0:T(8,128)(2,1)S(1)}, u32[]{:S(2)}, u32[]{:S(2)}) %collective-permute-start.1) | collective-permute-done | bytes 262176 | tf_op jit(solution)/shard_map/ppermute | solution.py:33
  89.1 3.8 %collective-permute-start.27 = (bf16[4,64,128]{2,1,0:T(8,128)(2,1)S(1)}, bf16[4,64,128]{2,1,0:T(8,128)(2,1)S(1)}, u32[]{:S(2)}, u32[]{:S(2)}) collective-permute-start(bf16[4,64,128]{2,1,0:T(8,128)(2,1)S(1)} %fusion.3.refs_0_), channel_id=1, source_target_pairs={{0,2},{2,0},{1,3},{3,1},{4,6},{6,4},{5,7},{7,5},{8,10},{10,8},{9,1... | collective-permute-start | bytes 196616 | tf_op jit(solution)/shard_map/ppermute | solution.py:25
  93.0 1.2 %collective-permute-start.29 = (bf16[4,64,128]{2,1,0:T(8,128)(2,1)S(1)}, bf16[4,64,128]{2,1,0:T(8,128)(2,1)S(1)}, u32[]{:S(2)}, u32[]{:S(2)}) collective-permute-start(bf16[4,64,128]{2,1,0:T(8,128)(2,1)S(1)} %collective-permute-done.25.refs_2_), channel_id=1, source_target_pairs={{0,2},{2,0},{1,3},{3,1},{4,6},{6,4},{5,7},{7,5},{8,10},{10,8},{9,1... | collective-permute-start | bytes 196616 | tf_op jit(solution)/shard_map/ppermute | solution.py:25
  94.2 1.1 %collective-permute-start.30 = (bf16[4,64,128]{2,1,0:T(8,128)(2,1)S(1)}, bf16[4,64,128]{2,1,0:T(8,128)(2,1)S(1)}, u32[]{:S(2)}, u32[]{:S(2)}) collective-permute-start(bf16[4,64,128]{2,1,0:T(8,128)(2,1)S(1)} %collective-permute-done.26.refs_3_), channel_id=1, source_target_pairs={{0,2},{2,0},{1,3},{3,1},{4,6},{6,4},{5,7},{7,5},{8,10},{10,8},{9,1... | collective-permute-start | bytes 196616 | tf_op jit(solution)/shard_map/ppermute | solution.py:25
  95.3 0.9 collective-permute-done.30.refs_7_
  96.2 1.1 %shard_map.85 = (f32[64,128]{1,0:T(8,128)S(1)}, f32[64,128]{1,0:T(8,128)S(1)}, f32[64,128]{1,0:T(8,128)S(1)}, f32[64,128]{1,0:T(8,128)S(1)}) custom-call(s32[5]{0:T(128)S(1)} %stack.35.where, f32[64,128]{1,0:T(8,128)S(1)} %copy-done.2, bf16[64,8192]{1,0:T(8,128)(2,1)S(1)} %copy-done, bf16[64,2048]{1,0:T(8,128)(2,1)S(1)} %collective-permute-done.b1, ...), custom_call_target="tpu_custom_call" | custom-call | tf_op jit(solution)/shard_map/pallas_call | solution.py:227
  97.2 1.8 %collective-permute-start.31 = (f32[64,128]{1,0:T(8,128)S(1)}, f32[64,128]{1,0:T(8,128)S(1)}, u32[]{:S(2)}, u32[]{:S(2)}) collective-permute-start(f32[64,128]{1,0:T(8,128)S(1)} %get-tuple-element.26), channel_id=1, source_target_pairs={{0,192},{64,0},{128,64},{192,128},{1,193},{65,1},{129,65},{193,129... | collective-permute-start | bytes 98312 | tf_op jit(solution)/shard_map/ppermute | solution.py:29
  99.1 0.7 collective-permute-start.33
  99.7 0.3 collective-permute-done.31
  100.1 3.3 %collective-permute-done.32 = f32[64,128]{1,0:T(8,128)S(1)} collective-permute-done((f32[64,128]{1,0:T(8,128)S(1)}, f32[64,128]{1,0:T(8,128)S(1)}, u32[]{:S(2)}, u32[]{:S(2)}) %collective-permute-start.32) | collective-permute-done | bytes 32800 | tf_op jit(solution)/shard_map/ppermute | solution.py:29
  103.4 0.6 add_add_fusion
  (57 shorter events, 2.1 us)
Async XLA Ops:
  0.8 5.5 %collective-permute-start.4 = (bf16[64,128]{1,0:T(8,128)(2,1)S(1)}, bf16[64,128]{1,0:T(8,128)(2,1)S(1)}, u32[]{:S(2)}, u32[]{:S(2)}) collective-permute-start(bf16[64,128]{1,0:T(8,128)(2,1)S(1)} %get-tuple-element.34), channel_id=1, source_target_pairs={{0,4},{4,0},{8,12},{12,8},{1,5},{5,1},{9,13},{13,9},{2,6},{6,2},{1... | collective-permute-start | bytes 49160 | tf_op jit(solution)/shard_map/ppermute | solution.py:42
  4.6 40.4 %collective-permute-start.13 = (bf16[256,768]{1,0:T(8,128)(2,1)}, bf16[256,768]{1,0:T(8,128)(2,1)S(1)}, u32[]{:S(2)}, u32[]{:S(2)}) collective-permute-start(bf16[256,768]{1,0:T(8,128)(2,1)} %bitcast.13), channel_id=1, source_target_pairs={{0,1},{1,0},{2,3},{3,2},{4,5},{5,4},{6,7},{7,6},{8,9},{9,8},{10,11... | collective-permute-start | bytes 1179656 | tf_op jit(solution)/shard_map/ppermute | solution.py:25
  6.2 12.5 %collective-permute-start.5 = (bf16[2,64,128]{2,1,0:T(8,128)(2,1)S(1)}, bf16[2,64,128]{2,1,0:T(8,128)(2,1)S(1)}, u32[]{:S(2)}, u32[]{:S(2)}) collective-permute-start(bf16[2,64,128]{2,1,0:T(8,128)(2,1)S(1)} %pad_maximum_fusion.1), channel_id=1, source_target_pairs={{0,12},{4,8},{8,4},{12,0},{1,13},{5,9},{9,5},{13,1},{2,14},{6,10},... | collective-permute-start | bytes 98312 | tf_op jit(solution)/shard_map/ppermute | solution.py:42
  18.7 18.7 %copy-start.3 = (bf16[1,256,512]{2,1,0:T(8,128)(2,1)S(1)}, bf16[1,256,512]{2,1,0:T(8,128)(2,1)}, u32[]{:S(2)}) copy-start(bf16[1,256,512]{2,1,0:T(8,128)(2,1)} %param.13) | copy-start | bytes 786436
  18.7 3.9 %collective-permute-start.6 = (bf16[4,64,128]{2,1,0:T(8,128)(2,1)S(1)}, bf16[4,64,128]{2,1,0:T(8,128)(2,1)S(1)}, u32[]{:S(2)}, u32[]{:S(2)}) collective-permute-start(bf16[4,64,128]{2,1,0:T(8,128)(2,1)S(1)} %pad_maximum_fusion), channel_id=1, source_target_pairs={{0,48},{16,0},{32,16},{48,32},{1,49},{17,1},{33,17},{49,33},{2,50}... | collective-permute-start | bytes 196616 | tf_op jit(solution)/shard_map/ppermute | solution.py:29
  21.3 4.7 %collective-permute-start.7 = (bf16[4,64,128]{2,1,0:T(8,128)(2,1)S(1)}, bf16[4,64,128]{2,1,0:T(8,128)(2,1)S(1)}, u32[]{:S(2)}, u32[]{:S(2)}) collective-permute-start(bf16[4,64,128]{2,1,0:T(8,128)(2,1)S(1)} %pad_maximum_fusion), channel_id=1, source_target_pairs={{0,32},{16,48},{32,0},{48,16},{1,33},{17,49},{33,1},{49,17},{2,34}... | collective-permute-start | bytes 196616 | tf_op jit(solution)/shard_map/ppermute | solution.py:29
  21.8 4.8 %collective-permute-start.8 = (bf16[4,64,128]{2,1,0:T(8,128)(2,1)S(1)}, bf16[4,64,128]{2,1,0:T(8,128)(2,1)S(1)}, u32[]{:S(2)}, u32[]{:S(2)}) collective-permute-start(bf16[4,64,128]{2,1,0:T(8,128)(2,1)S(1)} %pad_maximum_fusion), channel_id=1, source_target_pairs={{0,16},{16,32},{32,48},{48,0},{1,17},{17,33},{33,49},{49,1},{2,18}... | collective-permute-start | bytes 196616 | tf_op jit(solution)/shard_map/ppermute | solution.py:29
  26.0 6.3 %copy-start.4 = (s32[1,6]{1,0:T(1,128)S(1)}, s32[1,6]{1,0:T(1,128)}, u32[]{:S(2)}) copy-start(s32[1,6]{1,0:T(1,128)} %own_ids.3) | copy-start | bytes 76
  26.6 10.8 %collective-permute-start.10 = (bf16[16,64,128]{2,1,0:T(8,128)(2,1)S(1)}, bf16[16,64,128]{2,1,0:T(8,128)(2,1)S(1)}, u32[]{:S(2)}, u32[]{:S(2)}) collective-permute-start(bf16[16,64,128]{2,1,0:T(8,128)(2,1)S(1)} %constant_dynamic-update-slice_fusion.p0), channel_id=1, source_target_pairs={{0,128},{64,192},{128,0},{192,64},{1,129},{65,193},{129,1},{193,65... | collective-permute-start | bytes 786440 | tf_op jit(solution)/shard_map/ppermute | solution.py:29
  29.6 9.9 %collective-permute-start.11 = (bf16[16,64,128]{2,1,0:T(8,128)(2,1)S(1)}, bf16[16,64,128]{2,1,0:T(8,128)(2,1)S(1)}, u32[]{:S(2)}, u32[]{:S(2)}) collective-permute-start(bf16[16,64,128]{2,1,0:T(8,128)(2,1)S(1)} %constant_dynamic-update-slice_fusion.p0), channel_id=1, source_target_pairs={{0,64},{64,128},{128,192},{192,0},{1,65},{65,129},{129,193},{193,1... | collective-permute-start | bytes 786440 | tf_op jit(solution)/shard_map/ppermute | solution.py:29
  30.0 9.5 %collective-permute-start.9 = (bf16[16,64,128]{2,1,0:T(8,128)(2,1)S(1)}, bf16[16,64,128]{2,1,0:T(8,128)(2,1)S(1)}, u32[]{:S(2)}, u32[]{:S(2)}) collective-permute-start(bf16[16,64,128]{2,1,0:T(8,128)(2,1)S(1)} %constant_dynamic-update-slice_fusion.p0), channel_id=1, source_target_pairs={{0,192},{64,0},{128,64},{192,128},{1,193},{65,1},{129,65},{193,129... | collective-permute-start | bytes 786440 | tf_op jit(solution)/shard_map/ppermute | solution.py:29
  32.3 5.1 %collective-permute-start.3 = (s32[1,6]{1,0:T(1,128)S(1)}, s32[1,6]{1,0:T(1,128)S(1)}, u32[]{:S(2)}, u32[]{:S(2)}) collective-permute-start(s32[1,6]{1,0:T(1,128)S(1)} %copy-done.4), channel_id=1, source_target_pairs={{0,2},{2,0},{1,3},{3,1},{4,6},{6,4},{5,7},{7,5},{8,10},{10,8},{9,1... | collective-permute-start | bytes 80 | tf_op jit(solution)/shard_map/ppermute | solution.py:25
  37.4 7.6 %collective-permute-start.14 = (bf16[256,512]{1,0:T(8,128)(2,1)S(1)}, bf16[256,512]{1,0:T(8,128)(2,1)S(1)}, u32[]{:S(2)}, u32[]{:S(2)}) collective-permute-start(bf16[256,512]{1,0:T(8,128)(2,1)S(1)} %bitcast.15), channel_id=1, source_target_pairs={{0,1},{1,0},{2,3},{3,2},{4,5},{5,4},{6,7},{7,6},{8,9},{9,8},{10,11... | collective-permute-start | bytes 786440 | tf_op jit(solution)/shard_map/ppermute | solution.py:25
  37.5 7.5 %copy-start.1 = (bf16[1,256,768]{2,1,0:T(8,128)(2,1)S(1)}, bf16[1,256,768]{2,1,0:T(8,128)(2,1)}, u32[]{:S(2)}) copy-start(bf16[1,256,768]{2,1,0:T(8,128)(2,1)} %param.12) | copy-start | bytes 1179652
  40.6 4.4 %collective-permute-start.12 = (bf16[6,64,128]{2,1,0:T(8,128)(2,1)S(1)}, bf16[6,64,128]{2,1,0:T(8,128)(2,1)S(1)}, u32[]{:S(2)}, u32[]{:S(2)}) collective-permute-start(bf16[6,64,128]{2,1,0:T(8,128)(2,1)S(1)} %get-tuple-element.18), channel_id=1, source_target_pairs={{0,2},{2,0},{1,3},{3,1},{4,6},{6,4},{5,7},{7,5},{8,10},{10,8},{9,1... | collective-permute-start | bytes 294920 | tf_op jit(solution)/shard_map/ppermute | solution.py:25
  46.6 2.3 %collective-permute-start.15 = (f32[6,64,128]{2,1,0:T(8,128)S(1)}, f32[6,64,128]{2,1,0:T(8,128)S(1)}, u32[]{:S(2)}, u32[]{:S(2)}) collective-permute-start(f32[6,64,128]{2,1,0:T(8,128)S(1)} %get-tuple-element.20), channel_id=1, source_target_pairs={{0,2},{2,0},{1,3},{3,1},{4,6},{6,4},{5,7},{7,5},{8,10},{10,8},{9,1... | collective-permute-start | bytes 589832 | tf_op jit(solution)/shard_map/ppermute | solution.py:25
  49.8 8.8 %collective-permute-start.16 = (bf16[16,64,128]{2,1,0:T(8,128)(2,1)S(1)}, bf16[16,64,128]{2,1,0:T(8,128)(2,1)S(1)}, u32[]{:S(2)}, u32[]{:S(2)}) collective-permute-start(bf16[16,64,128]{2,1,0:T(8,128)(2,1)S(1)} %get-tuple-element.22), channel_id=1, source_target_pairs={{0,64},{64,128},{128,192},{192,0},{1,65},{65,129},{129,193},{193,1... | collective-permute-start | bytes 786440 | tf_op jit(solution)/shard_map/ppermute | solution.py:33
  50.3 14.1 %collective-permute-start.17 = (bf16[16,64,128]{2,1,0:T(8,128)(2,1)S(1)}, bf16[16,64,128]{2,1,0:T(8,128)(2,1)S(1)}, u32[]{:S(2)}, u32[]{:S(2)}) collective-permute-start(bf16[16,64,128]{2,1,0:T(8,128)(2,1)S(1)} %get-tuple-element.23), channel_id=1, source_target_pairs={{0,128},{64,192},{128,0},{192,64},{1,129},{65,193},{129,1},{193,65... | collective-permute-start | bytes 786440 | tf_op jit(solution)/shard_map/ppermute | solution.py:33
  52.7 11.8 %collective-permute-start.18 = (bf16[16,64,128]{2,1,0:T(8,128)(2,1)S(1)}, bf16[16,64,128]{2,1,0:T(8,128)(2,1)S(1)}, u32[]{:S(2)}, u32[]{:S(2)}) collective-permute-start(bf16[16,64,128]{2,1,0:T(8,128)(2,1)S(1)} %get-tuple-element.24), channel_id=1, source_target_pairs={{0,192},{64,0},{128,64},{192,128},{1,193},{65,1},{129,65},{193,129... | collective-permute-start | bytes 786440 | tf_op jit(solution)/shard_map/ppermute | solution.py:33
  64.5 3.5 %copy-start.2 = (f32[64,128]{1,0:T(8,128)S(1)}, f32[64,128]{1,0:T(8,128)}, u32[]{:S(2)}) copy-start(f32[64,128]{1,0:T(8,128)} %start.1) | copy-start | bytes 98308
  64.5 3.5 %copy-start.5 = (f32[64,128]{1,0:T(8,128)S(1)}, f32[64,128]{1,0:T(8,128)}, u32[]{:S(2)}) copy-start(f32[64,128]{1,0:T(8,128)} %param.9) | copy-start | bytes 98308
  64.5 3.5 %copy-start.6 = (f32[64]{0:T(128)S(1)}, f32[64]{0:T(128)}, u32[]{:S(2)}) copy-start(f32[64]{0:T(128)} %param.10) | copy-start | bytes 772
  64.7 10.8 %copy-start = (bf16[64,8192]{1,0:T(8,128)(2,1)S(1)}, bf16[64,8192]{1,0:T(8,128)(2,1)}, u32[]{:S(2)}) copy-start(bf16[64,8192]{1,0:T(8,128)(2,1)} %precond.1) | copy-start | bytes 3145732
  64.7 5.0 %collective-permute-start.19 = (bf16[4,64,128]{2,1,0:T(8,128)(2,1)S(1)}, bf16[4,64,128]{2,1,0:T(8,128)(2,1)S(1)}, u32[]{:S(2)}, u32[]{:S(2)}) collective-permute-start(bf16[4,64,128]{2,1,0:T(8,128)(2,1)S(1)} %get-tuple-element.38), channel_id=1, source_target_pairs={{0,16},{16,32},{32,48},{48,0},{1,17},{17,33},{33,49},{49,1},{2,18}... | collective-permute-start | bytes 196616 | tf_op jit(solution)/shard_map/ppermute | solution.py:33
  64.8 5.1 %collective-permute-start.20 = (bf16[4,64,128]{2,1,0:T(8,128)(2,1)S(1)}, bf16[4,64,128]{2,1,0:T(8,128)(2,1)S(1)}, u32[]{:S(2)}, u32[]{:S(2)}) collective-permute-start(bf16[4,64,128]{2,1,0:T(8,128)(2,1)S(1)} %get-tuple-element.40), channel_id=1, source_target_pairs={{0,32},{16,48},{32,0},{48,16},{1,33},{17,49},{33,1},{49,17},{2,34}... | collective-permute-start | bytes 196616 | tf_op jit(solution)/shard_map/ppermute | solution.py:33
  66.3 4.4 %collective-permute-start.21 = (bf16[4,64,128]{2,1,0:T(8,128)(2,1)S(1)}, bf16[4,64,128]{2,1,0:T(8,128)(2,1)S(1)}, u32[]{:S(2)}, u32[]{:S(2)}) collective-permute-start(bf16[4,64,128]{2,1,0:T(8,128)(2,1)S(1)} %get-tuple-element.39), channel_id=1, source_target_pairs={{0,48},{16,0},{32,16},{48,32},{1,49},{17,1},{33,17},{49,33},{2,50}... | collective-permute-start | bytes 196616 | tf_op jit(solution)/shard_map/ppermute | solution.py:33
  70.8 4.6 %collective-permute-start.22 = (bf16[4,64,128]{2,1,0:T(8,128)(2,1)S(1)}, bf16[4,64,128]{2,1,0:T(8,128)(2,1)S(1)}, u32[]{:S(2)}, u32[]{:S(2)}) collective-permute-start(bf16[4,64,128]{2,1,0:T(8,128)(2,1)S(1)} %get-tuple-element.29), channel_id=1, source_target_pairs={{0,4},{4,0},{8,12},{12,8},{1,5},{5,1},{9,13},{13,9},{2,6},{6,2},{1... | collective-permute-start | bytes 196616 | tf_op jit(solution)/shard_map/ppermute | solution.py:42
  75.4 5.3 %collective-permute-start.23 = (bf16[4,64,128]{2,1,0:T(8,128)(2,1)S(1)}, bf16[4,64,128]{2,1,0:T(8,128)(2,1)S(1)}, u32[]{:S(2)}, u32[]{:S(2)}) collective-permute-start(bf16[4,64,128]{2,1,0:T(8,128)(2,1)S(1)} %fusion.4), channel_id=1, source_target_pairs={{0,12},{4,8},{8,4},{12,0},{1,13},{5,9},{9,5},{13,1},{2,14},{6,10},... | collective-permute-start | bytes 196616 | tf_op jit(solution)/shard_map/ppermute | solution.py:42
  75.6 7.5 %collective-permute-start = (bf16[64,2048]{1,0:T(8,128)(2,1)S(1)}, bf16[64,2048]{1,0:T(8,128)(2,1)S(1)}, u32[]{:S(2)}, u32[]{:S(2)}) collective-permute-start(bf16[64,2048]{1,0:T(8,128)(2,1)S(1)} %get-tuple-element.37), channel_id=1, source_target_pairs={{0,64},{64,128},{128,192},{192,0},{1,65},{65,129},{129,193},{193,1... | collective-permute-start | bytes 786440 | tf_op jit(solution)/shard_map/ppermute | solution.py:33
  76.9 12.2 %collective-permute-start.1 = (bf16[64,2048]{1,0:T(8,128)(2,1)S(1)}, bf16[64,2048]{1,0:T(8,128)(2,1)S(1)}, u32[]{:S(2)}, u32[]{:S(2)}) collective-permute-start(bf16[64,2048]{1,0:T(8,128)(2,1)S(1)} %get-tuple-element.36), channel_id=1, source_target_pairs={{0,128},{64,192},{128,0},{192,64},{1,129},{65,193},{129,1},{193,65... | collective-permute-start | bytes 786440 | tf_op jit(solution)/shard_map/ppermute | solution.py:33
  80.1 15.2 %collective-permute-start.2 = (bf16[64,2048]{1,0:T(8,128)(2,1)S(1)}, bf16[64,2048]{1,0:T(8,128)(2,1)S(1)}, u32[]{:S(2)}, u32[]{:S(2)}) collective-permute-start(bf16[64,2048]{1,0:T(8,128)(2,1)S(1)} %get-tuple-element.35), channel_id=1, source_target_pairs={{0,192},{64,0},{128,64},{192,128},{1,193},{65,1},{129,65},{193,129... | collective-permute-start | bytes 786440 | tf_op jit(solution)/shard_map/ppermute | solution.py:33
  80.7 12.2 %collective-permute-start.24 = (bf16[4,64,128]{2,1,0:T(8,128)(2,1)S(1)}, bf16[4,64,128]{2,1,0:T(8,128)(2,1)S(1)}, u32[]{:S(2)}, u32[]{:S(2)}) collective-permute-start(bf16[4,64,128]{2,1,0:T(8,128)(2,1)S(1)} %fusion.3.refs_0_), channel_id=1, source_target_pairs={{0,48},{16,0},{32,16},{48,32},{1,49},{17,1},{33,17},{49,33},{2,50}... | collective-permute-start | bytes 196616 | tf_op jit(solution)/shard_map/ppermute | solution.py:29
  82.9 10.1 %collective-permute-start.25 = (bf16[4,64,128]{2,1,0:T(8,128)(2,1)S(1)}, bf16[4,64,128]{2,1,0:T(8,128)(2,1)S(1)}, u32[]{:S(2)}, u32[]{:S(2)}) collective-permute-start(bf16[4,64,128]{2,1,0:T(8,128)(2,1)S(1)} %fusion.3.refs_0_), channel_id=1, source_target_pairs={{0,32},{16,48},{32,0},{48,16},{1,33},{17,49},{33,1},{49,17},{2,34}... | collective-permute-start | bytes 196616 | tf_op jit(solution)/shard_map/ppermute | solution.py:29
  83.1 11.1 %collective-permute-start.26 = (bf16[4,64,128]{2,1,0:T(8,128)(2,1)S(1)}, bf16[4,64,128]{2,1,0:T(8,128)(2,1)S(1)}, u32[]{:S(2)}, u32[]{:S(2)}) collective-permute-start(bf16[4,64,128]{2,1,0:T(8,128)(2,1)S(1)} %fusion.3.refs_0_), channel_id=1, source_target_pairs={{0,16},{16,32},{32,48},{48,0},{1,17},{17,33},{33,49},{49,1},{2,18}... | collective-permute-start | bytes 196616 | tf_op jit(solution)/shard_map/ppermute | solution.py:29
  89.1 6.1 %collective-permute-start.27 = (bf16[4,64,128]{2,1,0:T(8,128)(2,1)S(1)}, bf16[4,64,128]{2,1,0:T(8,128)(2,1)S(1)}, u32[]{:S(2)}, u32[]{:S(2)}) collective-permute-start(bf16[4,64,128]{2,1,0:T(8,128)(2,1)S(1)} %fusion.3.refs_0_), channel_id=1, source_target_pairs={{0,2},{2,0},{1,3},{3,1},{4,6},{6,4},{5,7},{7,5},{8,10},{10,8},{9,1... | collective-permute-start | bytes 196616 | tf_op jit(solution)/shard_map/ppermute | solution.py:25
  93.0 2.3 %collective-permute-start.28 = (bf16[4,64,128]{2,1,0:T(8,128)(2,1)S(1)}, bf16[4,64,128]{2,1,0:T(8,128)(2,1)S(1)}, u32[]{:S(2)}, u32[]{:S(2)}) collective-permute-start(bf16[4,64,128]{2,1,0:T(8,128)(2,1)S(1)} %collective-permute-done.24.refs_1_), channel_id=1, source_target_pairs={{0,2},{2,0},{1,3},{3,1},{4,6},{6,4},{5,7},{7,5},{8,10},{10,8},{9,1... | collective-permute-start | bytes 196616 | tf_op jit(solution)/shard_map/ppermute | solution.py:25
  93.0 2.3 %collective-permute-start.29 = (bf16[4,64,128]{2,1,0:T(8,128)(2,1)S(1)}, bf16[4,64,128]{2,1,0:T(8,128)(2,1)S(1)}, u32[]{:S(2)}, u32[]{:S(2)}) collective-permute-start(bf16[4,64,128]{2,1,0:T(8,128)(2,1)S(1)} %collective-permute-done.25.refs_2_), channel_id=1, source_target_pairs={{0,2},{2,0},{1,3},{3,1},{4,6},{6,4},{5,7},{7,5},{8,10},{10,8},{9,1... | collective-permute-start | bytes 196616 | tf_op jit(solution)/shard_map/ppermute | solution.py:25
  94.2 2.0 %collective-permute-start.30 = (bf16[4,64,128]{2,1,0:T(8,128)(2,1)S(1)}, bf16[4,64,128]{2,1,0:T(8,128)(2,1)S(1)}, u32[]{:S(2)}, u32[]{:S(2)}) collective-permute-start(bf16[4,64,128]{2,1,0:T(8,128)(2,1)S(1)} %collective-permute-done.26.refs_3_), channel_id=1, source_target_pairs={{0,2},{2,0},{1,3},{3,1},{4,6},{6,4},{5,7},{7,5},{8,10},{10,8},{9,1... | collective-permute-start | bytes 196616 | tf_op jit(solution)/shard_map/ppermute | solution.py:25
  97.2 2.9 %collective-permute-start.31 = (f32[64,128]{1,0:T(8,128)S(1)}, f32[64,128]{1,0:T(8,128)S(1)}, u32[]{:S(2)}, u32[]{:S(2)}) collective-permute-start(f32[64,128]{1,0:T(8,128)S(1)} %get-tuple-element.26), channel_id=1, source_target_pairs={{0,192},{64,0},{128,64},{192,128},{1,193},{65,1},{129,65},{193,129... | collective-permute-start | bytes 98312 | tf_op jit(solution)/shard_map/ppermute | solution.py:29
  99.1 4.3 %collective-permute-start.32 = (f32[64,128]{1,0:T(8,128)S(1)}, f32[64,128]{1,0:T(8,128)S(1)}, u32[]{:S(2)}, u32[]{:S(2)}) collective-permute-start(f32[64,128]{1,0:T(8,128)S(1)} %get-tuple-element.27), channel_id=1, source_target_pairs={{0,128},{64,192},{128,0},{192,64},{1,129},{65,193},{129,1},{193,65... | collective-permute-start | bytes 98312 | tf_op jit(solution)/shard_map/ppermute | solution.py:29
  99.1 4.3 %collective-permute-start.33 = (f32[64,128]{1,0:T(8,128)S(1)}, f32[64,128]{1,0:T(8,128)S(1)}, u32[]{:S(2)}, u32[]{:S(2)}) collective-permute-start(f32[64,128]{1,0:T(8,128)S(1)} %get-tuple-element.28), channel_id=1, source_target_pairs={{0,64},{64,128},{128,192},{192,0},{1,65},{65,129},{129,193},{193,1... | collective-permute-start | bytes 98312 | tf_op jit(solution)/shard_map/ppermute | solution.py:29

commit v3 on v2

--- a/solution.py
+++ b/solution.py
@@ -54,25 +54,17 @@
 
 
 def place(tile, where):
-    dy = (tile // 16 - where[0]) % RING
-    dx = ((tile // 4) % 4 - where[1]) % RING
-    return dy, dx * 4 + line_slot(tile % 4, where[2])
-
-
-def pick_kernel(where, own_ids, other_ids, p0, p1, p2, p3, own_ref, other_ref):
-    pieces = (p0, p1, p2, p3)
+    return tile - tile % RING + line_slot(tile % RING, where[2])
+
+
+def pick_kernel(where, own_ids, other_ids, gathered, own_ref, other_ref):
     for ids, out in ((other_ids, other_ref), (own_ids, own_ref)):
         for j in range(ids.shape[1]):
-            dy, rest = place(ids[0, j], where)
-            for k, piece in enumerate(pieces):
-
-                @pl.when(dy == k)
-                def _():
-                    out[j] = piece[rest]
+            out[j] = gathered[place(ids[0, j], where)]
 
 
 def scenario_kernel(
-    where, count, own_picked, other_picked, border_own, border_other, inverse_own, inverse_other,
+    where, own_picked, other_picked, border_own, border_other, inverse_own, inverse_other,
     keep_ref, send_ref, picked, values,
 ):
     core, side = where[3], where[4]
@@ -84,7 +76,7 @@
     rows = lax.broadcasted_iota(jnp.int32, (half_rows, values.shape[1]), 0)
     own_start = pl.multiple_of(side * half_rows, half_rows)
     other_start = pl.multiple_of((1 - side) * half_rows, half_rows)
-    live = count[0]
+    live = where[5]
 
     def masked(product, start):
         return jnp.where(rows + start < live, product, 0.0).astype(BF16)
@@ -115,15 +107,12 @@
         send_ref[...] = term[:, 0]
 
 
-def scatter_kernel(where, own_ids, other_ids, keep, arrived, near, c1, c2, c3, total):
+def scatter_kernel(where, own_ids, other_ids, keep, arrived, out, total):
     total[...] = jnp.zeros_like(total)
     for ids, terms in ((own_ids, keep), (other_ids, arrived)):
         for j in range(ids.shape[1]):
-            dy, rest = place(ids[0, j], where)
-            total[dy * 16 + rest] += terms[j]
-    near[...] = total[0:16]
-    for k, chunk in enumerate((c1, c2, c3)):
-        chunk[...] = total[16 * (k + 1) : 16 * (k + 2)].astype(BF16)
+            total[place(ids[0, j], where)] += terms[j]
+    out[...] = total[...].astype(BF16)
 
 
 def update_kernel(where, start, precond, b1, b2, b3, *refs):
@@ -170,51 +159,54 @@
 ):
     rows, cols = start_guess.shape
     shape = jax.ShapeDtypeStruct
-    where = jnp.stack([lax.axis_index(a) for a in (Y, X, Z, CORE, SIDE)]).astype(jnp.int32)
+    where = jnp.stack(
+        [*(lax.axis_index(a).astype(jnp.int32) for a in (Y, X, Z, CORE, SIDE)), border_count[0]]
+    )
     border, inverse = border_block[0], coupling_inverse[0]
     tiles = column_tiles.shape[1]
+    everywhere = RING * RING * RING
 
     line = line_gather(start_guess.astype(BF16))
-    plane = jnp.concatenate(ring_pieces(line, X))
-    pieces = ring_pieces(plane, Y)
     span = preconditioner.shape[1] // RING
-    blocks = []
-    for k in range(1, RING):
+
+    def for_ahead(k):
         first = ((where[0] + k) % RING) * span
-        columns = lax.dynamic_slice_in_dim(preconditioner, first, span, 1)
-        blocks.append(to_ahead(columns, Y, k))
+        return lax.dynamic_slice_in_dim(preconditioner, first, span, 1)
+
+    block1 = to_ahead(for_ahead(1), Y, 1)
+    line, block1, border_late, inverse_late = lax.optimization_barrier((line, block1, border, inverse))
+    border_other = swap(border_late, SIDE)
+    inverse_other = swap(inverse_late, SIDE)
     other_tiles = swap(column_tiles, CORE)
-    border_other = swap(border, SIDE)
-    inverse_other = swap(inverse, SIDE)
+    copies = jnp.broadcast_to(line, (RING * RING, *line.shape))
+    gathered = lax.all_to_all(copies, (Y, X), 0, 0, tiled=True)
 
     own_half, for_other = call(
         pick_kernel,
-        [SMEM] * 3 + [VMEM] * 4,
+        [SMEM] * 3 + [VMEM],
         [shape((tiles, HALF, cols), BF16)] * 2,
-    )(where, column_tiles, other_tiles, *pieces)
+    )(where, column_tiles, other_tiles, gathered.reshape(everywhere, HALF, cols))
     other_half = swap(for_other, CORE)
+    gate, columns3 = lax.optimization_barrier((own_half, for_ahead(3)))
+    block3 = to_ahead(columns3, Y, 3)
     keep, send = call(
         scenario_kernel,
-        [SMEM] * 2 + [VMEM] * 6,
+        [SMEM] + [VMEM] * 6,
         [shape((tiles, HALF, cols), F32)] * 2,
         [pltpu.VMEM((tiles * TILE, cols), BF16), pltpu.VMEM((2 * border.shape[0], cols), BF16)],
-    )(where, border_count, own_half, other_half, border, border_other, inverse, inverse_other)
+    )(where, gate, other_half, border, border_other, inverse, inverse_other)
     arrived = swap(send, CORE)
-    chunk = (16, HALF, cols)
-    near, c1, c2, c3 = call(
+    spread = call(
         scatter_kernel,
         [SMEM] * 3 + [VMEM] * 2,
-        [shape(chunk, F32)] + [shape(chunk, BF16)] * 3,
-        [pltpu.VMEM((64, HALF, cols), F32)],
+        shape((everywhere, HALF, cols), BF16),
+        [pltpu.VMEM((everywhere, HALF, cols), F32)],
     )(where, column_tiles, other_tiles, keep, arrived)
-
-    plane = near
-    for k, c in enumerate((c1, c2, c3)):
-        plane = plane + to_ahead(c, Y, k + 1).astype(F32)
-    plane = plane.reshape(RING, RING, HALF, cols)
-    line = plane[0]
-    for k in range(1, RING):
-        line = line + to_ahead(plane[k].astype(BF16), X, k).astype(F32)
+    spread, block3 = lax.optimization_barrier((spread, block3))
+    terms = lax.all_to_all(spread.reshape(RING * RING, RING, HALF, cols), (Y, X), 0, 0, tiled=True)
+    line = terms.astype(F32).sum(axis=0)
+    columns2, line = lax.optimization_barrier((for_ahead(2), line))
+    block2 = to_ahead(columns2, Y, 2)
     own_terms = right_side - root_diagonal[:, None] * start_guess
     line = line + jnp.concatenate([own_terms[None], jnp.zeros_like(line[1:])])
     met = pair(Z, line.astype(BF16), True).astype(F32)
@@ -229,7 +221,7 @@
         [SMEM] + [VMEM] * 13,
         [shape((rows, cols), F32)] * RING,
         [pltpu.VMEM((span, cols), BF16)],
-    )(where, start_guess, preconditioner, *blocks, *mine, *partners)
+    )(where, start_guess, preconditioner, block1, block2, block3, *mine, *partners)
     out = parts[0]
     for k in range(1, RING):
         out = out + from_ahead(parts[k], Y, k)

time: 104 us -> 98.9 us (0.951)
  waiting for transfers between devices: 44.9 us -> 25.1 us
  blocking collectives: 0 us -> 19.4 us
  starting transfers between devices: 51.7 us -> 44.4 us
  local copies, waits for them, and re-layouts: 0.28 us -> 2.53 us
    all_to_all x0 -> x1, blocking collectives: none -> 19.4 us  [local(): lax.all_to_all(spread.reshape(RING * RING, RING, HALF, cols), (Y, X), 0,...]
    ppermute x9 -> x3, waiting for transfers between devices: 19.7 us -> 4.15 us  [to_ahead(): lax.ppermute(value, axis, [(i, (i + distance) % RING) for i in range(RING)])]
    ppermute x12 -> x6, starting transfers between devices: 14.7 us -> 4.04 us  [from_ahead(): lax.ppermute(value, axis, [(i, (i - distance) % RING) for i in range(RING)])]
    all_to_all x0 -> x1, waiting for transfers between devices: none -> 9.03 us  [local(): gathered = lax.all_to_all(copies, (Y, X), 0, 0, tiled=True)]
    ppermute x9 -> x3, starting transfers between devices: 10.9 us -> 2.47 us  [to_ahead(): lax.ppermute(value, axis, [(i, (i + distance) % RING) for i in range(RING)])]
    ppermute x12 -> x6, waiting for transfers between devices: 9.88 us -> 3.39 us  [from_ahead(): lax.ppermute(value, axis, [(i, (i - distance) % RING) for i in range(RING)])]
    ppermute x4, waiting for transfers between devices: 12.2 us -> 5.9 us  [pair(): return lax.ppermute(value, axis, list(enumerate(other)))]
    all_to_all x0 -> x1, starting transfers between devices: none -> 5.55 us  [local(): gathered = lax.all_to_all(copies, (Y, X), 0, 0, tiled=True)]
  transfers between devices with their start and end apart: 34 -> 23, of which waited for: 20 -> 13; matrix products, arithmetic and copies ran while one was open for 0% -> 1% of each run, Pallas kernels for 1% -> 3%
where the time goes in v3:
time: 98.9 us; the launch traced here: 98.1 us
  starting transfers between devices  44.4 us (45%)
  waiting for transfers between devices  25.1 us (25%)
  blocking collectives  19.4 us (20%)
  Pallas kernels  4.07 us (4%)
  local copies, waits for them, and re-layouts  2.53 us (3%)
  other arithmetic  1.8 us (2%)
    all_to_all x1, blocking collectives, local(): lax.all_to_all(spread.reshape(RING * RING, RING, HALF, cols), (Y, X), 0,...  19.4 us
    ppermute x9, starting transfers between devices, swap(): return lax.ppermute(value, axis, SWAP)  18.8 us
    ppermute x4, starting transfers between devices, pair(): return lax.ppermute(value, axis, list(enumerate(other)))  13.6 us
    all_to_all x1, waiting for transfers between devices, local(): gathered = lax.all_to_all(copies, (Y, X), 0, 0, tiled=True)  9.03 us
    ppermute x4, waiting for transfers between devices, pair(): return lax.ppermute(value, axis, list(enumerate(other)))  5.9 us
    all_to_all x1, starting transfers between devices, local(): gathered = lax.all_to_all(copies, (Y, X), 0, 0, tiled=True)  5.55 us
    ppermute x3, waiting for transfers between devices, to_ahead(): lax.ppermute(value, axis, [(i, (i + distance) % RING) for i in range(RING)])  4.15 us
    ppermute x6, starting transfers between devices, from_ahead(): lax.ppermute(value, axis, [(i, (i - distance) % RING) for i in range(RING)])  4.04 us
  transfers between devices with their start and end apart: 23, of which 13 were waited for; matrix products, arithmetic and copies ran while one was open for 1% of the time, Pallas kernels for 3%

profile of v3, /device:TPU:1, one launch (start us, length us, event | category | flops | bytes accessed | tf_op | source)
XLA Modules:
  0.0 98.1 jit_solution(2206447359923646308)
XLA Ops:
  0.0 0.9 subtract_bitcast_fusion
  0.9 3.9 %collective-permute-start = (bf16[64,128]{1,0:T(8,128)(2,1)S(1)}, bf16[64,128]{1,0:T(8,128)(2,1)S(1)}, u32[]{:S(2)}, u32[]{:S(2)}) collective-permute-start(bf16[64,128]{1,0:T(8,128)(2,1)S(1)} %get-tuple-element.51), channel_id=1, source_target_pairs={{0,4},{4,0},{8,12},{12,8},{1,5},{5,1},{9,13},{13,9},{2,6},{6,2},{1... | collective-permute-start | bytes 49160 | tf_op jit(solution)/shard_map/ppermute | solution.py:42
  4.8 1.2 %constant_dynamic-slice_fusion = (bf16[64,2048]{1,0:T(8,128)(2,1)S(1)}, bf16[64,2048]{1,0:T(8,128)(2,1)S(1)}, bf16[64,2048]{1,0:T(8,128)(2,1)S(1)}) fusion(bf16[64,8192]{1,0:T(8,128)(2,1)} %precond.1, s32[]{:T(128)S(6)} %select_n.29, s32[]{:T(128)S(6)} %select_n.27, s32[]{:T(128)S(6)} %select_n.25), kind=kLoop, calls=%fused_computation.10 | loop fusion | bytes 1572876 | tf_op jit(solution)/shard_map/dynamic_slice | solution.py:174
  6.0 1.4 %collective-permute-start.2 = (bf16[64,2048]{1,0:T(8,128)(2,1)S(1)}, bf16[64,2048]{1,0:T(8,128)(2,1)S(1)}, u32[]{:S(2)}, u32[]{:S(2)}) collective-permute-start(bf16[64,2048]{1,0:T(8,128)(2,1)S(1)} %get-tuple-element.43), channel_id=1, source_target_pairs={{0,64},{64,128},{128,192},{192,0},{1,65},{65,129},{129,193},{193,1... | collective-permute-start | bytes 786440 | tf_op jit(solution)/shard_map/ppermute | solution.py:33
  7.4 4.3 %collective-permute-start.1 = (bf16[2,64,128]{2,1,0:T(8,128)(2,1)S(1)}, bf16[2,64,128]{2,1,0:T(8,128)(2,1)S(1)}, u32[]{:S(2)}, u32[]{:S(2)}) collective-permute-start(bf16[2,64,128]{2,1,0:T(8,128)(2,1)S(1)} %pad_maximum_fusion.1), channel_id=1, source_target_pairs={{0,12},{4,8},{8,4},{12,0},{1,13},{5,9},{9,5},{13,1},{2,14},{6,10},... | collective-permute-start | bytes 98312 | tf_op jit(solution)/shard_map/ppermute | solution.py:42
  11.6 1.4 %collective-permute-done.1 = bf16[2,64,128]{2,1,0:T(8,128)(2,1)S(1)} collective-permute-done((bf16[2,64,128]{2,1,0:T(8,128)(2,1)S(1)}, bf16[2,64,128]{2,1,0:T(8,128)(2,1)S(1)}, u32[]{:S(2)}, u32[]{:S(2)}) %collective-permute-start.1) | collective-permute-done | bytes 32800 | tf_op jit(solution)/shard_map/ppermute | solution.py:42
  13.1 1.2 %collective-permute-done.2.b1 = bf16[64,2048]{1,0:T(8,128)(2,1)S(1)} collective-permute-done((bf16[64,2048]{1,0:T(8,128)(2,1)S(1)}, bf16[64,2048]{1,0:T(8,128)(2,1)S(1)}, u32[]{:S(2)}, u32[]{:S(2)}) %collective-permute-start.2) | collective-permute-done | bytes 262176 | tf_op jit(solution)/shard_map/ppermute | solution.py:33
  14.2 1.2 %broadcast_in_dim.8 = bf16[16,4,64,128]{3,2,1,0:T(8,128)(2,1)} broadcast(bf16[4,64,128]{2,1,0:T(8,128)(2,1)S(1)} %pad_maximum_fusion), dimensions={1,2,3} | broadcast | bytes 1114112 | tf_op jit(solution)/shard_map/broadcast_in_dim | solution.py:181
  15.5 5.5 %all-to-all-start = ((bf16[16,4,64,128]{3,2,1,0:T(8,128)(2,1)}), bf16[16,4,64,128]{3,2,1,0:T(8,128)(2,1)S(1)}, u32[]{:S(2)}, u32[]{:S(2)}) async-start(bf16[16,4,64,128]{3,2,1,0:T(8,128)(2,1)} %broadcast_in_dim.8), calls=%async_computation | async-start | bytes 2097152 | tf_op jit(solution)/shard_map/all_to_all | solution.py:182
  21.0 1.7 %collective-permute-start.5 = (bf16[256,768]{1,0:T(8,128)(2,1)S(1)}, bf16[256,768]{1,0:T(8,128)(2,1)S(1)}, u32[]{:S(2)}, u32[]{:S(2)}) collective-permute-start(bf16[256,768]{1,0:T(8,128)(2,1)S(1)} %bitcast.15), channel_id=1, source_target_pairs={{0,1},{1,0},{2,3},{3,2},{4,5},{5,4},{6,7},{7,6},{8,9},{9,8},{10,11... | collective-permute-start | bytes 1179656 | tf_op jit(solution)/shard_map/ppermute | solution.py:25
  22.8 0.1 collective-permute-start.6
  22.9 3.0 %collective-permute-start.3 = (s32[1,6]{1,0:T(1,128)S(1)}, s32[1,6]{1,0:T(1,128)S(1)}, u32[]{:S(2)}, u32[]{:S(2)}) collective-permute-start(s32[1,6]{1,0:T(1,128)S(1)} %copy-done.4), channel_id=1, source_target_pairs={{0,2},{2,0},{1,3},{3,1},{4,6},{6,4},{5,7},{7,5},{8,10},{10,8},{9,1... | collective-permute-start | bytes 80 | tf_op jit(solution)/shard_map/ppermute | solution.py:25
  26.5 0.1 stack.35.where
  26.6 0.1 collective-permute-done.3.other_ids
  26.7 9.0 %all-to-all-done = bf16[16,4,64,128]{3,2,1,0:T(8,128)(2,1)S(1)} async-done(((bf16[16,4,64,128]{3,2,1,0:T(8,128)(2,1)}), bf16[16,4,64,128]{3,2,1,0:T(8,128)(2,1)S(1)}, u32[]{:S(2)}, u32[]{:S(2)}) %all-to-all-start) | async-done | bytes 1048608 | tf_op jit(solution)/shard_map/all_to_all | solution.py:182
  35.7 0.6 shard_map.82
  36.3 3.9 %collective-permute-start.4 = (bf16[6,64,128]{2,1,0:T(8,128)(2,1)S(1)}, bf16[6,64,128]{2,1,0:T(8,128)(2,1)S(1)}, u32[]{:S(2)}, u32[]{:S(2)}) collective-permute-start(bf16[6,64,128]{2,1,0:T(8,128)(2,1)S(1)} %get-tuple-element.27), channel_id=1, source_target_pairs={{0,2},{2,0},{1,3},{3,1},{4,6},{6,4},{5,7},{7,5},{8,10},{10,8},{9,1... | collective-permute-start | bytes 294920 | tf_op jit(solution)/shard_map/ppermute | solution.py:25
  40.2 0.4 collective-permute-start.8
  40.6 0.6 collective-permute-done.4.other_picked
  41.2 1.6 %shard_map.83 = (f32[6,64,128]{2,1,0:T(8,128)S(1)}, f32[6,64,128]{2,1,0:T(8,128)S(1)}) custom-call(s32[6]{0:T(128)S(1)} %stack.35.where, bf16[6,64,128]{2,1,0:T(8,128)(2,1)S(1)} %get-tuple-element.26.own_picked, bf16[6,64,128]{2,1,0:T(8,128)(2,1)S(1)} %collective-permute-done.4.other_picked, bf16[256,768]{1,0:T(8,128)(2,1)S(1)} %bitcast.16, ...), custom_call_target="tpu_custom_call" | custom-call | tf_op jit(solution)/shard_map/pallas_call | solution.py:192
  42.8 0.4 collective-permute-start.7
  43.2 1.1 %collective-permute-done.7.arrived = f32[6,64,128]{2,1,0:T(8,128)S(1)} collective-permute-done((f32[6,64,128]{2,1,0:T(8,128)S(1)}, f32[6,64,128]{2,1,0:T(8,128)S(1)}, u32[]{:S(2)}, u32[]{:S(2)}) %collective-permute-start.7) | collective-permute-done | bytes 196640 | tf_op jit(solution)/shard_map/ppermute | solution.py:25
  44.3 0.9 shard_map.84
  45.1 3.0 %collective-permute-done.8.b3 = bf16[64,2048]{1,0:T(8,128)(2,1)S(1)} collective-permute-done((bf16[64,2048]{1,0:T(8,128)(2,1)S(1)}, bf16[64,2048]{1,0:T(8,128)(2,1)S(1)}, u32[]{:S(2)}, u32[]{:S(2)}) %collective-permute-start.8) | collective-permute-done | bytes 262176 | tf_op jit(solution)/shard_map/ppermute | solution.py:33
  48.1 19.4 %all_to_all.10 = bf16[16,4,64,128]{3,2,1,0:T(8,128)(2,1)S(1)} all-to-all(bf16[16,4,64,128]{3,2,1,0:T(8,128)(2,1)S(1)} %bitcast.14), channel_id=1, replica_groups=mesh['scen_0'=4,'scen_1'=4,'scen_2'=4,'rootr'=2,'rootc'=2] {'scen_0','sc..., dimensions={0} | all-to-all | bytes 2097152 | tf_op jit(solution)/shard_map/all_to_all | solution.py:206
  67.5 0.2 convert_reduce_fusion
  67.7 0.0 copy-start
  67.7 0.0 copy-start.3
  67.8 1.1 %collective-permute-start.10 = (bf16[4,64,128]{2,1,0:T(8,128)(2,1)S(1)}, bf16[4,64,128]{2,1,0:T(8,128)(2,1)S(1)}, u32[]{:S(2)}, u32[]{:S(2)}) collective-permute-start(bf16[4,64,128]{2,1,0:T(8,128)(2,1)S(1)} %fusion.1), channel_id=1, source_target_pairs={{0,4},{4,0},{8,12},{12,8},{1,5},{5,1},{9,13},{13,9},{2,6},{6,2},{1... | collective-permute-start | bytes 196616 | tf_op jit(solution)/shard_map/ppermute | solution.py:42
  68.8 3.0 %collective-permute-done.10 = bf16[4,64,128]{2,1,0:T(8,128)(2,1)S(1)} collective-permute-done((bf16[4,64,128]{2,1,0:T(8,128)(2,1)S(1)}, bf16[4,64,128]{2,1,0:T(8,128)(2,1)S(1)}, u32[]{:S(2)}, u32[]{:S(2)}) %collective-permute-start.10) | collective-permute-done | bytes 65568 | tf_op jit(solution)/shard_map/ppermute | solution.py:42
  71.9 4.3 %collective-permute-start.11 = (bf16[4,64,128]{2,1,0:T(8,128)(2,1)S(1)}, bf16[4,64,128]{2,1,0:T(8,128)(2,1)S(1)}, u32[]{:S(2)}, u32[]{:S(2)}) collective-permute-start(bf16[4,64,128]{2,1,0:T(8,128)(2,1)S(1)} %fusion.2), channel_id=1, source_target_pairs={{0,12},{4,8},{8,4},{12,0},{1,13},{5,9},{9,5},{13,1},{2,14},{6,10},... | collective-permute-start | bytes 196616 | tf_op jit(solution)/shard_map/ppermute | solution.py:42
  76.3 0.7 collective-permute-start.9
  77.0 1.4 %collective-permute-done.11 = bf16[4,64,128]{2,1,0:T(8,128)(2,1)S(1)} collective-permute-done((bf16[4,64,128]{2,1,0:T(8,128)(2,1)S(1)}, bf16[4,64,128]{2,1,0:T(8,128)(2,1)S(1)}, u32[]{:S(2)}, u32[]{:S(2)}) %collective-permute-start.11) | collective-permute-done | bytes 65568 | tf_op jit(solution)/shard_map/ppermute | solution.py:42
  78.5 0.3 collective-permute-start.12
  78.8 1.9 %collective-permute-start.13 = (bf16[4,64,128]{2,1,0:T(8,128)(2,1)S(1)}, bf16[4,64,128]{2,1,0:T(8,128)(2,1)S(1)}, u32[]{:S(2)}, u32[]{:S(2)}) collective-permute-start(bf16[4,64,128]{2,1,0:T(8,128)(2,1)S(1)} %fusion.refs_0_), channel_id=1, source_target_pairs={{0,32},{16,48},{32,0},{48,16},{1,33},{17,49},{33,1},{49,17},{2,34}... | collective-permute-start | bytes 196616 | tf_op jit(solution)/shard_map/ppermute | solution.py:29
  80.6 4.1 %collective-permute-start.15 = (bf16[4,64,128]{2,1,0:T(8,128)(2,1)S(1)}, bf16[4,64,128]{2,1,0:T(8,128)(2,1)S(1)}, u32[]{:S(2)}, u32[]{:S(2)}) collective-permute-start(bf16[4,64,128]{2,1,0:T(8,128)(2,1)S(1)} %fusion.refs_0_), channel_id=1, source_target_pairs={{0,2},{2,0},{1,3},{3,1},{4,6},{6,4},{5,7},{7,5},{8,10},{10,8},{9,1... | collective-permute-start | bytes 196616 | tf_op jit(solution)/shard_map/ppermute | solution.py:25
  84.8 1.6 %collective-permute-start.16 = (bf16[4,64,128]{2,1,0:T(8,128)(2,1)S(1)}, bf16[4,64,128]{2,1,0:T(8,128)(2,1)S(1)}, u32[]{:S(2)}, u32[]{:S(2)}) collective-permute-start(bf16[4,64,128]{2,1,0:T(8,128)(2,1)S(1)} %collective-permute-done.12.refs_1_), channel_id=1, source_target_pairs={{0,2},{2,0},{1,3},{3,1},{4,6},{6,4},{5,7},{7,5},{8,10},{10,8},{9,1... | collective-permute-start | bytes 196616 | tf_op jit(solution)/shard_map/ppermute | solution.py:25
  86.4 2.0 %collective-permute-start.17 = (bf16[4,64,128]{2,1,0:T(8,128)(2,1)S(1)}, bf16[4,64,128]{2,1,0:T(8,128)(2,1)S(1)}, u32[]{:S(2)}, u32[]{:S(2)}) collective-permute-start(bf16[4,64,128]{2,1,0:T(8,128)(2,1)S(1)} %collective-permute-done.13.refs_2_), channel_id=1, source_target_pairs={{0,2},{2,0},{1,3},{3,1},{4,6},{6,4},{5,7},{7,5},{8,10},{10,8},{9,1... | collective-permute-start | bytes 196616 | tf_op jit(solution)/shard_map/ppermute | solution.py:25
  88.4 1.8 %collective-permute-start.18 = (bf16[4,64,128]{2,1,0:T(8,128)(2,1)S(1)}, bf16[4,64,128]{2,1,0:T(8,128)(2,1)S(1)}, u32[]{:S(2)}, u32[]{:S(2)}) collective-permute-start(bf16[4,64,128]{2,1,0:T(8,128)(2,1)S(1)} %collective-permute-done.14.refs_3_), channel_id=1, source_target_pairs={{0,2},{2,0},{1,3},{3,1},{4,6},{6,4},{5,7},{7,5},{8,10},{10,8},{9,1... | collective-permute-start | bytes 196616 | tf_op jit(solution)/shard_map/ppermute | solution.py:25
  90.3 0.9 collective-permute-done.18.refs_7_
  91.2 1.0 %shard_map.85 = (f32[64,128]{1,0:T(8,128)S(1)}, f32[64,128]{1,0:T(8,128)S(1)}, f32[64,128]{1,0:T(8,128)S(1)}, f32[64,128]{1,0:T(8,128)S(1)}) custom-call(s32[6]{0:T(128)S(1)} %stack.35.where, f32[64,128]{1,0:T(8,128)S(1)} %copy-done.3, bf16[64,8192]{1,0:T(8,128)(2,1)S(1)} %copy-done, bf16[64,2048]{1,0:T(8,128)(2,1)S(1)} %collective-permute-done.2.b1, ...), custom_call_target="tpu_custom_call" | custom-call | tf_op jit(solution)/shard_map/pallas_call | solution.py:219
  92.2 0.7 collective-permute-start.19
  92.9 0.5 collective-permute-start.20
  93.3 0.8 collective-permute-start.21
  94.1 0.9 collective-permute-done.19
  95.1 2.1 %collective-permute-done.20 = f32[64,128]{1,0:T(8,128)S(1)} collective-permute-done((f32[64,128]{1,0:T(8,128)S(1)}, f32[64,128]{1,0:T(8,128)S(1)}, u32[]{:S(2)}, u32[]{:S(2)}) %collective-permute-start.20) | collective-permute-done | bytes 32800 | tf_op jit(solution)/shard_map/ppermute | solution.py:29
  97.1 0.4 collective-permute-done.21
  97.5 0.6 add_add_fusion
  (26 shorter events, 0.1 us)
Async XLA Ops:
  0.9 6.4 %collective-permute-start = (bf16[64,128]{1,0:T(8,128)(2,1)S(1)}, bf16[64,128]{1,0:T(8,128)(2,1)S(1)}, u32[]{:S(2)}, u32[]{:S(2)}) collective-permute-start(bf16[64,128]{1,0:T(8,128)(2,1)S(1)} %get-tuple-element.51), channel_id=1, source_target_pairs={{0,4},{4,0},{8,12},{12,8},{1,5},{5,1},{9,13},{13,9},{2,6},{6,2},{1... | collective-permute-start | bytes 49160 | tf_op jit(solution)/shard_map/ppermute | solution.py:42
  6.0 8.3 %collective-permute-start.2 = (bf16[64,2048]{1,0:T(8,128)(2,1)S(1)}, bf16[64,2048]{1,0:T(8,128)(2,1)S(1)}, u32[]{:S(2)}, u32[]{:S(2)}) collective-permute-start(bf16[64,2048]{1,0:T(8,128)(2,1)S(1)} %get-tuple-element.43), channel_id=1, source_target_pairs={{0,64},{64,128},{128,192},{192,0},{1,65},{65,129},{129,193},{193,1... | collective-permute-start | bytes 786440 | tf_op jit(solution)/shard_map/ppermute | solution.py:33
  7.4 5.7 %collective-permute-start.1 = (bf16[2,64,128]{2,1,0:T(8,128)(2,1)S(1)}, bf16[2,64,128]{2,1,0:T(8,128)(2,1)S(1)}, u32[]{:S(2)}, u32[]{:S(2)}) collective-permute-start(bf16[2,64,128]{2,1,0:T(8,128)(2,1)S(1)} %pad_maximum_fusion.1), channel_id=1, source_target_pairs={{0,12},{4,8},{8,4},{12,0},{1,13},{5,9},{9,5},{13,1},{2,14},{6,10},... | collective-permute-start | bytes 98312 | tf_op jit(solution)/shard_map/ppermute | solution.py:42
  15.5 5.6 %copy-start.1 = (bf16[1,256,768]{2,1,0:T(8,128)(2,1)S(1)}, bf16[1,256,768]{2,1,0:T(8,128)(2,1)}, u32[]{:S(2)}) copy-start(bf16[1,256,768]{2,1,0:T(8,128)(2,1)} %param.12) | copy-start | bytes 1179652
  15.5 7.3 %copy-start.2 = (bf16[1,256,512]{2,1,0:T(8,128)(2,1)S(1)}, bf16[1,256,512]{2,1,0:T(8,128)(2,1)}, u32[]{:S(2)}) copy-start(bf16[1,256,512]{2,1,0:T(8,128)(2,1)} %param.13) | copy-start | bytes 786436
  15.5 7.4 %copy-start.4 = (s32[1,6]{1,0:T(1,128)S(1)}, s32[1,6]{1,0:T(1,128)}, u32[]{:S(2)}) copy-start(s32[1,6]{1,0:T(1,128)} %own_ids.3) | copy-start | bytes 76
  15.5 20.2 %all-to-all-start = ((bf16[16,4,64,128]{3,2,1,0:T(8,128)(2,1)}), bf16[16,4,64,128]{3,2,1,0:T(8,128)(2,1)S(1)}, u32[]{:S(2)}, u32[]{:S(2)}) async-start(bf16[16,4,64,128]{3,2,1,0:T(8,128)(2,1)} %broadcast_in_dim.8), calls=%async_computation | async-start | bytes 2097152 | tf_op jit(solution)/shard_map/all_to_all | solution.py:182
  21.0 19.6 %collective-permute-start.5 = (bf16[256,768]{1,0:T(8,128)(2,1)S(1)}, bf16[256,768]{1,0:T(8,128)(2,1)S(1)}, u32[]{:S(2)}, u32[]{:S(2)}) collective-permute-start(bf16[256,768]{1,0:T(8,128)(2,1)S(1)} %bitcast.15), channel_id=1, source_target_pairs={{0,1},{1,0},{2,3},{3,2},{4,5},{5,4},{6,7},{7,6},{8,9},{9,8},{10,11... | collective-permute-start | bytes 1179656 | tf_op jit(solution)/shard_map/ppermute | solution.py:25
  22.8 17.9 %collective-permute-start.6 = (bf16[256,512]{1,0:T(8,128)(2,1)S(1)}, bf16[256,512]{1,0:T(8,128)(2,1)S(1)}, u32[]{:S(2)}, u32[]{:S(2)}) collective-permute-start(bf16[256,512]{1,0:T(8,128)(2,1)S(1)} %bitcast.17), channel_id=1, source_target_pairs={{0,1},{1,0},{2,3},{3,2},{4,5},{5,4},{6,7},{7,6},{8,9},{9,8},{10,11... | collective-permute-start | bytes 786440 | tf_op jit(solution)/shard_map/ppermute | solution.py:25
  22.9 3.8 %collective-permute-start.3 = (s32[1,6]{1,0:T(1,128)S(1)}, s32[1,6]{1,0:T(1,128)S(1)}, u32[]{:S(2)}, u32[]{:S(2)}) collective-permute-start(s32[1,6]{1,0:T(1,128)S(1)} %copy-done.4), channel_id=1, source_target_pairs={{0,2},{2,0},{1,3},{3,1},{4,6},{6,4},{5,7},{7,5},{8,10},{10,8},{9,1... | collective-permute-start | bytes 80 | tf_op jit(solution)/shard_map/ppermute | solution.py:25
  36.3 4.8 %collective-permute-start.4 = (bf16[6,64,128]{2,1,0:T(8,128)(2,1)S(1)}, bf16[6,64,128]{2,1,0:T(8,128)(2,1)S(1)}, u32[]{:S(2)}, u32[]{:S(2)}) collective-permute-start(bf16[6,64,128]{2,1,0:T(8,128)(2,1)S(1)} %get-tuple-element.27), channel_id=1, source_target_pairs={{0,2},{2,0},{1,3},{3,1},{4,6},{6,4},{5,7},{7,5},{8,10},{10,8},{9,1... | collective-permute-start | bytes 294920 | tf_op jit(solution)/shard_map/ppermute | solution.py:25
  40.2 7.9 %collective-permute-start.8 = (bf16[64,2048]{1,0:T(8,128)(2,1)S(1)}, bf16[64,2048]{1,0:T(8,128)(2,1)S(1)}, u32[]{:S(2)}, u32[]{:S(2)}) collective-permute-start(bf16[64,2048]{1,0:T(8,128)(2,1)S(1)} %get-tuple-element.32), channel_id=1, source_target_pairs={{0,192},{64,0},{128,64},{192,128},{1,193},{65,1},{129,65},{193,129... | collective-permute-start | bytes 786440 | tf_op jit(solution)/shard_map/ppermute | solution.py:33
  42.8 1.5 %collective-permute-start.7 = (f32[6,64,128]{2,1,0:T(8,128)S(1)}, f32[6,64,128]{2,1,0:T(8,128)S(1)}, u32[]{:S(2)}, u32[]{:S(2)}) collective-permute-start(f32[6,64,128]{2,1,0:T(8,128)S(1)} %get-tuple-element.31), channel_id=1, source_target_pairs={{0,2},{2,0},{1,3},{3,1},{4,6},{6,4},{5,7},{7,5},{8,10},{10,8},{9,1... | collective-permute-start | bytes 589832 | tf_op jit(solution)/shard_map/ppermute | solution.py:25
  67.7 23.4 %copy-start = (bf16[64,8192]{1,0:T(8,128)(2,1)S(1)}, bf16[64,8192]{1,0:T(8,128)(2,1)}, u32[]{:S(2)}) copy-start(bf16[64,8192]{1,0:T(8,128)(2,1)} %precond.1) | copy-start | bytes 3145732
  67.7 23.4 %copy-start.3 = (f32[64,128]{1,0:T(8,128)S(1)}, f32[64,128]{1,0:T(8,128)}, u32[]{:S(2)}) copy-start(f32[64,128]{1,0:T(8,128)} %start.1) | copy-start | bytes 98308
  67.8 4.1 %collective-permute-start.10 = (bf16[4,64,128]{2,1,0:T(8,128)(2,1)S(1)}, bf16[4,64,128]{2,1,0:T(8,128)(2,1)S(1)}, u32[]{:S(2)}, u32[]{:S(2)}) collective-permute-start(bf16[4,64,128]{2,1,0:T(8,128)(2,1)S(1)} %fusion.1), channel_id=1, source_target_pairs={{0,4},{4,0},{8,12},{12,8},{1,5},{5,1},{9,13},{13,9},{2,6},{6,2},{1... | collective-permute-start | bytes 196616 | tf_op jit(solution)/shard_map/ppermute | solution.py:42
  71.9 6.5 %collective-permute-start.11 = (bf16[4,64,128]{2,1,0:T(8,128)(2,1)S(1)}, bf16[4,64,128]{2,1,0:T(8,128)(2,1)S(1)}, u32[]{:S(2)}, u32[]{:S(2)}) collective-permute-start(bf16[4,64,128]{2,1,0:T(8,128)(2,1)S(1)} %fusion.2), channel_id=1, source_target_pairs={{0,12},{4,8},{8,4},{12,0},{1,13},{5,9},{9,5},{13,1},{2,14},{6,10},... | collective-permute-start | bytes 196616 | tf_op jit(solution)/shard_map/ppermute | solution.py:42
  76.3 14.0 %collective-permute-start.9 = (bf16[64,2048]{1,0:T(8,128)(2,1)S(1)}, bf16[64,2048]{1,0:T(8,128)(2,1)S(1)}, u32[]{:S(2)}, u32[]{:S(2)}) collective-permute-start(bf16[64,2048]{1,0:T(8,128)(2,1)S(1)} %get-tuple-element.34), channel_id=1, source_target_pairs={{0,128},{64,192},{128,0},{192,64},{1,129},{65,193},{129,1},{193,65... | collective-permute-start | bytes 786440 | tf_op jit(solution)/shard_map/ppermute | solution.py:33
  78.5 6.3 %collective-permute-start.12 = (bf16[4,64,128]{2,1,0:T(8,128)(2,1)S(1)}, bf16[4,64,128]{2,1,0:T(8,128)(2,1)S(1)}, u32[]{:S(2)}, u32[]{:S(2)}) collective-permute-start(bf16[4,64,128]{2,1,0:T(8,128)(2,1)S(1)} %fusion.refs_0_), channel_id=1, source_target_pairs={{0,48},{16,0},{32,16},{48,32},{1,49},{17,1},{33,17},{49,33},{2,50}... | collective-permute-start | bytes 196616 | tf_op jit(solution)/shard_map/ppermute | solution.py:29
  78.8 7.6 %collective-permute-start.13 = (bf16[4,64,128]{2,1,0:T(8,128)(2,1)S(1)}, bf16[4,64,128]{2,1,0:T(8,128)(2,1)S(1)}, u32[]{:S(2)}, u32[]{:S(2)}) collective-permute-start(bf16[4,64,128]{2,1,0:T(8,128)(2,1)S(1)} %fusion.refs_0_), channel_id=1, source_target_pairs={{0,32},{16,48},{32,0},{48,16},{1,33},{17,49},{33,1},{49,17},{2,34}... | collective-permute-start | bytes 196616 | tf_op jit(solution)/shard_map/ppermute | solution.py:29
  80.6 7.8 %collective-permute-start.14 = (bf16[4,64,128]{2,1,0:T(8,128)(2,1)S(1)}, bf16[4,64,128]{2,1,0:T(8,128)(2,1)S(1)}, u32[]{:S(2)}, u32[]{:S(2)}) collective-permute-start(bf16[4,64,128]{2,1,0:T(8,128)(2,1)S(1)} %fusion.refs_0_), channel_id=1, source_target_pairs={{0,16},{16,32},{32,48},{48,0},{1,17},{17,33},{33,49},{49,1},{2,18}... | collective-permute-start | bytes 196616 | tf_op jit(solution)/shard_map/ppermute | solution.py:29
  80.6 9.6 %collective-permute-start.15 = (bf16[4,64,128]{2,1,0:T(8,128)(2,1)S(1)}, bf16[4,64,128]{2,1,0:T(8,128)(2,1)S(1)}, u32[]{:S(2)}, u32[]{:S(2)}) collective-permute-start(bf16[4,64,128]{2,1,0:T(8,128)(2,1)S(1)} %fusion.refs_0_), channel_id=1, source_target_pairs={{0,2},{2,0},{1,3},{3,1},{4,6},{6,4},{5,7},{7,5},{8,10},{10,8},{9,1... | collective-permute-start | bytes 196616 | tf_op jit(solution)/shard_map/ppermute | solution.py:25
  84.8 5.5 %collective-permute-start.16 = (bf16[4,64,128]{2,1,0:T(8,128)(2,1)S(1)}, bf16[4,64,128]{2,1,0:T(8,128)(2,1)S(1)}, u32[]{:S(2)}, u32[]{:S(2)}) collective-permute-start(bf16[4,64,128]{2,1,0:T(8,128)(2,1)S(1)} %collective-permute-done.12.refs_1_), channel_id=1, source_target_pairs={{0,2},{2,0},{1,3},{3,1},{4,6},{6,4},{5,7},{7,5},{8,10},{10,8},{9,1... | collective-permute-start | bytes 196616 | tf_op jit(solution)/shard_map/ppermute | solution.py:25
  86.4 3.9 %collective-permute-start.17 = (bf16[4,64,128]{2,1,0:T(8,128)(2,1)S(1)}, bf16[4,64,128]{2,1,0:T(8,128)(2,1)S(1)}, u32[]{:S(2)}, u32[]{:S(2)}) collective-permute-start(bf16[4,64,128]{2,1,0:T(8,128)(2,1)S(1)} %collective-permute-done.13.refs_2_), channel_id=1, source_target_pairs={{0,2},{2,0},{1,3},{3,1},{4,6},{6,4},{5,7},{7,5},{8,10},{10,8},{9,1... | collective-permute-start | bytes 196616 | tf_op jit(solution)/shard_map/ppermute | solution.py:25
  88.4 2.7 %collective-permute-start.18 = (bf16[4,64,128]{2,1,0:T(8,128)(2,1)S(1)}, bf16[4,64,128]{2,1,0:T(8,128)(2,1)S(1)}, u32[]{:S(2)}, u32[]{:S(2)}) collective-permute-start(bf16[4,64,128]{2,1,0:T(8,128)(2,1)S(1)} %collective-permute-done.14.refs_3_), channel_id=1, source_target_pairs={{0,2},{2,0},{1,3},{3,1},{4,6},{6,4},{5,7},{7,5},{8,10},{10,8},{9,1... | collective-permute-start | bytes 196616 | tf_op jit(solution)/shard_map/ppermute | solution.py:25
  92.2 2.8 %collective-permute-start.19 = (f32[64,128]{1,0:T(8,128)S(1)}, f32[64,128]{1,0:T(8,128)S(1)}, u32[]{:S(2)}, u32[]{:S(2)}) collective-permute-start(f32[64,128]{1,0:T(8,128)S(1)} %get-tuple-element.38), channel_id=1, source_target_pairs={{0,192},{64,0},{128,64},{192,128},{1,193},{65,1},{129,65},{193,129... | collective-permute-start | bytes 98312 | tf_op jit(solution)/shard_map/ppermute | solution.py:29
  92.9 4.3 %collective-permute-start.20 = (f32[64,128]{1,0:T(8,128)S(1)}, f32[64,128]{1,0:T(8,128)S(1)}, u32[]{:S(2)}, u32[]{:S(2)}) collective-permute-start(f32[64,128]{1,0:T(8,128)S(1)} %get-tuple-element.39), channel_id=1, source_target_pairs={{0,128},{64,192},{128,0},{192,64},{1,129},{65,193},{129,1},{193,65... | collective-permute-start | bytes 98312 | tf_op jit(solution)/shard_map/ppermute | solution.py:29
  93.3 4.1 %collective-permute-start.21 = (f32[64,128]{1,0:T(8,128)S(1)}, f32[64,128]{1,0:T(8,128)S(1)}, u32[]{:S(2)}, u32[]{:S(2)}) collective-permute-start(f32[64,128]{1,0:T(8,128)S(1)} %get-tuple-element.40), channel_id=1, source_target_pairs={{0,64},{64,128},{128,192},{192,0},{1,65},{65,129},{129,193},{193,1... | collective-permute-start | bytes 98312 | tf_op jit(solution)/shard_map/ppermute | solution.py:29

commit v4 on v3

--- a/solution.py
+++ b/solution.py
@@ -169,17 +169,20 @@
     line = line_gather(start_guess.astype(BF16))
     span = preconditioner.shape[1] // RING
 
-    def for_ahead(k):
-        first = ((where[0] + k) % RING) * span
-        return lax.dynamic_slice_in_dim(preconditioner, first, span, 1)
-
-    block1 = to_ahead(for_ahead(1), Y, 1)
-    line, block1, border_late, inverse_late = lax.optimization_barrier((line, block1, border, inverse))
+    line, late, border_late, inverse_late = lax.optimization_barrier(
+        (line, preconditioner, border, inverse)
+    )
+    columns = [
+        lax.dynamic_slice_in_dim(late, ((where[0] + k) % RING) * span, span, 1)
+        for k in range(1, RING)
+    ]
+    block1, block3 = to_ahead(columns[0], Y, 1), to_ahead(columns[2], Y, 3)
     border_other = swap(border_late, SIDE)
     inverse_other = swap(inverse_late, SIDE)
     other_tiles = swap(column_tiles, CORE)
     copies = jnp.broadcast_to(line, (RING * RING, *line.shape))
     gathered = lax.all_to_all(copies, (Y, X), 0, 0, tiled=True)
+    gathered, block1, block3 = lax.optimization_barrier((gathered, block1, block3))
 
     own_half, for_other = call(
         pick_kernel,
@@ -187,14 +190,14 @@
         [shape((tiles, HALF, cols), BF16)] * 2,
     )(where, column_tiles, other_tiles, gathered.reshape(everywhere, HALF, cols))
     other_half = swap(for_other, CORE)
-    gate, columns3 = lax.optimization_barrier((own_half, for_ahead(3)))
-    block3 = to_ahead(columns3, Y, 3)
+    own_half, columns2 = lax.optimization_barrier((own_half, columns[1]))
+    block2 = to_ahead(columns2, Y, 2)
     keep, send = call(
         scenario_kernel,
         [SMEM] + [VMEM] * 6,
         [shape((tiles, HALF, cols), F32)] * 2,
         [pltpu.VMEM((tiles * TILE, cols), BF16), pltpu.VMEM((2 * border.shape[0], cols), BF16)],
-    )(where, gate, other_half, border, border_other, inverse, inverse_other)
+    )(where, own_half, other_half, border, border_other, inverse, inverse_other)
     arrived = swap(send, CORE)
     spread = call(
         scatter_kernel,
@@ -202,11 +205,9 @@
         shape((everywhere, HALF, cols), BF16),
         [pltpu.VMEM((everywhere, HALF, cols), F32)],
     )(where, column_tiles, other_tiles, keep, arrived)
-    spread, block3 = lax.optimization_barrier((spread, block3))
     terms = lax.all_to_all(spread.reshape(RING * RING, RING, HALF, cols), (Y, X), 0, 0, tiled=True)
+    terms, block2 = lax.optimization_barrier((terms, block2))
     line = terms.astype(F32).sum(axis=0)
-    columns2, line = lax.optimization_barrier((for_ahead(2), line))
-    block2 = to_ahead(columns2, Y, 2)
     own_terms = right_side - root_diagonal[:, None] * start_guess
     line = line + jnp.concatenate([own_terms[None], jnp.zeros_like(line[1:])])
     met = pair(Z, line.astype(BF16), True).astype(F32)

time: 98.9 us -> 107 us (1.082)
  blocking collectives: 19.4 us -> 0 us
  waiting for transfers between devices: 25.1 us -> 40.9 us
  starting transfers between devices: 44.4 us -> 55.1 us
  Pallas kernels: 4.07 us -> 5.54 us
    ppermute x3, waiting for transfers between devices: 4.15 us -> 27.3 us  [to_ahead(): lax.ppermute(value, axis, [(i, (i + distance) % RING) for i in range(RING)])]
    all_to_all x1 -> x0, blocking collectives: 19.4 us -> none  [local(): lax.all_to_all(spread.reshape(RING * RING, RING, HALF, cols), (Y, X), 0,...]
    all_to_all x1, waiting for transfers between devices: 9.03 us -> 0.01 us  [local(): gathered = lax.all_to_all(copies, (Y, X), 0, 0, tiled=True)]
    all_to_all x0 -> x1, starting transfers between devices: none -> 5.06 us  [local(): lax.all_to_all(spread.reshape(RING * RING, RING, HALF, cols), (Y, X), 0,...]
    ppermute x6, starting transfers between devices: 4.04 us -> 8.63 us  [from_ahead(): lax.ppermute(value, axis, [(i, (i - distance) % RING) for i in range(RING)])]
    ppermute x9, starting transfers between devices: 18.8 us -> 15 us  [swap(): return lax.ppermute(value, axis, SWAP)]
    ppermute x3, starting transfers between devices: 2.47 us -> 5.63 us  [to_ahead(): lax.ppermute(value, axis, [(i, (i + distance) % RING) for i in range(RING)])]
    ppermute x4, waiting for transfers between devices: 5.9 us -> 8.1 us  [pair(): return lax.ppermute(value, axis, list(enumerate(other)))]
  transfers between devices with their start and end apart: 23 -> 24, of which waited for: 13 -> 13; matrix products, arithmetic and copies ran while one was open for 1% -> 1% of each run, Pallas kernels for 3% -> 1%
where the time goes in v4:
time: 107 us; the launch traced here: 106 us
  starting transfers between devices  55.1 us (51%)
  waiting for transfers between devices  40.9 us (38%)
  Pallas kernels  5.54 us (5%)
  local copies, waits for them, and re-layouts  2.27 us (2%)
  other arithmetic  1.8 us (2%)
    ppermute x3, waiting for transfers between devices, to_ahead(): lax.ppermute(value, axis, [(i, (i + distance) % RING) for i in range(RING)])  27.3 us
    ppermute x9, starting transfers between devices, swap(): return lax.ppermute(value, axis, SWAP)  15 us
    ppermute x4, starting transfers between devices, pair(): return lax.ppermute(value, axis, list(enumerate(other)))  13.9 us
    ppermute x6, starting transfers between devices, from_ahead(): lax.ppermute(value, axis, [(i, (i - distance) % RING) for i in range(RING)])  8.63 us
    ppermute x4, waiting for transfers between devices, pair(): return lax.ppermute(value, axis, list(enumerate(other)))  8.1 us
    all_to_all x1, starting transfers between devices, local(): gathered = lax.all_to_all(copies, (Y, X), 0, 0, tiled=True)  6.89 us
    ppermute x3, starting transfers between devices, to_ahead(): lax.ppermute(value, axis, [(i, (i + distance) % RING) for i in range(RING)])  5.63 us
    all_to_all x1, starting transfers between devices, local(): lax.all_to_all(spread.reshape(RING * RING, RING, HALF, cols), (Y, X), 0,...  5.06 us
  transfers between devices with their start and end apart: 24, of which 13 were waited for; matrix products, arithmetic and copies ran while one was open for 1% of the time, Pallas kernels for 1%

profile of v4, /device:TPU:1, one launch (start us, length us, event | category | flops | bytes accessed | tf_op | source)
XLA Modules:
  0.0 106.4 jit_solution(11715080205698958211)
XLA Ops:
  0.0 0.9 subtract_bitcast_fusion
  0.9 3.9 %collective-permute-start = (bf16[64,128]{1,0:T(8,128)(2,1)S(1)}, bf16[64,128]{1,0:T(8,128)(2,1)S(1)}, u32[]{:S(2)}, u32[]{:S(2)}) collective-permute-start(bf16[64,128]{1,0:T(8,128)(2,1)S(1)} %get-tuple-element.53), channel_id=1, source_target_pairs={{0,4},{4,0},{8,12},{12,8},{1,5},{5,1},{9,13},{13,9},{2,6},{6,2},{1... | collective-permute-start | bytes 49160 | tf_op jit(solution)/shard_map/ppermute | solution.py:42
  4.8 1.1 %collective-permute-done = bf16[64,128]{1,0:T(8,128)(2,1)S(1)} collective-permute-done((bf16[64,128]{1,0:T(8,128)(2,1)S(1)}, bf16[64,128]{1,0:T(8,128)(2,1)S(1)}, u32[]{:S(2)}, u32[]{:S(2)}) %collective-permute-start) | collective-permute-done | bytes 16416 | tf_op jit(solution)/shard_map/ppermute | solution.py:42
  5.9 5.4 %collective-permute-start.1 = (bf16[2,64,128]{2,1,0:T(8,128)(2,1)S(1)}, bf16[2,64,128]{2,1,0:T(8,128)(2,1)S(1)}, u32[]{:S(2)}, u32[]{:S(2)}) collective-permute-start(bf16[2,64,128]{2,1,0:T(8,128)(2,1)S(1)} %pad_maximum_fusion.1), channel_id=1, source_target_pairs={{0,12},{4,8},{8,4},{12,0},{1,13},{5,9},{9,5},{13,1},{2,14},{6,10},... | collective-permute-start | bytes 98312 | tf_op jit(solution)/shard_map/ppermute | solution.py:42
  11.3 1.3 %collective-permute-done.1 = bf16[2,64,128]{2,1,0:T(8,128)(2,1)S(1)} collective-permute-done((bf16[2,64,128]{2,1,0:T(8,128)(2,1)S(1)}, bf16[2,64,128]{2,1,0:T(8,128)(2,1)S(1)}, u32[]{:S(2)}, u32[]{:S(2)}) %collective-permute-start.1) | collective-permute-done | bytes 32800 | tf_op jit(solution)/shard_map/ppermute | solution.py:42
  12.6 1.2 %broadcast_in_dim.8 = bf16[16,4,64,128]{3,2,1,0:T(8,128)(2,1)} broadcast(bf16[4,64,128]{2,1,0:T(8,128)(2,1)S(1)} %pad_maximum_fusion), dimensions={1,2,3} | broadcast | bytes 1114112 | tf_op jit(solution)/shard_map/broadcast_in_dim | solution.py:183
  13.9 6.9 %all-to-all-start = ((bf16[16,4,64,128]{3,2,1,0:T(8,128)(2,1)}), bf16[16,4,64,128]{3,2,1,0:T(8,128)(2,1)S(1)}, u32[]{:S(2)}, u32[]{:S(2)}) async-start(bf16[16,4,64,128]{3,2,1,0:T(8,128)(2,1)} %broadcast_in_dim.8), calls=%async_computation | async-start | bytes 2097152 | tf_op jit(solution)/shard_map/all_to_all | solution.py:184
  20.8 0.0 copy-start.2
  20.8 0.8 collective-permute-start.6
  21.7 0.9 constant_dynamic-slice_fusion
  22.6 1.4 %collective-permute-start.2 = (bf16[64,2048]{1,0:T(8,128)(2,1)}, bf16[64,2048]{1,0:T(8,128)(2,1)}, u32[]{:S(2)}, u32[]{:S(2)}) collective-permute-start(bf16[64,2048]{1,0:T(8,128)(2,1)} %get-tuple-element.45), channel_id=1, source_target_pairs={{0,64},{64,128},{128,192},{192,0},{1,65},{65,129},{129,193},{193,1... | collective-permute-start | bytes 786440 | tf_op jit(solution)/shard_map/ppermute | solution.py:33
  23.9 1.3 %collective-permute-start.3 = (bf16[64,2048]{1,0:T(8,128)(2,1)}, bf16[64,2048]{1,0:T(8,128)(2,1)}, u32[]{:S(2)}, u32[]{:S(2)}) collective-permute-start(bf16[64,2048]{1,0:T(8,128)(2,1)} %get-tuple-element.44), channel_id=1, source_target_pairs={{0,192},{64,0},{128,64},{192,128},{1,193},{65,1},{129,65},{193,129... | collective-permute-start | bytes 786440 | tf_op jit(solution)/shard_map/ppermute | solution.py:33
  25.2 0.7 collective-permute-start.7
  26.0 4.1 %collective-permute-start.4 = (s32[1,6]{1,0:T(1,128)S(1)}, s32[1,6]{1,0:T(1,128)S(1)}, u32[]{:S(2)}, u32[]{:S(2)}) collective-permute-start(s32[1,6]{1,0:T(1,128)S(1)} %copy-done.4), channel_id=1, source_target_pairs={{0,2},{2,0},{1,3},{3,1},{4,6},{6,4},{5,7},{7,5},{8,10},{10,8},{9,1... | collective-permute-start | bytes 80 | tf_op jit(solution)/shard_map/ppermute | solution.py:25
  30.7 0.1 stack.35.where
  30.8 10.2 %collective-permute-done.2.b1 = bf16[64,2048]{1,0:T(8,128)(2,1)} collective-permute-done((bf16[64,2048]{1,0:T(8,128)(2,1)}, bf16[64,2048]{1,0:T(8,128)(2,1)}, u32[]{:S(2)}, u32[]{:S(2)}) %collective-permute-start.2) | collective-permute-done | bytes 262176 | tf_op jit(solution)/shard_map/ppermute | solution.py:33
  41.0 0.6 shard_map.82
  41.6 1.8 %collective-permute-start.5 = (bf16[6,64,128]{2,1,0:T(8,128)(2,1)S(1)}, bf16[6,64,128]{2,1,0:T(8,128)(2,1)S(1)}, u32[]{:S(2)}, u32[]{:S(2)}) collective-permute-start(bf16[6,64,128]{2,1,0:T(8,128)(2,1)S(1)} %get-tuple-element.30), channel_id=1, source_target_pairs={{0,2},{2,0},{1,3},{3,1},{4,6},{6,4},{5,7},{7,5},{8,10},{10,8},{9,1... | collective-permute-start | bytes 294920 | tf_op jit(solution)/shard_map/ppermute | solution.py:25
  43.4 0.9 collective-permute-done.5.other_picked
  44.3 1.6 %shard_map.83 = (f32[6,64,128]{2,1,0:T(8,128)S(1)}, f32[6,64,128]{2,1,0:T(8,128)S(1)}) custom-call(s32[6]{0:T(128)S(1)} %stack.35.where, bf16[6,64,128]{2,1,0:T(8,128)(2,1)S(1)} %get-tuple-element.29.own_picked, bf16[6,64,128]{2,1,0:T(8,128)(2,1)S(1)} %collective-permute-done.5.other_picked, bf16[256,768]{1,0:T(8,128)(2,1)S(1)} %bitcast.15, ...), custom_call_target="tpu_custom_call" | custom-call | tf_op jit(solution)/shard_map/pallas_call | solution.py:195
  45.9 0.4 collective-permute-start.8
  46.3 1.1 %collective-permute-done.8.arrived = f32[6,64,128]{2,1,0:T(8,128)S(1)} collective-permute-done((f32[6,64,128]{2,1,0:T(8,128)S(1)}, f32[6,64,128]{2,1,0:T(8,128)S(1)}, u32[]{:S(2)}, u32[]{:S(2)}) %collective-permute-start.8) | collective-permute-done | bytes 196640 | tf_op jit(solution)/shard_map/ppermute | solution.py:25
  47.4 1.8 %shard_map.84 = bf16[64,64,128]{2,1,0:T(8,128)(2,1)} custom-call(s32[6]{0:T(128)S(1)} %stack.35.where, s32[1,6]{1,0:T(1,128)S(1)} %copy-done.4, s32[1,6]{1,0:T(1,128)S(1)} %collective-permute-done.4.other_ids, f32[6,64,128]{2,1,0:T(8,128)S(1)} %get-tuple-element.33.keep, f32[6,64,128]{2,1,0:T(8,128)S(1)} %collective-permute-done.8.arrived), custom_call_target="tpu_custom_call" | custom-call | tf_op jit(solution)/shard_map/pallas_call | solution.py:202
  49.2 5.1 %all-to-all-start.1 = ((bf16[16,4,64,128]{3,2,1,0:T(8,128)(2,1)}), bf16[16,4,64,128]{3,2,1,0:T(8,128)(2,1)S(1)}, u32[]{:S(2)}, u32[]{:S(2)}) async-start(bf16[16,4,64,128]{3,2,1,0:T(8,128)(2,1)} %bitcast.10), calls=%async_computation.1 | async-start | bytes 2097152 | tf_op jit(solution)/shard_map/all_to_all | solution.py:208
  54.3 3.0 %collective-permute-start.9 = (bf16[64,2048]{1,0:T(8,128)(2,1)S(1)}, bf16[64,2048]{1,0:T(8,128)(2,1)S(1)}, u32[]{:S(2)}, u32[]{:S(2)}) collective-permute-start(bf16[64,2048]{1,0:T(8,128)(2,1)S(1)} %copy-done.5), channel_id=1, source_target_pairs={{0,128},{64,192},{128,0},{192,64},{1,129},{65,193},{129,1},{193,65... | collective-permute-start | bytes 786440 | tf_op jit(solution)/shard_map/ppermute | solution.py:33
  57.3 17.1 %collective-permute-done.9.b2 = bf16[64,2048]{1,0:T(8,128)(2,1)S(1)} collective-permute-done((bf16[64,2048]{1,0:T(8,128)(2,1)S(1)}, bf16[64,2048]{1,0:T(8,128)(2,1)S(1)}, u32[]{:S(2)}, u32[]{:S(2)}) %collective-permute-start.9) | collective-permute-done | bytes 262176 | tf_op jit(solution)/shard_map/ppermute | solution.py:33
  74.4 0.2 convert_reduce_fusion
  74.6 1.4 %collective-permute-start.10 = (bf16[4,64,128]{2,1,0:T(8,128)(2,1)S(1)}, bf16[4,64,128]{2,1,0:T(8,128)(2,1)S(1)}, u32[]{:S(2)}, u32[]{:S(2)}) collective-permute-start(bf16[4,64,128]{2,1,0:T(8,128)(2,1)S(1)} %fusion.1), channel_id=1, source_target_pairs={{0,4},{4,0},{8,12},{12,8},{1,5},{5,1},{9,13},{13,9},{2,6},{6,2},{1... | collective-permute-start | bytes 196616 | tf_op jit(solution)/shard_map/ppermute | solution.py:42
  76.1 3.4 %collective-permute-done.10 = bf16[4,64,128]{2,1,0:T(8,128)(2,1)S(1)} collective-permute-done((bf16[4,64,128]{2,1,0:T(8,128)(2,1)S(1)}, bf16[4,64,128]{2,1,0:T(8,128)(2,1)S(1)}, u32[]{:S(2)}, u32[]{:S(2)}) %collective-permute-start.10) | collective-permute-done | bytes 65568 | tf_op jit(solution)/shard_map/ppermute | solution.py:42
  79.5 3.1 %collective-permute-start.11 = (bf16[4,64,128]{2,1,0:T(8,128)(2,1)S(1)}, bf16[4,64,128]{2,1,0:T(8,128)(2,1)S(1)}, u32[]{:S(2)}, u32[]{:S(2)}) collective-permute-start(bf16[4,64,128]{2,1,0:T(8,128)(2,1)S(1)} %fusion.2), channel_id=1, source_target_pairs={{0,12},{4,8},{8,4},{12,0},{1,13},{5,9},{9,5},{13,1},{2,14},{6,10},... | collective-permute-start | bytes 196616 | tf_op jit(solution)/shard_map/ppermute | solution.py:42
  82.6 2.3 %collective-permute-done.11 = bf16[4,64,128]{2,1,0:T(8,128)(2,1)S(1)} collective-permute-done((bf16[4,64,128]{2,1,0:T(8,128)(2,1)S(1)}, bf16[4,64,128]{2,1,0:T(8,128)(2,1)S(1)}, u32[]{:S(2)}, u32[]{:S(2)}) %collective-permute-start.11) | collective-permute-done | bytes 65568 | tf_op jit(solution)/shard_map/ppermute | solution.py:42
  85.0 2.7 %collective-permute-start.12 = (bf16[4,64,128]{2,1,0:T(8,128)(2,1)S(1)}, bf16[4,64,128]{2,1,0:T(8,128)(2,1)S(1)}, u32[]{:S(2)}, u32[]{:S(2)}) collective-permute-start(bf16[4,64,128]{2,1,0:T(8,128)(2,1)S(1)} %fusion.refs_0_), channel_id=1, source_target_pairs={{0,48},{16,0},{32,16},{48,32},{1,49},{17,1},{33,17},{49,33},{2,50}... | collective-permute-start | bytes 196616 | tf_op jit(solution)/shard_map/ppermute | solution.py:29
  87.7 2.3 %collective-permute-start.13 = (bf16[4,64,128]{2,1,0:T(8,128)(2,1)S(1)}, bf16[4,64,128]{2,1,0:T(8,128)(2,1)S(1)}, u32[]{:S(2)}, u32[]{:S(2)}) collective-permute-start(bf16[4,64,128]{2,1,0:T(8,128)(2,1)S(1)} %fusion.refs_0_), channel_id=1, source_target_pairs={{0,32},{16,48},{32,0},{48,16},{1,33},{17,49},{33,1},{49,17},{2,34}... | collective-permute-start | bytes 196616 | tf_op jit(solution)/shard_map/ppermute | solution.py:29
  89.9 0.8 collective-permute-start.14
  90.7 2.8 %collective-permute-start.15 = (bf16[4,64,128]{2,1,0:T(8,128)(2,1)S(1)}, bf16[4,64,128]{2,1,0:T(8,128)(2,1)S(1)}, u32[]{:S(2)}, u32[]{:S(2)}) collective-permute-start(bf16[4,64,128]{2,1,0:T(8,128)(2,1)S(1)} %fusion.refs_0_), channel_id=1, source_target_pairs={{0,2},{2,0},{1,3},{3,1},{4,6},{6,4},{5,7},{7,5},{8,10},{10,8},{9,1... | collective-permute-start | bytes 196616 | tf_op jit(solution)/shard_map/ppermute | solution.py:25
  93.5 0.2 collective-permute-start.16
  93.8 3.5 %collective-permute-start.17 = (bf16[4,64,128]{2,1,0:T(8,128)(2,1)S(1)}, bf16[4,64,128]{2,1,0:T(8,128)(2,1)S(1)}, u32[]{:S(2)}, u32[]{:S(2)}) collective-permute-start(bf16[4,64,128]{2,1,0:T(8,128)(2,1)S(1)} %collective-permute-done.13.refs_2_), channel_id=1, source_target_pairs={{0,2},{2,0},{1,3},{3,1},{4,6},{6,4},{5,7},{7,5},{8,10},{10,8},{9,1... | collective-permute-start | bytes 196616 | tf_op jit(solution)/shard_map/ppermute | solution.py:25
  97.2 0.7 collective-permute-start.18
  97.9 0.2 collective-permute-done.17.refs_6_
  98.1 0.7 collective-permute-done.18.refs_7_
  98.8 1.5 %shard_map.85 = (f32[64,128]{1,0:T(8,128)S(1)}, f32[64,128]{1,0:T(8,128)S(1)}, f32[64,128]{1,0:T(8,128)S(1)}, f32[64,128]{1,0:T(8,128)S(1)}) custom-call(s32[6]{0:T(128)S(1)} %stack.35.where, f32[64,128]{1,0:T(8,128)S(1)} %copy-done.3, bf16[64,8192]{1,0:T(8,128)(2,1)S(1)} %copy-done, bf16[64,2048]{1,0:T(8,128)(2,1)} %collective-permute-done.2.b1, ...), custom_call_target="tpu_custom_call" | custom-call | tf_op jit(solution)/shard_map/pallas_call | solution.py:220
  100.3 0.4 collective-permute-start.21
  100.8 2.0 %collective-permute-start.20 = (f32[64,128]{1,0:T(8,128)S(1)}, f32[64,128]{1,0:T(8,128)S(1)}, u32[]{:S(2)}, u32[]{:S(2)}) collective-permute-start(f32[64,128]{1,0:T(8,128)S(1)} %get-tuple-element.41), channel_id=1, source_target_pairs={{0,128},{64,192},{128,0},{192,64},{1,129},{65,193},{129,1},{193,65... | collective-permute-start | bytes 98312 | tf_op jit(solution)/shard_map/ppermute | solution.py:29
  102.8 0.5 collective-permute-start.19
  103.3 1.2 %collective-permute-done.21 = f32[64,128]{1,0:T(8,128)S(1)} collective-permute-done((f32[64,128]{1,0:T(8,128)S(1)}, f32[64,128]{1,0:T(8,128)S(1)}, u32[]{:S(2)}, u32[]{:S(2)}) %collective-permute-start.21) | collective-permute-done | bytes 32800 | tf_op jit(solution)/shard_map/ppermute | solution.py:29
  104.4 0.9 collective-permute-done.20
  105.3 0.5 collective-permute-done.19
  105.8 0.6 add_add_fusion
  (29 shorter events, 0.2 us)
Async XLA Ops:
  0.9 5.0 %collective-permute-start = (bf16[64,128]{1,0:T(8,128)(2,1)S(1)}, bf16[64,128]{1,0:T(8,128)(2,1)S(1)}, u32[]{:S(2)}, u32[]{:S(2)}) collective-permute-start(bf16[64,128]{1,0:T(8,128)(2,1)S(1)} %get-tuple-element.53), channel_id=1, source_target_pairs={{0,4},{4,0},{8,12},{12,8},{1,5},{5,1},{9,13},{13,9},{2,6},{6,2},{1... | collective-permute-start | bytes 49160 | tf_op jit(solution)/shard_map/ppermute | solution.py:42
  5.9 6.7 %collective-permute-start.1 = (bf16[2,64,128]{2,1,0:T(8,128)(2,1)S(1)}, bf16[2,64,128]{2,1,0:T(8,128)(2,1)S(1)}, u32[]{:S(2)}, u32[]{:S(2)}) collective-permute-start(bf16[2,64,128]{2,1,0:T(8,128)(2,1)S(1)} %pad_maximum_fusion.1), channel_id=1, source_target_pairs={{0,12},{4,8},{8,4},{12,0},{1,13},{5,9},{9,5},{13,1},{2,14},{6,10},... | collective-permute-start | bytes 98312 | tf_op jit(solution)/shard_map/ppermute | solution.py:42
  13.9 7.0 %copy-start.1 = (bf16[1,256,768]{2,1,0:T(8,128)(2,1)S(1)}, bf16[1,256,768]{2,1,0:T(8,128)(2,1)}, u32[]{:S(2)}) copy-start(bf16[1,256,768]{2,1,0:T(8,128)(2,1)} %param.12) | copy-start | bytes 1179652
  13.9 7.8 %copy-start = (bf16[64,8192]{1,0:T(8,128)(2,1)S(1)}, bf16[64,8192]{1,0:T(8,128)(2,1)}, u32[]{:S(2)}) copy-start(bf16[64,8192]{1,0:T(8,128)(2,1)} %precond.1) | copy-start | bytes 3145732
  13.9 27.1 %all-to-all-start = ((bf16[16,4,64,128]{3,2,1,0:T(8,128)(2,1)}), bf16[16,4,64,128]{3,2,1,0:T(8,128)(2,1)S(1)}, u32[]{:S(2)}, u32[]{:S(2)}) async-start(bf16[16,4,64,128]{3,2,1,0:T(8,128)(2,1)} %broadcast_in_dim.8), calls=%async_computation | async-start | bytes 2097152 | tf_op jit(solution)/shard_map/all_to_all | solution.py:184
  20.8 4.5 %copy-start.2 = (bf16[1,256,512]{2,1,0:T(8,128)(2,1)S(1)}, bf16[1,256,512]{2,1,0:T(8,128)(2,1)}, u32[]{:S(2)}) copy-start(bf16[1,256,512]{2,1,0:T(8,128)(2,1)} %param.13) | copy-start | bytes 786436
  20.8 5.2 %copy-start.4 = (s32[1,6]{1,0:T(1,128)S(1)}, s32[1,6]{1,0:T(1,128)}, u32[]{:S(2)}) copy-start(s32[1,6]{1,0:T(1,128)} %own_ids.3) | copy-start | bytes 76
  20.8 22.5 %collective-permute-start.6 = (bf16[256,768]{1,0:T(8,128)(2,1)S(1)}, bf16[256,768]{1,0:T(8,128)(2,1)S(1)}, u32[]{:S(2)}, u32[]{:S(2)}) collective-permute-start(bf16[256,768]{1,0:T(8,128)(2,1)S(1)} %bitcast.14), channel_id=1, source_target_pairs={{0,1},{1,0},{2,3},{3,2},{4,5},{5,4},{6,7},{7,6},{8,9},{9,8},{10,11... | collective-permute-start | bytes 1179656 | tf_op jit(solution)/shard_map/ppermute | solution.py:25
  22.6 18.4 %collective-permute-start.2 = (bf16[64,2048]{1,0:T(8,128)(2,1)}, bf16[64,2048]{1,0:T(8,128)(2,1)}, u32[]{:S(2)}, u32[]{:S(2)}) collective-permute-start(bf16[64,2048]{1,0:T(8,128)(2,1)} %get-tuple-element.45), channel_id=1, source_target_pairs={{0,64},{64,128},{128,192},{192,0},{1,65},{65,129},{129,193},{193,1... | collective-permute-start | bytes 786440 | tf_op jit(solution)/shard_map/ppermute | solution.py:33
  23.9 17.0 %collective-permute-start.3 = (bf16[64,2048]{1,0:T(8,128)(2,1)}, bf16[64,2048]{1,0:T(8,128)(2,1)}, u32[]{:S(2)}, u32[]{:S(2)}) collective-permute-start(bf16[64,2048]{1,0:T(8,128)(2,1)} %get-tuple-element.44), channel_id=1, source_target_pairs={{0,192},{64,0},{128,64},{192,128},{1,193},{65,1},{129,65},{193,129... | collective-permute-start | bytes 786440 | tf_op jit(solution)/shard_map/ppermute | solution.py:33
  25.2 18.1 %collective-permute-start.7 = (bf16[256,512]{1,0:T(8,128)(2,1)S(1)}, bf16[256,512]{1,0:T(8,128)(2,1)S(1)}, u32[]{:S(2)}, u32[]{:S(2)}) collective-permute-start(bf16[256,512]{1,0:T(8,128)(2,1)S(1)} %bitcast.16), channel_id=1, source_target_pairs={{0,1},{1,0},{2,3},{3,2},{4,5},{5,4},{6,7},{7,6},{8,9},{9,8},{10,11... | collective-permute-start | bytes 786440 | tf_op jit(solution)/shard_map/ppermute | solution.py:25
  26.0 15.0 %collective-permute-start.4 = (s32[1,6]{1,0:T(1,128)S(1)}, s32[1,6]{1,0:T(1,128)S(1)}, u32[]{:S(2)}, u32[]{:S(2)}) collective-permute-start(s32[1,6]{1,0:T(1,128)S(1)} %copy-done.4), channel_id=1, source_target_pairs={{0,2},{2,0},{1,3},{3,1},{4,6},{6,4},{5,7},{7,5},{8,10},{10,8},{9,1... | collective-permute-start | bytes 80 | tf_op jit(solution)/shard_map/ppermute | solution.py:25
  41.6 2.7 %collective-permute-start.5 = (bf16[6,64,128]{2,1,0:T(8,128)(2,1)S(1)}, bf16[6,64,128]{2,1,0:T(8,128)(2,1)S(1)}, u32[]{:S(2)}, u32[]{:S(2)}) collective-permute-start(bf16[6,64,128]{2,1,0:T(8,128)(2,1)S(1)} %get-tuple-element.30), channel_id=1, source_target_pairs={{0,2},{2,0},{1,3},{3,1},{4,6},{6,4},{5,7},{7,5},{8,10},{10,8},{9,1... | collective-permute-start | bytes 294920 | tf_op jit(solution)/shard_map/ppermute | solution.py:25
  45.9 1.5 %collective-permute-start.8 = (f32[6,64,128]{2,1,0:T(8,128)S(1)}, f32[6,64,128]{2,1,0:T(8,128)S(1)}, u32[]{:S(2)}, u32[]{:S(2)}) collective-permute-start(f32[6,64,128]{2,1,0:T(8,128)S(1)} %get-tuple-element.34), channel_id=1, source_target_pairs={{0,2},{2,0},{1,3},{3,1},{4,6},{6,4},{5,7},{7,5},{8,10},{10,8},{9,1... | collective-permute-start | bytes 589832 | tf_op jit(solution)/shard_map/ppermute | solution.py:25
  49.2 5.1 %copy-start.5 = (bf16[64,2048]{1,0:T(8,128)(2,1)S(1)}, bf16[64,2048]{1,0:T(8,128)(2,1)}, u32[]{:S(2)}) copy-start(bf16[64,2048]{1,0:T(8,128)(2,1)} %get-tuple-element.35) | copy-start | bytes 786436
  49.2 25.1 %all-to-all-start.1 = ((bf16[16,4,64,128]{3,2,1,0:T(8,128)(2,1)}), bf16[16,4,64,128]{3,2,1,0:T(8,128)(2,1)S(1)}, u32[]{:S(2)}, u32[]{:S(2)}) async-start(bf16[16,4,64,128]{3,2,1,0:T(8,128)(2,1)} %bitcast.10), calls=%async_computation.1 | async-start | bytes 2097152 | tf_op jit(solution)/shard_map/all_to_all | solution.py:208
  54.3 20.1 %collective-permute-start.9 = (bf16[64,2048]{1,0:T(8,128)(2,1)S(1)}, bf16[64,2048]{1,0:T(8,128)(2,1)S(1)}, u32[]{:S(2)}, u32[]{:S(2)}) collective-permute-start(bf16[64,2048]{1,0:T(8,128)(2,1)S(1)} %copy-done.5), channel_id=1, source_target_pairs={{0,128},{64,192},{128,0},{192,64},{1,129},{65,193},{129,1},{193,65... | collective-permute-start | bytes 786440 | tf_op jit(solution)/shard_map/ppermute | solution.py:33
  74.6 24.2 %copy-start.3 = (f32[64,128]{1,0:T(8,128)S(1)}, f32[64,128]{1,0:T(8,128)}, u32[]{:S(2)}) copy-start(f32[64,128]{1,0:T(8,128)} %start.1) | copy-start | bytes 98308
  74.6 4.8 %collective-permute-start.10 = (bf16[4,64,128]{2,1,0:T(8,128)(2,1)S(1)}, bf16[4,64,128]{2,1,0:T(8,128)(2,1)S(1)}, u32[]{:S(2)}, u32[]{:S(2)}) collective-permute-start(bf16[4,64,128]{2,1,0:T(8,128)(2,1)S(1)} %fusion.1), channel_id=1, source_target_pairs={{0,4},{4,0},{8,12},{12,8},{1,5},{5,1},{9,13},{13,9},{2,6},{6,2},{1... | collective-permute-start | bytes 196616 | tf_op jit(solution)/shard_map/ppermute | solution.py:42
  79.5 5.5 %collective-permute-start.11 = (bf16[4,64,128]{2,1,0:T(8,128)(2,1)S(1)}, bf16[4,64,128]{2,1,0:T(8,128)(2,1)S(1)}, u32[]{:S(2)}, u32[]{:S(2)}) collective-permute-start(bf16[4,64,128]{2,1,0:T(8,128)(2,1)S(1)} %fusion.2), channel_id=1, source_target_pairs={{0,12},{4,8},{8,4},{12,0},{1,13},{5,9},{9,5},{13,1},{2,14},{6,10},... | collective-permute-start | bytes 196616 | tf_op jit(solution)/shard_map/ppermute | solution.py:42
  85.0 8.6 %collective-permute-start.12 = (bf16[4,64,128]{2,1,0:T(8,128)(2,1)S(1)}, bf16[4,64,128]{2,1,0:T(8,128)(2,1)S(1)}, u32[]{:S(2)}, u32[]{:S(2)}) collective-permute-start(bf16[4,64,128]{2,1,0:T(8,128)(2,1)S(1)} %fusion.refs_0_), channel_id=1, source_target_pairs={{0,48},{16,0},{32,16},{48,32},{1,49},{17,1},{33,17},{49,33},{2,50}... | collective-permute-start | bytes 196616 | tf_op jit(solution)/shard_map/ppermute | solution.py:29
  87.7 6.1 %collective-permute-start.13 = (bf16[4,64,128]{2,1,0:T(8,128)(2,1)S(1)}, bf16[4,64,128]{2,1,0:T(8,128)(2,1)S(1)}, u32[]{:S(2)}, u32[]{:S(2)}) collective-permute-start(bf16[4,64,128]{2,1,0:T(8,128)(2,1)S(1)} %fusion.refs_0_), channel_id=1, source_target_pairs={{0,32},{16,48},{32,0},{48,16},{1,33},{17,49},{33,1},{49,17},{2,34}... | collective-permute-start | bytes 196616 | tf_op jit(solution)/shard_map/ppermute | solution.py:29
  89.9 7.3 %collective-permute-start.14 = (bf16[4,64,128]{2,1,0:T(8,128)(2,1)S(1)}, bf16[4,64,128]{2,1,0:T(8,128)(2,1)S(1)}, u32[]{:S(2)}, u32[]{:S(2)}) collective-permute-start(bf16[4,64,128]{2,1,0:T(8,128)(2,1)S(1)} %fusion.refs_0_), channel_id=1, source_target_pairs={{0,16},{16,32},{32,48},{48,0},{1,17},{17,33},{33,49},{49,1},{2,18}... | collective-permute-start | bytes 196616 | tf_op jit(solution)/shard_map/ppermute | solution.py:29
  90.7 7.2 %collective-permute-start.15 = (bf16[4,64,128]{2,1,0:T(8,128)(2,1)S(1)}, bf16[4,64,128]{2,1,0:T(8,128)(2,1)S(1)}, u32[]{:S(2)}, u32[]{:S(2)}) collective-permute-start(bf16[4,64,128]{2,1,0:T(8,128)(2,1)S(1)} %fusion.refs_0_), channel_id=1, source_target_pairs={{0,2},{2,0},{1,3},{3,1},{4,6},{6,4},{5,7},{7,5},{8,10},{10,8},{9,1... | collective-permute-start | bytes 196616 | tf_op jit(solution)/shard_map/ppermute | solution.py:25
  93.5 4.4 %collective-permute-start.16 = (bf16[4,64,128]{2,1,0:T(8,128)(2,1)S(1)}, bf16[4,64,128]{2,1,0:T(8,128)(2,1)S(1)}, u32[]{:S(2)}, u32[]{:S(2)}) collective-permute-start(bf16[4,64,128]{2,1,0:T(8,128)(2,1)S(1)} %collective-permute-done.12.refs_1_), channel_id=1, source_target_pairs={{0,2},{2,0},{1,3},{3,1},{4,6},{6,4},{5,7},{7,5},{8,10},{10,8},{9,1... | collective-permute-start | bytes 196616 | tf_op jit(solution)/shard_map/ppermute | solution.py:25
  93.8 4.4 %collective-permute-start.17 = (bf16[4,64,128]{2,1,0:T(8,128)(2,1)S(1)}, bf16[4,64,128]{2,1,0:T(8,128)(2,1)S(1)}, u32[]{:S(2)}, u32[]{:S(2)}) collective-permute-start(bf16[4,64,128]{2,1,0:T(8,128)(2,1)S(1)} %collective-permute-done.13.refs_2_), channel_id=1, source_target_pairs={{0,2},{2,0},{1,3},{3,1},{4,6},{6,4},{5,7},{7,5},{8,10},{10,8},{9,1... | collective-permute-start | bytes 196616 | tf_op jit(solution)/shard_map/ppermute | solution.py:25
  97.2 1.6 %collective-permute-start.18 = (bf16[4,64,128]{2,1,0:T(8,128)(2,1)S(1)}, bf16[4,64,128]{2,1,0:T(8,128)(2,1)S(1)}, u32[]{:S(2)}, u32[]{:S(2)}) collective-permute-start(bf16[4,64,128]{2,1,0:T(8,128)(2,1)S(1)} %collective-permute-done.14.refs_3_), channel_id=1, source_target_pairs={{0,2},{2,0},{1,3},{3,1},{4,6},{6,4},{5,7},{7,5},{8,10},{10,8},{9,1... | collective-permute-start | bytes 196616 | tf_op jit(solution)/shard_map/ppermute | solution.py:25
  100.3 4.1 %collective-permute-start.21 = (f32[64,128]{1,0:T(8,128)S(1)}, f32[64,128]{1,0:T(8,128)S(1)}, u32[]{:S(2)}, u32[]{:S(2)}) collective-permute-start(f32[64,128]{1,0:T(8,128)S(1)} %get-tuple-element.42), channel_id=1, source_target_pairs={{0,64},{64,128},{128,192},{192,0},{1,65},{65,129},{129,193},{193,1... | collective-permute-start | bytes 98312 | tf_op jit(solution)/shard_map/ppermute | solution.py:29
  100.8 4.6 %collective-permute-start.20 = (f32[64,128]{1,0:T(8,128)S(1)}, f32[64,128]{1,0:T(8,128)S(1)}, u32[]{:S(2)}, u32[]{:S(2)}) collective-permute-start(f32[64,128]{1,0:T(8,128)S(1)} %get-tuple-element.41), channel_id=1, source_target_pairs={{0,128},{64,192},{128,0},{192,64},{1,129},{65,193},{129,1},{193,65... | collective-permute-start | bytes 98312 | tf_op jit(solution)/shard_map/ppermute | solution.py:29
  102.8 3.1 %collective-permute-start.19 = (f32[64,128]{1,0:T(8,128)S(1)}, f32[64,128]{1,0:T(8,128)S(1)}, u32[]{:S(2)}, u32[]{:S(2)}) collective-permute-start(f32[64,128]{1,0:T(8,128)S(1)} %get-tuple-element.40), channel_id=1, source_target_pairs={{0,192},{64,0},{128,64},{192,128},{1,193},{65,1},{129,65},{193,129... | collective-permute-start | bytes 98312 | tf_op jit(solution)/shard_map/ppermute | solution.py:29

commit v5 on v3

--- a/solution.py
+++ b/solution.py
@@ -25,42 +25,22 @@
     return lax.ppermute(value, axis, SWAP)
 
 
-def from_ahead(value, axis, distance):
-    return lax.ppermute(value, axis, [(i, (i - distance) % RING) for i in range(RING)])
-
-
 def to_ahead(value, axis, distance):
     return lax.ppermute(value, axis, [(i, (i + distance) % RING) for i in range(RING)])
 
 
-def ring_pieces(value, axis):
-    return [value] + [from_ahead(value, axis, k) for k in range(1, RING)]
-
-
-def pair(axis, value, first):
-    other = [1, 0, 3, 2] if first else [3, 2, 1, 0]
-    return lax.ppermute(value, axis, list(enumerate(other)))
-
-
-def line_gather(value):
-    two = jnp.stack([value, pair(Z, value, True)])
-    return jnp.concatenate([two, pair(Z, two, False)])
-
-
-def line_slot(tile_z, z):
-    return jnp.where(
-        tile_z == z, 0, jnp.where(tile_z == (z ^ 1), 1, jnp.where(tile_z == 3 - z, 2, 3))
-    )
-
-
-def place(tile, where):
-    return tile - tile % RING + line_slot(tile % RING, where[2])
-
-
-def pick_kernel(where, own_ids, other_ids, gathered, own_ref, other_ref):
+def exchange(pieces, axes):
+    return lax.all_to_all(pieces, axes, 0, 0, tiled=True)
+
+
+def everyones(value, axes, count):
+    return exchange(jnp.broadcast_to(value, (count, *value.shape)), axes)
+
+
+def pick_kernel(own_ids, other_ids, gathered, own_ref, other_ref):
     for ids, out in ((other_ids, other_ref), (own_ids, own_ref)):
         for j in range(ids.shape[1]):
-            out[j] = gathered[place(ids[0, j], where)]
+            out[j] = gathered[ids[0, j]]
 
 
 def scenario_kernel(
@@ -107,32 +87,27 @@
         send_ref[...] = term[:, 0]
 
 
-def scatter_kernel(where, own_ids, other_ids, keep, arrived, out, total):
+def scatter_kernel(own_ids, other_ids, keep, arrived, out, total):
     total[...] = jnp.zeros_like(total)
     for ids, terms in ((own_ids, keep), (other_ids, arrived)):
         for j in range(ids.shape[1]):
-            total[place(ids[0, j], where)] += terms[j]
+            total[ids[0, j]] += terms[j]
     out[...] = total[...].astype(BF16)
 
 
-def update_kernel(where, start, precond, b1, b2, b3, *refs):
-    pieces, (o0, o1, o2, o3, whole) = refs[:8], refs[8:]
-    y, x, z, core = where[0], where[1], where[2], where[3]
-    slots = (z, z ^ 1, 3 - z, (3 - z) ^ 1)
-    for side in range(2):
+def update_kernel(where, start, precond, b1, b2, b3, mine, partners, out, whole):
+    y, core = where[0], where[3]
+    for side, piece in enumerate((mine, partners)):
         half = core if side == 0 else 1 - core
-        for i in range(RING):
-            piece = pieces[side * RING + i]
-            base = ((x + i) % RING) * 4
-            for j in range(RING):
-                at = pl.multiple_of((base + slots[j]) * TILE + half * HALF, HALF)
-                whole[pl.ds(at, HALF), :] = piece[j]
+        for tile in range(piece.shape[0]):
+            at = pl.multiple_of(tile * TILE + half * HALF, HALF)
+            whole[pl.ds(at, HALF), :] = piece[tile]
     operand = whole[...]
     span = operand.shape[0]
     own = precond[:, pl.ds(pl.multiple_of(y * span, span), span)]
-    o0[...] = start[...] + jnp.dot(own, operand, preferred_element_type=F32)
-    for block, out in ((b1, o1), (b2, o2), (b3, o3)):
-        out[...] = jnp.dot(block[...], operand, preferred_element_type=F32)
+    out[y] = start[...] + jnp.dot(own, operand, preferred_element_type=F32)
+    for k, block in enumerate((b1, b2, b3)):
+        out[(y + RING - 1 - k) % RING] = jnp.dot(block[...], operand, preferred_element_type=F32)
 
 
 def call(kernel, specs, outs, scratch=(), flops=0, moved=0):
@@ -166,66 +141,59 @@
     tiles = column_tiles.shape[1]
     everywhere = RING * RING * RING
 
-    line = line_gather(start_guess.astype(BF16))
+    line = everyones(start_guess.astype(BF16), Z, RING)
     span = preconditioner.shape[1] // RING
 
     def for_ahead(k):
         first = ((where[0] + k) % RING) * span
         return lax.dynamic_slice_in_dim(preconditioner, first, span, 1)
 
-    block1 = to_ahead(for_ahead(1), Y, 1)
-    line, block1, border_late, inverse_late = lax.optimization_barrier((line, block1, border, inverse))
+    block1, block3 = to_ahead(for_ahead(1), Y, 1), to_ahead(for_ahead(3), Y, 3)
+    line, block1, block3, border_late, inverse_late = lax.optimization_barrier(
+        (line, block1, block3, border, inverse)
+    )
     border_other = swap(border_late, SIDE)
     inverse_other = swap(inverse_late, SIDE)
     other_tiles = swap(column_tiles, CORE)
-    copies = jnp.broadcast_to(line, (RING * RING, *line.shape))
-    gathered = lax.all_to_all(copies, (Y, X), 0, 0, tiled=True)
+    gathered = everyones(line, (Y, X), RING * RING)
 
     own_half, for_other = call(
         pick_kernel,
-        [SMEM] * 3 + [VMEM],
+        [SMEM] * 2 + [VMEM],
         [shape((tiles, HALF, cols), BF16)] * 2,
-    )(where, column_tiles, other_tiles, gathered.reshape(everywhere, HALF, cols))
+    )(column_tiles, other_tiles, gathered.reshape(everywhere, HALF, cols))
     other_half = swap(for_other, CORE)
-    gate, columns3 = lax.optimization_barrier((own_half, for_ahead(3)))
-    block3 = to_ahead(columns3, Y, 3)
     keep, send = call(
         scenario_kernel,
         [SMEM] + [VMEM] * 6,
         [shape((tiles, HALF, cols), F32)] * 2,
         [pltpu.VMEM((tiles * TILE, cols), BF16), pltpu.VMEM((2 * border.shape[0], cols), BF16)],
-    )(where, gate, other_half, border, border_other, inverse, inverse_other)
+    )(where, own_half, other_half, border, border_other, inverse, inverse_other)
     arrived = swap(send, CORE)
     spread = call(
         scatter_kernel,
-        [SMEM] * 3 + [VMEM] * 2,
+        [SMEM] * 2 + [VMEM] * 2,
         shape((everywhere, HALF, cols), BF16),
         [pltpu.VMEM((everywhere, HALF, cols), F32)],
-    )(where, column_tiles, other_tiles, keep, arrived)
-    spread, block3 = lax.optimization_barrier((spread, block3))
-    terms = lax.all_to_all(spread.reshape(RING * RING, RING, HALF, cols), (Y, X), 0, 0, tiled=True)
+    )(column_tiles, other_tiles, keep, arrived)
+    terms = exchange(spread.reshape(RING * RING, RING, HALF, cols), (Y, X))
     line = terms.astype(F32).sum(axis=0)
     columns2, line = lax.optimization_barrier((for_ahead(2), line))
     block2 = to_ahead(columns2, Y, 2)
     own_terms = right_side - root_diagonal[:, None] * start_guess
-    line = line + jnp.concatenate([own_terms[None], jnp.zeros_like(line[1:])])
-    met = pair(Z, line.astype(BF16), True).astype(F32)
-    line = line + jnp.stack([met[1], met[0], met[3], met[2]])
-    met = pair(Z, line.astype(BF16), False).astype(F32)
-    line = line + jnp.concatenate([met[2:], met[:2]])
-
-    mine = ring_pieces(line.astype(BF16), X)
-    partners = [swap(piece, CORE) for piece in mine]
+    mine_here = (jnp.arange(RING) == where[2])[:, None, None]
+    line = line + jnp.where(mine_here, own_terms, 0.0)
+    line = everyones(line.astype(BF16), Z, RING).astype(F32).sum(axis=0)
+
+    mine = everyones(line.astype(BF16), X, RING).reshape(RING * RING, HALF, cols)
+    partners = swap(mine, CORE)
     parts = call(
         update_kernel,
-        [SMEM] + [VMEM] * 13,
-        [shape((rows, cols), F32)] * RING,
+        [SMEM] + [VMEM] * 7,
+        shape((RING, rows, cols), F32),
         [pltpu.VMEM((span, cols), BF16)],
-    )(where, start_guess, preconditioner, block1, block2, block3, *mine, *partners)
-    out = parts[0]
-    for k in range(1, RING):
-        out = out + from_ahead(parts[k], Y, k)
-    return out
+    )(where, start_guess, preconditioner, block1, block2, block3, mine, partners)
+    return exchange(parts, Y).sum(axis=0)
 
 
 def solution(mesh):

time: 98.9 us -> 109 us (1.10)
  blocking collectives: 19.4 us -> 33.4 us
  starting transfers between devices: 44.4 us -> 32.4 us
  waiting for transfers between devices: 25.1 us -> 32.2 us
    all_to_all x1 -> x3, waiting for transfers between devices: 9.03 us -> 28.9 us  [exchange(): return lax.all_to_all(pieces, axes, 0, 0, tiled=True)]
    ppermute x10 -> x0, starting transfers between devices: 17.6 us -> none  [the longest x4 13.6 us: pair(): return lax.ppermute(value, axis, list(enumerate(other)))]
    all_to_all x1 -> x3, blocking collectives: 19.4 us -> 33.4 us  [exchange(): return lax.all_to_all(pieces, axes, 0, 0, tiled=True)]
    ppermute x10 -> x0, waiting for transfers between devices: 9.29 us -> none  [the longest x4 5.9 us: pair(): return lax.ppermute(value, axis, list(enumerate(other)))]
    all_to_all x1 -> x3, starting transfers between devices: 5.55 us -> 12.6 us  [exchange(): return lax.all_to_all(pieces, axes, 0, 0, tiled=True)]
    ppermute x9 -> x6, starting transfers between devices: 18.8 us -> 14.3 us  [swap(): return lax.ppermute(value, axis, SWAP)]
    ppermute x3, waiting for transfers between devices: 4.15 us -> 0.01 us  [to_ahead(): lax.ppermute(value, axis, [(i, (i + distance) % RING) for i in range(RING)])]
    ppermute x3, starting transfers between devices: 2.47 us -> 5.59 us  [to_ahead(): lax.ppermute(value, axis, [(i, (i + distance) % RING) for i in range(RING)])]
  transfers between devices with their start and end apart: 23 -> 12, of which waited for: 13 -> 7; matrix products, arithmetic and copies ran while one was open for 1% -> 0% of each run, Pallas kernels for 3% -> 1%
where the time goes in v5:
time: 109 us; the launch traced here: 108 us
  blocking collectives  33.4 us (31%)
  starting transfers between devices  32.4 us (30%)
  waiting for transfers between devices  32.2 us (30%)
  Pallas kernels  4.94 us (5%)
  local copies, waits for them, and re-layouts  3.32 us (3%)
    all_to_all x3, blocking collectives, exchange(): return lax.all_to_all(pieces, axes, 0, 0, tiled=True)  33.4 us
    all_to_all x3, waiting for transfers between devices, exchange(): return lax.all_to_all(pieces, axes, 0, 0, tiled=True)  28.9 us
    ppermute x6, starting transfers between devices, swap(): return lax.ppermute(value, axis, SWAP)  14.3 us
    all_to_all x3, starting transfers between devices, exchange(): return lax.all_to_all(pieces, axes, 0, 0, tiled=True)  12.6 us
    ppermute x3, starting transfers between devices, to_ahead(): lax.ppermute(value, axis, [(i, (i + distance) % RING) for i in range(RING)])  5.59 us
    ppermute x6, waiting for transfers between devices, swap(): return lax.ppermute(value, axis, SWAP)  3.28 us
  transfers between devices with their start and end apart: 12, of which 7 were waited for; matrix products, arithmetic and copies ran while one was open for 0% of the time, Pallas kernels for 1%

profile of v5, /device:TPU:1, one launch (start us, length us, event | category | flops | bytes accessed | tf_op | source)
XLA Modules:
  0.0 108.2 jit_solution(12359672691432399248)
XLA Ops:
  0.0 0.0 copy-start.6
  0.1 1.2 %constant_dynamic-slice_fusion = (bf16[64,2048]{1,0:T(8,128)(2,1)S(1)}, bf16[64,2048]{1,0:T(8,128)(2,1)S(1)}, bf16[64,2048]{1,0:T(8,128)(2,1)S(1)}) fusion(bf16[64,8192]{1,0:T(8,128)(2,1)} %precond.1, s32[]{:T(128)S(6)} %select_n.33, s32[]{:T(128)S(6)} %select_n.31, s32[]{:T(128)S(6)} %select_n.29), kind=kLoop, calls=%fused_computation.3 | loop fusion | bytes 1572876 | tf_op jit(solution)/shard_map/dynamic_slice | solution.py:149
  1.2 2.2 %collective-permute-start = (bf16[64,2048]{1,0:T(8,128)(2,1)S(1)}, bf16[64,2048]{1,0:T(8,128)(2,1)S(1)}, u32[]{:S(2)}, u32[]{:S(2)}) collective-permute-start(bf16[64,2048]{1,0:T(8,128)(2,1)S(1)} %get-tuple-element.29), channel_id=1, source_target_pairs={{0,64},{64,128},{128,192},{192,0},{1,65},{65,129},{129,193},{193,1... | collective-permute-start | bytes 786440 | tf_op jit(solution)/shard_map/ppermute | solution.py:29
  3.4 1.5 %collective-permute-start.1 = (bf16[64,2048]{1,0:T(8,128)(2,1)S(1)}, bf16[64,2048]{1,0:T(8,128)(2,1)S(1)}, u32[]{:S(2)}, u32[]{:S(2)}) collective-permute-start(bf16[64,2048]{1,0:T(8,128)(2,1)S(1)} %get-tuple-element.28), channel_id=1, source_target_pairs={{0,192},{64,0},{128,64},{192,128},{1,193},{65,1},{129,65},{193,129... | collective-permute-start | bytes 786440 | tf_op jit(solution)/shard_map/ppermute | solution.py:29
  5.0 0.0 copy-done.6
  5.0 0.0 copy-done.3
  5.0 0.0 copy-done.5
  5.0 0.1 multiply_subtract_fusion
  5.1 15.0 %all_to_all.30 = bf16[4,64,128]{2,1,0:T(8,128)(2,1)S(1)} all-to-all(bf16[4,64,128]{2,1,0:T(8,128)(2,1)S(1)} %broadcast_in_dim.30), channel_id=1, replica_groups=mesh['scen_0'=4,'scen_1'=4,'scen_2'=4,'rootr'=2,'rootc'=2] {'scen_2'}, dimensions={0} | all-to-all | bytes 131072 | tf_op jit(solution)/shard_map/all_to_all | solution.py:33
  20.1 0.0 collective-permute-done.b1
  20.1 0.0 collective-permute-done.1.b3
  20.1 1.2 %broadcast_in_dim.31 = bf16[16,4,64,128]{3,2,1,0:T(8,128)(2,1)} broadcast(bf16[4,64,128]{2,1,0:T(8,128)(2,1)S(1)} %all_to_all.30), dimensions={1,2,3} | broadcast | bytes 1114112 | tf_op jit(solution)/shard_map/broadcast_in_dim | solution.py:37
  21.4 5.5 %all-to-all-start.1 = ((bf16[16,4,64,128]{3,2,1,0:T(8,128)(2,1)}), bf16[16,4,64,128]{3,2,1,0:T(8,128)(2,1)S(1)}, u32[]{:S(2)}, u32[]{:S(2)}) async-start(bf16[16,4,64,128]{3,2,1,0:T(8,128)(2,1)} %broadcast_in_dim.31), calls=%async_computation.1 | async-start | bytes 2097152 | tf_op jit(solution)/shard_map/all_to_all | solution.py:33
  26.9 0.0 copy-done.1
  26.9 0.8 collective-permute-start.4
  27.7 0.0 copy-done.2
  27.7 0.7 collective-permute-start.5
  28.5 0.0 copy-done.4
  28.5 3.5 %collective-permute-start.2 = (s32[1,6]{1,0:T(1,128)S(1)}, s32[1,6]{1,0:T(1,128)S(1)}, u32[]{:S(2)}, u32[]{:S(2)}) collective-permute-start(s32[1,6]{1,0:T(1,128)S(1)} %copy-done.4), channel_id=1, source_target_pairs={{0,2},{2,0},{1,3},{3,1},{4,6},{6,4},{5,7},{7,5},{8,10},{10,8},{9,1... | collective-permute-start | bytes 80 | tf_op jit(solution)/shard_map/ppermute | solution.py:25
  32.0 0.8 collective-permute-done.2.other_ids
  32.8 8.5 %all-to-all-done.1 = bf16[16,4,64,128]{3,2,1,0:T(8,128)(2,1)S(1)} async-done(((bf16[16,4,64,128]{3,2,1,0:T(8,128)(2,1)}), bf16[16,4,64,128]{3,2,1,0:T(8,128)(2,1)S(1)}, u32[]{:S(2)}, u32[]{:S(2)}) %all-to-all-start.1) | async-done | bytes 1048608 | tf_op jit(solution)/shard_map/all_to_all | solution.py:33
  41.3 0.6 shard_map.82
  41.8 4.3 %collective-permute-start.3 = (bf16[6,64,128]{2,1,0:T(8,128)(2,1)S(1)}, bf16[6,64,128]{2,1,0:T(8,128)(2,1)S(1)}, u32[]{:S(2)}, u32[]{:S(2)}) collective-permute-start(bf16[6,64,128]{2,1,0:T(8,128)(2,1)S(1)} %get-tuple-element.19), channel_id=1, source_target_pairs={{0,2},{2,0},{1,3},{3,1},{4,6},{6,4},{5,7},{7,5},{8,10},{10,8},{9,1... | collective-permute-start | bytes 294920 | tf_op jit(solution)/shard_map/ppermute | solution.py:25
  46.7 0.1 stack.23.where
  46.8 0.0 collective-permute-done.5.inverse_other
  46.8 0.0 collective-permute-done.4.border_other
  46.8 0.2 collective-permute-done.3.other_picked
  47.0 1.6 %shard_map.83 = (f32[6,64,128]{2,1,0:T(8,128)S(1)}, f32[6,64,128]{2,1,0:T(8,128)S(1)}) custom-call(s32[6]{0:T(128)S(1)} %stack.23.where, bf16[6,64,128]{2,1,0:T(8,128)(2,1)S(1)} %get-tuple-element.18.own_picked, bf16[6,64,128]{2,1,0:T(8,128)(2,1)S(1)} %collective-permute-done.3.other_picked, bf16[256,768]{1,0:T(8,128)(2,1)S(1)} %bitcast.14, ...), custom_call_target="tpu_custom_call" | custom-call | tf_op jit(solution)/shard_map/pallas_call | solution.py:166
  48.6 0.4 collective-permute-start.6
  49.0 1.1 %collective-permute-done.6.arrived = f32[6,64,128]{2,1,0:T(8,128)S(1)} collective-permute-done((f32[6,64,128]{2,1,0:T(8,128)S(1)}, f32[6,64,128]{2,1,0:T(8,128)S(1)}, u32[]{:S(2)}, u32[]{:S(2)}) %collective-permute-start.6) | collective-permute-done | bytes 196640 | tf_op jit(solution)/shard_map/ppermute | solution.py:25
  50.1 1.8 %shard_map.84 = bf16[64,64,128]{2,1,0:T(8,128)(2,1)} custom-call(s32[1,6]{1,0:T(1,128)S(1)} %copy-done.4, s32[1,6]{1,0:T(1,128)S(1)} %collective-permute-done.2.other_ids, f32[6,64,128]{2,1,0:T(8,128)S(1)} %get-tuple-element.22.keep, f32[6,64,128]{2,1,0:T(8,128)S(1)} %collective-permute-done.6.arrived), custom_call_target="tpu_custom_call" | custom-call | tf_op jit(solution)/shard_map/pallas_call | solution.py:173
  51.9 3.7 %all-to-all-start.2 = ((bf16[16,4,64,128]{3,2,1,0:T(8,128)(2,1)}), bf16[16,4,64,128]{3,2,1,0:T(8,128)(2,1)S(1)}, u32[]{:S(2)}, u32[]{:S(2)}) async-start(bf16[16,4,64,128]{3,2,1,0:T(8,128)(2,1)} %bitcast.8), calls=%async_computation.2 | async-start | bytes 2097152 | tf_op jit(solution)/shard_map/all_to_all | solution.py:33
  55.6 16.8 %all-to-all-done.2 = bf16[16,4,64,128]{3,2,1,0:T(8,128)(2,1)S(1)} async-done(((bf16[16,4,64,128]{3,2,1,0:T(8,128)(2,1)}), bf16[16,4,64,128]{3,2,1,0:T(8,128)(2,1)S(1)}, u32[]{:S(2)}, u32[]{:S(2)}) %all-to-all-start.2) | async-done | bytes 1048608 | tf_op jit(solution)/shard_map/all_to_all | solution.py:33
  72.4 0.2 convert_reduce_fusion
  72.6 0.1 add_convert_fusion
  72.7 0.0 copy-start
  72.7 11.0 %all_to_all.31 = bf16[4,4,64,128]{3,2,1,0:T(8,128)(2,1)S(1)} all-to-all(bf16[4,4,64,128]{3,2,1,0:T(8,128)(2,1)S(1)} %broadcast_in_dim.35), channel_id=1, replica_groups=mesh['scen_0'=4,'scen_1'=4,'scen_2'=4,'rootr'=2,'rootc'=2] {'scen_2'}, dimensions={0} | all-to-all | bytes 524288 | tf_op jit(solution)/shard_map/all_to_all | solution.py:33
  83.8 0.7 broadcast_in_dim.36
  84.5 3.4 %all-to-all-start.4 = ((bf16[4,4,64,128]{3,2,1,0:T(8,128)(2,1)}), bf16[4,4,64,128]{3,2,1,0:T(8,128)(2,1)S(1)}, u32[]{:S(2)}, u32[]{:S(2)}) async-start(bf16[4,4,64,128]{3,2,1,0:T(8,128)(2,1)} %broadcast_in_dim.36), calls=%async_computation.4 | async-start | bytes 524288 | tf_op jit(solution)/shard_map/all_to_all | solution.py:33
  87.9 1.9 %collective-permute-start.7 = (bf16[64,2048]{1,0:T(8,128)(2,1)S(1)}, bf16[64,2048]{1,0:T(8,128)(2,1)S(1)}, u32[]{:S(2)}, u32[]{:S(2)}) collective-permute-start(bf16[64,2048]{1,0:T(8,128)(2,1)S(1)} %get-tuple-element.24), channel_id=1, source_target_pairs={{0,128},{64,192},{128,0},{192,64},{1,129},{65,193},{129,1},{193,65... | collective-permute-start | bytes 786440 | tf_op jit(solution)/shard_map/ppermute | solution.py:29
  89.8 3.7 %all-to-all-done.4 = bf16[4,4,64,128]{3,2,1,0:T(8,128)(2,1)S(1)} async-done(((bf16[4,4,64,128]{3,2,1,0:T(8,128)(2,1)}), bf16[4,4,64,128]{3,2,1,0:T(8,128)(2,1)S(1)}, u32[]{:S(2)}, u32[]{:S(2)}) %all-to-all-start.4) | async-done | bytes 262176 | tf_op jit(solution)/shard_map/all_to_all | solution.py:33
  93.4 4.5 %collective-permute-start.8 = (bf16[16,64,128]{2,1,0:T(8,128)(2,1)S(1)}, bf16[16,64,128]{2,1,0:T(8,128)(2,1)S(1)}, u32[]{:S(2)}, u32[]{:S(2)}) collective-permute-start(bf16[16,64,128]{2,1,0:T(8,128)(2,1)S(1)} %bitcast.11), channel_id=1, source_target_pairs={{0,2},{2,0},{1,3},{3,1},{4,6},{6,4},{5,7},{7,5},{8,10},{10,8},{9,1... | collective-permute-start | bytes 786440 | tf_op jit(solution)/shard_map/ppermute | solution.py:25
  97.9 0.0 collective-permute-done.7.b2
  97.9 1.2 %collective-permute-done.8.partners = bf16[16,64,128]{2,1,0:T(8,128)(2,1)S(1)} collective-permute-done((bf16[16,64,128]{2,1,0:T(8,128)(2,1)S(1)}, bf16[16,64,128]{2,1,0:T(8,128)(2,1)S(1)}, u32[]{:S(2)}, u32[]{:S(2)}) %collective-permute-start.8) | collective-permute-done | bytes 262176 | tf_op jit(solution)/shard_map/ppermute | solution.py:25
  99.1 0.0 copy-done
  99.1 1.0 shard_map.85
  100.1 7.4 %all_to_all.32 = f32[4,64,128]{2,1,0:T(8,128)S(1)} all-to-all(f32[4,64,128]{2,1,0:T(8,128)S(1)} %shard_map.85), channel_id=1, replica_groups=mesh['scen_0'=4,'scen_1'=4,'scen_2'=4,'rootr'=2,'rootc'=2] {'scen_0'}, dimensions={0} | all-to-all | bytes 262144 | tf_op jit(solution)/shard_map/all_to_all | solution.py:33
  107.5 0.6 reduce_sum.32
  (9 shorter events, 0.1 us)
Async XLA Ops:
  0.0 5.0 %copy-start.6 = (f32[64]{0:T(128)S(1)}, f32[64]{0:T(128)}, u32[]{:S(2)}) copy-start(f32[64]{0:T(128)} %param.10) | copy-start | bytes 772
  0.0 5.0 %copy-start.3 = (f32[64,128]{1,0:T(8,128)S(1)}, f32[64,128]{1,0:T(8,128)}, u32[]{:S(2)}) copy-start(f32[64,128]{1,0:T(8,128)} %start.1) | copy-start | bytes 98308
  0.0 5.0 %copy-start.5 = (f32[64,128]{1,0:T(8,128)S(1)}, f32[64,128]{1,0:T(8,128)}, u32[]{:S(2)}) copy-start(f32[64,128]{1,0:T(8,128)} %param.9) | copy-start | bytes 98308
  1.2 18.9 %collective-permute-start = (bf16[64,2048]{1,0:T(8,128)(2,1)S(1)}, bf16[64,2048]{1,0:T(8,128)(2,1)S(1)}, u32[]{:S(2)}, u32[]{:S(2)}) collective-permute-start(bf16[64,2048]{1,0:T(8,128)(2,1)S(1)} %get-tuple-element.29), channel_id=1, source_target_pairs={{0,64},{64,128},{128,192},{192,0},{1,65},{65,129},{129,193},{193,1... | collective-permute-start | bytes 786440 | tf_op jit(solution)/shard_map/ppermute | solution.py:29
  3.4 16.7 %collective-permute-start.1 = (bf16[64,2048]{1,0:T(8,128)(2,1)S(1)}, bf16[64,2048]{1,0:T(8,128)(2,1)S(1)}, u32[]{:S(2)}, u32[]{:S(2)}) collective-permute-start(bf16[64,2048]{1,0:T(8,128)(2,1)S(1)} %get-tuple-element.28), channel_id=1, source_target_pairs={{0,192},{64,0},{128,64},{192,128},{1,193},{65,1},{129,65},{193,129... | collective-permute-start | bytes 786440 | tf_op jit(solution)/shard_map/ppermute | solution.py:29
  21.4 5.5 %copy-start.1 = (bf16[1,256,768]{2,1,0:T(8,128)(2,1)S(1)}, bf16[1,256,768]{2,1,0:T(8,128)(2,1)}, u32[]{:S(2)}) copy-start(bf16[1,256,768]{2,1,0:T(8,128)(2,1)} %param.12) | copy-start | bytes 1179652
  21.4 6.4 %copy-start.2 = (bf16[1,256,512]{2,1,0:T(8,128)(2,1)S(1)}, bf16[1,256,512]{2,1,0:T(8,128)(2,1)}, u32[]{:S(2)}) copy-start(bf16[1,256,512]{2,1,0:T(8,128)(2,1)} %param.13) | copy-start | bytes 786436
  21.4 7.1 %copy-start.4 = (s32[1,6]{1,0:T(1,128)S(1)}, s32[1,6]{1,0:T(1,128)}, u32[]{:S(2)}) copy-start(s32[1,6]{1,0:T(1,128)} %own_ids.3) | copy-start | bytes 76
  21.4 19.9 %all-to-all-start.1 = ((bf16[16,4,64,128]{3,2,1,0:T(8,128)(2,1)}), bf16[16,4,64,128]{3,2,1,0:T(8,128)(2,1)S(1)}, u32[]{:S(2)}, u32[]{:S(2)}) async-start(bf16[16,4,64,128]{3,2,1,0:T(8,128)(2,1)} %broadcast_in_dim.31), calls=%async_computation.1 | async-start | bytes 2097152 | tf_op jit(solution)/shard_map/all_to_all | solution.py:33
  26.9 19.9 %collective-permute-start.4 = (bf16[256,768]{1,0:T(8,128)(2,1)S(1)}, bf16[256,768]{1,0:T(8,128)(2,1)S(1)}, u32[]{:S(2)}, u32[]{:S(2)}) collective-permute-start(bf16[256,768]{1,0:T(8,128)(2,1)S(1)} %bitcast.13), channel_id=1, source_target_pairs={{0,1},{1,0},{2,3},{3,2},{4,5},{5,4},{6,7},{7,6},{8,9},{9,8},{10,11... | collective-permute-start | bytes 1179656 | tf_op jit(solution)/shard_map/ppermute | solution.py:25
  27.7 19.1 %collective-permute-start.5 = (bf16[256,512]{1,0:T(8,128)(2,1)S(1)}, bf16[256,512]{1,0:T(8,128)(2,1)S(1)}, u32[]{:S(2)}, u32[]{:S(2)}) collective-permute-start(bf16[256,512]{1,0:T(8,128)(2,1)S(1)} %bitcast.15), channel_id=1, source_target_pairs={{0,1},{1,0},{2,3},{3,2},{4,5},{5,4},{6,7},{7,6},{8,9},{9,8},{10,11... | collective-permute-start | bytes 786440 | tf_op jit(solution)/shard_map/ppermute | solution.py:25
  28.5 4.3 %collective-permute-start.2 = (s32[1,6]{1,0:T(1,128)S(1)}, s32[1,6]{1,0:T(1,128)S(1)}, u32[]{:S(2)}, u32[]{:S(2)}) collective-permute-start(s32[1,6]{1,0:T(1,128)S(1)} %copy-done.4), channel_id=1, source_target_pairs={{0,2},{2,0},{1,3},{3,1},{4,6},{6,4},{5,7},{7,5},{8,10},{10,8},{9,1... | collective-permute-start | bytes 80 | tf_op jit(solution)/shard_map/ppermute | solution.py:25
  41.8 5.2 %collective-permute-start.3 = (bf16[6,64,128]{2,1,0:T(8,128)(2,1)S(1)}, bf16[6,64,128]{2,1,0:T(8,128)(2,1)S(1)}, u32[]{:S(2)}, u32[]{:S(2)}) collective-permute-start(bf16[6,64,128]{2,1,0:T(8,128)(2,1)S(1)} %get-tuple-element.19), channel_id=1, source_target_pairs={{0,2},{2,0},{1,3},{3,1},{4,6},{6,4},{5,7},{7,5},{8,10},{10,8},{9,1... | collective-permute-start | bytes 294920 | tf_op jit(solution)/shard_map/ppermute | solution.py:25
  48.6 1.5 %collective-permute-start.6 = (f32[6,64,128]{2,1,0:T(8,128)S(1)}, f32[6,64,128]{2,1,0:T(8,128)S(1)}, u32[]{:S(2)}, u32[]{:S(2)}) collective-permute-start(f32[6,64,128]{2,1,0:T(8,128)S(1)} %get-tuple-element.23), channel_id=1, source_target_pairs={{0,2},{2,0},{1,3},{3,1},{4,6},{6,4},{5,7},{7,5},{8,10},{10,8},{9,1... | collective-permute-start | bytes 589832 | tf_op jit(solution)/shard_map/ppermute | solution.py:25
  51.9 20.4 %all-to-all-start.2 = ((bf16[16,4,64,128]{3,2,1,0:T(8,128)(2,1)}), bf16[16,4,64,128]{3,2,1,0:T(8,128)(2,1)S(1)}, u32[]{:S(2)}, u32[]{:S(2)}) async-start(bf16[16,4,64,128]{3,2,1,0:T(8,128)(2,1)} %bitcast.8), calls=%async_computation.2 | async-start | bytes 2097152 | tf_op jit(solution)/shard_map/all_to_all | solution.py:33
  72.7 26.4 %copy-start = (bf16[64,8192]{1,0:T(8,128)(2,1)S(1)}, bf16[64,8192]{1,0:T(8,128)(2,1)}, u32[]{:S(2)}) copy-start(bf16[64,8192]{1,0:T(8,128)(2,1)} %precond.1) | copy-start | bytes 3145732
  84.5 8.9 %all-to-all-start.4 = ((bf16[4,4,64,128]{3,2,1,0:T(8,128)(2,1)}), bf16[4,4,64,128]{3,2,1,0:T(8,128)(2,1)S(1)}, u32[]{:S(2)}, u32[]{:S(2)}) async-start(bf16[4,4,64,128]{3,2,1,0:T(8,128)(2,1)} %broadcast_in_dim.36), calls=%async_computation.4 | async-start | bytes 524288 | tf_op jit(solution)/shard_map/all_to_all | solution.py:33
  87.9 10.0 %collective-permute-start.7 = (bf16[64,2048]{1,0:T(8,128)(2,1)S(1)}, bf16[64,2048]{1,0:T(8,128)(2,1)S(1)}, u32[]{:S(2)}, u32[]{:S(2)}) collective-permute-start(bf16[64,2048]{1,0:T(8,128)(2,1)S(1)} %get-tuple-element.24), channel_id=1, source_target_pairs={{0,128},{64,192},{128,0},{192,64},{1,129},{65,193},{129,1},{193,65... | collective-permute-start | bytes 786440 | tf_op jit(solution)/shard_map/ppermute | solution.py:29
  93.4 5.7 %collective-permute-start.8 = (bf16[16,64,128]{2,1,0:T(8,128)(2,1)S(1)}, bf16[16,64,128]{2,1,0:T(8,128)(2,1)S(1)}, u32[]{:S(2)}, u32[]{:S(2)}) collective-permute-start(bf16[16,64,128]{2,1,0:T(8,128)(2,1)S(1)} %bitcast.11), channel_id=1, source_target_pairs={{0,2},{2,0},{1,3},{3,1},{4,6},{6,4},{5,7},{7,5},{8,10},{10,8},{9,1... | collective-permute-start | bytes 786440 | tf_op jit(solution)/shard_map/ppermute | solution.py:25

commit v6 on v4

--- a/solution.py
+++ b/solution.py
@@ -115,24 +115,26 @@
     out[...] = total[...].astype(BF16)
 
 
-def update_kernel(where, start, precond, b1, b2, b3, *refs):
-    pieces, (o0, o1, o2, o3, whole) = refs[:8], refs[8:]
-    y, x, z, core = where[0], where[1], where[2], where[3]
+def update_kernel(where, start, precond, here, there, mine, partners, o0, o1, o2, o3, whole):
+    y, x, z, core, side = where[0], where[1], where[2], where[3], where[4]
     slots = (z, z ^ 1, 3 - z, (3 - z) ^ 1)
-    for side in range(2):
-        half = core if side == 0 else 1 - core
+    for which, plane in enumerate((mine, partners)):
+        half = core if which == 0 else 1 - core
         for i in range(RING):
-            piece = pieces[side * RING + i]
             base = ((x + i) % RING) * 4
             for j in range(RING):
                 at = pl.multiple_of((base + slots[j]) * TILE + half * HALF, HALF)
-                whole[pl.ds(at, HALF), :] = piece[j]
-    operand = whole[...]
-    span = operand.shape[0]
+                whole[pl.ds(at, HALF), :] = plane[i * RING + j]
+    span = whole.shape[0]
     own = precond[:, pl.ds(pl.multiple_of(y * span, span), span)]
-    o0[...] = start[...] + jnp.dot(own, operand, preferred_element_type=F32)
-    for block, out in ((b1, o1), (b2, o2), (b3, o3)):
-        out[...] = jnp.dot(block[...], operand, preferred_element_type=F32)
+    o0[...] = start[...] + jnp.dot(own, whole[...], preferred_element_type=F32)
+    part = span // 2
+    ours = whole[pl.ds(pl.multiple_of(side * part, part), part), :]
+    theirs = whole[pl.ds(pl.multiple_of((1 - side) * part, part), part), :]
+    for k, out in enumerate((o1, o2, o3)):
+        out[...] = jnp.dot(here[k], ours, preferred_element_type=F32) + jnp.dot(
+            there[k], theirs, preferred_element_type=F32
+        )
 
 
 def call(kernel, specs, outs, scratch=(), flops=0, moved=0):
@@ -166,23 +168,29 @@
     tiles = column_tiles.shape[1]
     everywhere = RING * RING * RING
 
-    line = line_gather(start_guess.astype(BF16))
     span = preconditioner.shape[1] // RING
-
-    line, late, border_late, inverse_late = lax.optimization_barrier(
-        (line, preconditioner, border, inverse)
-    )
-    columns = [
-        lax.dynamic_slice_in_dim(late, ((where[0] + k) % RING) * span, span, 1)
-        for k in range(1, RING)
-    ]
-    block1, block3 = to_ahead(columns[0], Y, 1), to_ahead(columns[2], Y, 3)
+    part = span // 2
+
+    def for_ahead(source, k):
+        first = ((where[0] + k) % RING) * span + where[4] * part
+        return lax.dynamic_slice_in_dim(source, first, part, 1)
+
+    low = start_guess.astype(BF16)
+    two = jnp.stack([low, pair(Z, low, True)])
+    block1, block3 = to_ahead(for_ahead(preconditioner, 1), Y, 1), to_ahead(for_ahead(preconditioner, 3), Y, 3)
+    two, late = lax.optimization_barrier((two, for_ahead(preconditioner, 2)))
+    line = jnp.concatenate([two, pair(Z, two, False)])
+    block2 = to_ahead(late, Y, 2)
+    line, block1, block2, block3, border_late, inverse_late = lax.optimization_barrier(
+        (line, block1, block2, block3, border, inverse)
+    )
+    here = jnp.stack([block1, block2, block3])
     border_other = swap(border_late, SIDE)
     inverse_other = swap(inverse_late, SIDE)
+    there = swap(here, SIDE)
     other_tiles = swap(column_tiles, CORE)
     copies = jnp.broadcast_to(line, (RING * RING, *line.shape))
     gathered = lax.all_to_all(copies, (Y, X), 0, 0, tiled=True)
-    gathered, block1, block3 = lax.optimization_barrier((gathered, block1, block3))
 
     own_half, for_other = call(
         pick_kernel,
@@ -190,8 +198,6 @@
         [shape((tiles, HALF, cols), BF16)] * 2,
     )(where, column_tiles, other_tiles, gathered.reshape(everywhere, HALF, cols))
     other_half = swap(for_other, CORE)
-    own_half, columns2 = lax.optimization_barrier((own_half, columns[1]))
-    block2 = to_ahead(columns2, Y, 2)
     keep, send = call(
         scenario_kernel,
         [SMEM] + [VMEM] * 6,
@@ -206,7 +212,7 @@
         [pltpu.VMEM((everywhere, HALF, cols), F32)],
     )(where, column_tiles, other_tiles, keep, arrived)
     terms = lax.all_to_all(spread.reshape(RING * RING, RING, HALF, cols), (Y, X), 0, 0, tiled=True)
-    terms, block2 = lax.optimization_barrier((terms, block2))
+    terms, there = lax.optimization_barrier((terms, there))
     line = terms.astype(F32).sum(axis=0)
     own_terms = right_side - root_diagonal[:, None] * start_guess
     line = line + jnp.concatenate([own_terms[None], jnp.zeros_like(line[1:])])
@@ -215,14 +221,14 @@
     met = pair(Z, line.astype(BF16), False).astype(F32)
     line = line + jnp.concatenate([met[2:], met[:2]])
 
-    mine = ring_pieces(line.astype(BF16), X)
-    partners = [swap(piece, CORE) for piece in mine]
+    mine = jnp.concatenate(ring_pieces(line.astype(BF16), X))
+    partners = swap(mine, CORE)
     parts = call(
         update_kernel,
-        [SMEM] + [VMEM] * 13,
+        [SMEM] + [VMEM] * 6,
         [shape((rows, cols), F32)] * RING,
         [pltpu.VMEM((span, cols), BF16)],
-    )(where, start_guess, preconditioner, block1, block2, block3, *mine, *partners)
+    )(where, start_guess, preconditioner, here, there, mine, partners)
     out = parts[0]
     for k in range(1, RING):
         out = out + from_ahead(parts[k], Y, k)

time: 107 us -> 103 us (0.963)
  starting transfers between devices: 55.1 us -> 48.2 us
  waiting for transfers between devices: 40.9 us -> 44.6 us
    ppermute x3, waiting for transfers between devices: 27.3 us -> 4.33 us  [to_ahead(): lax.ppermute(value, axis, [(i, (i + distance) % RING) for i in range(RING)])]
    ppermute x9 -> x7, waiting for transfers between devices: 2.94 us -> 12.9 us  [swap(): return lax.ppermute(value, axis, SWAP)]
    all_to_all x1, waiting for transfers between devices: 0.01 us -> 8.01 us  [local(): gathered = lax.all_to_all(copies, (Y, X), 0, 0, tiled=True)]
    all_to_all x1, waiting for transfers between devices: 0.01 us -> 6.64 us  [local(): lax.all_to_all(spread.reshape(RING * RING, RING, HALF, cols), (Y, X), 0,...]
    ppermute x4, starting transfers between devices: 13.9 us -> 10.6 us  [pair(): return lax.ppermute(value, axis, list(enumerate(other)))]
    ppermute x9 -> x7, starting transfers between devices: 15 us -> 16.6 us  [swap(): return lax.ppermute(value, axis, SWAP)]
    ppermute x6, starting transfers between devices: 8.63 us -> 7.09 us  [from_ahead(): lax.ppermute(value, axis, [(i, (i - distance) % RING) for i in range(RING)])]
    all_to_all x1, starting transfers between devices: 5.06 us -> 3.65 us  [local(): lax.all_to_all(spread.reshape(RING * RING, RING, HALF, cols), (Y, X), 0,...]
  transfers between devices with their start and end apart: 24 -> 22, of which waited for: 13 -> 17; matrix products, arithmetic and copies ran while one was open for 1% -> 1% of each run, Pallas kernels for 1% -> 1%
where the time goes in v6:
time: 103 us
  starting transfers between devices  48.2 us (47%)
  waiting for transfers between devices  44.6 us (43%)
  Pallas kernels  5.05 us (5%)
  local copies, waits for them, and re-layouts  2.41 us (2%)
  other arithmetic  1.88 us (2%)
    ppermute x7, starting transfers between devices, swap(): return lax.ppermute(value, axis, SWAP)  16.6 us
    ppermute x7, waiting for transfers between devices, swap(): return lax.ppermute(value, axis, SWAP)  12.9 us
    ppermute x4, starting transfers between devices, pair(): return lax.ppermute(value, axis, list(enumerate(other)))  10.6 us
    ppermute x4, waiting for transfers between devices, pair(): return lax.ppermute(value, axis, list(enumerate(other)))  8.83 us
    all_to_all x1, waiting for transfers between devices, local(): gathered = lax.all_to_all(copies, (Y, X), 0, 0, tiled=True)  8.01 us
    ppermute x6, starting transfers between devices, from_ahead(): lax.ppermute(value, axis, [(i, (i - distance) % RING) for i in range(RING)])  7.09 us
    all_to_all x1, waiting for transfers between devices, local(): lax.all_to_all(spread.reshape(RING * RING, RING, HALF, cols), (Y, X), 0,...  6.64 us
    all_to_all x1, starting transfers between devices, local(): gathered = lax.all_to_all(copies, (Y, X), 0, 0, tiled=True)  5.89 us
  transfers between devices with their start and end apart: 22, of which 17 were waited for; matrix products, arithmetic and copies ran while one was open for 1% of the time, Pallas kernels for 1%

profile of v6, /device:TPU:1, one launch (start us, length us, event | category | flops | bytes accessed | tf_op | source)
XLA Modules:
  0.0 102.9 jit_solution(3384783160077368611)
XLA Ops:
  0.0 0.9 subtract_bitcast_fusion
  0.9 3.9 %collective-permute-start = (bf16[64,128]{1,0:T(8,128)(2,1)S(1)}, bf16[64,128]{1,0:T(8,128)(2,1)S(1)}, u32[]{:S(2)}, u32[]{:S(2)}) collective-permute-start(bf16[64,128]{1,0:T(8,128)(2,1)S(1)} %get-tuple-element.51), channel_id=1, source_target_pairs={{0,4},{4,0},{8,12},{12,8},{1,5},{5,1},{9,13},{13,9},{2,6},{6,2},{1... | collective-permute-start | bytes 49160 | tf_op jit(solution)/shard_map/ppermute | solution.py:42
  4.8 1.1 %constant_dynamic-slice_fusion = (bf16[64,1024]{1,0:T(8,128)(2,1)S(1)}, bf16[64,1024]{1,0:T(8,128)(2,1)S(1)}, bf16[64,1024]{1,0:T(8,128)(2,1)S(1)}) fusion(bf16[64,8192]{1,0:T(8,128)(2,1)} %precond.1, s32[]{:T(128)S(6)} %select_n.29, s32[]{:T(128)S(6)} %select_n.27, s32[]{:T(128)S(6)} %select_n.25), kind=kLoop, calls=%fused_computation.12 | loop fusion | bytes 786444 | tf_op jit(solution)/shard_map/dynamic_slice | solution.py:176
  5.9 5.4 %collective-permute-start.1 = (bf16[2,64,128]{2,1,0:T(8,128)(2,1)S(1)}, bf16[2,64,128]{2,1,0:T(8,128)(2,1)S(1)}, u32[]{:S(2)}, u32[]{:S(2)}) collective-permute-start(bf16[2,64,128]{2,1,0:T(8,128)(2,1)S(1)} %pad_maximum_fusion.3), channel_id=1, source_target_pairs={{0,12},{4,8},{8,4},{12,0},{1,13},{5,9},{9,5},{13,1},{2,14},{6,10},... | collective-permute-start | bytes 98312 | tf_op jit(solution)/shard_map/ppermute | solution.py:42
  11.3 1.3 %collective-permute-start.2 = (bf16[64,1024]{1,0:T(8,128)(2,1)S(1)}, bf16[64,1024]{1,0:T(8,128)(2,1)S(1)}, u32[]{:S(2)}, u32[]{:S(2)}) collective-permute-start(bf16[64,1024]{1,0:T(8,128)(2,1)S(1)} %get-tuple-element.42), channel_id=1, source_target_pairs={{0,64},{64,128},{128,192},{192,0},{1,65},{65,129},{129,193},{193,1... | collective-permute-start | bytes 393224 | tf_op jit(solution)/shard_map/ppermute | solution.py:33
  12.6 1.4 %collective-permute-start.4 = (bf16[64,1024]{1,0:T(8,128)(2,1)S(1)}, bf16[64,1024]{1,0:T(8,128)(2,1)S(1)}, u32[]{:S(2)}, u32[]{:S(2)}) collective-permute-start(bf16[64,1024]{1,0:T(8,128)(2,1)S(1)} %get-tuple-element.41), channel_id=1, source_target_pairs={{0,192},{64,0},{128,64},{192,128},{1,193},{65,1},{129,65},{193,129... | collective-permute-start | bytes 393224 | tf_op jit(solution)/shard_map/ppermute | solution.py:33
  14.0 1.6 %collective-permute-start.3 = (bf16[64,1024]{1,0:T(8,128)(2,1)S(1)}, bf16[64,1024]{1,0:T(8,128)(2,1)S(1)}, u32[]{:S(2)}, u32[]{:S(2)}) collective-permute-start(bf16[64,1024]{1,0:T(8,128)(2,1)S(1)} %get-tuple-element.24), channel_id=1, source_target_pairs={{0,128},{64,192},{128,0},{192,64},{1,129},{65,193},{129,1},{193,65... | collective-permute-start | bytes 393224 | tf_op jit(solution)/shard_map/ppermute | solution.py:33
  15.7 0.7 collective-permute-done.2
  16.4 3.6 %collective-permute-done.3 = bf16[64,1024]{1,0:T(8,128)(2,1)S(1)} collective-permute-done((bf16[64,1024]{1,0:T(8,128)(2,1)S(1)}, bf16[64,1024]{1,0:T(8,128)(2,1)S(1)}, u32[]{:S(2)}, u32[]{:S(2)}) %collective-permute-start.3) | collective-permute-done | bytes 131104 | tf_op jit(solution)/shard_map/ppermute | solution.py:33
  20.0 1.2 %broadcast_in_dim.8 = bf16[16,4,64,128]{3,2,1,0:T(8,128)(2,1)} broadcast(bf16[4,64,128]{2,1,0:T(8,128)(2,1)S(1)} %pad_maximum_fusion.2), dimensions={1,2,3} | broadcast | bytes 1114112 | tf_op jit(solution)/shard_map/broadcast_in_dim | solution.py:192
  21.3 5.9 %all-to-all-start = ((bf16[16,4,64,128]{3,2,1,0:T(8,128)(2,1)}), bf16[16,4,64,128]{3,2,1,0:T(8,128)(2,1)S(1)}, u32[]{:S(2)}, u32[]{:S(2)}) async-start(bf16[16,4,64,128]{3,2,1,0:T(8,128)(2,1)} %broadcast_in_dim.8), calls=%async_computation | async-start | bytes 2097152 | tf_op jit(solution)/shard_map/all_to_all | solution.py:193
  27.2 0.8 collective-permute-start.7
  28.0 0.7 collective-permute-start.8
  28.7 3.7 %collective-permute-start.5 = (s32[1,6]{1,0:T(1,128)S(1)}, s32[1,6]{1,0:T(1,128)S(1)}, u32[]{:S(2)}, u32[]{:S(2)}) collective-permute-start(s32[1,6]{1,0:T(1,128)S(1)} %copy-done.4), channel_id=1, source_target_pairs={{0,2},{2,0},{1,3},{3,1},{4,6},{6,4},{5,7},{7,5},{8,10},{10,8},{9,1... | collective-permute-start | bytes 80 | tf_op jit(solution)/shard_map/ppermute | solution.py:25
  33.1 0.1 stack.47.where
  33.2 0.1 collective-permute-done.5.other_ids
  33.3 8.0 %all-to-all-done = bf16[16,4,64,128]{3,2,1,0:T(8,128)(2,1)S(1)} async-done(((bf16[16,4,64,128]{3,2,1,0:T(8,128)(2,1)}), bf16[16,4,64,128]{3,2,1,0:T(8,128)(2,1)S(1)}, u32[]{:S(2)}, u32[]{:S(2)}) %all-to-all-start) | async-done | bytes 1048608 | tf_op jit(solution)/shard_map/all_to_all | solution.py:193
  41.3 0.6 shard_map.82
  41.9 4.5 %collective-permute-start.6 = (bf16[6,64,128]{2,1,0:T(8,128)(2,1)S(1)}, bf16[6,64,128]{2,1,0:T(8,128)(2,1)S(1)}, u32[]{:S(2)}, u32[]{:S(2)}) collective-permute-start(bf16[6,64,128]{2,1,0:T(8,128)(2,1)S(1)} %get-tuple-element.30), channel_id=1, source_target_pairs={{0,2},{2,0},{1,3},{3,1},{4,6},{6,4},{5,7},{7,5},{8,10},{10,8},{9,1... | collective-permute-start | bytes 294920 | tf_op jit(solution)/shard_map/ppermute | solution.py:25
  46.4 0.9 collective-permute-done.6.other_picked
  47.4 1.6 %shard_map.83 = (f32[6,64,128]{2,1,0:T(8,128)S(1)}, f32[6,64,128]{2,1,0:T(8,128)S(1)}) custom-call(s32[6]{0:T(128)S(1)} %stack.47.where, bf16[6,64,128]{2,1,0:T(8,128)(2,1)S(1)} %get-tuple-element.29.own_picked, bf16[6,64,128]{2,1,0:T(8,128)(2,1)S(1)} %collective-permute-done.6.other_picked, bf16[256,768]{1,0:T(8,128)(2,1)S(1)} %bitcast.18, ...), custom_call_target="tpu_custom_call" | custom-call | tf_op jit(solution)/shard_map/pallas_call | solution.py:201
  48.9 0.4 collective-permute-start.9
  49.4 1.1 %collective-permute-done.9.arrived = f32[6,64,128]{2,1,0:T(8,128)S(1)} collective-permute-done((f32[6,64,128]{2,1,0:T(8,128)S(1)}, f32[6,64,128]{2,1,0:T(8,128)S(1)}, u32[]{:S(2)}, u32[]{:S(2)}) %collective-permute-start.9) | collective-permute-done | bytes 196640 | tf_op jit(solution)/shard_map/ppermute | solution.py:25
  50.5 1.8 %shard_map.84 = bf16[64,64,128]{2,1,0:T(8,128)(2,1)} custom-call(s32[6]{0:T(128)S(1)} %stack.47.where, s32[1,6]{1,0:T(1,128)S(1)} %copy-done.4, s32[1,6]{1,0:T(1,128)S(1)} %collective-permute-done.5.other_ids, f32[6,64,128]{2,1,0:T(8,128)S(1)} %get-tuple-element.33.keep, f32[6,64,128]{2,1,0:T(8,128)S(1)} %collective-permute-done.9.arrived), custom_call_target="tpu_custom_call" | custom-call | tf_op jit(solution)/shard_map/pallas_call | solution.py:208
  52.3 3.7 %all-to-all-start.1 = ((bf16[16,4,64,128]{3,2,1,0:T(8,128)(2,1)}), bf16[16,4,64,128]{3,2,1,0:T(8,128)(2,1)S(1)}, u32[]{:S(2)}, u32[]{:S(2)}) async-start(bf16[16,4,64,128]{3,2,1,0:T(8,128)(2,1)} %bitcast.13), calls=%async_computation.1 | async-start | bytes 2097152 | tf_op jit(solution)/shard_map/all_to_all | solution.py:214
  56.0 0.8 collective-permute-start.10
  56.8 9.6 %collective-permute-done.10.there = bf16[3,64,1024]{2,1,0:T(8,128)(2,1)S(1)} collective-permute-done((bf16[3,64,1024]{2,1,0:T(8,128)(2,1)S(1)}, bf16[3,64,1024]{2,1,0:T(8,128)(2,1)S(1)}, u32[]{:S(2)}, u32[]{:S(2)}) %collective-permute-start.10) | collective-permute-done | bytes 393248 | tf_op jit(solution)/shard_map/ppermute | solution.py:25
  66.4 6.6 %all-to-all-done.1 = bf16[16,4,64,128]{3,2,1,0:T(8,128)(2,1)S(1)} async-done(((bf16[16,4,64,128]{3,2,1,0:T(8,128)(2,1)}), bf16[16,4,64,128]{3,2,1,0:T(8,128)(2,1)S(1)}, u32[]{:S(2)}, u32[]{:S(2)}) %all-to-all-start.1) | async-done | bytes 1048608 | tf_op jit(solution)/shard_map/all_to_all | solution.py:214
  73.1 0.2 convert_reduce_fusion
  73.3 1.3 %collective-permute-start.11 = (bf16[4,64,128]{2,1,0:T(8,128)(2,1)S(1)}, bf16[4,64,128]{2,1,0:T(8,128)(2,1)S(1)}, u32[]{:S(2)}, u32[]{:S(2)}) collective-permute-start(bf16[4,64,128]{2,1,0:T(8,128)(2,1)S(1)} %fusion.1), channel_id=1, source_target_pairs={{0,4},{4,0},{8,12},{12,8},{1,5},{5,1},{9,13},{13,9},{2,6},{6,2},{1... | collective-permute-start | bytes 196616 | tf_op jit(solution)/shard_map/ppermute | solution.py:42
  74.6 3.5 %collective-permute-done.11 = bf16[4,64,128]{2,1,0:T(8,128)(2,1)S(1)} collective-permute-done((bf16[4,64,128]{2,1,0:T(8,128)(2,1)S(1)}, bf16[4,64,128]{2,1,0:T(8,128)(2,1)S(1)}, u32[]{:S(2)}, u32[]{:S(2)}) %collective-permute-start.11) | collective-permute-done | bytes 65568 | tf_op jit(solution)/shard_map/ppermute | solution.py:42
  78.2 0.1 collective-permute-start.12
  78.3 5.2 %collective-permute-done.12 = bf16[4,64,128]{2,1,0:T(8,128)(2,1)S(1)} collective-permute-done((bf16[4,64,128]{2,1,0:T(8,128)(2,1)S(1)}, bf16[4,64,128]{2,1,0:T(8,128)(2,1)S(1)}, u32[]{:S(2)}, u32[]{:S(2)}) %collective-permute-start.12) | collective-permute-done | bytes 65568 | tf_op jit(solution)/shard_map/ppermute | solution.py:42
  83.5 0.1 collective-permute-start.15
  83.6 2.3 %collective-permute-start.14 = (bf16[4,64,128]{2,1,0:T(8,128)(2,1)S(1)}, bf16[4,64,128]{2,1,0:T(8,128)(2,1)S(1)}, u32[]{:S(2)}, u32[]{:S(2)}) collective-permute-start(bf16[4,64,128]{2,1,0:T(8,128)(2,1)S(1)} %fusion), channel_id=1, source_target_pairs={{0,32},{16,48},{32,0},{48,16},{1,33},{17,49},{33,1},{49,17},{2,34}... | collective-permute-start | bytes 196616 | tf_op jit(solution)/shard_map/ppermute | solution.py:29
  85.9 2.0 %collective-permute-start.13 = (bf16[4,64,128]{2,1,0:T(8,128)(2,1)S(1)}, bf16[4,64,128]{2,1,0:T(8,128)(2,1)S(1)}, u32[]{:S(2)}, u32[]{:S(2)}) collective-permute-start(bf16[4,64,128]{2,1,0:T(8,128)(2,1)S(1)} %fusion), channel_id=1, source_target_pairs={{0,48},{16,0},{32,16},{48,32},{1,49},{17,1},{33,17},{49,33},{2,50}... | collective-permute-start | bytes 196616 | tf_op jit(solution)/shard_map/ppermute | solution.py:29
  87.9 0.8 collective-permute-done.15
  88.6 0.6 collective-permute-done.13
  89.3 5.5 %collective-permute-start.16 = (bf16[16,64,128]{2,1,0:T(8,128)(2,1)S(1)}, bf16[16,64,128]{2,1,0:T(8,128)(2,1)S(1)}, u32[]{:S(2)}, u32[]{:S(2)}) collective-permute-start(bf16[16,64,128]{2,1,0:T(8,128)(2,1)S(1)} %pad_maximum_fusion.1.mine), channel_id=1, source_target_pairs={{0,2},{2,0},{1,3},{3,1},{4,6},{6,4},{5,7},{7,5},{8,10},{10,8},{9,1... | collective-permute-start | bytes 786440 | tf_op jit(solution)/shard_map/ppermute | solution.py:25
  94.8 1.2 %collective-permute-done.16.partners = bf16[16,64,128]{2,1,0:T(8,128)(2,1)S(1)} collective-permute-done((bf16[16,64,128]{2,1,0:T(8,128)(2,1)S(1)}, bf16[16,64,128]{2,1,0:T(8,128)(2,1)S(1)}, u32[]{:S(2)}, u32[]{:S(2)}) %collective-permute-start.16) | collective-permute-done | bytes 262176 | tf_op jit(solution)/shard_map/ppermute | solution.py:25
  96.0 1.0 %shard_map.85 = (f32[64,128]{1,0:T(8,128)S(1)}, f32[64,128]{1,0:T(8,128)S(1)}, f32[64,128]{1,0:T(8,128)S(1)}, f32[64,128]{1,0:T(8,128)S(1)}) custom-call(s32[6]{0:T(128)S(1)} %stack.47.where, f32[64,128]{1,0:T(8,128)S(1)} %copy-done.3, bf16[64,8192]{1,0:T(8,128)(2,1)S(1)} %copy-done, bf16[3,64,1024]{2,1,0:T(8,128)(2,1)S(1)} %pad_maximum_fusion.here, ...), custom_call_target="tpu_custom_call" | custom-call | tf_op jit(solution)/shard_map/pallas_call | solution.py:226
  97.0 0.1 collective-permute-start.19
  97.1 1.4 %collective-permute-start.18 = (f32[64,128]{1,0:T(8,128)S(1)}, f32[64,128]{1,0:T(8,128)S(1)}, u32[]{:S(2)}, u32[]{:S(2)}) collective-permute-start(f32[64,128]{1,0:T(8,128)S(1)} %get-tuple-element.39), channel_id=1, source_target_pairs={{0,128},{64,192},{128,0},{192,64},{1,129},{65,193},{129,1},{193,65... | collective-permute-start | bytes 98312 | tf_op jit(solution)/shard_map/ppermute | solution.py:29
  98.5 1.3 %collective-permute-start.17 = (f32[64,128]{1,0:T(8,128)S(1)}, f32[64,128]{1,0:T(8,128)S(1)}, u32[]{:S(2)}, u32[]{:S(2)}) collective-permute-start(f32[64,128]{1,0:T(8,128)S(1)} %get-tuple-element.38), channel_id=1, source_target_pairs={{0,192},{64,0},{128,64},{192,128},{1,193},{65,1},{129,65},{193,129... | collective-permute-start | bytes 98312 | tf_op jit(solution)/shard_map/ppermute | solution.py:29
  99.8 1.3 %collective-permute-done.19 = f32[64,128]{1,0:T(8,128)S(1)} collective-permute-done((f32[64,128]{1,0:T(8,128)S(1)}, f32[64,128]{1,0:T(8,128)S(1)}, u32[]{:S(2)}, u32[]{:S(2)}) %collective-permute-start.19) | collective-permute-done | bytes 32800 | tf_op jit(solution)/shard_map/ppermute | solution.py:29
  101.1 0.4 collective-permute-done.18
  101.5 0.8 collective-permute-done.17
  102.3 0.6 add_add_fusion
  (25 shorter events, 0.3 us)
Async XLA Ops:
  0.9 5.0 %collective-permute-start = (bf16[64,128]{1,0:T(8,128)(2,1)S(1)}, bf16[64,128]{1,0:T(8,128)(2,1)S(1)}, u32[]{:S(2)}, u32[]{:S(2)}) collective-permute-start(bf16[64,128]{1,0:T(8,128)(2,1)S(1)} %get-tuple-element.51), channel_id=1, source_target_pairs={{0,4},{4,0},{8,12},{12,8},{1,5},{5,1},{9,13},{13,9},{2,6},{6,2},{1... | collective-permute-start | bytes 49160 | tf_op jit(solution)/shard_map/ppermute | solution.py:42
  5.9 9.8 %collective-permute-start.1 = (bf16[2,64,128]{2,1,0:T(8,128)(2,1)S(1)}, bf16[2,64,128]{2,1,0:T(8,128)(2,1)S(1)}, u32[]{:S(2)}, u32[]{:S(2)}) collective-permute-start(bf16[2,64,128]{2,1,0:T(8,128)(2,1)S(1)} %pad_maximum_fusion.3), channel_id=1, source_target_pairs={{0,12},{4,8},{8,4},{12,0},{1,13},{5,9},{9,5},{13,1},{2,14},{6,10},... | collective-permute-start | bytes 98312 | tf_op jit(solution)/shard_map/ppermute | solution.py:42
  11.3 5.1 %collective-permute-start.2 = (bf16[64,1024]{1,0:T(8,128)(2,1)S(1)}, bf16[64,1024]{1,0:T(8,128)(2,1)S(1)}, u32[]{:S(2)}, u32[]{:S(2)}) collective-permute-start(bf16[64,1024]{1,0:T(8,128)(2,1)S(1)} %get-tuple-element.42), channel_id=1, source_target_pairs={{0,64},{64,128},{128,192},{192,0},{1,65},{65,129},{129,193},{193,1... | collective-permute-start | bytes 393224 | tf_op jit(solution)/shard_map/ppermute | solution.py:33
  12.6 3.8 %collective-permute-start.4 = (bf16[64,1024]{1,0:T(8,128)(2,1)S(1)}, bf16[64,1024]{1,0:T(8,128)(2,1)S(1)}, u32[]{:S(2)}, u32[]{:S(2)}) collective-permute-start(bf16[64,1024]{1,0:T(8,128)(2,1)S(1)} %get-tuple-element.41), channel_id=1, source_target_pairs={{0,192},{64,0},{128,64},{192,128},{1,193},{65,1},{129,65},{193,129... | collective-permute-start | bytes 393224 | tf_op jit(solution)/shard_map/ppermute | solution.py:33
  14.0 6.0 %collective-permute-start.3 = (bf16[64,1024]{1,0:T(8,128)(2,1)S(1)}, bf16[64,1024]{1,0:T(8,128)(2,1)S(1)}, u32[]{:S(2)}, u32[]{:S(2)}) collective-permute-start(bf16[64,1024]{1,0:T(8,128)(2,1)S(1)} %get-tuple-element.24), channel_id=1, source_target_pairs={{0,128},{64,192},{128,0},{192,64},{1,129},{65,193},{129,1},{193,65... | collective-permute-start | bytes 393224 | tf_op jit(solution)/shard_map/ppermute | solution.py:33
  21.3 5.9 %copy-start.1 = (bf16[1,256,768]{2,1,0:T(8,128)(2,1)S(1)}, bf16[1,256,768]{2,1,0:T(8,128)(2,1)}, u32[]{:S(2)}) copy-start(bf16[1,256,768]{2,1,0:T(8,128)(2,1)} %param.12) | copy-start | bytes 1179652
  21.3 6.7 %copy-start.2 = (bf16[1,256,512]{2,1,0:T(8,128)(2,1)S(1)}, bf16[1,256,512]{2,1,0:T(8,128)(2,1)}, u32[]{:S(2)}) copy-start(bf16[1,256,512]{2,1,0:T(8,128)(2,1)} %param.13) | copy-start | bytes 786436
  21.3 7.5 %copy-start.4 = (s32[1,6]{1,0:T(1,128)S(1)}, s32[1,6]{1,0:T(1,128)}, u32[]{:S(2)}) copy-start(s32[1,6]{1,0:T(1,128)} %own_ids.3) | copy-start | bytes 76
  21.3 20.0 %all-to-all-start = ((bf16[16,4,64,128]{3,2,1,0:T(8,128)(2,1)}), bf16[16,4,64,128]{3,2,1,0:T(8,128)(2,1)S(1)}, u32[]{:S(2)}, u32[]{:S(2)}) async-start(bf16[16,4,64,128]{3,2,1,0:T(8,128)(2,1)} %broadcast_in_dim.8), calls=%async_computation | async-start | bytes 2097152 | tf_op jit(solution)/shard_map/all_to_all | solution.py:193
  27.2 19.3 %collective-permute-start.7 = (bf16[256,768]{1,0:T(8,128)(2,1)S(1)}, bf16[256,768]{1,0:T(8,128)(2,1)S(1)}, u32[]{:S(2)}, u32[]{:S(2)}) collective-permute-start(bf16[256,768]{1,0:T(8,128)(2,1)S(1)} %bitcast.17), channel_id=1, source_target_pairs={{0,1},{1,0},{2,3},{3,2},{4,5},{5,4},{6,7},{7,6},{8,9},{9,8},{10,11... | collective-permute-start | bytes 1179656 | tf_op jit(solution)/shard_map/ppermute | solution.py:25
  28.0 18.4 %collective-permute-start.8 = (bf16[256,512]{1,0:T(8,128)(2,1)S(1)}, bf16[256,512]{1,0:T(8,128)(2,1)S(1)}, u32[]{:S(2)}, u32[]{:S(2)}) collective-permute-start(bf16[256,512]{1,0:T(8,128)(2,1)S(1)} %bitcast.19), channel_id=1, source_target_pairs={{0,1},{1,0},{2,3},{3,2},{4,5},{5,4},{6,7},{7,6},{8,9},{9,8},{10,11... | collective-permute-start | bytes 786440 | tf_op jit(solution)/shard_map/ppermute | solution.py:25
  28.7 4.5 %collective-permute-start.5 = (s32[1,6]{1,0:T(1,128)S(1)}, s32[1,6]{1,0:T(1,128)S(1)}, u32[]{:S(2)}, u32[]{:S(2)}) collective-permute-start(s32[1,6]{1,0:T(1,128)S(1)} %copy-done.4), channel_id=1, source_target_pairs={{0,2},{2,0},{1,3},{3,1},{4,6},{6,4},{5,7},{7,5},{8,10},{10,8},{9,1... | collective-permute-start | bytes 80 | tf_op jit(solution)/shard_map/ppermute | solution.py:25
  41.9 5.5 %collective-permute-start.6 = (bf16[6,64,128]{2,1,0:T(8,128)(2,1)S(1)}, bf16[6,64,128]{2,1,0:T(8,128)(2,1)S(1)}, u32[]{:S(2)}, u32[]{:S(2)}) collective-permute-start(bf16[6,64,128]{2,1,0:T(8,128)(2,1)S(1)} %get-tuple-element.30), channel_id=1, source_target_pairs={{0,2},{2,0},{1,3},{3,1},{4,6},{6,4},{5,7},{7,5},{8,10},{10,8},{9,1... | collective-permute-start | bytes 294920 | tf_op jit(solution)/shard_map/ppermute | solution.py:25
  48.9 1.5 %collective-permute-start.9 = (f32[6,64,128]{2,1,0:T(8,128)S(1)}, f32[6,64,128]{2,1,0:T(8,128)S(1)}, u32[]{:S(2)}, u32[]{:S(2)}) collective-permute-start(f32[6,64,128]{2,1,0:T(8,128)S(1)} %get-tuple-element.34), channel_id=1, source_target_pairs={{0,2},{2,0},{1,3},{3,1},{4,6},{6,4},{5,7},{7,5},{8,10},{10,8},{9,1... | collective-permute-start | bytes 589832 | tf_op jit(solution)/shard_map/ppermute | solution.py:25
  52.3 20.8 %all-to-all-start.1 = ((bf16[16,4,64,128]{3,2,1,0:T(8,128)(2,1)}), bf16[16,4,64,128]{3,2,1,0:T(8,128)(2,1)S(1)}, u32[]{:S(2)}, u32[]{:S(2)}) async-start(bf16[16,4,64,128]{3,2,1,0:T(8,128)(2,1)} %bitcast.13), calls=%async_computation.1 | async-start | bytes 2097152 | tf_op jit(solution)/shard_map/all_to_all | solution.py:214
  56.0 10.4 %collective-permute-start.10 = (bf16[3,64,1024]{2,1,0:T(8,128)(2,1)S(1)}, bf16[3,64,1024]{2,1,0:T(8,128)(2,1)S(1)}, u32[]{:S(2)}, u32[]{:S(2)}) collective-permute-start(bf16[3,64,1024]{2,1,0:T(8,128)(2,1)S(1)} %pad_maximum_fusion.here), channel_id=1, source_target_pairs={{0,1},{1,0},{2,3},{3,2},{4,5},{5,4},{6,7},{7,6},{8,9},{9,8},{10,11... | collective-permute-start | bytes 1179656 | tf_op jit(solution)/shard_map/ppermute | solution.py:25
  73.3 22.7 %copy-start = (bf16[64,8192]{1,0:T(8,128)(2,1)S(1)}, bf16[64,8192]{1,0:T(8,128)(2,1)}, u32[]{:S(2)}) copy-start(bf16[64,8192]{1,0:T(8,128)(2,1)} %precond.1) | copy-start | bytes 3145732
  73.3 22.7 %copy-start.3 = (f32[64,128]{1,0:T(8,128)S(1)}, f32[64,128]{1,0:T(8,128)}, u32[]{:S(2)}) copy-start(f32[64,128]{1,0:T(8,128)} %start.1) | copy-start | bytes 98308
  73.3 4.8 %collective-permute-start.11 = (bf16[4,64,128]{2,1,0:T(8,128)(2,1)S(1)}, bf16[4,64,128]{2,1,0:T(8,128)(2,1)S(1)}, u32[]{:S(2)}, u32[]{:S(2)}) collective-permute-start(bf16[4,64,128]{2,1,0:T(8,128)(2,1)S(1)} %fusion.1), channel_id=1, source_target_pairs={{0,4},{4,0},{8,12},{12,8},{1,5},{5,1},{9,13},{13,9},{2,6},{6,2},{1... | collective-permute-start | bytes 196616 | tf_op jit(solution)/shard_map/ppermute | solution.py:42
  78.2 5.3 %collective-permute-start.12 = (bf16[4,64,128]{2,1,0:T(8,128)(2,1)S(1)}, bf16[4,64,128]{2,1,0:T(8,128)(2,1)S(1)}, u32[]{:S(2)}, u32[]{:S(2)}) collective-permute-start(bf16[4,64,128]{2,1,0:T(8,128)(2,1)S(1)} %fusion.2), channel_id=1, source_target_pairs={{0,12},{4,8},{8,4},{12,0},{1,13},{5,9},{9,5},{13,1},{2,14},{6,10},... | collective-permute-start | bytes 196616 | tf_op jit(solution)/shard_map/ppermute | solution.py:42
  83.5 5.1 %collective-permute-start.15 = (bf16[4,64,128]{2,1,0:T(8,128)(2,1)S(1)}, bf16[4,64,128]{2,1,0:T(8,128)(2,1)S(1)}, u32[]{:S(2)}, u32[]{:S(2)}) collective-permute-start(bf16[4,64,128]{2,1,0:T(8,128)(2,1)S(1)} %fusion), channel_id=1, source_target_pairs={{0,16},{16,32},{32,48},{48,0},{1,17},{17,33},{33,49},{49,1},{2,18}... | collective-permute-start | bytes 196616 | tf_op jit(solution)/shard_map/ppermute | solution.py:29
  83.6 5.0 %collective-permute-start.14 = (bf16[4,64,128]{2,1,0:T(8,128)(2,1)S(1)}, bf16[4,64,128]{2,1,0:T(8,128)(2,1)S(1)}, u32[]{:S(2)}, u32[]{:S(2)}) collective-permute-start(bf16[4,64,128]{2,1,0:T(8,128)(2,1)S(1)} %fusion), channel_id=1, source_target_pairs={{0,32},{16,48},{32,0},{48,16},{1,33},{17,49},{33,1},{49,17},{2,34}... | collective-permute-start | bytes 196616 | tf_op jit(solution)/shard_map/ppermute | solution.py:29
  85.9 3.3 %collective-permute-start.13 = (bf16[4,64,128]{2,1,0:T(8,128)(2,1)S(1)}, bf16[4,64,128]{2,1,0:T(8,128)(2,1)S(1)}, u32[]{:S(2)}, u32[]{:S(2)}) collective-permute-start(bf16[4,64,128]{2,1,0:T(8,128)(2,1)S(1)} %fusion), channel_id=1, source_target_pairs={{0,48},{16,0},{32,16},{48,32},{1,49},{17,1},{33,17},{49,33},{2,50}... | collective-permute-start | bytes 196616 | tf_op jit(solution)/shard_map/ppermute | solution.py:29
  89.3 6.7 %collective-permute-start.16 = (bf16[16,64,128]{2,1,0:T(8,128)(2,1)S(1)}, bf16[16,64,128]{2,1,0:T(8,128)(2,1)S(1)}, u32[]{:S(2)}, u32[]{:S(2)}) collective-permute-start(bf16[16,64,128]{2,1,0:T(8,128)(2,1)S(1)} %pad_maximum_fusion.1.mine), channel_id=1, source_target_pairs={{0,2},{2,0},{1,3},{3,1},{4,6},{6,4},{5,7},{7,5},{8,10},{10,8},{9,1... | collective-permute-start | bytes 786440 | tf_op jit(solution)/shard_map/ppermute | solution.py:25
  97.0 4.1 %collective-permute-start.19 = (f32[64,128]{1,0:T(8,128)S(1)}, f32[64,128]{1,0:T(8,128)S(1)}, u32[]{:S(2)}, u32[]{:S(2)}) collective-permute-start(f32[64,128]{1,0:T(8,128)S(1)} %get-tuple-element.40), channel_id=1, source_target_pairs={{0,64},{64,128},{128,192},{192,0},{1,65},{65,129},{129,193},{193,1... | collective-permute-start | bytes 98312 | tf_op jit(solution)/shard_map/ppermute | solution.py:29
  97.1 4.4 %collective-permute-start.18 = (f32[64,128]{1,0:T(8,128)S(1)}, f32[64,128]{1,0:T(8,128)S(1)}, u32[]{:S(2)}, u32[]{:S(2)}) collective-permute-start(f32[64,128]{1,0:T(8,128)S(1)} %get-tuple-element.39), channel_id=1, source_target_pairs={{0,128},{64,192},{128,0},{192,64},{1,129},{65,193},{129,1},{193,65... | collective-permute-start | bytes 98312 | tf_op jit(solution)/shard_map/ppermute | solution.py:29
  98.5 3.8 %collective-permute-start.17 = (f32[64,128]{1,0:T(8,128)S(1)}, f32[64,128]{1,0:T(8,128)S(1)}, u32[]{:S(2)}, u32[]{:S(2)}) collective-permute-start(f32[64,128]{1,0:T(8,128)S(1)} %get-tuple-element.38), channel_id=1, source_target_pairs={{0,192},{64,0},{128,64},{192,128},{1,193},{65,1},{129,65},{193,129... | collective-permute-start | bytes 98312 | tf_op jit(solution)/shard_map/ppermute | solution.py:29

commit v7 on v3

--- a/solution.py
+++ b/solution.py
@@ -55,6 +55,14 @@
 
 def place(tile, where):
     return tile - tile % RING + line_slot(tile % RING, where[2])
+
+
+def copies_kernel(line, out, done):
+    copies = [pltpu.make_async_copy(line, out.at[k], done.at[k]) for k in range(out.shape[0])]
+    for copy in copies:
+        copy.start()
+    for copy in copies:
+        copy.wait()
 
 
 def pick_kernel(where, own_ids, other_ids, gathered, own_ref, other_ref):
@@ -108,11 +116,17 @@
 
 
 def scatter_kernel(where, own_ids, other_ids, keep, arrived, out, total):
-    total[...] = jnp.zeros_like(total)
-    for ids, terms in ((own_ids, keep), (other_ids, arrived)):
-        for j in range(ids.shape[1]):
-            total[place(ids[0, j], where)] += terms[j]
-    out[...] = total[...].astype(BF16)
+    both = ((own_ids, keep), (other_ids, arrived))
+    spots = [[place(ids[0, j], where) for j in range(ids.shape[1])] for ids, _ in both]
+    out[...] = jnp.zeros_like(out)
+    for spot in spots[1]:
+        total[spot] = jnp.zeros_like(total[spot])
+    for j, spot in enumerate(spots[0]):
+        total[spot] = keep[j]
+    for j, spot in enumerate(spots[1]):
+        total[spot] += arrived[j]
+    for spot in spots[0] + spots[1]:
+        out[spot] = total[spot].astype(BF16)
 
 
 def update_kernel(where, start, precond, b1, b2, b3, *refs):
@@ -178,7 +192,14 @@
     border_other = swap(border_late, SIDE)
     inverse_other = swap(inverse_late, SIDE)
     other_tiles = swap(column_tiles, CORE)
-    copies = jnp.broadcast_to(line, (RING * RING, *line.shape))
+    copies = pl.pallas_call(
+        copies_kernel,
+        out_shape=shape((RING * RING, *line.shape), BF16),
+        in_specs=[VMEM],
+        out_specs=pl.BlockSpec(memory_space=pl.ANY),
+        scratch_shapes=[pltpu.SemaphoreType.DMA((RING * RING,))],
+        cost_estimate=pl.CostEstimate(flops=0, bytes_accessed=2**20, transcendentals=0),
+    )(line)
     gathered = lax.all_to_all(copies, (Y, X), 0, 0, tiled=True)
 
     own_half, for_other = call(
@@ -187,14 +208,12 @@
         [shape((tiles, HALF, cols), BF16)] * 2,
     )(where, column_tiles, other_tiles, gathered.reshape(everywhere, HALF, cols))
     other_half = swap(for_other, CORE)
-    gate, columns3 = lax.optimization_barrier((own_half, for_ahead(3)))
-    block3 = to_ahead(columns3, Y, 3)
     keep, send = call(
         scenario_kernel,
         [SMEM] + [VMEM] * 6,
         [shape((tiles, HALF, cols), F32)] * 2,
         [pltpu.VMEM((tiles * TILE, cols), BF16), pltpu.VMEM((2 * border.shape[0], cols), BF16)],
-    )(where, gate, other_half, border, border_other, inverse, inverse_other)
+    )(where, own_half, other_half, border, border_other, inverse, inverse_other)
     arrived = swap(send, CORE)
     spread = call(
         scatter_kernel,
@@ -202,11 +221,10 @@
         shape((everywhere, HALF, cols), BF16),
         [pltpu.VMEM((everywhere, HALF, cols), F32)],
     )(where, column_tiles, other_tiles, keep, arrived)
-    spread, block3 = lax.optimization_barrier((spread, block3))
     terms = lax.all_to_all(spread.reshape(RING * RING, RING, HALF, cols), (Y, X), 0, 0, tiled=True)
     line = terms.astype(F32).sum(axis=0)
-    columns2, line = lax.optimization_barrier((for_ahead(2), line))
-    block2 = to_ahead(columns2, Y, 2)
+    columns2, columns3, line = lax.optimization_barrier((for_ahead(2), for_ahead(3), line))
+    block2, block3 = to_ahead(columns2, Y, 2), to_ahead(columns3, Y, 3)
     own_terms = right_side - root_diagonal[:, None] * start_guess
     line = line + jnp.concatenate([own_terms[None], jnp.zeros_like(line[1:])])
     met = pair(Z, line.astype(BF16), True).astype(F32)

time: 98.9 us -> 97 us (0.981)
  waiting for transfers between devices: 25.1 us -> 20.4 us
  starting transfers between devices: 44.4 us -> 46.3 us
  Pallas kernels: 4.07 us -> 5.95 us
  local copies, waits for them, and re-layouts: 2.53 us -> 1.31 us
    ppermute x3, waiting for transfers between devices: 4.15 us -> 0.58 us  [to_ahead(): lax.ppermute(value, axis, [(i, (i + distance) % RING) for i in range(RING)])]
    pallas_call x0 -> x1, Pallas kernels: none -> 1.95 us  [local(): pl.pallas_call(copies_kernel, out_shape=shape((RING * RING, *line.shape),...]
    ppermute x6, starting transfers between devices: 4.04 us -> 5.87 us  [from_ahead(): lax.ppermute(value, axis, [(i, (i - distance) % RING) for i in range(RING)])]
    ppermute x4, waiting for transfers between devices: 5.9 us -> 4.5 us  [pair(): return lax.ppermute(value, axis, list(enumerate(other)))]
    broadcast_in_dim x1 -> x0, local copies, waits for them, and re-layouts: 1.23 us -> none  [local(): copies = jnp.broadcast_to(line, (RING * RING, *line.shape))]
  transfers between devices with their start and end apart: 23 -> 23, of which waited for: 13 -> 14; matrix products, arithmetic and copies ran while one was open for 1% -> 2% of each run, Pallas kernels for 3% -> 1%
where the time goes in v7:
time: 97 us; the launch traced here: 96.7 us
  starting transfers between devices  46.3 us (48%)
  waiting for transfers between devices  20.4 us (21%)
  blocking collectives  19.5 us (20%)
  Pallas kernels  5.95 us (6%)
  other arithmetic  2.42 us (2%)
  local copies, waits for them, and re-layouts  1.31 us (1%)
    all_to_all x1, blocking collectives, local(): lax.all_to_all(spread.reshape(RING * RING, RING, HALF, cols), (Y, X), 0,...  19.5 us
    ppermute x9, starting transfers between devices, swap(): return lax.ppermute(value, axis, SWAP)  18 us
    ppermute x4, starting transfers between devices, pair(): return lax.ppermute(value, axis, list(enumerate(other)))  13.2 us
    all_to_all x1, waiting for transfers between devices, local(): gathered = lax.all_to_all(copies, (Y, X), 0, 0, tiled=True)  8.79 us
    all_to_all x1, starting transfers between devices, local(): gathered = lax.all_to_all(copies, (Y, X), 0, 0, tiled=True)  6.04 us
    ppermute x6, starting transfers between devices, from_ahead(): lax.ppermute(value, axis, [(i, (i - distance) % RING) for i in range(RING)])  5.87 us
    ppermute x4, waiting for transfers between devices, pair(): return lax.ppermute(value, axis, list(enumerate(other)))  4.5 us
    ppermute x9, waiting for transfers between devices, swap(): return lax.ppermute(value, axis, SWAP)  3.36 us
  transfers between devices with their start and end apart: 23, of which 14 were waited for; matrix products, arithmetic and copies ran while one was open for 2% of the time, Pallas kernels for 1%

profile of v7, /device:TPU:1, one launch (start us, length us, event | category | flops | bytes accessed | tf_op | source)
XLA Modules:
  0.0 96.7 jit_solution(12863029233136008168)
XLA Ops:
  0.0 0.9 subtract_bitcast_fusion
  0.9 3.9 %collective-permute-start = (bf16[64,128]{1,0:T(8,128)(2,1)S(1)}, bf16[64,128]{1,0:T(8,128)(2,1)S(1)}, u32[]{:S(2)}, u32[]{:S(2)}) collective-permute-start(bf16[64,128]{1,0:T(8,128)(2,1)S(1)} %get-tuple-element.45), channel_id=1, source_target_pairs={{0,4},{4,0},{8,12},{12,8},{1,5},{5,1},{9,13},{13,9},{2,6},{6,2},{1... | collective-permute-start | bytes 49160 | tf_op jit(solution)/shard_map/ppermute | solution.py:42
  4.8 1.2 %constant_dynamic-slice_fusion = (bf16[64,2048]{1,0:T(8,128)(2,1)S(1)}, bf16[64,2048]{1,0:T(8,128)(2,1)S(1)}, bf16[64,2048]{1,0:T(8,128)(2,1)S(1)}) fusion(bf16[64,8192]{1,0:T(8,128)(2,1)} %precond.1, s32[]{:T(128)S(6)} %select_n.29, s32[]{:T(128)S(6)} %select_n.27, s32[]{:T(128)S(6)} %select_n.25), kind=kLoop, calls=%fused_computation.10 | loop fusion | bytes 1572876 | tf_op jit(solution)/shard_map/dynamic_slice | solution.py:188
  6.0 1.4 %collective-permute-start.2 = (bf16[64,2048]{1,0:T(8,128)(2,1)S(1)}, bf16[64,2048]{1,0:T(8,128)(2,1)S(1)}, u32[]{:S(2)}, u32[]{:S(2)}) collective-permute-start(bf16[64,2048]{1,0:T(8,128)(2,1)S(1)} %get-tuple-element.37), channel_id=1, source_target_pairs={{0,64},{64,128},{128,192},{192,0},{1,65},{65,129},{129,193},{193,1... | collective-permute-start | bytes 786440 | tf_op jit(solution)/shard_map/ppermute | solution.py:33
  7.4 4.3 %collective-permute-start.1 = (bf16[2,64,128]{2,1,0:T(8,128)(2,1)S(1)}, bf16[2,64,128]{2,1,0:T(8,128)(2,1)S(1)}, u32[]{:S(2)}, u32[]{:S(2)}) collective-permute-start(bf16[2,64,128]{2,1,0:T(8,128)(2,1)S(1)} %pad_maximum_fusion.1), channel_id=1, source_target_pairs={{0,12},{4,8},{8,4},{12,0},{1,13},{5,9},{9,5},{13,1},{2,14},{6,10},... | collective-permute-start | bytes 98312 | tf_op jit(solution)/shard_map/ppermute | solution.py:42
  11.6 1.4 %collective-permute-done.1 = bf16[2,64,128]{2,1,0:T(8,128)(2,1)S(1)} collective-permute-done((bf16[2,64,128]{2,1,0:T(8,128)(2,1)S(1)}, bf16[2,64,128]{2,1,0:T(8,128)(2,1)S(1)}, u32[]{:S(2)}, u32[]{:S(2)}) %collective-permute-start.1) | collective-permute-done | bytes 32800 | tf_op jit(solution)/shard_map/ppermute | solution.py:42
  13.0 0.6 pad_maximum_fusion.line
  13.7 0.6 collective-permute-done.2.b1
  14.2 2.0 %shard_map.82 = bf16[16,4,64,128]{3,2,1,0:T(8,128)(2,1)} custom-call(bf16[4,64,128]{2,1,0:T(8,128)(2,1)} %pad_maximum_fusion.line), custom_call_target="tpu_custom_call" | custom-call | bytes 1048576 | tf_op jit(solution)/shard_map/pallas_call | solution.py:195
  16.2 6.0 %all-to-all-start = ((bf16[16,4,64,128]{3,2,1,0:T(8,128)(2,1)}), bf16[16,4,64,128]{3,2,1,0:T(8,128)(2,1)S(1)}, u32[]{:S(2)}, u32[]{:S(2)}) async-start(bf16[16,4,64,128]{3,2,1,0:T(8,128)(2,1)} %shard_map.82), calls=%async_computation | async-start | bytes 2097152 | tf_op jit(solution)/shard_map/all_to_all | solution.py:203
  22.3 1.3 %collective-permute-start.5 = (bf16[256,768]{1,0:T(8,128)(2,1)S(1)}, bf16[256,768]{1,0:T(8,128)(2,1)S(1)}, u32[]{:S(2)}, u32[]{:S(2)}) collective-permute-start(bf16[256,768]{1,0:T(8,128)(2,1)S(1)} %bitcast.15), channel_id=1, source_target_pairs={{0,1},{1,0},{2,3},{3,2},{4,5},{5,4},{6,7},{7,6},{8,9},{9,8},{10,11... | collective-permute-start | bytes 1179656 | tf_op jit(solution)/shard_map/ppermute | solution.py:25
  23.6 0.2 collective-permute-start.6
  23.9 3.4 %collective-permute-start.3 = (s32[1,6]{1,0:T(1,128)S(1)}, s32[1,6]{1,0:T(1,128)S(1)}, u32[]{:S(2)}, u32[]{:S(2)}) collective-permute-start(s32[1,6]{1,0:T(1,128)S(1)} %copy-done.4), channel_id=1, source_target_pairs={{0,2},{2,0},{1,3},{3,1},{4,6},{6,4},{5,7},{7,5},{8,10},{10,8},{9,1... | collective-permute-start | bytes 80 | tf_op jit(solution)/shard_map/ppermute | solution.py:25
  27.9 0.1 stack.35.where
  28.0 0.1 collective-permute-done.3.other_ids
  28.1 8.8 %all-to-all-done = bf16[16,4,64,128]{3,2,1,0:T(8,128)(2,1)S(1)} async-done(((bf16[16,4,64,128]{3,2,1,0:T(8,128)(2,1)}), bf16[16,4,64,128]{3,2,1,0:T(8,128)(2,1)S(1)}, u32[]{:S(2)}, u32[]{:S(2)}) %all-to-all-start) | async-done | bytes 1048608 | tf_op jit(solution)/shard_map/all_to_all | solution.py:203
  36.9 0.6 shard_map.83
  37.5 4.1 %collective-permute-start.4 = (bf16[6,64,128]{2,1,0:T(8,128)(2,1)S(1)}, bf16[6,64,128]{2,1,0:T(8,128)(2,1)S(1)}, u32[]{:S(2)}, u32[]{:S(2)}) collective-permute-start(bf16[6,64,128]{2,1,0:T(8,128)(2,1)S(1)} %get-tuple-element.23), channel_id=1, source_target_pairs={{0,2},{2,0},{1,3},{3,1},{4,6},{6,4},{5,7},{7,5},{8,10},{10,8},{9,1... | collective-permute-start | bytes 294920 | tf_op jit(solution)/shard_map/ppermute | solution.py:25
  41.6 0.9 collective-permute-done.4.other_picked
  42.5 1.6 %shard_map.84 = (f32[6,64,128]{2,1,0:T(8,128)S(1)}, f32[6,64,128]{2,1,0:T(8,128)S(1)}) custom-call(s32[6]{0:T(128)S(1)} %stack.35.where, bf16[6,64,128]{2,1,0:T(8,128)(2,1)S(1)} %get-tuple-element.22.own_picked, bf16[6,64,128]{2,1,0:T(8,128)(2,1)S(1)} %collective-permute-done.4.other_picked, bf16[256,768]{1,0:T(8,128)(2,1)S(1)} %bitcast.16, ...), custom_call_target="tpu_custom_call" | custom-call | tf_op jit(solution)/shard_map/pallas_call | solution.py:211
  44.1 0.4 collective-permute-start.7
  44.5 1.1 %collective-permute-done.7.arrived = f32[6,64,128]{2,1,0:T(8,128)S(1)} collective-permute-done((f32[6,64,128]{2,1,0:T(8,128)S(1)}, f32[6,64,128]{2,1,0:T(8,128)S(1)}, u32[]{:S(2)}, u32[]{:S(2)}) %collective-permute-start.7) | collective-permute-done | bytes 196640 | tf_op jit(solution)/shard_map/ppermute | solution.py:25
  45.6 0.8 shard_map.85
  46.4 19.5 %all_to_all.10 = bf16[16,4,64,128]{3,2,1,0:T(8,128)(2,1)S(1)} all-to-all(bf16[16,4,64,128]{3,2,1,0:T(8,128)(2,1)S(1)} %bitcast.14), channel_id=1, replica_groups=mesh['scen_0'=4,'scen_1'=4,'scen_2'=4,'rootr'=2,'rootc'=2] {'scen_0','sc..., dimensions={0} | all-to-all | bytes 2097152 | tf_op jit(solution)/shard_map/all_to_all | solution.py:224
  65.8 0.2 convert_reduce_fusion
  66.1 1.2 %collective-permute-start.10 = (bf16[4,64,128]{2,1,0:T(8,128)(2,1)S(1)}, bf16[4,64,128]{2,1,0:T(8,128)(2,1)S(1)}, u32[]{:S(2)}, u32[]{:S(2)}) collective-permute-start(bf16[4,64,128]{2,1,0:T(8,128)(2,1)S(1)} %fusion.1), channel_id=1, source_target_pairs={{0,4},{4,0},{8,12},{12,8},{1,5},{5,1},{9,13},{13,9},{2,6},{6,2},{1... | collective-permute-start | bytes 196616 | tf_op jit(solution)/shard_map/ppermute | solution.py:42
  67.2 2.9 %collective-permute-done.10 = bf16[4,64,128]{2,1,0:T(8,128)(2,1)S(1)} collective-permute-done((bf16[4,64,128]{2,1,0:T(8,128)(2,1)S(1)}, bf16[4,64,128]{2,1,0:T(8,128)(2,1)S(1)}, u32[]{:S(2)}, u32[]{:S(2)}) %collective-permute-start.10) | collective-permute-done | bytes 65568 | tf_op jit(solution)/shard_map/ppermute | solution.py:42
  70.2 3.9 %collective-permute-start.11 = (bf16[4,64,128]{2,1,0:T(8,128)(2,1)S(1)}, bf16[4,64,128]{2,1,0:T(8,128)(2,1)S(1)}, u32[]{:S(2)}, u32[]{:S(2)}) collective-permute-start(bf16[4,64,128]{2,1,0:T(8,128)(2,1)S(1)} %fusion.2), channel_id=1, source_target_pairs={{0,12},{4,8},{8,4},{12,0},{1,13},{5,9},{9,5},{13,1},{2,14},{6,10},... | collective-permute-start | bytes 196616 | tf_op jit(solution)/shard_map/ppermute | solution.py:42
  74.1 0.9 collective-permute-start.8
  75.0 0.9 collective-permute-start.9
  75.9 0.2 collective-permute-done.11
  76.1 0.8 collective-permute-start.12
  76.9 1.3 %collective-permute-start.13 = (bf16[4,64,128]{2,1,0:T(8,128)(2,1)S(1)}, bf16[4,64,128]{2,1,0:T(8,128)(2,1)S(1)}, u32[]{:S(2)}, u32[]{:S(2)}) collective-permute-start(bf16[4,64,128]{2,1,0:T(8,128)(2,1)S(1)} %fusion.refs_0_), channel_id=1, source_target_pairs={{0,32},{16,48},{32,0},{48,16},{1,33},{17,49},{33,1},{49,17},{2,34}... | collective-permute-start | bytes 196616 | tf_op jit(solution)/shard_map/ppermute | solution.py:29
  78.2 0.4 collective-permute-start.14
  78.6 0.6 collective-permute-done.12.refs_1_
  79.3 4.8 %collective-permute-start.15 = (bf16[4,64,128]{2,1,0:T(8,128)(2,1)S(1)}, bf16[4,64,128]{2,1,0:T(8,128)(2,1)S(1)}, u32[]{:S(2)}, u32[]{:S(2)}) collective-permute-start(bf16[4,64,128]{2,1,0:T(8,128)(2,1)S(1)} %fusion.refs_0_), channel_id=1, source_target_pairs={{0,2},{2,0},{1,3},{3,1},{4,6},{6,4},{5,7},{7,5},{8,10},{10,8},{9,1... | collective-permute-start | bytes 196616 | tf_op jit(solution)/shard_map/ppermute | solution.py:25
  84.0 2.9 %collective-permute-start.16 = (bf16[4,64,128]{2,1,0:T(8,128)(2,1)S(1)}, bf16[4,64,128]{2,1,0:T(8,128)(2,1)S(1)}, u32[]{:S(2)}, u32[]{:S(2)}) collective-permute-start(bf16[4,64,128]{2,1,0:T(8,128)(2,1)S(1)} %collective-permute-done.12.refs_1_), channel_id=1, source_target_pairs={{0,2},{2,0},{1,3},{3,1},{4,6},{6,4},{5,7},{7,5},{8,10},{10,8},{9,1... | collective-permute-start | bytes 196616 | tf_op jit(solution)/shard_map/ppermute | solution.py:25
  87.0 0.9 collective-permute-start.17
  87.9 0.9 collective-permute-done.17.refs_6_
  88.8 0.4 collective-permute-done.18.refs_7_
  89.2 1.0 %shard_map.86 = (f32[64,128]{1,0:T(8,128)S(1)}, f32[64,128]{1,0:T(8,128)S(1)}, f32[64,128]{1,0:T(8,128)S(1)}, f32[64,128]{1,0:T(8,128)S(1)}) custom-call(s32[6]{0:T(128)S(1)} %stack.35.where, f32[64,128]{1,0:T(8,128)S(1)} %copy-done.3, bf16[64,8192]{1,0:T(8,128)(2,1)S(1)} %copy-done, bf16[64,2048]{1,0:T(8,128)(2,1)S(1)} %collective-permute-done.2.b1, ...), custom_call_target="tpu_custom_call" | custom-call | tf_op jit(solution)/shard_map/pallas_call | solution.py:237
  90.2 0.3 collective-permute-start.21
  90.5 2.4 %collective-permute-start.20 = (f32[64,128]{1,0:T(8,128)S(1)}, f32[64,128]{1,0:T(8,128)S(1)}, u32[]{:S(2)}, u32[]{:S(2)}) collective-permute-start(f32[64,128]{1,0:T(8,128)S(1)} %get-tuple-element.33), channel_id=1, source_target_pairs={{0,128},{64,192},{128,0},{192,64},{1,129},{65,193},{129,1},{193,65... | collective-permute-start | bytes 98312 | tf_op jit(solution)/shard_map/ppermute | solution.py:29
  92.9 0.6 collective-permute-start.19
  93.5 0.7 collective-permute-done.21
  94.3 0.9 collective-permute-done.20
  95.1 0.9 collective-permute-done.19
  96.0 0.6 add_add_fusion
  (26 shorter events, 0.2 us)
Async XLA Ops:
  0.9 6.4 %collective-permute-start = (bf16[64,128]{1,0:T(8,128)(2,1)S(1)}, bf16[64,128]{1,0:T(8,128)(2,1)S(1)}, u32[]{:S(2)}, u32[]{:S(2)}) collective-permute-start(bf16[64,128]{1,0:T(8,128)(2,1)S(1)} %get-tuple-element.45), channel_id=1, source_target_pairs={{0,4},{4,0},{8,12},{12,8},{1,5},{5,1},{9,13},{13,9},{2,6},{6,2},{1... | collective-permute-start | bytes 49160 | tf_op jit(solution)/shard_map/ppermute | solution.py:42
  6.0 8.3 %collective-permute-start.2 = (bf16[64,2048]{1,0:T(8,128)(2,1)S(1)}, bf16[64,2048]{1,0:T(8,128)(2,1)S(1)}, u32[]{:S(2)}, u32[]{:S(2)}) collective-permute-start(bf16[64,2048]{1,0:T(8,128)(2,1)S(1)} %get-tuple-element.37), channel_id=1, source_target_pairs={{0,64},{64,128},{128,192},{192,0},{1,65},{65,129},{129,193},{193,1... | collective-permute-start | bytes 786440 | tf_op jit(solution)/shard_map/ppermute | solution.py:33
  7.4 5.7 %collective-permute-start.1 = (bf16[2,64,128]{2,1,0:T(8,128)(2,1)S(1)}, bf16[2,64,128]{2,1,0:T(8,128)(2,1)S(1)}, u32[]{:S(2)}, u32[]{:S(2)}) collective-permute-start(bf16[2,64,128]{2,1,0:T(8,128)(2,1)S(1)} %pad_maximum_fusion.1), channel_id=1, source_target_pairs={{0,12},{4,8},{8,4},{12,0},{1,13},{5,9},{9,5},{13,1},{2,14},{6,10},... | collective-permute-start | bytes 98312 | tf_op jit(solution)/shard_map/ppermute | solution.py:42
  16.2 6.1 %copy-start.1 = (bf16[1,256,768]{2,1,0:T(8,128)(2,1)S(1)}, bf16[1,256,768]{2,1,0:T(8,128)(2,1)}, u32[]{:S(2)}) copy-start(bf16[1,256,768]{2,1,0:T(8,128)(2,1)} %param.12) | copy-start | bytes 1179652
  16.2 7.4 %copy-start.2 = (bf16[1,256,512]{2,1,0:T(8,128)(2,1)S(1)}, bf16[1,256,512]{2,1,0:T(8,128)(2,1)}, u32[]{:S(2)}) copy-start(bf16[1,256,512]{2,1,0:T(8,128)(2,1)} %param.13) | copy-start | bytes 786436
  16.2 7.6 %copy-start.4 = (s32[1,6]{1,0:T(1,128)S(1)}, s32[1,6]{1,0:T(1,128)}, u32[]{:S(2)}) copy-start(s32[1,6]{1,0:T(1,128)} %own_ids.3) | copy-start | bytes 76
  16.2 20.6 %all-to-all-start = ((bf16[16,4,64,128]{3,2,1,0:T(8,128)(2,1)}), bf16[16,4,64,128]{3,2,1,0:T(8,128)(2,1)S(1)}, u32[]{:S(2)}, u32[]{:S(2)}) async-start(bf16[16,4,64,128]{3,2,1,0:T(8,128)(2,1)} %shard_map.82), calls=%async_computation | async-start | bytes 2097152 | tf_op jit(solution)/shard_map/all_to_all | solution.py:203
  22.3 19.3 %collective-permute-start.5 = (bf16[256,768]{1,0:T(8,128)(2,1)S(1)}, bf16[256,768]{1,0:T(8,128)(2,1)S(1)}, u32[]{:S(2)}, u32[]{:S(2)}) collective-permute-start(bf16[256,768]{1,0:T(8,128)(2,1)S(1)} %bitcast.15), channel_id=1, source_target_pairs={{0,1},{1,0},{2,3},{3,2},{4,5},{5,4},{6,7},{7,6},{8,9},{9,8},{10,11... | collective-permute-start | bytes 1179656 | tf_op jit(solution)/shard_map/ppermute | solution.py:25
  23.6 17.9 %collective-permute-start.6 = (bf16[256,512]{1,0:T(8,128)(2,1)S(1)}, bf16[256,512]{1,0:T(8,128)(2,1)S(1)}, u32[]{:S(2)}, u32[]{:S(2)}) collective-permute-start(bf16[256,512]{1,0:T(8,128)(2,1)S(1)} %bitcast.17), channel_id=1, source_target_pairs={{0,1},{1,0},{2,3},{3,2},{4,5},{5,4},{6,7},{7,6},{8,9},{9,8},{10,11... | collective-permute-start | bytes 786440 | tf_op jit(solution)/shard_map/ppermute | solution.py:25
  23.9 4.2 %collective-permute-start.3 = (s32[1,6]{1,0:T(1,128)S(1)}, s32[1,6]{1,0:T(1,128)S(1)}, u32[]{:S(2)}, u32[]{:S(2)}) collective-permute-start(s32[1,6]{1,0:T(1,128)S(1)} %copy-done.4), channel_id=1, source_target_pairs={{0,2},{2,0},{1,3},{3,1},{4,6},{6,4},{5,7},{7,5},{8,10},{10,8},{9,1... | collective-permute-start | bytes 80 | tf_op jit(solution)/shard_map/ppermute | solution.py:25
  37.5 5.0 %collective-permute-start.4 = (bf16[6,64,128]{2,1,0:T(8,128)(2,1)S(1)}, bf16[6,64,128]{2,1,0:T(8,128)(2,1)S(1)}, u32[]{:S(2)}, u32[]{:S(2)}) collective-permute-start(bf16[6,64,128]{2,1,0:T(8,128)(2,1)S(1)} %get-tuple-element.23), channel_id=1, source_target_pairs={{0,2},{2,0},{1,3},{3,1},{4,6},{6,4},{5,7},{7,5},{8,10},{10,8},{9,1... | collective-permute-start | bytes 294920 | tf_op jit(solution)/shard_map/ppermute | solution.py:25
  44.1 1.5 %collective-permute-start.7 = (f32[6,64,128]{2,1,0:T(8,128)S(1)}, f32[6,64,128]{2,1,0:T(8,128)S(1)}, u32[]{:S(2)}, u32[]{:S(2)}) collective-permute-start(f32[6,64,128]{2,1,0:T(8,128)S(1)} %get-tuple-element.27), channel_id=1, source_target_pairs={{0,2},{2,0},{1,3},{3,1},{4,6},{6,4},{5,7},{7,5},{8,10},{10,8},{9,1... | collective-permute-start | bytes 589832 | tf_op jit(solution)/shard_map/ppermute | solution.py:25
  66.0 23.1 %copy-start = (bf16[64,8192]{1,0:T(8,128)(2,1)S(1)}, bf16[64,8192]{1,0:T(8,128)(2,1)}, u32[]{:S(2)}) copy-start(bf16[64,8192]{1,0:T(8,128)(2,1)} %precond.1) | copy-start | bytes 3145732
  66.0 23.1 %copy-start.3 = (f32[64,128]{1,0:T(8,128)S(1)}, f32[64,128]{1,0:T(8,128)}, u32[]{:S(2)}) copy-start(f32[64,128]{1,0:T(8,128)} %start.1) | copy-start | bytes 98308
  66.1 4.1 %collective-permute-start.10 = (bf16[4,64,128]{2,1,0:T(8,128)(2,1)S(1)}, bf16[4,64,128]{2,1,0:T(8,128)(2,1)S(1)}, u32[]{:S(2)}, u32[]{:S(2)}) collective-permute-start(bf16[4,64,128]{2,1,0:T(8,128)(2,1)S(1)} %fusion.1), channel_id=1, source_target_pairs={{0,4},{4,0},{8,12},{12,8},{1,5},{5,1},{9,13},{13,9},{2,6},{6,2},{1... | collective-permute-start | bytes 196616 | tf_op jit(solution)/shard_map/ppermute | solution.py:42
  70.2 5.8 %collective-permute-start.11 = (bf16[4,64,128]{2,1,0:T(8,128)(2,1)S(1)}, bf16[4,64,128]{2,1,0:T(8,128)(2,1)S(1)}, u32[]{:S(2)}, u32[]{:S(2)}) collective-permute-start(bf16[4,64,128]{2,1,0:T(8,128)(2,1)S(1)} %fusion.2), channel_id=1, source_target_pairs={{0,12},{4,8},{8,4},{12,0},{1,13},{5,9},{9,5},{13,1},{2,14},{6,10},... | collective-permute-start | bytes 196616 | tf_op jit(solution)/shard_map/ppermute | solution.py:42
  74.1 13.8 %collective-permute-start.8 = (bf16[64,2048]{1,0:T(8,128)(2,1)S(1)}, bf16[64,2048]{1,0:T(8,128)(2,1)S(1)}, u32[]{:S(2)}, u32[]{:S(2)}) collective-permute-start(bf16[64,2048]{1,0:T(8,128)(2,1)S(1)} %get-tuple-element.28), channel_id=1, source_target_pairs={{0,128},{64,192},{128,0},{192,64},{1,129},{65,193},{129,1},{193,65... | collective-permute-start | bytes 786440 | tf_op jit(solution)/shard_map/ppermute | solution.py:33
  75.0 12.9 %collective-permute-start.9 = (bf16[64,2048]{1,0:T(8,128)(2,1)S(1)}, bf16[64,2048]{1,0:T(8,128)(2,1)S(1)}, u32[]{:S(2)}, u32[]{:S(2)}) collective-permute-start(bf16[64,2048]{1,0:T(8,128)(2,1)S(1)} %get-tuple-element.29), channel_id=1, source_target_pairs={{0,192},{64,0},{128,64},{192,128},{1,193},{65,1},{129,65},{193,129... | collective-permute-start | bytes 786440 | tf_op jit(solution)/shard_map/ppermute | solution.py:33
  76.1 3.2 %collective-permute-start.12 = (bf16[4,64,128]{2,1,0:T(8,128)(2,1)S(1)}, bf16[4,64,128]{2,1,0:T(8,128)(2,1)S(1)}, u32[]{:S(2)}, u32[]{:S(2)}) collective-permute-start(bf16[4,64,128]{2,1,0:T(8,128)(2,1)S(1)} %fusion.refs_0_), channel_id=1, source_target_pairs={{0,48},{16,0},{32,16},{48,32},{1,49},{17,1},{33,17},{49,33},{2,50}... | collective-permute-start | bytes 196616 | tf_op jit(solution)/shard_map/ppermute | solution.py:29
  76.9 7.2 %collective-permute-start.13 = (bf16[4,64,128]{2,1,0:T(8,128)(2,1)S(1)}, bf16[4,64,128]{2,1,0:T(8,128)(2,1)S(1)}, u32[]{:S(2)}, u32[]{:S(2)}) collective-permute-start(bf16[4,64,128]{2,1,0:T(8,128)(2,1)S(1)} %fusion.refs_0_), channel_id=1, source_target_pairs={{0,32},{16,48},{32,0},{48,16},{1,33},{17,49},{33,1},{49,17},{2,34}... | collective-permute-start | bytes 196616 | tf_op jit(solution)/shard_map/ppermute | solution.py:29
  78.2 8.8 %collective-permute-start.14 = (bf16[4,64,128]{2,1,0:T(8,128)(2,1)S(1)}, bf16[4,64,128]{2,1,0:T(8,128)(2,1)S(1)}, u32[]{:S(2)}, u32[]{:S(2)}) collective-permute-start(bf16[4,64,128]{2,1,0:T(8,128)(2,1)S(1)} %fusion.refs_0_), channel_id=1, source_target_pairs={{0,16},{16,32},{32,48},{48,0},{1,17},{17,33},{33,49},{49,1},{2,18}... | collective-permute-start | bytes 196616 | tf_op jit(solution)/shard_map/ppermute | solution.py:29
  79.3 8.6 %collective-permute-start.15 = (bf16[4,64,128]{2,1,0:T(8,128)(2,1)S(1)}, bf16[4,64,128]{2,1,0:T(8,128)(2,1)S(1)}, u32[]{:S(2)}, u32[]{:S(2)}) collective-permute-start(bf16[4,64,128]{2,1,0:T(8,128)(2,1)S(1)} %fusion.refs_0_), channel_id=1, source_target_pairs={{0,2},{2,0},{1,3},{3,1},{4,6},{6,4},{5,7},{7,5},{8,10},{10,8},{9,1... | collective-permute-start | bytes 196616 | tf_op jit(solution)/shard_map/ppermute | solution.py:25
  84.0 3.9 %collective-permute-start.16 = (bf16[4,64,128]{2,1,0:T(8,128)(2,1)S(1)}, bf16[4,64,128]{2,1,0:T(8,128)(2,1)S(1)}, u32[]{:S(2)}, u32[]{:S(2)}) collective-permute-start(bf16[4,64,128]{2,1,0:T(8,128)(2,1)S(1)} %collective-permute-done.12.refs_1_), channel_id=1, source_target_pairs={{0,2},{2,0},{1,3},{3,1},{4,6},{6,4},{5,7},{7,5},{8,10},{10,8},{9,1... | collective-permute-start | bytes 196616 | tf_op jit(solution)/shard_map/ppermute | solution.py:25
  87.0 1.8 %collective-permute-start.17 = (bf16[4,64,128]{2,1,0:T(8,128)(2,1)S(1)}, bf16[4,64,128]{2,1,0:T(8,128)(2,1)S(1)}, u32[]{:S(2)}, u32[]{:S(2)}) collective-permute-start(bf16[4,64,128]{2,1,0:T(8,128)(2,1)S(1)} %collective-permute-done.13.refs_2_), channel_id=1, source_target_pairs={{0,2},{2,0},{1,3},{3,1},{4,6},{6,4},{5,7},{7,5},{8,10},{10,8},{9,1... | collective-permute-start | bytes 196616 | tf_op jit(solution)/shard_map/ppermute | solution.py:25
  87.9 1.3 %collective-permute-start.18 = (bf16[4,64,128]{2,1,0:T(8,128)(2,1)S(1)}, bf16[4,64,128]{2,1,0:T(8,128)(2,1)S(1)}, u32[]{:S(2)}, u32[]{:S(2)}) collective-permute-start(bf16[4,64,128]{2,1,0:T(8,128)(2,1)S(1)} %collective-permute-done.14.refs_3_), channel_id=1, source_target_pairs={{0,2},{2,0},{1,3},{3,1},{4,6},{6,4},{5,7},{7,5},{8,10},{10,8},{9,1... | collective-permute-start | bytes 196616 | tf_op jit(solution)/shard_map/ppermute | solution.py:25
  90.2 4.1 %collective-permute-start.21 = (f32[64,128]{1,0:T(8,128)S(1)}, f32[64,128]{1,0:T(8,128)S(1)}, u32[]{:S(2)}, u32[]{:S(2)}) collective-permute-start(f32[64,128]{1,0:T(8,128)S(1)} %get-tuple-element.34), channel_id=1, source_target_pairs={{0,64},{64,128},{128,192},{192,0},{1,65},{65,129},{129,193},{193,1... | collective-permute-start | bytes 98312 | tf_op jit(solution)/shard_map/ppermute | solution.py:29
  90.5 4.6 %collective-permute-start.20 = (f32[64,128]{1,0:T(8,128)S(1)}, f32[64,128]{1,0:T(8,128)S(1)}, u32[]{:S(2)}, u32[]{:S(2)}) collective-permute-start(f32[64,128]{1,0:T(8,128)S(1)} %get-tuple-element.33), channel_id=1, source_target_pairs={{0,128},{64,192},{128,0},{192,64},{1,129},{65,193},{129,1},{193,65... | collective-permute-start | bytes 98312 | tf_op jit(solution)/shard_map/ppermute | solution.py:29
  92.9 3.1 %collective-permute-start.19 = (f32[64,128]{1,0:T(8,128)S(1)}, f32[64,128]{1,0:T(8,128)S(1)}, u32[]{:S(2)}, u32[]{:S(2)}) collective-permute-start(f32[64,128]{1,0:T(8,128)S(1)} %get-tuple-element.32), channel_id=1, source_target_pairs={{0,192},{64,0},{128,64},{192,128},{1,193},{65,1},{129,65},{193,129... | collective-permute-start | bytes 98312 | tf_op jit(solution)/shard_map/ppermute | solution.py:29

commit v8 on v7

--- a/solution.py
+++ b/solution.py
@@ -55,14 +55,6 @@
 
 def place(tile, where):
     return tile - tile % RING + line_slot(tile % RING, where[2])
-
-
-def copies_kernel(line, out, done):
-    copies = [pltpu.make_async_copy(line, out.at[k], done.at[k]) for k in range(out.shape[0])]
-    for copy in copies:
-        copy.start()
-    for copy in copies:
-        copy.wait()
 
 
 def pick_kernel(where, own_ids, other_ids, gathered, own_ref, other_ref):
@@ -188,18 +180,13 @@
         return lax.dynamic_slice_in_dim(preconditioner, first, span, 1)
 
     block1 = to_ahead(for_ahead(1), Y, 1)
-    line, block1, border_late, inverse_late = lax.optimization_barrier((line, block1, border, inverse))
+    line, block1, border_late, inverse_late, right_side = lax.optimization_barrier(
+        (line, block1, border, inverse, right_side)
+    )
     border_other = swap(border_late, SIDE)
     inverse_other = swap(inverse_late, SIDE)
     other_tiles = swap(column_tiles, CORE)
-    copies = pl.pallas_call(
-        copies_kernel,
-        out_shape=shape((RING * RING, *line.shape), BF16),
-        in_specs=[VMEM],
-        out_specs=pl.BlockSpec(memory_space=pl.ANY),
-        scratch_shapes=[pltpu.SemaphoreType.DMA((RING * RING,))],
-        cost_estimate=pl.CostEstimate(flops=0, bytes_accessed=2**20, transcendentals=0),
-    )(line)
+    copies = jnp.broadcast_to(line, (RING * RING, *line.shape))
     gathered = lax.all_to_all(copies, (Y, X), 0, 0, tiled=True)
 
     own_half, for_other = call(

time: 97 us -> 98.2 us (1.012)
  blocking collectives: 19.5 us -> 0 us
  waiting for transfers between devices: 20.4 us -> 36.4 us
  starting transfers between devices: 46.3 us -> 50.7 us
  local copies, waits for them, and re-layouts: 1.31 us -> 2.54 us
  Pallas kernels: 5.95 us -> 4.95 us
    all_to_all x1 -> x0, blocking collectives: 19.5 us -> none  [local(): lax.all_to_all(spread.reshape(RING * RING, RING, HALF, cols), (Y, X), 0,...]
    all_to_all x0 -> x1, waiting for transfers between devices: none -> 16.3 us  [local(): lax.all_to_all(spread.reshape(RING * RING, RING, HALF, cols), (Y, X), 0,...]
    all_to_all x0 -> x1, starting transfers between devices: none -> 3.78 us  [local(): lax.all_to_all(spread.reshape(RING * RING, RING, HALF, cols), (Y, X), 0,...]
    pallas_call x1 -> x0, Pallas kernels: 1.95 us -> none  [local(): pl.pallas_call(copies_kernel, out_shape=shape((RING * RING, *line.shape),...]
    ppermute x4, starting transfers between devices: 13.2 us -> 14.8 us  [pair(): return lax.ppermute(value, axis, list(enumerate(other)))]
    broadcast_in_dim x0 -> x1, local copies, waits for them, and re-layouts: none -> 1.23 us  [local(): copies = jnp.broadcast_to(line, (RING * RING, *line.shape))]
  transfers between devices with their start and end apart: 23 -> 24, of which waited for: 14 -> 15; matrix products, arithmetic and copies ran while one was open for 2% -> 1% of each run, Pallas kernels for 1% -> 1%
where the time goes in v8:
time: 98.2 us; the launch traced here: 97.3 us
  starting transfers between devices  50.7 us (52%)
  waiting for transfers between devices  36.4 us (37%)
  Pallas kernels  4.95 us (5%)
  local copies, waits for them, and re-layouts  2.54 us (3%)
  other arithmetic  1.81 us (2%)
    ppermute x9, starting transfers between devices, swap(): return lax.ppermute(value, axis, SWAP)  17.4 us
    all_to_all x1, waiting for transfers between devices, local(): lax.all_to_all(spread.reshape(RING * RING, RING, HALF, cols), (Y, X), 0,...  16.3 us
    ppermute x4, starting transfers between devices, pair(): return lax.ppermute(value, axis, list(enumerate(other)))  14.8 us
    all_to_all x1, waiting for transfers between devices, local(): gathered = lax.all_to_all(copies, (Y, X), 0, 0, tiled=True)  9.03 us
    ppermute x6, starting transfers between devices, from_ahead(): lax.ppermute(value, axis, [(i, (i - distance) % RING) for i in range(RING)])  6.29 us
    all_to_all x1, starting transfers between devices, local(): gathered = lax.all_to_all(copies, (Y, X), 0, 0, tiled=True)  5.55 us
    ppermute x4, waiting for transfers between devices, pair(): return lax.ppermute(value, axis, list(enumerate(other)))  4.11 us
    all_to_all x1, starting transfers between devices, local(): lax.all_to_all(spread.reshape(RING * RING, RING, HALF, cols), (Y, X), 0,...  3.78 us
  transfers between devices with their start and end apart: 24, of which 15 were waited for; matrix products, arithmetic and copies ran while one was open for 1% of the time, Pallas kernels for 1%

profile of v8, /device:TPU:1, one launch (start us, length us, event | category | flops | bytes accessed | tf_op | source)
XLA Modules:
  0.0 97.3 jit_solution(5893110308135228038)
XLA Ops:
  0.0 0.8 convert_element_type.21
  0.8 3.8 %collective-permute-start = (bf16[64,128]{1,0:T(8,128)(2,1)S(1)}, bf16[64,128]{1,0:T(8,128)(2,1)S(1)}, u32[]{:S(2)}, u32[]{:S(2)}) collective-permute-start(bf16[64,128]{1,0:T(8,128)(2,1)S(1)} %convert_element_type.21), channel_id=1, source_target_pairs={{0,4},{4,0},{8,12},{12,8},{1,5},{5,1},{9,13},{13,9},{2,6},{6,2},{1... | collective-permute-start | bytes 49160 | tf_op jit(solution)/shard_map/ppermute | solution.py:42
  4.7 1.2 %constant_dynamic-slice_fusion = (bf16[64,2048]{1,0:T(8,128)(2,1)S(1)}, bf16[64,2048]{1,0:T(8,128)(2,1)S(1)}, bf16[64,2048]{1,0:T(8,128)(2,1)S(1)}) fusion(bf16[64,8192]{1,0:T(8,128)(2,1)} %precond.1, s32[]{:T(128)S(6)} %select_n.29, s32[]{:T(128)S(6)} %select_n.27, s32[]{:T(128)S(6)} %select_n.25), kind=kLoop, calls=%fused_computation.10 | loop fusion | bytes 1572876 | tf_op jit(solution)/shard_map/dynamic_slice | solution.py:180
  5.8 1.4 %collective-permute-start.2 = (bf16[64,2048]{1,0:T(8,128)(2,1)S(1)}, bf16[64,2048]{1,0:T(8,128)(2,1)S(1)}, u32[]{:S(2)}, u32[]{:S(2)}) collective-permute-start(bf16[64,2048]{1,0:T(8,128)(2,1)S(1)} %get-tuple-element.39), channel_id=1, source_target_pairs={{0,64},{64,128},{128,192},{192,0},{1,65},{65,129},{129,193},{193,1... | collective-permute-start | bytes 786440 | tf_op jit(solution)/shard_map/ppermute | solution.py:33
  7.2 4.3 %collective-permute-start.1 = (bf16[2,64,128]{2,1,0:T(8,128)(2,1)S(1)}, bf16[2,64,128]{2,1,0:T(8,128)(2,1)S(1)}, u32[]{:S(2)}, u32[]{:S(2)}) collective-permute-start(bf16[2,64,128]{2,1,0:T(8,128)(2,1)S(1)} %pad_maximum_fusion.1), channel_id=1, source_target_pairs={{0,12},{4,8},{8,4},{12,0},{1,13},{5,9},{9,5},{13,1},{2,14},{6,10},... | collective-permute-start | bytes 98312 | tf_op jit(solution)/shard_map/ppermute | solution.py:42
  11.5 1.4 %collective-permute-done.1 = bf16[2,64,128]{2,1,0:T(8,128)(2,1)S(1)} collective-permute-done((bf16[2,64,128]{2,1,0:T(8,128)(2,1)S(1)}, bf16[2,64,128]{2,1,0:T(8,128)(2,1)S(1)}, u32[]{:S(2)}, u32[]{:S(2)}) %collective-permute-start.1) | collective-permute-done | bytes 32800 | tf_op jit(solution)/shard_map/ppermute | solution.py:42
  12.9 1.2 %collective-permute-done.2.b1 = bf16[64,2048]{1,0:T(8,128)(2,1)S(1)} collective-permute-done((bf16[64,2048]{1,0:T(8,128)(2,1)S(1)}, bf16[64,2048]{1,0:T(8,128)(2,1)S(1)}, u32[]{:S(2)}, u32[]{:S(2)}) %collective-permute-start.2) | collective-permute-done | bytes 262176 | tf_op jit(solution)/shard_map/ppermute | solution.py:33
  14.1 1.2 %broadcast_in_dim.8 = bf16[16,4,64,128]{3,2,1,0:T(8,128)(2,1)} broadcast(bf16[4,64,128]{2,1,0:T(8,128)(2,1)S(1)} %pad_maximum_fusion), dimensions={1,2,3} | broadcast | bytes 1114112 | tf_op jit(solution)/shard_map/broadcast_in_dim | solution.py:189
  15.3 5.5 %all-to-all-start = ((bf16[16,4,64,128]{3,2,1,0:T(8,128)(2,1)}), bf16[16,4,64,128]{3,2,1,0:T(8,128)(2,1)S(1)}, u32[]{:S(2)}, u32[]{:S(2)}) async-start(bf16[16,4,64,128]{3,2,1,0:T(8,128)(2,1)} %broadcast_in_dim.8), calls=%async_computation | async-start | bytes 2097152 | tf_op jit(solution)/shard_map/all_to_all | solution.py:190
  20.9 1.7 %collective-permute-start.5 = (bf16[256,768]{1,0:T(8,128)(2,1)S(1)}, bf16[256,768]{1,0:T(8,128)(2,1)S(1)}, u32[]{:S(2)}, u32[]{:S(2)}) collective-permute-start(bf16[256,768]{1,0:T(8,128)(2,1)S(1)} %bitcast.15), channel_id=1, source_target_pairs={{0,1},{1,0},{2,3},{3,2},{4,5},{5,4},{6,7},{7,6},{8,9},{9,8},{10,11... | collective-permute-start | bytes 1179656 | tf_op jit(solution)/shard_map/ppermute | solution.py:25
  22.6 0.1 collective-permute-start.6
  22.8 3.0 %collective-permute-start.3 = (s32[1,6]{1,0:T(1,128)S(1)}, s32[1,6]{1,0:T(1,128)S(1)}, u32[]{:S(2)}, u32[]{:S(2)}) collective-permute-start(s32[1,6]{1,0:T(1,128)S(1)} %copy-done.4), channel_id=1, source_target_pairs={{0,2},{2,0},{1,3},{3,1},{4,6},{6,4},{5,7},{7,5},{8,10},{10,8},{9,1... | collective-permute-start | bytes 80 | tf_op jit(solution)/shard_map/ppermute | solution.py:25
  26.4 0.1 stack.35.where
  26.5 0.1 collective-permute-done.3.other_ids
  26.6 9.0 %all-to-all-done = bf16[16,4,64,128]{3,2,1,0:T(8,128)(2,1)S(1)} async-done(((bf16[16,4,64,128]{3,2,1,0:T(8,128)(2,1)}), bf16[16,4,64,128]{3,2,1,0:T(8,128)(2,1)S(1)}, u32[]{:S(2)}, u32[]{:S(2)}) %all-to-all-start) | async-done | bytes 1048608 | tf_op jit(solution)/shard_map/all_to_all | solution.py:190
  35.6 0.6 shard_map.82
  36.2 3.9 %collective-permute-start.4 = (bf16[6,64,128]{2,1,0:T(8,128)(2,1)S(1)}, bf16[6,64,128]{2,1,0:T(8,128)(2,1)S(1)}, u32[]{:S(2)}, u32[]{:S(2)}) collective-permute-start(bf16[6,64,128]{2,1,0:T(8,128)(2,1)S(1)} %get-tuple-element.24), channel_id=1, source_target_pairs={{0,2},{2,0},{1,3},{3,1},{4,6},{6,4},{5,7},{7,5},{8,10},{10,8},{9,1... | collective-permute-start | bytes 294920 | tf_op jit(solution)/shard_map/ppermute | solution.py:25
  40.1 0.9 collective-permute-done.4.other_picked
  41.1 1.6 %shard_map.83 = (f32[6,64,128]{2,1,0:T(8,128)S(1)}, f32[6,64,128]{2,1,0:T(8,128)S(1)}) custom-call(s32[6]{0:T(128)S(1)} %stack.35.where, bf16[6,64,128]{2,1,0:T(8,128)(2,1)S(1)} %get-tuple-element.23.own_picked, bf16[6,64,128]{2,1,0:T(8,128)(2,1)S(1)} %collective-permute-done.4.other_picked, bf16[256,768]{1,0:T(8,128)(2,1)S(1)} %bitcast.16, ...), custom_call_target="tpu_custom_call" | custom-call | tf_op jit(solution)/shard_map/pallas_call | solution.py:198
  42.6 0.4 collective-permute-start.7
  43.1 1.1 %collective-permute-done.7.arrived = f32[6,64,128]{2,1,0:T(8,128)S(1)} collective-permute-done((f32[6,64,128]{2,1,0:T(8,128)S(1)}, f32[6,64,128]{2,1,0:T(8,128)S(1)}, u32[]{:S(2)}, u32[]{:S(2)}) %collective-permute-start.7) | collective-permute-done | bytes 196640 | tf_op jit(solution)/shard_map/ppermute | solution.py:25
  44.2 1.7 %shard_map.84 = bf16[64,64,128]{2,1,0:T(8,128)(2,1)} custom-call(s32[6]{0:T(128)S(1)} %stack.35.where, s32[1,6]{1,0:T(1,128)S(1)} %copy-done.4, s32[1,6]{1,0:T(1,128)S(1)} %collective-permute-done.3.other_ids, f32[6,64,128]{2,1,0:T(8,128)S(1)} %get-tuple-element.27.keep, f32[6,64,128]{2,1,0:T(8,128)S(1)} %collective-permute-done.7.arrived), custom_call_target="tpu_custom_call" | custom-call | tf_op jit(solution)/shard_map/pallas_call | solution.py:205
  45.9 3.8 %all-to-all-start.1 = ((bf16[16,4,64,128]{3,2,1,0:T(8,128)(2,1)}), bf16[16,4,64,128]{3,2,1,0:T(8,128)(2,1)S(1)}, u32[]{:S(2)}, u32[]{:S(2)}) async-start(bf16[16,4,64,128]{3,2,1,0:T(8,128)(2,1)} %bitcast.10), calls=%async_computation.1 | async-start | bytes 2097152 | tf_op jit(solution)/shard_map/all_to_all | solution.py:211
  49.8 16.3 %all-to-all-done.1 = bf16[16,4,64,128]{3,2,1,0:T(8,128)(2,1)S(1)} async-done(((bf16[16,4,64,128]{3,2,1,0:T(8,128)(2,1)}), bf16[16,4,64,128]{3,2,1,0:T(8,128)(2,1)S(1)}, u32[]{:S(2)}, u32[]{:S(2)}) %all-to-all-start.1) | async-done | bytes 1048608 | tf_op jit(solution)/shard_map/all_to_all | solution.py:211
  66.1 0.2 convert_reduce_fusion
  66.3 1.9 %collective-permute-start.10 = (bf16[4,64,128]{2,1,0:T(8,128)(2,1)S(1)}, bf16[4,64,128]{2,1,0:T(8,128)(2,1)S(1)}, u32[]{:S(2)}, u32[]{:S(2)}) collective-permute-start(bf16[4,64,128]{2,1,0:T(8,128)(2,1)S(1)} %fusion.1), channel_id=1, source_target_pairs={{0,4},{4,0},{8,12},{12,8},{1,5},{5,1},{9,13},{13,9},{2,6},{6,2},{1... | collective-permute-start | bytes 196616 | tf_op jit(solution)/shard_map/ppermute | solution.py:42
  68.2 2.2 %collective-permute-done.10 = bf16[4,64,128]{2,1,0:T(8,128)(2,1)S(1)} collective-permute-done((bf16[4,64,128]{2,1,0:T(8,128)(2,1)S(1)}, bf16[4,64,128]{2,1,0:T(8,128)(2,1)S(1)}, u32[]{:S(2)}, u32[]{:S(2)}) %collective-permute-start.10) | collective-permute-done | bytes 65568 | tf_op jit(solution)/shard_map/ppermute | solution.py:42
  70.5 4.8 %collective-permute-start.11 = (bf16[4,64,128]{2,1,0:T(8,128)(2,1)S(1)}, bf16[4,64,128]{2,1,0:T(8,128)(2,1)S(1)}, u32[]{:S(2)}, u32[]{:S(2)}) collective-permute-start(bf16[4,64,128]{2,1,0:T(8,128)(2,1)S(1)} %fusion.2), channel_id=1, source_target_pairs={{0,12},{4,8},{8,4},{12,0},{1,13},{5,9},{9,5},{13,1},{2,14},{6,10},... | collective-permute-start | bytes 196616 | tf_op jit(solution)/shard_map/ppermute | solution.py:42
  75.3 0.4 collective-permute-start.8
  75.6 1.2 %collective-permute-start.9 = (bf16[64,2048]{1,0:T(8,128)(2,1)S(1)}, bf16[64,2048]{1,0:T(8,128)(2,1)S(1)}, u32[]{:S(2)}, u32[]{:S(2)}) collective-permute-start(bf16[64,2048]{1,0:T(8,128)(2,1)S(1)} %get-tuple-element.30), channel_id=1, source_target_pairs={{0,192},{64,0},{128,64},{192,128},{1,193},{65,1},{129,65},{193,129... | collective-permute-start | bytes 786440 | tf_op jit(solution)/shard_map/ppermute | solution.py:33
  76.8 0.5 collective-permute-done.11
  77.3 0.5 collective-permute-start.12
  77.8 2.2 %collective-permute-start.13 = (bf16[4,64,128]{2,1,0:T(8,128)(2,1)S(1)}, bf16[4,64,128]{2,1,0:T(8,128)(2,1)S(1)}, u32[]{:S(2)}, u32[]{:S(2)}) collective-permute-start(bf16[4,64,128]{2,1,0:T(8,128)(2,1)S(1)} %fusion.refs_0_), channel_id=1, source_target_pairs={{0,32},{16,48},{32,0},{48,16},{1,33},{17,49},{33,1},{49,17},{2,34}... | collective-permute-start | bytes 196616 | tf_op jit(solution)/shard_map/ppermute | solution.py:29
  80.0 0.8 collective-permute-start.14
  80.7 4.5 %collective-permute-start.15 = (bf16[4,64,128]{2,1,0:T(8,128)(2,1)S(1)}, bf16[4,64,128]{2,1,0:T(8,128)(2,1)S(1)}, u32[]{:S(2)}, u32[]{:S(2)}) collective-permute-start(bf16[4,64,128]{2,1,0:T(8,128)(2,1)S(1)} %fusion.refs_0_), channel_id=1, source_target_pairs={{0,2},{2,0},{1,3},{3,1},{4,6},{6,4},{5,7},{7,5},{8,10},{10,8},{9,1... | collective-permute-start | bytes 196616 | tf_op jit(solution)/shard_map/ppermute | solution.py:25
  85.2 3.1 %collective-permute-start.16 = (bf16[4,64,128]{2,1,0:T(8,128)(2,1)S(1)}, bf16[4,64,128]{2,1,0:T(8,128)(2,1)S(1)}, u32[]{:S(2)}, u32[]{:S(2)}) collective-permute-start(bf16[4,64,128]{2,1,0:T(8,128)(2,1)S(1)} %collective-permute-done.12.refs_1_), channel_id=1, source_target_pairs={{0,2},{2,0},{1,3},{3,1},{4,6},{6,4},{5,7},{7,5},{8,10},{10,8},{9,1... | collective-permute-start | bytes 196616 | tf_op jit(solution)/shard_map/ppermute | solution.py:25
  88.4 0.6 collective-permute-start.17
  89.1 0.2 collective-permute-done.16.refs_5_
  89.3 0.7 collective-permute-done.17.refs_6_
  89.9 0.4 collective-permute-done.18.refs_7_
  90.3 1.0 %shard_map.85 = (f32[64,128]{1,0:T(8,128)S(1)}, f32[64,128]{1,0:T(8,128)S(1)}, f32[64,128]{1,0:T(8,128)S(1)}, f32[64,128]{1,0:T(8,128)S(1)}) custom-call(s32[6]{0:T(128)S(1)} %stack.35.where, f32[64,128]{1,0:T(8,128)S(1)} %copy-done.1, bf16[64,8192]{1,0:T(8,128)(2,1)S(1)} %copy-done, bf16[64,2048]{1,0:T(8,128)(2,1)S(1)} %collective-permute-done.2.b1, ...), custom_call_target="tpu_custom_call" | custom-call | tf_op jit(solution)/shard_map/pallas_call | solution.py:224
  91.3 0.1 collective-permute-start.21
  91.4 2.1 %collective-permute-start.20 = (f32[64,128]{1,0:T(8,128)S(1)}, f32[64,128]{1,0:T(8,128)S(1)}, u32[]{:S(2)}, u32[]{:S(2)}) collective-permute-start(f32[64,128]{1,0:T(8,128)S(1)} %get-tuple-element.35), channel_id=1, source_target_pairs={{0,128},{64,192},{128,0},{192,64},{1,129},{65,193},{129,1},{193,65... | collective-permute-start | bytes 98312 | tf_op jit(solution)/shard_map/ppermute | solution.py:29
  93.6 0.6 collective-permute-start.19
  94.2 1.2 %collective-permute-done.21 = f32[64,128]{1,0:T(8,128)S(1)} collective-permute-done((f32[64,128]{1,0:T(8,128)S(1)}, f32[64,128]{1,0:T(8,128)S(1)}, u32[]{:S(2)}, u32[]{:S(2)}) %collective-permute-start.21) | collective-permute-done | bytes 32800 | tf_op jit(solution)/shard_map/ppermute | solution.py:29
  95.4 0.8 collective-permute-done.20
  96.1 0.5 collective-permute-done.19
  96.6 0.6 add_add_fusion
  (33 shorter events, 0.2 us)
Async XLA Ops:
  0.0 7.2 %copy-start.1 = (f32[64,128]{1,0:T(8,128)S(1)}, f32[64,128]{1,0:T(8,128)}, u32[]{:S(2)}) copy-start(f32[64,128]{1,0:T(8,128)} %start.1) | copy-start | bytes 98308
  0.8 6.4 %collective-permute-start = (bf16[64,128]{1,0:T(8,128)(2,1)S(1)}, bf16[64,128]{1,0:T(8,128)(2,1)S(1)}, u32[]{:S(2)}, u32[]{:S(2)}) collective-permute-start(bf16[64,128]{1,0:T(8,128)(2,1)S(1)} %convert_element_type.21), channel_id=1, source_target_pairs={{0,4},{4,0},{8,12},{12,8},{1,5},{5,1},{9,13},{13,9},{2,6},{6,2},{1... | collective-permute-start | bytes 49160 | tf_op jit(solution)/shard_map/ppermute | solution.py:42
  5.8 8.3 %collective-permute-start.2 = (bf16[64,2048]{1,0:T(8,128)(2,1)S(1)}, bf16[64,2048]{1,0:T(8,128)(2,1)S(1)}, u32[]{:S(2)}, u32[]{:S(2)}) collective-permute-start(bf16[64,2048]{1,0:T(8,128)(2,1)S(1)} %get-tuple-element.39), channel_id=1, source_target_pairs={{0,64},{64,128},{128,192},{192,0},{1,65},{65,129},{129,193},{193,1... | collective-permute-start | bytes 786440 | tf_op jit(solution)/shard_map/ppermute | solution.py:33
  7.2 5.7 %collective-permute-start.1 = (bf16[2,64,128]{2,1,0:T(8,128)(2,1)S(1)}, bf16[2,64,128]{2,1,0:T(8,128)(2,1)S(1)}, u32[]{:S(2)}, u32[]{:S(2)}) collective-permute-start(bf16[2,64,128]{2,1,0:T(8,128)(2,1)S(1)} %pad_maximum_fusion.1), channel_id=1, source_target_pairs={{0,12},{4,8},{8,4},{12,0},{1,13},{5,9},{9,5},{13,1},{2,14},{6,10},... | collective-permute-start | bytes 98312 | tf_op jit(solution)/shard_map/ppermute | solution.py:42
  15.3 5.6 %copy-start.2 = (bf16[1,256,768]{2,1,0:T(8,128)(2,1)S(1)}, bf16[1,256,768]{2,1,0:T(8,128)(2,1)}, u32[]{:S(2)}) copy-start(bf16[1,256,768]{2,1,0:T(8,128)(2,1)} %param.12) | copy-start | bytes 1179652
  15.3 7.3 %copy-start.3 = (bf16[1,256,512]{2,1,0:T(8,128)(2,1)S(1)}, bf16[1,256,512]{2,1,0:T(8,128)(2,1)}, u32[]{:S(2)}) copy-start(bf16[1,256,512]{2,1,0:T(8,128)(2,1)} %param.13) | copy-start | bytes 786436
  15.3 7.4 %copy-start.4 = (s32[1,6]{1,0:T(1,128)S(1)}, s32[1,6]{1,0:T(1,128)}, u32[]{:S(2)}) copy-start(s32[1,6]{1,0:T(1,128)} %own_ids.3) | copy-start | bytes 76
  15.3 20.2 %all-to-all-start = ((bf16[16,4,64,128]{3,2,1,0:T(8,128)(2,1)}), bf16[16,4,64,128]{3,2,1,0:T(8,128)(2,1)S(1)}, u32[]{:S(2)}, u32[]{:S(2)}) async-start(bf16[16,4,64,128]{3,2,1,0:T(8,128)(2,1)} %broadcast_in_dim.8), calls=%async_computation | async-start | bytes 2097152 | tf_op jit(solution)/shard_map/all_to_all | solution.py:190
  20.9 19.2 %collective-permute-start.5 = (bf16[256,768]{1,0:T(8,128)(2,1)S(1)}, bf16[256,768]{1,0:T(8,128)(2,1)S(1)}, u32[]{:S(2)}, u32[]{:S(2)}) collective-permute-start(bf16[256,768]{1,0:T(8,128)(2,1)S(1)} %bitcast.15), channel_id=1, source_target_pairs={{0,1},{1,0},{2,3},{3,2},{4,5},{5,4},{6,7},{7,6},{8,9},{9,8},{10,11... | collective-permute-start | bytes 1179656 | tf_op jit(solution)/shard_map/ppermute | solution.py:25
  22.6 17.5 %collective-permute-start.6 = (bf16[256,512]{1,0:T(8,128)(2,1)S(1)}, bf16[256,512]{1,0:T(8,128)(2,1)S(1)}, u32[]{:S(2)}, u32[]{:S(2)}) collective-permute-start(bf16[256,512]{1,0:T(8,128)(2,1)S(1)} %bitcast.17), channel_id=1, source_target_pairs={{0,1},{1,0},{2,3},{3,2},{4,5},{5,4},{6,7},{7,6},{8,9},{9,8},{10,11... | collective-permute-start | bytes 786440 | tf_op jit(solution)/shard_map/ppermute | solution.py:25
  22.8 3.8 %collective-permute-start.3 = (s32[1,6]{1,0:T(1,128)S(1)}, s32[1,6]{1,0:T(1,128)S(1)}, u32[]{:S(2)}, u32[]{:S(2)}) collective-permute-start(s32[1,6]{1,0:T(1,128)S(1)} %copy-done.4), channel_id=1, source_target_pairs={{0,2},{2,0},{1,3},{3,1},{4,6},{6,4},{5,7},{7,5},{8,10},{10,8},{9,1... | collective-permute-start | bytes 80 | tf_op jit(solution)/shard_map/ppermute | solution.py:25
  36.2 4.8 %collective-permute-start.4 = (bf16[6,64,128]{2,1,0:T(8,128)(2,1)S(1)}, bf16[6,64,128]{2,1,0:T(8,128)(2,1)S(1)}, u32[]{:S(2)}, u32[]{:S(2)}) collective-permute-start(bf16[6,64,128]{2,1,0:T(8,128)(2,1)S(1)} %get-tuple-element.24), channel_id=1, source_target_pairs={{0,2},{2,0},{1,3},{3,1},{4,6},{6,4},{5,7},{7,5},{8,10},{10,8},{9,1... | collective-permute-start | bytes 294920 | tf_op jit(solution)/shard_map/ppermute | solution.py:25
  42.6 1.5 %collective-permute-start.7 = (f32[6,64,128]{2,1,0:T(8,128)S(1)}, f32[6,64,128]{2,1,0:T(8,128)S(1)}, u32[]{:S(2)}, u32[]{:S(2)}) collective-permute-start(f32[6,64,128]{2,1,0:T(8,128)S(1)} %get-tuple-element.28), channel_id=1, source_target_pairs={{0,2},{2,0},{1,3},{3,1},{4,6},{6,4},{5,7},{7,5},{8,10},{10,8},{9,1... | collective-permute-start | bytes 589832 | tf_op jit(solution)/shard_map/ppermute | solution.py:25
  45.9 3.8 %copy-start.5 = (f32[64,128]{1,0:T(8,128)S(1)}, f32[64,128]{1,0:T(8,128)}, u32[]{:S(2)}) copy-start(f32[64,128]{1,0:T(8,128)} %param.9) | copy-start | bytes 98308
  45.9 3.8 %copy-start.6 = (f32[64]{0:T(128)S(1)}, f32[64]{0:T(128)}, u32[]{:S(2)}) copy-start(f32[64]{0:T(128)} %param.10) | copy-start | bytes 772
  45.9 20.2 %all-to-all-start.1 = ((bf16[16,4,64,128]{3,2,1,0:T(8,128)(2,1)}), bf16[16,4,64,128]{3,2,1,0:T(8,128)(2,1)S(1)}, u32[]{:S(2)}, u32[]{:S(2)}) async-start(bf16[16,4,64,128]{3,2,1,0:T(8,128)(2,1)} %bitcast.10), calls=%async_computation.1 | async-start | bytes 2097152 | tf_op jit(solution)/shard_map/all_to_all | solution.py:211
  66.3 24.0 %copy-start = (bf16[64,8192]{1,0:T(8,128)(2,1)S(1)}, bf16[64,8192]{1,0:T(8,128)(2,1)}, u32[]{:S(2)}) copy-start(bf16[64,8192]{1,0:T(8,128)(2,1)} %precond.1) | copy-start | bytes 3145732
  66.3 4.1 %collective-permute-start.10 = (bf16[4,64,128]{2,1,0:T(8,128)(2,1)S(1)}, bf16[4,64,128]{2,1,0:T(8,128)(2,1)S(1)}, u32[]{:S(2)}, u32[]{:S(2)}) collective-permute-start(bf16[4,64,128]{2,1,0:T(8,128)(2,1)S(1)} %fusion.1), channel_id=1, source_target_pairs={{0,4},{4,0},{8,12},{12,8},{1,5},{5,1},{9,13},{13,9},{2,6},{6,2},{1... | collective-permute-start | bytes 196616 | tf_op jit(solution)/shard_map/ppermute | solution.py:42
  70.5 6.8 %collective-permute-start.11 = (bf16[4,64,128]{2,1,0:T(8,128)(2,1)S(1)}, bf16[4,64,128]{2,1,0:T(8,128)(2,1)S(1)}, u32[]{:S(2)}, u32[]{:S(2)}) collective-permute-start(bf16[4,64,128]{2,1,0:T(8,128)(2,1)S(1)} %fusion.2), channel_id=1, source_target_pairs={{0,12},{4,8},{8,4},{12,0},{1,13},{5,9},{9,5},{13,1},{2,14},{6,10},... | collective-permute-start | bytes 196616 | tf_op jit(solution)/shard_map/ppermute | solution.py:42
  75.3 13.8 %collective-permute-start.8 = (bf16[64,2048]{1,0:T(8,128)(2,1)S(1)}, bf16[64,2048]{1,0:T(8,128)(2,1)S(1)}, u32[]{:S(2)}, u32[]{:S(2)}) collective-permute-start(bf16[64,2048]{1,0:T(8,128)(2,1)S(1)} %get-tuple-element.29), channel_id=1, source_target_pairs={{0,128},{64,192},{128,0},{192,64},{1,129},{65,193},{129,1},{193,65... | collective-permute-start | bytes 786440 | tf_op jit(solution)/shard_map/ppermute | solution.py:33
  75.6 13.4 %collective-permute-start.9 = (bf16[64,2048]{1,0:T(8,128)(2,1)S(1)}, bf16[64,2048]{1,0:T(8,128)(2,1)S(1)}, u32[]{:S(2)}, u32[]{:S(2)}) collective-permute-start(bf16[64,2048]{1,0:T(8,128)(2,1)S(1)} %get-tuple-element.30), channel_id=1, source_target_pairs={{0,192},{64,0},{128,64},{192,128},{1,193},{65,1},{129,65},{193,129... | collective-permute-start | bytes 786440 | tf_op jit(solution)/shard_map/ppermute | solution.py:33
  77.3 3.4 %collective-permute-start.12 = (bf16[4,64,128]{2,1,0:T(8,128)(2,1)S(1)}, bf16[4,64,128]{2,1,0:T(8,128)(2,1)S(1)}, u32[]{:S(2)}, u32[]{:S(2)}) collective-permute-start(bf16[4,64,128]{2,1,0:T(8,128)(2,1)S(1)} %fusion.refs_0_), channel_id=1, source_target_pairs={{0,48},{16,0},{32,16},{48,32},{1,49},{17,1},{33,17},{49,33},{2,50}... | collective-permute-start | bytes 196616 | tf_op jit(solution)/shard_map/ppermute | solution.py:29
  77.8 7.4 %collective-permute-start.13 = (bf16[4,64,128]{2,1,0:T(8,128)(2,1)S(1)}, bf16[4,64,128]{2,1,0:T(8,128)(2,1)S(1)}, u32[]{:S(2)}, u32[]{:S(2)}) collective-permute-start(bf16[4,64,128]{2,1,0:T(8,128)(2,1)S(1)} %fusion.refs_0_), channel_id=1, source_target_pairs={{0,32},{16,48},{32,0},{48,16},{1,33},{17,49},{33,1},{49,17},{2,34}... | collective-permute-start | bytes 196616 | tf_op jit(solution)/shard_map/ppermute | solution.py:29
  80.0 8.4 %collective-permute-start.14 = (bf16[4,64,128]{2,1,0:T(8,128)(2,1)S(1)}, bf16[4,64,128]{2,1,0:T(8,128)(2,1)S(1)}, u32[]{:S(2)}, u32[]{:S(2)}) collective-permute-start(bf16[4,64,128]{2,1,0:T(8,128)(2,1)S(1)} %fusion.refs_0_), channel_id=1, source_target_pairs={{0,16},{16,32},{32,48},{48,0},{1,17},{17,33},{33,49},{49,1},{2,18}... | collective-permute-start | bytes 196616 | tf_op jit(solution)/shard_map/ppermute | solution.py:29
  80.7 8.3 %collective-permute-start.15 = (bf16[4,64,128]{2,1,0:T(8,128)(2,1)S(1)}, bf16[4,64,128]{2,1,0:T(8,128)(2,1)S(1)}, u32[]{:S(2)}, u32[]{:S(2)}) collective-permute-start(bf16[4,64,128]{2,1,0:T(8,128)(2,1)S(1)} %fusion.refs_0_), channel_id=1, source_target_pairs={{0,2},{2,0},{1,3},{3,1},{4,6},{6,4},{5,7},{7,5},{8,10},{10,8},{9,1... | collective-permute-start | bytes 196616 | tf_op jit(solution)/shard_map/ppermute | solution.py:25
  85.2 4.0 %collective-permute-start.16 = (bf16[4,64,128]{2,1,0:T(8,128)(2,1)S(1)}, bf16[4,64,128]{2,1,0:T(8,128)(2,1)S(1)}, u32[]{:S(2)}, u32[]{:S(2)}) collective-permute-start(bf16[4,64,128]{2,1,0:T(8,128)(2,1)S(1)} %collective-permute-done.12.refs_1_), channel_id=1, source_target_pairs={{0,2},{2,0},{1,3},{3,1},{4,6},{6,4},{5,7},{7,5},{8,10},{10,8},{9,1... | collective-permute-start | bytes 196616 | tf_op jit(solution)/shard_map/ppermute | solution.py:25
  88.4 1.6 %collective-permute-start.17 = (bf16[4,64,128]{2,1,0:T(8,128)(2,1)S(1)}, bf16[4,64,128]{2,1,0:T(8,128)(2,1)S(1)}, u32[]{:S(2)}, u32[]{:S(2)}) collective-permute-start(bf16[4,64,128]{2,1,0:T(8,128)(2,1)S(1)} %collective-permute-done.13.refs_2_), channel_id=1, source_target_pairs={{0,2},{2,0},{1,3},{3,1},{4,6},{6,4},{5,7},{7,5},{8,10},{10,8},{9,1... | collective-permute-start | bytes 196616 | tf_op jit(solution)/shard_map/ppermute | solution.py:25
  89.0 1.3 %collective-permute-start.18 = (bf16[4,64,128]{2,1,0:T(8,128)(2,1)S(1)}, bf16[4,64,128]{2,1,0:T(8,128)(2,1)S(1)}, u32[]{:S(2)}, u32[]{:S(2)}) collective-permute-start(bf16[4,64,128]{2,1,0:T(8,128)(2,1)S(1)} %collective-permute-done.14.refs_3_), channel_id=1, source_target_pairs={{0,2},{2,0},{1,3},{3,1},{4,6},{6,4},{5,7},{7,5},{8,10},{10,8},{9,1... | collective-permute-start | bytes 196616 | tf_op jit(solution)/shard_map/ppermute | solution.py:25
  91.3 4.1 %collective-permute-start.21 = (f32[64,128]{1,0:T(8,128)S(1)}, f32[64,128]{1,0:T(8,128)S(1)}, u32[]{:S(2)}, u32[]{:S(2)}) collective-permute-start(f32[64,128]{1,0:T(8,128)S(1)} %get-tuple-element.36), channel_id=1, source_target_pairs={{0,64},{64,128},{128,192},{192,0},{1,65},{65,129},{129,193},{193,1... | collective-permute-start | bytes 98312 | tf_op jit(solution)/shard_map/ppermute | solution.py:29
  91.4 4.7 %collective-permute-start.20 = (f32[64,128]{1,0:T(8,128)S(1)}, f32[64,128]{1,0:T(8,128)S(1)}, u32[]{:S(2)}, u32[]{:S(2)}) collective-permute-start(f32[64,128]{1,0:T(8,128)S(1)} %get-tuple-element.35), channel_id=1, source_target_pairs={{0,128},{64,192},{128,0},{192,64},{1,129},{65,193},{129,1},{193,65... | collective-permute-start | bytes 98312 | tf_op jit(solution)/shard_map/ppermute | solution.py:29
  93.6 3.1 %collective-permute-start.19 = (f32[64,128]{1,0:T(8,128)S(1)}, f32[64,128]{1,0:T(8,128)S(1)}, u32[]{:S(2)}, u32[]{:S(2)}) collective-permute-start(f32[64,128]{1,0:T(8,128)S(1)} %get-tuple-element.34), channel_id=1, source_target_pairs={{0,192},{64,0},{128,64},{192,128},{1,193},{65,1},{129,65},{193,129... | collective-permute-start | bytes 98312 | tf_op jit(solution)/shard_map/ppermute | solution.py:29

commit v9 on v8

--- a/solution.py
+++ b/solution.py
@@ -180,9 +180,7 @@
         return lax.dynamic_slice_in_dim(preconditioner, first, span, 1)
 
     block1 = to_ahead(for_ahead(1), Y, 1)
-    line, block1, border_late, inverse_late, right_side = lax.optimization_barrier(
-        (line, block1, border, inverse, right_side)
-    )
+    line, block1, border_late, inverse_late = lax.optimization_barrier((line, block1, border, inverse))
     border_other = swap(border_late, SIDE)
     inverse_other = swap(inverse_late, SIDE)
     other_tiles = swap(column_tiles, CORE)

time: 98.2 us -> 96.2 us (0.980)
  blocking collectives: 0 us -> 19.7 us
  waiting for transfers between devices: 36.4 us -> 21.5 us
  starting transfers between devices: 50.7 us -> 45.6 us
    all_to_all x0 -> x1, blocking collectives: none -> 19.7 us  [local(): lax.all_to_all(spread.reshape(RING * RING, RING, HALF, cols), (Y, X), 0,...]
    all_to_all x1 -> x0, waiting for transfers between devices: 16.3 us -> none  [local(): lax.all_to_all(spread.reshape(RING * RING, RING, HALF, cols), (Y, X), 0,...]
    all_to_all x1 -> x0, starting transfers between devices: 3.78 us -> none  [local(): lax.all_to_all(spread.reshape(RING * RING, RING, HALF, cols), (Y, X), 0,...]
    ppermute x4, starting transfers between devices: 14.8 us -> 13.3 us  [pair(): return lax.ppermute(value, axis, list(enumerate(other)))]
  transfers between devices with their start and end apart: 24 -> 23, of which waited for: 15 -> 14; matrix products, arithmetic and copies ran while one was open for 1% -> 1% of each run, Pallas kernels for 1% -> 1%
where the time goes in v9:
time: 96.2 us; the launch traced here: 95.9 us
  starting transfers between devices  45.6 us (47%)
  waiting for transfers between devices  21.5 us (22%)
  blocking collectives  19.7 us (20%)
  Pallas kernels  4 us (4%)
  local copies, waits for them, and re-layouts  2.53 us (3%)
  other arithmetic  1.8 us (2%)
    all_to_all x1, blocking collectives, local(): lax.all_to_all(spread.reshape(RING * RING, RING, HALF, cols), (Y, X), 0,...  19.7 us
    ppermute x9, starting transfers between devices, swap(): return lax.ppermute(value, axis, SWAP)  17.7 us
    ppermute x4, starting transfers between devices, pair(): return lax.ppermute(value, axis, list(enumerate(other)))  13.3 us
    all_to_all x1, waiting for transfers between devices, local(): gathered = lax.all_to_all(copies, (Y, X), 0, 0, tiled=True)  9.03 us
    ppermute x6, starting transfers between devices, from_ahead(): lax.ppermute(value, axis, [(i, (i - distance) % RING) for i in range(RING)])  5.9 us
    all_to_all x1, starting transfers between devices, local(): gathered = lax.all_to_all(copies, (Y, X), 0, 0, tiled=True)  5.55 us
    ppermute x4, waiting for transfers between devices, pair(): return lax.ppermute(value, axis, list(enumerate(other)))  4.79 us
    ppermute x9, waiting for transfers between devices, swap(): return lax.ppermute(value, axis, SWAP)  3.36 us
  transfers between devices with their start and end apart: 23, of which 14 were waited for; matrix products, arithmetic and copies ran while one was open for 1% of the time, Pallas kernels for 1%

profile of v9, /device:TPU:1, one launch (start us, length us, event | category | flops | bytes accessed | tf_op | source)
XLA Modules:
  0.0 95.9 jit_solution(17713162456332244282)
XLA Ops:
  0.0 0.9 subtract_bitcast_fusion
  0.9 3.9 %collective-permute-start = (bf16[64,128]{1,0:T(8,128)(2,1)S(1)}, bf16[64,128]{1,0:T(8,128)(2,1)S(1)}, u32[]{:S(2)}, u32[]{:S(2)}) collective-permute-start(bf16[64,128]{1,0:T(8,128)(2,1)S(1)} %get-tuple-element.45), channel_id=1, source_target_pairs={{0,4},{4,0},{8,12},{12,8},{1,5},{5,1},{9,13},{13,9},{2,6},{6,2},{1... | collective-permute-start | bytes 49160 | tf_op jit(solution)/shard_map/ppermute | solution.py:42
  4.8 1.2 %constant_dynamic-slice_fusion = (bf16[64,2048]{1,0:T(8,128)(2,1)S(1)}, bf16[64,2048]{1,0:T(8,128)(2,1)S(1)}, bf16[64,2048]{1,0:T(8,128)(2,1)S(1)}) fusion(bf16[64,8192]{1,0:T(8,128)(2,1)} %precond.1, s32[]{:T(128)S(6)} %select_n.29, s32[]{:T(128)S(6)} %select_n.27, s32[]{:T(128)S(6)} %select_n.25), kind=kLoop, calls=%fused_computation.10 | loop fusion | bytes 1572876 | tf_op jit(solution)/shard_map/dynamic_slice | solution.py:180
  6.0 1.4 %collective-permute-start.2 = (bf16[64,2048]{1,0:T(8,128)(2,1)S(1)}, bf16[64,2048]{1,0:T(8,128)(2,1)S(1)}, u32[]{:S(2)}, u32[]{:S(2)}) collective-permute-start(bf16[64,2048]{1,0:T(8,128)(2,1)S(1)} %get-tuple-element.37), channel_id=1, source_target_pairs={{0,64},{64,128},{128,192},{192,0},{1,65},{65,129},{129,193},{193,1... | collective-permute-start | bytes 786440 | tf_op jit(solution)/shard_map/ppermute | solution.py:33
  7.4 4.3 %collective-permute-start.1 = (bf16[2,64,128]{2,1,0:T(8,128)(2,1)S(1)}, bf16[2,64,128]{2,1,0:T(8,128)(2,1)S(1)}, u32[]{:S(2)}, u32[]{:S(2)}) collective-permute-start(bf16[2,64,128]{2,1,0:T(8,128)(2,1)S(1)} %pad_maximum_fusion.1), channel_id=1, source_target_pairs={{0,12},{4,8},{8,4},{12,0},{1,13},{5,9},{9,5},{13,1},{2,14},{6,10},... | collective-permute-start | bytes 98312 | tf_op jit(solution)/shard_map/ppermute | solution.py:42
  11.6 1.4 %collective-permute-done.1 = bf16[2,64,128]{2,1,0:T(8,128)(2,1)S(1)} collective-permute-done((bf16[2,64,128]{2,1,0:T(8,128)(2,1)S(1)}, bf16[2,64,128]{2,1,0:T(8,128)(2,1)S(1)}, u32[]{:S(2)}, u32[]{:S(2)}) %collective-permute-start.1) | collective-permute-done | bytes 32800 | tf_op jit(solution)/shard_map/ppermute | solution.py:42
  13.1 1.2 %collective-permute-done.2.b1 = bf16[64,2048]{1,0:T(8,128)(2,1)S(1)} collective-permute-done((bf16[64,2048]{1,0:T(8,128)(2,1)S(1)}, bf16[64,2048]{1,0:T(8,128)(2,1)S(1)}, u32[]{:S(2)}, u32[]{:S(2)}) %collective-permute-start.2) | collective-permute-done | bytes 262176 | tf_op jit(solution)/shard_map/ppermute | solution.py:33
  14.2 1.2 %broadcast_in_dim.8 = bf16[16,4,64,128]{3,2,1,0:T(8,128)(2,1)} broadcast(bf16[4,64,128]{2,1,0:T(8,128)(2,1)S(1)} %pad_maximum_fusion), dimensions={1,2,3} | broadcast | bytes 1114112 | tf_op jit(solution)/shard_map/broadcast_in_dim | solution.py:187
  15.5 5.5 %all-to-all-start = ((bf16[16,4,64,128]{3,2,1,0:T(8,128)(2,1)}), bf16[16,4,64,128]{3,2,1,0:T(8,128)(2,1)S(1)}, u32[]{:S(2)}, u32[]{:S(2)}) async-start(bf16[16,4,64,128]{3,2,1,0:T(8,128)(2,1)} %broadcast_in_dim.8), calls=%async_computation | async-start | bytes 2097152 | tf_op jit(solution)/shard_map/all_to_all | solution.py:188
  21.0 1.7 %collective-permute-start.5 = (bf16[256,768]{1,0:T(8,128)(2,1)S(1)}, bf16[256,768]{1,0:T(8,128)(2,1)S(1)}, u32[]{:S(2)}, u32[]{:S(2)}) collective-permute-start(bf16[256,768]{1,0:T(8,128)(2,1)S(1)} %bitcast.15), channel_id=1, source_target_pairs={{0,1},{1,0},{2,3},{3,2},{4,5},{5,4},{6,7},{7,6},{8,9},{9,8},{10,11... | collective-permute-start | bytes 1179656 | tf_op jit(solution)/shard_map/ppermute | solution.py:25
  22.8 0.1 collective-permute-start.6
  22.9 3.0 %collective-permute-start.3 = (s32[1,6]{1,0:T(1,128)S(1)}, s32[1,6]{1,0:T(1,128)S(1)}, u32[]{:S(2)}, u32[]{:S(2)}) collective-permute-start(s32[1,6]{1,0:T(1,128)S(1)} %copy-done.4), channel_id=1, source_target_pairs={{0,2},{2,0},{1,3},{3,1},{4,6},{6,4},{5,7},{7,5},{8,10},{10,8},{9,1... | collective-permute-start | bytes 80 | tf_op jit(solution)/shard_map/ppermute | solution.py:25
  26.5 0.1 stack.35.where
  26.6 0.1 collective-permute-done.3.other_ids
  26.7 9.0 %all-to-all-done = bf16[16,4,64,128]{3,2,1,0:T(8,128)(2,1)S(1)} async-done(((bf16[16,4,64,128]{3,2,1,0:T(8,128)(2,1)}), bf16[16,4,64,128]{3,2,1,0:T(8,128)(2,1)S(1)}, u32[]{:S(2)}, u32[]{:S(2)}) %all-to-all-start) | async-done | bytes 1048608 | tf_op jit(solution)/shard_map/all_to_all | solution.py:188
  35.7 0.6 shard_map.82
  36.3 3.9 %collective-permute-start.4 = (bf16[6,64,128]{2,1,0:T(8,128)(2,1)S(1)}, bf16[6,64,128]{2,1,0:T(8,128)(2,1)S(1)}, u32[]{:S(2)}, u32[]{:S(2)}) collective-permute-start(bf16[6,64,128]{2,1,0:T(8,128)(2,1)S(1)} %get-tuple-element.23), channel_id=1, source_target_pairs={{0,2},{2,0},{1,3},{3,1},{4,6},{6,4},{5,7},{7,5},{8,10},{10,8},{9,1... | collective-permute-start | bytes 294920 | tf_op jit(solution)/shard_map/ppermute | solution.py:25
  40.3 0.9 collective-permute-done.4.other_picked
  41.2 1.6 %shard_map.83 = (f32[6,64,128]{2,1,0:T(8,128)S(1)}, f32[6,64,128]{2,1,0:T(8,128)S(1)}) custom-call(s32[6]{0:T(128)S(1)} %stack.35.where, bf16[6,64,128]{2,1,0:T(8,128)(2,1)S(1)} %get-tuple-element.22.own_picked, bf16[6,64,128]{2,1,0:T(8,128)(2,1)S(1)} %collective-permute-done.4.other_picked, bf16[256,768]{1,0:T(8,128)(2,1)S(1)} %bitcast.16, ...), custom_call_target="tpu_custom_call" | custom-call | tf_op jit(solution)/shard_map/pallas_call | solution.py:196
  42.8 0.4 collective-permute-start.7
  43.2 1.1 %collective-permute-done.7.arrived = f32[6,64,128]{2,1,0:T(8,128)S(1)} collective-permute-done((f32[6,64,128]{2,1,0:T(8,128)S(1)}, f32[6,64,128]{2,1,0:T(8,128)S(1)}, u32[]{:S(2)}, u32[]{:S(2)}) %collective-permute-start.7) | collective-permute-done | bytes 196640 | tf_op jit(solution)/shard_map/ppermute | solution.py:25
  44.3 0.8 shard_map.84
  45.1 19.7 %all_to_all.10 = bf16[16,4,64,128]{3,2,1,0:T(8,128)(2,1)S(1)} all-to-all(bf16[16,4,64,128]{3,2,1,0:T(8,128)(2,1)S(1)} %bitcast.14), channel_id=1, replica_groups=mesh['scen_0'=4,'scen_1'=4,'scen_2'=4,'rootr'=2,'rootc'=2] {'scen_0','sc..., dimensions={0} | all-to-all | bytes 2097152 | tf_op jit(solution)/shard_map/all_to_all | solution.py:209
  64.7 0.2 convert_reduce_fusion
  65.0 0.9 collective-permute-start.10
  65.9 3.2 %collective-permute-done.10 = bf16[4,64,128]{2,1,0:T(8,128)(2,1)S(1)} collective-permute-done((bf16[4,64,128]{2,1,0:T(8,128)(2,1)S(1)}, bf16[4,64,128]{2,1,0:T(8,128)(2,1)S(1)}, u32[]{:S(2)}, u32[]{:S(2)}) %collective-permute-start.10) | collective-permute-done | bytes 65568 | tf_op jit(solution)/shard_map/ppermute | solution.py:42
  69.1 4.2 %collective-permute-start.11 = (bf16[4,64,128]{2,1,0:T(8,128)(2,1)S(1)}, bf16[4,64,128]{2,1,0:T(8,128)(2,1)S(1)}, u32[]{:S(2)}, u32[]{:S(2)}) collective-permute-start(bf16[4,64,128]{2,1,0:T(8,128)(2,1)S(1)} %fusion.2), channel_id=1, source_target_pairs={{0,12},{4,8},{8,4},{12,0},{1,13},{5,9},{9,5},{13,1},{2,14},{6,10},... | collective-permute-start | bytes 196616 | tf_op jit(solution)/shard_map/ppermute | solution.py:42
  73.3 0.9 collective-permute-start.8
  74.2 0.9 collective-permute-start.9
  75.1 0.2 collective-permute-done.11
  75.3 0.8 collective-permute-start.12
  76.1 1.3 %collective-permute-start.13 = (bf16[4,64,128]{2,1,0:T(8,128)(2,1)S(1)}, bf16[4,64,128]{2,1,0:T(8,128)(2,1)S(1)}, u32[]{:S(2)}, u32[]{:S(2)}) collective-permute-start(bf16[4,64,128]{2,1,0:T(8,128)(2,1)S(1)} %fusion.refs_0_), channel_id=1, source_target_pairs={{0,32},{16,48},{32,0},{48,16},{1,33},{17,49},{33,1},{49,17},{2,34}... | collective-permute-start | bytes 196616 | tf_op jit(solution)/shard_map/ppermute | solution.py:29
  77.5 0.4 collective-permute-start.14
  77.9 0.6 collective-permute-done.12.refs_1_
  78.5 4.7 %collective-permute-start.15 = (bf16[4,64,128]{2,1,0:T(8,128)(2,1)S(1)}, bf16[4,64,128]{2,1,0:T(8,128)(2,1)S(1)}, u32[]{:S(2)}, u32[]{:S(2)}) collective-permute-start(bf16[4,64,128]{2,1,0:T(8,128)(2,1)S(1)} %fusion.refs_0_), channel_id=1, source_target_pairs={{0,2},{2,0},{1,3},{3,1},{4,6},{6,4},{5,7},{7,5},{8,10},{10,8},{9,1... | collective-permute-start | bytes 196616 | tf_op jit(solution)/shard_map/ppermute | solution.py:25
  83.2 3.0 %collective-permute-start.16 = (bf16[4,64,128]{2,1,0:T(8,128)(2,1)S(1)}, bf16[4,64,128]{2,1,0:T(8,128)(2,1)S(1)}, u32[]{:S(2)}, u32[]{:S(2)}) collective-permute-start(bf16[4,64,128]{2,1,0:T(8,128)(2,1)S(1)} %collective-permute-done.12.refs_1_), channel_id=1, source_target_pairs={{0,2},{2,0},{1,3},{3,1},{4,6},{6,4},{5,7},{7,5},{8,10},{10,8},{9,1... | collective-permute-start | bytes 196616 | tf_op jit(solution)/shard_map/ppermute | solution.py:25
  86.2 0.9 collective-permute-start.17
  87.1 0.0 collective-permute-done.16.refs_5_
  87.1 0.9 collective-permute-done.17.refs_6_
  88.0 0.4 collective-permute-done.18.refs_7_
  88.3 1.0 %shard_map.85 = (f32[64,128]{1,0:T(8,128)S(1)}, f32[64,128]{1,0:T(8,128)S(1)}, f32[64,128]{1,0:T(8,128)S(1)}, f32[64,128]{1,0:T(8,128)S(1)}) custom-call(s32[6]{0:T(128)S(1)} %stack.35.where, f32[64,128]{1,0:T(8,128)S(1)} %copy-done.3, bf16[64,8192]{1,0:T(8,128)(2,1)S(1)} %copy-done, bf16[64,2048]{1,0:T(8,128)(2,1)S(1)} %collective-permute-done.2.b1, ...), custom_call_target="tpu_custom_call" | custom-call | tf_op jit(solution)/shard_map/pallas_call | solution.py:222
  89.4 0.4 collective-permute-start.21
  89.8 2.4 %collective-permute-start.20 = (f32[64,128]{1,0:T(8,128)S(1)}, f32[64,128]{1,0:T(8,128)S(1)}, u32[]{:S(2)}, u32[]{:S(2)}) collective-permute-start(f32[64,128]{1,0:T(8,128)S(1)} %get-tuple-element.33), channel_id=1, source_target_pairs={{0,128},{64,192},{128,0},{192,64},{1,129},{65,193},{129,1},{193,65... | collective-permute-start | bytes 98312 | tf_op jit(solution)/shard_map/ppermute | solution.py:29
  92.2 0.6 collective-permute-start.19
  92.7 0.7 collective-permute-done.21
  93.4 0.9 collective-permute-done.20
  94.3 0.9 collective-permute-done.19
  95.3 0.6 add_add_fusion
  (26 shorter events, 0.1 us)
Async XLA Ops:
  0.9 6.4 %collective-permute-start = (bf16[64,128]{1,0:T(8,128)(2,1)S(1)}, bf16[64,128]{1,0:T(8,128)(2,1)S(1)}, u32[]{:S(2)}, u32[]{:S(2)}) collective-permute-start(bf16[64,128]{1,0:T(8,128)(2,1)S(1)} %get-tuple-element.45), channel_id=1, source_target_pairs={{0,4},{4,0},{8,12},{12,8},{1,5},{5,1},{9,13},{13,9},{2,6},{6,2},{1... | collective-permute-start | bytes 49160 | tf_op jit(solution)/shard_map/ppermute | solution.py:42
  6.0 8.3 %collective-permute-start.2 = (bf16[64,2048]{1,0:T(8,128)(2,1)S(1)}, bf16[64,2048]{1,0:T(8,128)(2,1)S(1)}, u32[]{:S(2)}, u32[]{:S(2)}) collective-permute-start(bf16[64,2048]{1,0:T(8,128)(2,1)S(1)} %get-tuple-element.37), channel_id=1, source_target_pairs={{0,64},{64,128},{128,192},{192,0},{1,65},{65,129},{129,193},{193,1... | collective-permute-start | bytes 786440 | tf_op jit(solution)/shard_map/ppermute | solution.py:33
  7.4 5.7 %collective-permute-start.1 = (bf16[2,64,128]{2,1,0:T(8,128)(2,1)S(1)}, bf16[2,64,128]{2,1,0:T(8,128)(2,1)S(1)}, u32[]{:S(2)}, u32[]{:S(2)}) collective-permute-start(bf16[2,64,128]{2,1,0:T(8,128)(2,1)S(1)} %pad_maximum_fusion.1), channel_id=1, source_target_pairs={{0,12},{4,8},{8,4},{12,0},{1,13},{5,9},{9,5},{13,1},{2,14},{6,10},... | collective-permute-start | bytes 98312 | tf_op jit(solution)/shard_map/ppermute | solution.py:42
  15.5 5.6 %copy-start.1 = (bf16[1,256,768]{2,1,0:T(8,128)(2,1)S(1)}, bf16[1,256,768]{2,1,0:T(8,128)(2,1)}, u32[]{:S(2)}) copy-start(bf16[1,256,768]{2,1,0:T(8,128)(2,1)} %param.12) | copy-start | bytes 1179652
  15.5 7.3 %copy-start.2 = (bf16[1,256,512]{2,1,0:T(8,128)(2,1)S(1)}, bf16[1,256,512]{2,1,0:T(8,128)(2,1)}, u32[]{:S(2)}) copy-start(bf16[1,256,512]{2,1,0:T(8,128)(2,1)} %param.13) | copy-start | bytes 786436
  15.5 7.4 %copy-start.4 = (s32[1,6]{1,0:T(1,128)S(1)}, s32[1,6]{1,0:T(1,128)}, u32[]{:S(2)}) copy-start(s32[1,6]{1,0:T(1,128)} %own_ids.3) | copy-start | bytes 76
  15.5 20.2 %all-to-all-start = ((bf16[16,4,64,128]{3,2,1,0:T(8,128)(2,1)}), bf16[16,4,64,128]{3,2,1,0:T(8,128)(2,1)S(1)}, u32[]{:S(2)}, u32[]{:S(2)}) async-start(bf16[16,4,64,128]{3,2,1,0:T(8,128)(2,1)} %broadcast_in_dim.8), calls=%async_computation | async-start | bytes 2097152 | tf_op jit(solution)/shard_map/all_to_all | solution.py:188
  21.0 19.2 %collective-permute-start.5 = (bf16[256,768]{1,0:T(8,128)(2,1)S(1)}, bf16[256,768]{1,0:T(8,128)(2,1)S(1)}, u32[]{:S(2)}, u32[]{:S(2)}) collective-permute-start(bf16[256,768]{1,0:T(8,128)(2,1)S(1)} %bitcast.15), channel_id=1, source_target_pairs={{0,1},{1,0},{2,3},{3,2},{4,5},{5,4},{6,7},{7,6},{8,9},{9,8},{10,11... | collective-permute-start | bytes 1179656 | tf_op jit(solution)/shard_map/ppermute | solution.py:25
  22.8 17.5 %collective-permute-start.6 = (bf16[256,512]{1,0:T(8,128)(2,1)S(1)}, bf16[256,512]{1,0:T(8,128)(2,1)S(1)}, u32[]{:S(2)}, u32[]{:S(2)}) collective-permute-start(bf16[256,512]{1,0:T(8,128)(2,1)S(1)} %bitcast.17), channel_id=1, source_target_pairs={{0,1},{1,0},{2,3},{3,2},{4,5},{5,4},{6,7},{7,6},{8,9},{9,8},{10,11... | collective-permute-start | bytes 786440 | tf_op jit(solution)/shard_map/ppermute | solution.py:25
  22.9 3.8 %collective-permute-start.3 = (s32[1,6]{1,0:T(1,128)S(1)}, s32[1,6]{1,0:T(1,128)S(1)}, u32[]{:S(2)}, u32[]{:S(2)}) collective-permute-start(s32[1,6]{1,0:T(1,128)S(1)} %copy-done.4), channel_id=1, source_target_pairs={{0,2},{2,0},{1,3},{3,1},{4,6},{6,4},{5,7},{7,5},{8,10},{10,8},{9,1... | collective-permute-start | bytes 80 | tf_op jit(solution)/shard_map/ppermute | solution.py:25
  36.3 4.8 %collective-permute-start.4 = (bf16[6,64,128]{2,1,0:T(8,128)(2,1)S(1)}, bf16[6,64,128]{2,1,0:T(8,128)(2,1)S(1)}, u32[]{:S(2)}, u32[]{:S(2)}) collective-permute-start(bf16[6,64,128]{2,1,0:T(8,128)(2,1)S(1)} %get-tuple-element.23), channel_id=1, source_target_pairs={{0,2},{2,0},{1,3},{3,1},{4,6},{6,4},{5,7},{7,5},{8,10},{10,8},{9,1... | collective-permute-start | bytes 294920 | tf_op jit(solution)/shard_map/ppermute | solution.py:25
  42.8 1.5 %collective-permute-start.7 = (f32[6,64,128]{2,1,0:T(8,128)S(1)}, f32[6,64,128]{2,1,0:T(8,128)S(1)}, u32[]{:S(2)}, u32[]{:S(2)}) collective-permute-start(f32[6,64,128]{2,1,0:T(8,128)S(1)} %get-tuple-element.27), channel_id=1, source_target_pairs={{0,2},{2,0},{1,3},{3,1},{4,6},{6,4},{5,7},{7,5},{8,10},{10,8},{9,1... | collective-permute-start | bytes 589832 | tf_op jit(solution)/shard_map/ppermute | solution.py:25
  64.9 23.4 %copy-start = (bf16[64,8192]{1,0:T(8,128)(2,1)S(1)}, bf16[64,8192]{1,0:T(8,128)(2,1)}, u32[]{:S(2)}) copy-start(bf16[64,8192]{1,0:T(8,128)(2,1)} %precond.1) | copy-start | bytes 3145732
  64.9 23.4 %copy-start.3 = (f32[64,128]{1,0:T(8,128)S(1)}, f32[64,128]{1,0:T(8,128)}, u32[]{:S(2)}) copy-start(f32[64,128]{1,0:T(8,128)} %start.1) | copy-start | bytes 98308
  65.0 4.1 %collective-permute-start.10 = (bf16[4,64,128]{2,1,0:T(8,128)(2,1)S(1)}, bf16[4,64,128]{2,1,0:T(8,128)(2,1)S(1)}, u32[]{:S(2)}, u32[]{:S(2)}) collective-permute-start(bf16[4,64,128]{2,1,0:T(8,128)(2,1)S(1)} %fusion.1), channel_id=1, source_target_pairs={{0,4},{4,0},{8,12},{12,8},{1,5},{5,1},{9,13},{13,9},{2,6},{6,2},{1... | collective-permute-start | bytes 196616 | tf_op jit(solution)/shard_map/ppermute | solution.py:42
  69.1 6.1 %collective-permute-start.11 = (bf16[4,64,128]{2,1,0:T(8,128)(2,1)S(1)}, bf16[4,64,128]{2,1,0:T(8,128)(2,1)S(1)}, u32[]{:S(2)}, u32[]{:S(2)}) collective-permute-start(bf16[4,64,128]{2,1,0:T(8,128)(2,1)S(1)} %fusion.2), channel_id=1, source_target_pairs={{0,12},{4,8},{8,4},{12,0},{1,13},{5,9},{9,5},{13,1},{2,14},{6,10},... | collective-permute-start | bytes 196616 | tf_op jit(solution)/shard_map/ppermute | solution.py:42
  73.3 13.7 %collective-permute-start.8 = (bf16[64,2048]{1,0:T(8,128)(2,1)S(1)}, bf16[64,2048]{1,0:T(8,128)(2,1)S(1)}, u32[]{:S(2)}, u32[]{:S(2)}) collective-permute-start(bf16[64,2048]{1,0:T(8,128)(2,1)S(1)} %get-tuple-element.28), channel_id=1, source_target_pairs={{0,128},{64,192},{128,0},{192,64},{1,129},{65,193},{129,1},{193,65... | collective-permute-start | bytes 786440 | tf_op jit(solution)/shard_map/ppermute | solution.py:33
  74.2 12.9 %collective-permute-start.9 = (bf16[64,2048]{1,0:T(8,128)(2,1)S(1)}, bf16[64,2048]{1,0:T(8,128)(2,1)S(1)}, u32[]{:S(2)}, u32[]{:S(2)}) collective-permute-start(bf16[64,2048]{1,0:T(8,128)(2,1)S(1)} %get-tuple-element.29), channel_id=1, source_target_pairs={{0,192},{64,0},{128,64},{192,128},{1,193},{65,1},{129,65},{193,129... | collective-permute-start | bytes 786440 | tf_op jit(solution)/shard_map/ppermute | solution.py:33
  75.3 3.2 %collective-permute-start.12 = (bf16[4,64,128]{2,1,0:T(8,128)(2,1)S(1)}, bf16[4,64,128]{2,1,0:T(8,128)(2,1)S(1)}, u32[]{:S(2)}, u32[]{:S(2)}) collective-permute-start(bf16[4,64,128]{2,1,0:T(8,128)(2,1)S(1)} %fusion.refs_0_), channel_id=1, source_target_pairs={{0,48},{16,0},{32,16},{48,32},{1,49},{17,1},{33,17},{49,33},{2,50}... | collective-permute-start | bytes 196616 | tf_op jit(solution)/shard_map/ppermute | solution.py:29
  76.1 7.1 %collective-permute-start.13 = (bf16[4,64,128]{2,1,0:T(8,128)(2,1)S(1)}, bf16[4,64,128]{2,1,0:T(8,128)(2,1)S(1)}, u32[]{:S(2)}, u32[]{:S(2)}) collective-permute-start(bf16[4,64,128]{2,1,0:T(8,128)(2,1)S(1)} %fusion.refs_0_), channel_id=1, source_target_pairs={{0,32},{16,48},{32,0},{48,16},{1,33},{17,49},{33,1},{49,17},{2,34}... | collective-permute-start | bytes 196616 | tf_op jit(solution)/shard_map/ppermute | solution.py:29
  77.5 8.8 %collective-permute-start.14 = (bf16[4,64,128]{2,1,0:T(8,128)(2,1)S(1)}, bf16[4,64,128]{2,1,0:T(8,128)(2,1)S(1)}, u32[]{:S(2)}, u32[]{:S(2)}) collective-permute-start(bf16[4,64,128]{2,1,0:T(8,128)(2,1)S(1)} %fusion.refs_0_), channel_id=1, source_target_pairs={{0,16},{16,32},{32,48},{48,0},{1,17},{17,33},{33,49},{49,1},{2,18}... | collective-permute-start | bytes 196616 | tf_op jit(solution)/shard_map/ppermute | solution.py:29
  78.5 8.6 %collective-permute-start.15 = (bf16[4,64,128]{2,1,0:T(8,128)(2,1)S(1)}, bf16[4,64,128]{2,1,0:T(8,128)(2,1)S(1)}, u32[]{:S(2)}, u32[]{:S(2)}) collective-permute-start(bf16[4,64,128]{2,1,0:T(8,128)(2,1)S(1)} %fusion.refs_0_), channel_id=1, source_target_pairs={{0,2},{2,0},{1,3},{3,1},{4,6},{6,4},{5,7},{7,5},{8,10},{10,8},{9,1... | collective-permute-start | bytes 196616 | tf_op jit(solution)/shard_map/ppermute | solution.py:25
  83.2 3.9 %collective-permute-start.16 = (bf16[4,64,128]{2,1,0:T(8,128)(2,1)S(1)}, bf16[4,64,128]{2,1,0:T(8,128)(2,1)S(1)}, u32[]{:S(2)}, u32[]{:S(2)}) collective-permute-start(bf16[4,64,128]{2,1,0:T(8,128)(2,1)S(1)} %collective-permute-done.12.refs_1_), channel_id=1, source_target_pairs={{0,2},{2,0},{1,3},{3,1},{4,6},{6,4},{5,7},{7,5},{8,10},{10,8},{9,1... | collective-permute-start | bytes 196616 | tf_op jit(solution)/shard_map/ppermute | solution.py:25
  86.2 1.8 %collective-permute-start.17 = (bf16[4,64,128]{2,1,0:T(8,128)(2,1)S(1)}, bf16[4,64,128]{2,1,0:T(8,128)(2,1)S(1)}, u32[]{:S(2)}, u32[]{:S(2)}) collective-permute-start(bf16[4,64,128]{2,1,0:T(8,128)(2,1)S(1)} %collective-permute-done.13.refs_2_), channel_id=1, source_target_pairs={{0,2},{2,0},{1,3},{3,1},{4,6},{6,4},{5,7},{7,5},{8,10},{10,8},{9,1... | collective-permute-start | bytes 196616 | tf_op jit(solution)/shard_map/ppermute | solution.py:25
  87.1 1.3 %collective-permute-start.18 = (bf16[4,64,128]{2,1,0:T(8,128)(2,1)S(1)}, bf16[4,64,128]{2,1,0:T(8,128)(2,1)S(1)}, u32[]{:S(2)}, u32[]{:S(2)}) collective-permute-start(bf16[4,64,128]{2,1,0:T(8,128)(2,1)S(1)} %collective-permute-done.14.refs_3_), channel_id=1, source_target_pairs={{0,2},{2,0},{1,3},{3,1},{4,6},{6,4},{5,7},{7,5},{8,10},{10,8},{9,1... | collective-permute-start | bytes 196616 | tf_op jit(solution)/shard_map/ppermute | solution.py:25
  89.4 4.1 %collective-permute-start.21 = (f32[64,128]{1,0:T(8,128)S(1)}, f32[64,128]{1,0:T(8,128)S(1)}, u32[]{:S(2)}, u32[]{:S(2)}) collective-permute-start(f32[64,128]{1,0:T(8,128)S(1)} %get-tuple-element.34), channel_id=1, source_target_pairs={{0,64},{64,128},{128,192},{192,0},{1,65},{65,129},{129,193},{193,1... | collective-permute-start | bytes 98312 | tf_op jit(solution)/shard_map/ppermute | solution.py:29
  89.8 4.6 %collective-permute-start.20 = (f32[64,128]{1,0:T(8,128)S(1)}, f32[64,128]{1,0:T(8,128)S(1)}, u32[]{:S(2)}, u32[]{:S(2)}) collective-permute-start(f32[64,128]{1,0:T(8,128)S(1)} %get-tuple-element.33), channel_id=1, source_target_pairs={{0,128},{64,192},{128,0},{192,64},{1,129},{65,193},{129,1},{193,65... | collective-permute-start | bytes 98312 | tf_op jit(solution)/shard_map/ppermute | solution.py:29
  92.2 3.1 %collective-permute-start.19 = (f32[64,128]{1,0:T(8,128)S(1)}, f32[64,128]{1,0:T(8,128)S(1)}, u32[]{:S(2)}, u32[]{:S(2)}) collective-permute-start(f32[64,128]{1,0:T(8,128)S(1)} %get-tuple-element.32), channel_id=1, source_target_pairs={{0,192},{64,0},{128,64},{192,128},{1,193},{65,1},{129,65},{193,129... | collective-permute-start | bytes 98312 | tf_op jit(solution)/shard_map/ppermute | solution.py:29

commit v10 on v9

--- a/solution.py
+++ b/solution.py
@@ -35,6 +35,19 @@
 
 def ring_pieces(value, axis):
     return [value] + [from_ahead(value, axis, k) for k in range(1, RING)]
+
+
+def across(value, distance, turn):
+    pairs = []
+    for y in range(RING):
+        for x in range(RING):
+            for core in range(2):
+                if core == turn:
+                    there = ((y + distance) % RING, x)
+                else:
+                    there = (y, (x + distance) % RING)
+                pairs.append(((y * RING + x) * 2 + core, (there[0] * RING + there[1]) * 2 + core))
+    return lax.ppermute(value, (Y, X, CORE), pairs)
 
 
 def pair(axis, value, first):
@@ -107,18 +120,39 @@
         send_ref[...] = term[:, 0]
 
 
-def scatter_kernel(where, own_ids, other_ids, keep, arrived, out, total):
-    both = ((own_ids, keep), (other_ids, arrived))
-    spots = [[place(ids[0, j], where) for j in range(ids.shape[1])] for ids, _ in both]
-    out[...] = jnp.zeros_like(out)
-    for spot in spots[1]:
+def spread_place(tile, where):
+    dy = (tile // 16 - where[0] + RING) % RING
+    dx = ((tile // RING) % RING - where[1] + RING) % RING
+    slot = line_slot(tile % RING, where[2])
+    first = where[3] == 0
+    return jnp.where(first, dy, dx), jnp.where(first, dx, dy) * RING + slot
+
+
+def scatter_kernel(where, own_ids, other_ids, keep, arrived, near, c1, c2, c3, total):
+    spots = []
+    for ids in (own_ids, other_ids):
+        for j in range(ids.shape[1]):
+            chunk, rest = spread_place(ids[0, j], where)
+            spots.append((chunk, rest, chunk * 16 + rest))
+    half = len(spots) // 2
+    near_rows = near.shape[0]
+    total[0:near_rows] = jnp.zeros_like(near)
+    chunks = (c1, c2, c3)
+    for chunk in chunks:
+        chunk[...] = jnp.zeros_like(chunk)
+    for _, _, spot in spots[half:]:
         total[spot] = jnp.zeros_like(total[spot])
-    for j, spot in enumerate(spots[0]):
+    for j, (_, _, spot) in enumerate(spots[:half]):
         total[spot] = keep[j]
-    for j, spot in enumerate(spots[1]):
+    for j, (_, _, spot) in enumerate(spots[half:]):
         total[spot] += arrived[j]
-    for spot in spots[0] + spots[1]:
-        out[spot] = total[spot].astype(BF16)
+    near[...] = total[0:near_rows]
+    for chunk, rest, spot in spots:
+        for k, out in enumerate(chunks):
+
+            @pl.when(chunk == k + 1)
+            def _():
+                out[rest] = total[spot].astype(BF16)
 
 
 def update_kernel(where, start, precond, b1, b2, b3, *refs):
@@ -200,14 +234,21 @@
         [pltpu.VMEM((tiles * TILE, cols), BF16), pltpu.VMEM((2 * border.shape[0], cols), BF16)],
     )(where, own_half, other_half, border, border_other, inverse, inverse_other)
     arrived = swap(send, CORE)
-    spread = call(
+    near_tiles = RING * RING
+    near_shape = (near_tiles, HALF, cols)
+    near, *chunks = call(
         scatter_kernel,
         [SMEM] * 3 + [VMEM] * 2,
-        shape((everywhere, HALF, cols), BF16),
+        [shape(near_shape, F32)] + [shape(near_shape, BF16)] * (RING - 1),
         [pltpu.VMEM((everywhere, HALF, cols), F32)],
     )(where, column_tiles, other_tiles, keep, arrived)
-    terms = lax.all_to_all(spread.reshape(RING * RING, RING, HALF, cols), (Y, X), 0, 0, tiled=True)
-    line = terms.astype(F32).sum(axis=0)
+    plane = near
+    for k, chunk in enumerate(chunks):
+        plane = plane + across(chunk, k + 1, 0).astype(F32)
+    plane = plane.reshape(RING, RING, HALF, cols)
+    line = plane[0]
+    for k in range(1, RING):
+        line = line + across(plane[k].astype(BF16), k, 1).astype(F32)
     columns2, columns3, line = lax.optimization_barrier((for_ahead(2), for_ahead(3), line))
     block2, block3 = to_ahead(columns2, Y, 2), to_ahead(columns3, Y, 3)
     own_terms = right_side - root_diagonal[:, None] * start_guess

time: 96.2 us -> 94.6 us (0.983)
  blocking collectives: 19.7 us -> 0 us
  waiting for transfers between devices: 21.5 us -> 34.9 us
  starting transfers between devices: 45.6 us -> 49.8 us
    all_to_all x1 -> x0, blocking collectives: 19.7 us -> none  [local(): lax.all_to_all(spread.reshape(RING * RING, RING, HALF, cols), (Y, X), 0,...]
    ppermute x0 -> x6, waiting for transfers between devices: none -> 12.2 us  [across(): return lax.ppermute(value, (Y, X, CORE), pairs)]
    ppermute x0 -> x6, starting transfers between devices: none -> 4.83 us  [across(): return lax.ppermute(value, (Y, X, CORE), pairs)]
  transfers between devices with their start and end apart: 23 -> 29, of which waited for: 14 -> 21; matrix products, arithmetic and copies ran while one was open for 1% -> 1% of each run, Pallas kernels for 1% -> 1%
where the time goes in v10:
time: 94.6 us; the launch traced here: 94.4 us
  starting transfers between devices  49.8 us (53%)
  waiting for transfers between devices  34.9 us (37%)
  Pallas kernels  4.5 us (5%)
  local copies, waits for them, and re-layouts  2.56 us (3%)
  other arithmetic  1.79 us (2%)
    ppermute x9, starting transfers between devices, swap(): return lax.ppermute(value, axis, SWAP)  17.4 us
    ppermute x4, starting transfers between devices, pair(): return lax.ppermute(value, axis, list(enumerate(other)))  13.8 us
    ppermute x6, waiting for transfers between devices, across(): return lax.ppermute(value, (Y, X, CORE), pairs)  12.2 us
    all_to_all x1, waiting for transfers between devices, local(): gathered = lax.all_to_all(copies, (Y, X), 0, 0, tiled=True)  9.03 us
    all_to_all x1, starting transfers between devices, local(): gathered = lax.all_to_all(copies, (Y, X), 0, 0, tiled=True)  5.55 us
    ppermute x6, starting transfers between devices, from_ahead(): lax.ppermute(value, axis, [(i, (i - distance) % RING) for i in range(RING)])  5.24 us
    ppermute x4, waiting for transfers between devices, pair(): return lax.ppermute(value, axis, list(enumerate(other)))  5.08 us
    ppermute x6, starting transfers between devices, across(): return lax.ppermute(value, (Y, X, CORE), pairs)  4.83 us
  transfers between devices with their start and end apart: 29, of which 21 were waited for; matrix products, arithmetic and copies ran while one was open for 1% of the time, Pallas kernels for 1%

profile of v10, /device:TPU:1, one launch (start us, length us, event | category | flops | bytes accessed | tf_op | source)
XLA Modules:
  0.0 94.4 jit_solution(5136856043797401544)
XLA Ops:
  0.0 0.9 subtract_bitcast_fusion
  0.9 3.9 %collective-permute-start = (bf16[64,128]{1,0:T(8,128)(2,1)S(1)}, bf16[64,128]{1,0:T(8,128)(2,1)S(1)}, u32[]{:S(2)}, u32[]{:S(2)}) collective-permute-start(bf16[64,128]{1,0:T(8,128)(2,1)S(1)} %get-tuple-element.58), channel_id=1, source_target_pairs={{0,4},{4,0},{8,12},{12,8},{1,5},{5,1},{9,13},{13,9},{2,6},{6,2},{1... | collective-permute-start | bytes 49160 | tf_op jit(solution)/shard_map/ppermute | solution.py:55
  4.8 1.2 %constant_dynamic-slice_fusion = (bf16[64,2048]{1,0:T(8,128)(2,1)S(1)}, bf16[64,2048]{1,0:T(8,128)(2,1)S(1)}, bf16[64,2048]{1,0:T(8,128)(2,1)S(1)}) fusion(bf16[64,8192]{1,0:T(8,128)(2,1)} %precond.1, s32[]{:T(128)S(6)} %select_n.29, s32[]{:T(128)S(6)} %select_n.27, s32[]{:T(128)S(6)} %select_n.25), kind=kLoop, calls=%fused_computation.13 | loop fusion | bytes 1572876 | tf_op jit(solution)/shard_map/dynamic_slice | solution.py:214
  6.0 1.4 %collective-permute-start.2 = (bf16[64,2048]{1,0:T(8,128)(2,1)S(1)}, bf16[64,2048]{1,0:T(8,128)(2,1)S(1)}, u32[]{:S(2)}, u32[]{:S(2)}) collective-permute-start(bf16[64,2048]{1,0:T(8,128)(2,1)S(1)} %get-tuple-element.47), channel_id=1, source_target_pairs={{0,64},{64,128},{128,192},{192,0},{1,65},{65,129},{129,193},{193,1... | collective-permute-start | bytes 786440 | tf_op jit(solution)/shard_map/ppermute | solution.py:33
  7.4 4.3 %collective-permute-start.1 = (bf16[2,64,128]{2,1,0:T(8,128)(2,1)S(1)}, bf16[2,64,128]{2,1,0:T(8,128)(2,1)S(1)}, u32[]{:S(2)}, u32[]{:S(2)}) collective-permute-start(bf16[2,64,128]{2,1,0:T(8,128)(2,1)S(1)} %pad_maximum_fusion.1), channel_id=1, source_target_pairs={{0,12},{4,8},{8,4},{12,0},{1,13},{5,9},{9,5},{13,1},{2,14},{6,10},... | collective-permute-start | bytes 98312 | tf_op jit(solution)/shard_map/ppermute | solution.py:55
  11.6 1.4 %collective-permute-done.1 = bf16[2,64,128]{2,1,0:T(8,128)(2,1)S(1)} collective-permute-done((bf16[2,64,128]{2,1,0:T(8,128)(2,1)S(1)}, bf16[2,64,128]{2,1,0:T(8,128)(2,1)S(1)}, u32[]{:S(2)}, u32[]{:S(2)}) %collective-permute-start.1) | collective-permute-done | bytes 32800 | tf_op jit(solution)/shard_map/ppermute | solution.py:55
  13.1 1.2 %collective-permute-done.2.b1 = bf16[64,2048]{1,0:T(8,128)(2,1)S(1)} collective-permute-done((bf16[64,2048]{1,0:T(8,128)(2,1)S(1)}, bf16[64,2048]{1,0:T(8,128)(2,1)S(1)}, u32[]{:S(2)}, u32[]{:S(2)}) %collective-permute-start.2) | collective-permute-done | bytes 262176 | tf_op jit(solution)/shard_map/ppermute | solution.py:33
  14.2 1.2 %broadcast_in_dim.8 = bf16[16,4,64,128]{3,2,1,0:T(8,128)(2,1)} broadcast(bf16[4,64,128]{2,1,0:T(8,128)(2,1)S(1)} %pad_maximum_fusion), dimensions={1,2,3} | broadcast | bytes 1114112 | tf_op jit(solution)/shard_map/broadcast_in_dim | solution.py:221
  15.5 5.5 %all-to-all-start = ((bf16[16,4,64,128]{3,2,1,0:T(8,128)(2,1)}), bf16[16,4,64,128]{3,2,1,0:T(8,128)(2,1)S(1)}, u32[]{:S(2)}, u32[]{:S(2)}) async-start(bf16[16,4,64,128]{3,2,1,0:T(8,128)(2,1)} %broadcast_in_dim.8), calls=%async_computation | async-start | bytes 2097152 | tf_op jit(solution)/shard_map/all_to_all | solution.py:222
  21.1 1.7 %collective-permute-start.5 = (bf16[256,768]{1,0:T(8,128)(2,1)S(1)}, bf16[256,768]{1,0:T(8,128)(2,1)S(1)}, u32[]{:S(2)}, u32[]{:S(2)}) collective-permute-start(bf16[256,768]{1,0:T(8,128)(2,1)S(1)} %bitcast.13), channel_id=1, source_target_pairs={{0,1},{1,0},{2,3},{3,2},{4,5},{5,4},{6,7},{7,6},{8,9},{9,8},{10,11... | collective-permute-start | bytes 1179656 | tf_op jit(solution)/shard_map/ppermute | solution.py:25
  22.9 3.0 %collective-permute-start.3 = (s32[1,6]{1,0:T(1,128)S(1)}, s32[1,6]{1,0:T(1,128)S(1)}, u32[]{:S(2)}, u32[]{:S(2)}) collective-permute-start(s32[1,6]{1,0:T(1,128)S(1)} %copy-done.4), channel_id=1, source_target_pairs={{0,2},{2,0},{1,3},{3,1},{4,6},{6,4},{5,7},{7,5},{8,10},{10,8},{9,1... | collective-permute-start | bytes 80 | tf_op jit(solution)/shard_map/ppermute | solution.py:25
  26.7 9.0 %all-to-all-done = bf16[16,4,64,128]{3,2,1,0:T(8,128)(2,1)S(1)} async-done(((bf16[16,4,64,128]{3,2,1,0:T(8,128)(2,1)}), bf16[16,4,64,128]{3,2,1,0:T(8,128)(2,1)S(1)}, u32[]{:S(2)}, u32[]{:S(2)}) %all-to-all-start) | async-done | bytes 1048608 | tf_op jit(solution)/shard_map/all_to_all | solution.py:222
  35.7 0.6 shard_map.82
  36.4 3.9 %collective-permute-start.4 = (bf16[6,64,128]{2,1,0:T(8,128)(2,1)S(1)}, bf16[6,64,128]{2,1,0:T(8,128)(2,1)S(1)}, u32[]{:S(2)}, u32[]{:S(2)}) collective-permute-start(bf16[6,64,128]{2,1,0:T(8,128)(2,1)S(1)} %get-tuple-element.27), channel_id=1, source_target_pairs={{0,2},{2,0},{1,3},{3,1},{4,6},{6,4},{5,7},{7,5},{8,10},{10,8},{9,1... | collective-permute-start | bytes 294920 | tf_op jit(solution)/shard_map/ppermute | solution.py:25
  40.3 0.9 collective-permute-done.4.other_picked
  41.2 1.6 %shard_map.83 = (f32[6,64,128]{2,1,0:T(8,128)S(1)}, f32[6,64,128]{2,1,0:T(8,128)S(1)}) custom-call(s32[6]{0:T(128)S(1)} %stack.35.where, bf16[6,64,128]{2,1,0:T(8,128)(2,1)S(1)} %get-tuple-element.26.own_picked, bf16[6,64,128]{2,1,0:T(8,128)(2,1)S(1)} %collective-permute-done.4.other_picked, bf16[256,768]{1,0:T(8,128)(2,1)S(1)} %bitcast.14, ...), custom_call_target="tpu_custom_call" | custom-call | tf_op jit(solution)/shard_map/pallas_call | solution.py:230
  42.8 0.4 collective-permute-start.7
  43.2 1.1 %collective-permute-done.7.arrived = f32[6,64,128]{2,1,0:T(8,128)S(1)} collective-permute-done((f32[6,64,128]{2,1,0:T(8,128)S(1)}, f32[6,64,128]{2,1,0:T(8,128)S(1)}, u32[]{:S(2)}, u32[]{:S(2)}) %collective-permute-start.7) | collective-permute-done | bytes 196640 | tf_op jit(solution)/shard_map/ppermute | solution.py:25
  44.3 1.3 %shard_map.84 = (f32[16,64,128]{2,1,0:T(8,128)S(1)}, bf16[16,64,128]{2,1,0:T(8,128)(2,1)S(1)}, bf16[16,64,128]{2,1,0:T(8,128)(2,1)S(1)}, bf16[16,64,128]{2,1,0:T(8,128)(2,1)S(1)}) custom-call(s32[6]{0:T(128)S(1)} %stack.35.where, s32[1,6]{1,0:T(1,128)S(1)} %copy-done.4, s32[1,6]{1,0:T(1,128)S(1)} %collective-permute-done.3.other_ids, ...), custom_call_target="tpu_custom_call" | custom-call | tf_op jit(solution)/shard_map/pallas_call | solution.py:239
  45.7 2.0 %collective-permute-start.9 = (bf16[16,64,128]{2,1,0:T(8,128)(2,1)S(1)}, bf16[16,64,128]{2,1,0:T(8,128)(2,1)S(1)}, u32[]{:S(2)}, u32[]{:S(2)}) collective-permute-start(bf16[16,64,128]{2,1,0:T(8,128)(2,1)S(1)} %get-tuple-element.34), channel_id=1, source_target_pairs={{0,128},{2,34},{16,144},{18,50},{32,160},{34,2},{48,176},{50,18},{... | collective-permute-start | bytes 786440 | tf_op jit(solution)/shard_map/ppermute | solution.py:50
  47.7 3.5 %collective-permute-done.10 = bf16[16,64,128]{2,1,0:T(8,128)(2,1)S(1)} collective-permute-done((bf16[16,64,128]{2,1,0:T(8,128)(2,1)S(1)}, bf16[16,64,128]{2,1,0:T(8,128)(2,1)S(1)}, u32[]{:S(2)}, u32[]{:S(2)}) %collective-permute-start.10) | collective-permute-done | bytes 262176 | tf_op jit(solution)/shard_map/ppermute | solution.py:50
  51.2 1.6 %collective-permute-done.9 = bf16[16,64,128]{2,1,0:T(8,128)(2,1)S(1)} collective-permute-done((bf16[16,64,128]{2,1,0:T(8,128)(2,1)S(1)}, bf16[16,64,128]{2,1,0:T(8,128)(2,1)S(1)}, u32[]{:S(2)}, u32[]{:S(2)}) %collective-permute-start.9) | collective-permute-done | bytes 262176 | tf_op jit(solution)/shard_map/ppermute | solution.py:50
  52.8 2.8 %collective-permute-done.8 = bf16[16,64,128]{2,1,0:T(8,128)(2,1)S(1)} collective-permute-done((bf16[16,64,128]{2,1,0:T(8,128)(2,1)S(1)}, bf16[16,64,128]{2,1,0:T(8,128)(2,1)S(1)}, u32[]{:S(2)}, u32[]{:S(2)}) %collective-permute-start.8) | collective-permute-done | bytes 262176 | tf_op jit(solution)/shard_map/ppermute | solution.py:50
  55.8 1.7 %collective-permute-start.13 = (bf16[4,64,128]{2,1,0:T(8,128)(2,1)S(1)}, bf16[4,64,128]{2,1,0:T(8,128)(2,1)S(1)}, u32[]{:S(2)}, u32[]{:S(2)}) collective-permute-start(bf16[4,64,128]{2,1,0:T(8,128)(2,1)S(1)} %get-tuple-element.49), channel_id=1, source_target_pairs={{0,48},{2,194},{16,0},{18,210},{32,16},{34,226},{48,32},{50,242},{... | collective-permute-start | bytes 196616 | tf_op jit(solution)/shard_map/ppermute | solution.py:50
  57.4 0.6 collective-permute-start.12
  58.0 0.5 collective-permute-start.11
  58.5 0.5 collective-permute-done.13
  59.0 3.1 %collective-permute-done.12 = bf16[4,64,128]{2,1,0:T(8,128)(2,1)S(1)} collective-permute-done((bf16[4,64,128]{2,1,0:T(8,128)(2,1)S(1)}, bf16[4,64,128]{2,1,0:T(8,128)(2,1)S(1)}, u32[]{:S(2)}, u32[]{:S(2)}) %collective-permute-start.12) | collective-permute-done | bytes 65568 | tf_op jit(solution)/shard_map/ppermute | solution.py:50
  62.1 0.7 collective-permute-done.11
  62.8 1.0 %collective-permute-start.16 = (bf16[4,64,128]{2,1,0:T(8,128)(2,1)S(1)}, bf16[4,64,128]{2,1,0:T(8,128)(2,1)S(1)}, u32[]{:S(2)}, u32[]{:S(2)}) collective-permute-start(bf16[4,64,128]{2,1,0:T(8,128)(2,1)S(1)} %fusion.3), channel_id=1, source_target_pairs={{0,4},{4,0},{8,12},{12,8},{1,5},{5,1},{9,13},{13,9},{2,6},{6,2},{1... | collective-permute-start | bytes 196616 | tf_op jit(solution)/shard_map/ppermute | solution.py:55
  63.9 3.1 %collective-permute-done.16 = bf16[4,64,128]{2,1,0:T(8,128)(2,1)S(1)} collective-permute-done((bf16[4,64,128]{2,1,0:T(8,128)(2,1)S(1)}, bf16[4,64,128]{2,1,0:T(8,128)(2,1)S(1)}, u32[]{:S(2)}, u32[]{:S(2)}) %collective-permute-start.16) | collective-permute-done | bytes 65568 | tf_op jit(solution)/shard_map/ppermute | solution.py:55
  67.0 4.6 %collective-permute-start.17 = (bf16[4,64,128]{2,1,0:T(8,128)(2,1)S(1)}, bf16[4,64,128]{2,1,0:T(8,128)(2,1)S(1)}, u32[]{:S(2)}, u32[]{:S(2)}) collective-permute-start(bf16[4,64,128]{2,1,0:T(8,128)(2,1)S(1)} %fusion.4), channel_id=1, source_target_pairs={{0,12},{4,8},{8,4},{12,0},{1,13},{5,9},{9,5},{13,1},{2,14},{6,10},... | collective-permute-start | bytes 196616 | tf_op jit(solution)/shard_map/ppermute | solution.py:55
  71.5 0.8 collective-permute-start.14
  72.3 0.8 collective-permute-start.15
  73.1 0.6 collective-permute-done.17
  73.8 0.7 collective-permute-start.18
  74.5 1.1 %collective-permute-start.19 = (bf16[4,64,128]{2,1,0:T(8,128)(2,1)S(1)}, bf16[4,64,128]{2,1,0:T(8,128)(2,1)S(1)}, u32[]{:S(2)}, u32[]{:S(2)}) collective-permute-start(bf16[4,64,128]{2,1,0:T(8,128)(2,1)S(1)} %fusion.2.refs_0_), channel_id=1, source_target_pairs={{0,32},{16,48},{32,0},{48,16},{1,33},{17,49},{33,1},{49,17},{2,34}... | collective-permute-start | bytes 196616 | tf_op jit(solution)/shard_map/ppermute | solution.py:29
  75.9 1.4 %collective-permute-done.18.refs_1_ = bf16[4,64,128]{2,1,0:T(8,128)(2,1)S(1)} collective-permute-done((bf16[4,64,128]{2,1,0:T(8,128)(2,1)S(1)}, bf16[4,64,128]{2,1,0:T(8,128)(2,1)S(1)}, u32[]{:S(2)}, u32[]{:S(2)}) %collective-permute-start.18) | collective-permute-done | bytes 65568 | tf_op jit(solution)/shard_map/ppermute | solution.py:29
  77.3 5.3 %collective-permute-start.21 = (bf16[4,64,128]{2,1,0:T(8,128)(2,1)S(1)}, bf16[4,64,128]{2,1,0:T(8,128)(2,1)S(1)}, u32[]{:S(2)}, u32[]{:S(2)}) collective-permute-start(bf16[4,64,128]{2,1,0:T(8,128)(2,1)S(1)} %fusion.2.refs_0_), channel_id=1, source_target_pairs={{0,2},{2,0},{1,3},{3,1},{4,6},{6,4},{5,7},{7,5},{8,10},{10,8},{9,1... | collective-permute-start | bytes 196616 | tf_op jit(solution)/shard_map/ppermute | solution.py:25
  82.6 2.3 %collective-permute-start.22 = (bf16[4,64,128]{2,1,0:T(8,128)(2,1)S(1)}, bf16[4,64,128]{2,1,0:T(8,128)(2,1)S(1)}, u32[]{:S(2)}, u32[]{:S(2)}) collective-permute-start(bf16[4,64,128]{2,1,0:T(8,128)(2,1)S(1)} %collective-permute-done.18.refs_1_), channel_id=1, source_target_pairs={{0,2},{2,0},{1,3},{3,1},{4,6},{6,4},{5,7},{7,5},{8,10},{10,8},{9,1... | collective-permute-start | bytes 196616 | tf_op jit(solution)/shard_map/ppermute | solution.py:25
  84.9 0.7 collective-permute-start.23
  85.8 0.7 collective-permute-done.23.refs_6_
  86.8 1.0 %shard_map.85 = (f32[64,128]{1,0:T(8,128)S(1)}, f32[64,128]{1,0:T(8,128)S(1)}, f32[64,128]{1,0:T(8,128)S(1)}, f32[64,128]{1,0:T(8,128)S(1)}) custom-call(s32[6]{0:T(128)S(1)} %stack.35.where, f32[64,128]{1,0:T(8,128)S(1)} %copy-done.3, bf16[64,8192]{1,0:T(8,128)(2,1)S(1)} %copy-done, bf16[64,2048]{1,0:T(8,128)(2,1)S(1)} %collective-permute-done.2.b1, ...), custom_call_target="tpu_custom_call" | custom-call | tf_op jit(solution)/shard_map/pallas_call | solution.py:263
  88.2 2.4 %collective-permute-start.26 = (f32[64,128]{1,0:T(8,128)S(1)}, f32[64,128]{1,0:T(8,128)S(1)}, u32[]{:S(2)}, u32[]{:S(2)}) collective-permute-start(f32[64,128]{1,0:T(8,128)S(1)} %get-tuple-element.41), channel_id=1, source_target_pairs={{0,128},{64,192},{128,0},{192,64},{1,129},{65,193},{129,1},{193,65... | collective-permute-start | bytes 98312 | tf_op jit(solution)/shard_map/ppermute | solution.py:29
  91.0 0.9 collective-permute-done.27
  91.9 0.9 collective-permute-done.26
  92.8 0.9 collective-permute-done.25
  93.7 0.6 add_add_fusion
  (39 shorter events, 2.3 us)
Async XLA Ops:
  0.9 6.4 %collective-permute-start = (bf16[64,128]{1,0:T(8,128)(2,1)S(1)}, bf16[64,128]{1,0:T(8,128)(2,1)S(1)}, u32[]{:S(2)}, u32[]{:S(2)}) collective-permute-start(bf16[64,128]{1,0:T(8,128)(2,1)S(1)} %get-tuple-element.58), channel_id=1, source_target_pairs={{0,4},{4,0},{8,12},{12,8},{1,5},{5,1},{9,13},{13,9},{2,6},{6,2},{1... | collective-permute-start | bytes 49160 | tf_op jit(solution)/shard_map/ppermute | solution.py:55
  6.0 8.3 %collective-permute-start.2 = (bf16[64,2048]{1,0:T(8,128)(2,1)S(1)}, bf16[64,2048]{1,0:T(8,128)(2,1)S(1)}, u32[]{:S(2)}, u32[]{:S(2)}) collective-permute-start(bf16[64,2048]{1,0:T(8,128)(2,1)S(1)} %get-tuple-element.47), channel_id=1, source_target_pairs={{0,64},{64,128},{128,192},{192,0},{1,65},{65,129},{129,193},{193,1... | collective-permute-start | bytes 786440 | tf_op jit(solution)/shard_map/ppermute | solution.py:33
  7.4 5.7 %collective-permute-start.1 = (bf16[2,64,128]{2,1,0:T(8,128)(2,1)S(1)}, bf16[2,64,128]{2,1,0:T(8,128)(2,1)S(1)}, u32[]{:S(2)}, u32[]{:S(2)}) collective-permute-start(bf16[2,64,128]{2,1,0:T(8,128)(2,1)S(1)} %pad_maximum_fusion.1), channel_id=1, source_target_pairs={{0,12},{4,8},{8,4},{12,0},{1,13},{5,9},{9,5},{13,1},{2,14},{6,10},... | collective-permute-start | bytes 98312 | tf_op jit(solution)/shard_map/ppermute | solution.py:55
  15.5 5.6 %copy-start.1 = (bf16[1,256,768]{2,1,0:T(8,128)(2,1)S(1)}, bf16[1,256,768]{2,1,0:T(8,128)(2,1)}, u32[]{:S(2)}) copy-start(bf16[1,256,768]{2,1,0:T(8,128)(2,1)} %param.12) | copy-start | bytes 1179652
  15.5 7.3 %copy-start.2 = (bf16[1,256,512]{2,1,0:T(8,128)(2,1)S(1)}, bf16[1,256,512]{2,1,0:T(8,128)(2,1)}, u32[]{:S(2)}) copy-start(bf16[1,256,512]{2,1,0:T(8,128)(2,1)} %param.13) | copy-start | bytes 786436
  15.5 7.4 %copy-start.4 = (s32[1,6]{1,0:T(1,128)S(1)}, s32[1,6]{1,0:T(1,128)}, u32[]{:S(2)}) copy-start(s32[1,6]{1,0:T(1,128)} %own_ids.3) | copy-start | bytes 76
  15.5 20.2 %all-to-all-start = ((bf16[16,4,64,128]{3,2,1,0:T(8,128)(2,1)}), bf16[16,4,64,128]{3,2,1,0:T(8,128)(2,1)S(1)}, u32[]{:S(2)}, u32[]{:S(2)}) async-start(bf16[16,4,64,128]{3,2,1,0:T(8,128)(2,1)} %broadcast_in_dim.8), calls=%async_computation | async-start | bytes 2097152 | tf_op jit(solution)/shard_map/all_to_all | solution.py:222
  21.1 19.2 %collective-permute-start.5 = (bf16[256,768]{1,0:T(8,128)(2,1)S(1)}, bf16[256,768]{1,0:T(8,128)(2,1)S(1)}, u32[]{:S(2)}, u32[]{:S(2)}) collective-permute-start(bf16[256,768]{1,0:T(8,128)(2,1)S(1)} %bitcast.13), channel_id=1, source_target_pairs={{0,1},{1,0},{2,3},{3,2},{4,5},{5,4},{6,7},{7,6},{8,9},{9,8},{10,11... | collective-permute-start | bytes 1179656 | tf_op jit(solution)/shard_map/ppermute | solution.py:25
  22.8 17.5 %collective-permute-start.6 = (bf16[256,512]{1,0:T(8,128)(2,1)S(1)}, bf16[256,512]{1,0:T(8,128)(2,1)S(1)}, u32[]{:S(2)}, u32[]{:S(2)}) collective-permute-start(bf16[256,512]{1,0:T(8,128)(2,1)S(1)} %bitcast.15), channel_id=1, source_target_pairs={{0,1},{1,0},{2,3},{3,2},{4,5},{5,4},{6,7},{7,6},{8,9},{9,8},{10,11... | collective-permute-start | bytes 786440 | tf_op jit(solution)/shard_map/ppermute | solution.py:25
  22.9 3.8 %collective-permute-start.3 = (s32[1,6]{1,0:T(1,128)S(1)}, s32[1,6]{1,0:T(1,128)S(1)}, u32[]{:S(2)}, u32[]{:S(2)}) collective-permute-start(s32[1,6]{1,0:T(1,128)S(1)} %copy-done.4), channel_id=1, source_target_pairs={{0,2},{2,0},{1,3},{3,1},{4,6},{6,4},{5,7},{7,5},{8,10},{10,8},{9,1... | collective-permute-start | bytes 80 | tf_op jit(solution)/shard_map/ppermute | solution.py:25
  36.4 4.8 %collective-permute-start.4 = (bf16[6,64,128]{2,1,0:T(8,128)(2,1)S(1)}, bf16[6,64,128]{2,1,0:T(8,128)(2,1)S(1)}, u32[]{:S(2)}, u32[]{:S(2)}) collective-permute-start(bf16[6,64,128]{2,1,0:T(8,128)(2,1)S(1)} %get-tuple-element.27), channel_id=1, source_target_pairs={{0,2},{2,0},{1,3},{3,1},{4,6},{6,4},{5,7},{7,5},{8,10},{10,8},{9,1... | collective-permute-start | bytes 294920 | tf_op jit(solution)/shard_map/ppermute | solution.py:25
  42.8 1.5 %collective-permute-start.7 = (f32[6,64,128]{2,1,0:T(8,128)S(1)}, f32[6,64,128]{2,1,0:T(8,128)S(1)}, u32[]{:S(2)}, u32[]{:S(2)}) collective-permute-start(f32[6,64,128]{2,1,0:T(8,128)S(1)} %get-tuple-element.31), channel_id=1, source_target_pairs={{0,2},{2,0},{1,3},{3,1},{4,6},{6,4},{5,7},{7,5},{8,10},{10,8},{9,1... | collective-permute-start | bytes 589832 | tf_op jit(solution)/shard_map/ppermute | solution.py:25
  45.6 5.6 %collective-permute-start.10 = (bf16[16,64,128]{2,1,0:T(8,128)(2,1)S(1)}, bf16[16,64,128]{2,1,0:T(8,128)(2,1)S(1)}, u32[]{:S(2)}, u32[]{:S(2)}) collective-permute-start(bf16[16,64,128]{2,1,0:T(8,128)(2,1)S(1)} %get-tuple-element.35), channel_id=1, source_target_pairs={{0,192},{2,50},{16,208},{18,2},{32,224},{34,18},{48,240},{50,34},{... | collective-permute-start | bytes 786440 | tf_op jit(solution)/shard_map/ppermute | solution.py:50
  45.7 7.1 %collective-permute-start.9 = (bf16[16,64,128]{2,1,0:T(8,128)(2,1)S(1)}, bf16[16,64,128]{2,1,0:T(8,128)(2,1)S(1)}, u32[]{:S(2)}, u32[]{:S(2)}) collective-permute-start(bf16[16,64,128]{2,1,0:T(8,128)(2,1)S(1)} %get-tuple-element.34), channel_id=1, source_target_pairs={{0,128},{2,34},{16,144},{18,50},{32,160},{34,2},{48,176},{50,18},{... | collective-permute-start | bytes 786440 | tf_op jit(solution)/shard_map/ppermute | solution.py:50
  47.7 7.9 %collective-permute-start.8 = (bf16[16,64,128]{2,1,0:T(8,128)(2,1)S(1)}, bf16[16,64,128]{2,1,0:T(8,128)(2,1)S(1)}, u32[]{:S(2)}, u32[]{:S(2)}) collective-permute-start(bf16[16,64,128]{2,1,0:T(8,128)(2,1)S(1)} %get-tuple-element.33), channel_id=1, source_target_pairs={{0,64},{2,18},{16,80},{18,34},{32,96},{34,50},{48,112},{50,2},{64,... | collective-permute-start | bytes 786440 | tf_op jit(solution)/shard_map/ppermute | solution.py:50
  55.8 31.1 %copy-start = (bf16[64,8192]{1,0:T(8,128)(2,1)S(1)}, bf16[64,8192]{1,0:T(8,128)(2,1)}, u32[]{:S(2)}) copy-start(bf16[64,8192]{1,0:T(8,128)(2,1)} %precond.1) | copy-start | bytes 3145732
  55.8 3.2 %collective-permute-start.13 = (bf16[4,64,128]{2,1,0:T(8,128)(2,1)S(1)}, bf16[4,64,128]{2,1,0:T(8,128)(2,1)S(1)}, u32[]{:S(2)}, u32[]{:S(2)}) collective-permute-start(bf16[4,64,128]{2,1,0:T(8,128)(2,1)S(1)} %get-tuple-element.49), channel_id=1, source_target_pairs={{0,48},{2,194},{16,0},{18,210},{32,16},{34,226},{48,32},{50,242},{... | collective-permute-start | bytes 196616 | tf_op jit(solution)/shard_map/ppermute | solution.py:50
  57.4 4.7 %collective-permute-start.12 = (bf16[4,64,128]{2,1,0:T(8,128)(2,1)S(1)}, bf16[4,64,128]{2,1,0:T(8,128)(2,1)S(1)}, u32[]{:S(2)}, u32[]{:S(2)}) collective-permute-start(bf16[4,64,128]{2,1,0:T(8,128)(2,1)S(1)} %get-tuple-element.50), channel_id=1, source_target_pairs={{0,32},{2,130},{16,48},{18,146},{32,0},{34,162},{48,16},{50,178},{... | collective-permute-start | bytes 196616 | tf_op jit(solution)/shard_map/ppermute | solution.py:50
  58.0 4.8 %collective-permute-start.11 = (bf16[4,64,128]{2,1,0:T(8,128)(2,1)S(1)}, bf16[4,64,128]{2,1,0:T(8,128)(2,1)S(1)}, u32[]{:S(2)}, u32[]{:S(2)}) collective-permute-start(bf16[4,64,128]{2,1,0:T(8,128)(2,1)S(1)} %get-tuple-element.48), channel_id=1, source_target_pairs={{0,16},{2,66},{16,32},{18,82},{32,48},{34,98},{48,0},{50,114},{64,... | collective-permute-start | bytes 196616 | tf_op jit(solution)/shard_map/ppermute | solution.py:50
  62.8 4.1 %collective-permute-start.16 = (bf16[4,64,128]{2,1,0:T(8,128)(2,1)S(1)}, bf16[4,64,128]{2,1,0:T(8,128)(2,1)S(1)}, u32[]{:S(2)}, u32[]{:S(2)}) collective-permute-start(bf16[4,64,128]{2,1,0:T(8,128)(2,1)S(1)} %fusion.3), channel_id=1, source_target_pairs={{0,4},{4,0},{8,12},{12,8},{1,5},{5,1},{9,13},{13,9},{2,6},{6,2},{1... | collective-permute-start | bytes 196616 | tf_op jit(solution)/shard_map/ppermute | solution.py:55
  67.0 6.8 %collective-permute-start.17 = (bf16[4,64,128]{2,1,0:T(8,128)(2,1)S(1)}, bf16[4,64,128]{2,1,0:T(8,128)(2,1)S(1)}, u32[]{:S(2)}, u32[]{:S(2)}) collective-permute-start(bf16[4,64,128]{2,1,0:T(8,128)(2,1)S(1)} %fusion.4), channel_id=1, source_target_pairs={{0,12},{4,8},{8,4},{12,0},{1,13},{5,9},{9,5},{13,1},{2,14},{6,10},... | collective-permute-start | bytes 196616 | tf_op jit(solution)/shard_map/ppermute | solution.py:55
  71.5 14.0 %collective-permute-start.14 = (bf16[64,2048]{1,0:T(8,128)(2,1)S(1)}, bf16[64,2048]{1,0:T(8,128)(2,1)S(1)}, u32[]{:S(2)}, u32[]{:S(2)}) collective-permute-start(bf16[64,2048]{1,0:T(8,128)(2,1)S(1)} %get-tuple-element.36), channel_id=1, source_target_pairs={{0,128},{64,192},{128,0},{192,64},{1,129},{65,193},{129,1},{193,65... | collective-permute-start | bytes 786440 | tf_op jit(solution)/shard_map/ppermute | solution.py:33
  72.3 13.3 %collective-permute-start.15 = (bf16[64,2048]{1,0:T(8,128)(2,1)S(1)}, bf16[64,2048]{1,0:T(8,128)(2,1)S(1)}, u32[]{:S(2)}, u32[]{:S(2)}) collective-permute-start(bf16[64,2048]{1,0:T(8,128)(2,1)S(1)} %get-tuple-element.37), channel_id=1, source_target_pairs={{0,192},{64,0},{128,64},{192,128},{1,193},{65,1},{129,65},{193,129... | collective-permute-start | bytes 786440 | tf_op jit(solution)/shard_map/ppermute | solution.py:33
  73.7 13.1 %copy-start.3 = (f32[64,128]{1,0:T(8,128)S(1)}, f32[64,128]{1,0:T(8,128)}, u32[]{:S(2)}) copy-start(f32[64,128]{1,0:T(8,128)} %start.1) | copy-start | bytes 98308
  73.8 3.5 %collective-permute-start.18 = (bf16[4,64,128]{2,1,0:T(8,128)(2,1)S(1)}, bf16[4,64,128]{2,1,0:T(8,128)(2,1)S(1)}, u32[]{:S(2)}, u32[]{:S(2)}) collective-permute-start(bf16[4,64,128]{2,1,0:T(8,128)(2,1)S(1)} %fusion.2.refs_0_), channel_id=1, source_target_pairs={{0,48},{16,0},{32,16},{48,32},{1,49},{17,1},{33,17},{49,33},{2,50}... | collective-permute-start | bytes 196616 | tf_op jit(solution)/shard_map/ppermute | solution.py:29
  74.5 8.1 %collective-permute-start.19 = (bf16[4,64,128]{2,1,0:T(8,128)(2,1)S(1)}, bf16[4,64,128]{2,1,0:T(8,128)(2,1)S(1)}, u32[]{:S(2)}, u32[]{:S(2)}) collective-permute-start(bf16[4,64,128]{2,1,0:T(8,128)(2,1)S(1)} %fusion.2.refs_0_), channel_id=1, source_target_pairs={{0,32},{16,48},{32,0},{48,16},{1,33},{17,49},{33,1},{49,17},{2,34}... | collective-permute-start | bytes 196616 | tf_op jit(solution)/shard_map/ppermute | solution.py:29
  75.5 9.3 %collective-permute-start.20 = (bf16[4,64,128]{2,1,0:T(8,128)(2,1)S(1)}, bf16[4,64,128]{2,1,0:T(8,128)(2,1)S(1)}, u32[]{:S(2)}, u32[]{:S(2)}) collective-permute-start(bf16[4,64,128]{2,1,0:T(8,128)(2,1)S(1)} %fusion.2.refs_0_), channel_id=1, source_target_pairs={{0,16},{16,32},{32,48},{48,0},{1,17},{17,33},{33,49},{49,1},{2,18}... | collective-permute-start | bytes 196616 | tf_op jit(solution)/shard_map/ppermute | solution.py:29
  77.3 8.3 %collective-permute-start.21 = (bf16[4,64,128]{2,1,0:T(8,128)(2,1)S(1)}, bf16[4,64,128]{2,1,0:T(8,128)(2,1)S(1)}, u32[]{:S(2)}, u32[]{:S(2)}) collective-permute-start(bf16[4,64,128]{2,1,0:T(8,128)(2,1)S(1)} %fusion.2.refs_0_), channel_id=1, source_target_pairs={{0,2},{2,0},{1,3},{3,1},{4,6},{6,4},{5,7},{7,5},{8,10},{10,8},{9,1... | collective-permute-start | bytes 196616 | tf_op jit(solution)/shard_map/ppermute | solution.py:25
  82.6 3.2 %collective-permute-start.22 = (bf16[4,64,128]{2,1,0:T(8,128)(2,1)S(1)}, bf16[4,64,128]{2,1,0:T(8,128)(2,1)S(1)}, u32[]{:S(2)}, u32[]{:S(2)}) collective-permute-start(bf16[4,64,128]{2,1,0:T(8,128)(2,1)S(1)} %collective-permute-done.18.refs_1_), channel_id=1, source_target_pairs={{0,2},{2,0},{1,3},{3,1},{4,6},{6,4},{5,7},{7,5},{8,10},{10,8},{9,1... | collective-permute-start | bytes 196616 | tf_op jit(solution)/shard_map/ppermute | solution.py:25
  84.9 1.6 %collective-permute-start.23 = (bf16[4,64,128]{2,1,0:T(8,128)(2,1)S(1)}, bf16[4,64,128]{2,1,0:T(8,128)(2,1)S(1)}, u32[]{:S(2)}, u32[]{:S(2)}) collective-permute-start(bf16[4,64,128]{2,1,0:T(8,128)(2,1)S(1)} %collective-permute-done.19.refs_2_), channel_id=1, source_target_pairs={{0,2},{2,0},{1,3},{3,1},{4,6},{6,4},{5,7},{7,5},{8,10},{10,8},{9,1... | collective-permute-start | bytes 196616 | tf_op jit(solution)/shard_map/ppermute | solution.py:25
  85.6 1.3 %collective-permute-start.24 = (bf16[4,64,128]{2,1,0:T(8,128)(2,1)S(1)}, bf16[4,64,128]{2,1,0:T(8,128)(2,1)S(1)}, u32[]{:S(2)}, u32[]{:S(2)}) collective-permute-start(bf16[4,64,128]{2,1,0:T(8,128)(2,1)S(1)} %collective-permute-done.20.refs_3_), channel_id=1, source_target_pairs={{0,2},{2,0},{1,3},{3,1},{4,6},{6,4},{5,7},{7,5},{8,10},{10,8},{9,1... | collective-permute-start | bytes 196616 | tf_op jit(solution)/shard_map/ppermute | solution.py:25
  87.9 4.1 %collective-permute-start.27 = (f32[64,128]{1,0:T(8,128)S(1)}, f32[64,128]{1,0:T(8,128)S(1)}, u32[]{:S(2)}, u32[]{:S(2)}) collective-permute-start(f32[64,128]{1,0:T(8,128)S(1)} %get-tuple-element.42), channel_id=1, source_target_pairs={{0,64},{64,128},{128,192},{192,0},{1,65},{65,129},{129,193},{193,1... | collective-permute-start | bytes 98312 | tf_op jit(solution)/shard_map/ppermute | solution.py:29
  88.2 4.6 %collective-permute-start.26 = (f32[64,128]{1,0:T(8,128)S(1)}, f32[64,128]{1,0:T(8,128)S(1)}, u32[]{:S(2)}, u32[]{:S(2)}) collective-permute-start(f32[64,128]{1,0:T(8,128)S(1)} %get-tuple-element.41), channel_id=1, source_target_pairs={{0,128},{64,192},{128,0},{192,64},{1,129},{65,193},{129,1},{193,65... | collective-permute-start | bytes 98312 | tf_op jit(solution)/shard_map/ppermute | solution.py:29
  90.6 3.1 %collective-permute-start.25 = (f32[64,128]{1,0:T(8,128)S(1)}, f32[64,128]{1,0:T(8,128)S(1)}, u32[]{:S(2)}, u32[]{:S(2)}) collective-permute-start(f32[64,128]{1,0:T(8,128)S(1)} %get-tuple-element.40), channel_id=1, source_target_pairs={{0,192},{64,0},{128,64},{192,128},{1,193},{65,1},{129,65},{193,129... | collective-permute-start | bytes 98312 | tf_op jit(solution)/shard_map/ppermute | solution.py:29

commit v11 on v10

--- a/solution.py
+++ b/solution.py
@@ -66,14 +66,23 @@
     )
 
 
-def place(tile, where):
-    return tile - tile % RING + line_slot(tile % RING, where[2])
-
-
-def pick_kernel(where, own_ids, other_ids, gathered, own_ref, other_ref):
+def spread_place(tile, where):
+    dy = (tile // 16 - where[0] + RING) % RING
+    dx = ((tile // RING) % RING - where[1] + RING) % RING
+    slot = line_slot(tile % RING, where[2])
+    first = where[3] == 0
+    return jnp.where(first, dy, dx), jnp.where(first, dx, dy) * RING + slot
+
+
+def pick_kernel(where, own_ids, other_ids, p0, p1, p2, p3, own_ref, other_ref):
     for ids, out in ((other_ids, other_ref), (own_ids, own_ref)):
         for j in range(ids.shape[1]):
-            out[j] = gathered[place(ids[0, j], where)]
+            chunk, rest = spread_place(ids[0, j], where)
+            for k, piece in enumerate((p0, p1, p2, p3)):
+
+                @pl.when(chunk == k)
+                def _():
+                    out[j] = piece[rest]
 
 
 def scenario_kernel(
@@ -118,14 +127,6 @@
     def _():
         keep_ref[...] = term[:, 1]
         send_ref[...] = term[:, 0]
-
-
-def spread_place(tile, where):
-    dy = (tile // 16 - where[0] + RING) % RING
-    dx = ((tile // RING) % RING - where[1] + RING) % RING
-    slot = line_slot(tile % RING, where[2])
-    first = where[3] == 0
-    return jnp.where(first, dy, dx), jnp.where(first, dx, dy) * RING + slot
 
 
 def scatter_kernel(where, own_ids, other_ids, keep, arrived, near, c1, c2, c3, total):
@@ -214,18 +215,20 @@
         return lax.dynamic_slice_in_dim(preconditioner, first, span, 1)
 
     block1 = to_ahead(for_ahead(1), Y, 1)
-    line, block1, border_late, inverse_late = lax.optimization_barrier((line, block1, border, inverse))
+    other_tiles = swap(column_tiles, CORE)
+    line, block1, other_tiles, border_late, inverse_late = lax.optimization_barrier(
+        (line, block1, other_tiles, border, inverse)
+    )
     border_other = swap(border_late, SIDE)
     inverse_other = swap(inverse_late, SIDE)
-    other_tiles = swap(column_tiles, CORE)
-    copies = jnp.broadcast_to(line, (RING * RING, *line.shape))
-    gathered = lax.all_to_all(copies, (Y, X), 0, 0, tiled=True)
+    plane = jnp.concatenate([line] + [across(line, -k, 1) for k in range(1, RING)])
+    gathered = [plane] + [across(plane, -k, 0) for k in range(1, RING)]
 
     own_half, for_other = call(
         pick_kernel,
-        [SMEM] * 3 + [VMEM],
+        [SMEM] * 3 + [VMEM] * 4,
         [shape((tiles, HALF, cols), BF16)] * 2,
-    )(where, column_tiles, other_tiles, gathered.reshape(everywhere, HALF, cols))
+    )(where, column_tiles, other_tiles, *gathered)
     other_half = swap(for_other, CORE)
     keep, send = call(
         scenario_kernel,

time: 94.6 us -> 94.5 us (level)
  starting transfers between devices: 49.8 us -> 55.8 us
  waiting for transfers between devices: 34.9 us -> 29.5 us
  local copies, waits for them, and re-layouts: 2.56 us -> 1.41 us
    ppermute x6 -> x12, starting transfers between devices: 4.83 us -> 17.2 us  [across(): return lax.ppermute(value, (Y, X, CORE), pairs)]
    all_to_all x1 -> x0, waiting for transfers between devices: 9.03 us -> none  [local(): gathered = lax.all_to_all(copies, (Y, X), 0, 0, tiled=True)]
    all_to_all x1 -> x0, starting transfers between devices: 5.55 us -> none  [local(): gathered = lax.all_to_all(copies, (Y, X), 0, 0, tiled=True)]
    ppermute x6 -> x12, waiting for transfers between devices: 12.2 us -> 16.1 us  [across(): return lax.ppermute(value, (Y, X, CORE), pairs)]
    ppermute x6, waiting for transfers between devices: 4.13 us -> 6.67 us  [from_ahead(): lax.ppermute(value, axis, [(i, (i - distance) % RING) for i in range(RING)])]
    ppermute x4, waiting for transfers between devices: 5.08 us -> 3.03 us  [pair(): return lax.ppermute(value, axis, list(enumerate(other)))]
    broadcast_in_dim x1 -> x0, local copies, waits for them, and re-layouts: 1.24 us -> none  [local(): copies = jnp.broadcast_to(line, (RING * RING, *line.shape))]
    ppermute x3, waiting for transfers between devices: 1.18 us -> 0.01 us  [to_ahead(): lax.ppermute(value, axis, [(i, (i + distance) % RING) for i in range(RING)])]
  transfers between devices with their start and end apart: 29 -> 34, of which waited for: 21 -> 19; matrix products, arithmetic and copies ran while one was open for 1% -> 1% of each run, Pallas kernels for 1% -> 1%
where the time goes in v11:
time: 94.5 us; the launch traced here: 94.3 us
  starting transfers between devices  55.8 us (59%)
  waiting for transfers between devices  29.5 us (31%)
  Pallas kernels  4.95 us (5%)
  other arithmetic  1.8 us (2%)
  local copies, waits for them, and re-layouts  1.41 us (1%)
    ppermute x12, starting transfers between devices, across(): return lax.ppermute(value, (Y, X, CORE), pairs)  17.2 us
    ppermute x9, starting transfers between devices, swap(): return lax.ppermute(value, axis, SWAP)  16.4 us
    ppermute x12, waiting for transfers between devices, across(): return lax.ppermute(value, (Y, X, CORE), pairs)  16.1 us
    ppermute x4, starting transfers between devices, pair(): return lax.ppermute(value, axis, list(enumerate(other)))  13.6 us
    ppermute x6, waiting for transfers between devices, from_ahead(): lax.ppermute(value, axis, [(i, (i - distance) % RING) for i in range(RING)])  6.67 us
    ppermute x6, starting transfers between devices, from_ahead(): lax.ppermute(value, axis, [(i, (i - distance) % RING) for i in range(RING)])  4.57 us
    ppermute x3, starting transfers between devices, to_ahead(): lax.ppermute(value, axis, [(i, (i + distance) % RING) for i in range(RING)])  3.97 us
    ppermute x9, waiting for transfers between devices, swap(): return lax.ppermute(value, axis, SWAP)  3.74 us
  transfers between devices with their start and end apart: 34, of which 19 were waited for; matrix products, arithmetic and copies ran while one was open for 1% of the time, Pallas kernels for 1%

profile of v11, /device:TPU:1, one launch (start us, length us, event | category | flops | bytes accessed | tf_op | source)
XLA Modules:
  0.0 94.3 jit_solution(15325698823524102672)
XLA Ops:
  0.0 0.9 subtract_bitcast_fusion
  0.9 3.9 %collective-permute-start = (bf16[64,128]{1,0:T(8,128)(2,1)S(1)}, bf16[64,128]{1,0:T(8,128)(2,1)S(1)}, u32[]{:S(2)}, u32[]{:S(2)}) collective-permute-start(bf16[64,128]{1,0:T(8,128)(2,1)S(1)} %get-tuple-element.60), channel_id=1, source_target_pairs={{0,4},{4,0},{8,12},{12,8},{1,5},{5,1},{9,13},{13,9},{2,6},{6,2},{1... | collective-permute-start | bytes 49160 | tf_op jit(solution)/shard_map/ppermute | solution.py:55
  4.8 1.2 %constant_dynamic-slice_fusion = (bf16[64,2048]{1,0:T(8,128)(2,1)S(1)}, bf16[64,2048]{1,0:T(8,128)(2,1)S(1)}, bf16[64,2048]{1,0:T(8,128)(2,1)S(1)}) fusion(bf16[64,8192]{1,0:T(8,128)(2,1)} %precond.1, s32[]{:T(128)S(6)} %select_n.29, s32[]{:T(128)S(6)} %select_n.27, s32[]{:T(128)S(6)} %select_n.25), kind=kLoop, calls=%fused_computation.17 | loop fusion | bytes 1572876 | tf_op jit(solution)/shard_map/dynamic_slice | solution.py:215
  6.0 1.4 %collective-permute-start.2 = (bf16[64,2048]{1,0:T(8,128)(2,1)S(1)}, bf16[64,2048]{1,0:T(8,128)(2,1)S(1)}, u32[]{:S(2)}, u32[]{:S(2)}) collective-permute-start(bf16[64,2048]{1,0:T(8,128)(2,1)S(1)} %get-tuple-element.49), channel_id=1, source_target_pairs={{0,64},{64,128},{128,192},{192,0},{1,65},{65,129},{129,193},{193,1... | collective-permute-start | bytes 786440 | tf_op jit(solution)/shard_map/ppermute | solution.py:33
  7.4 4.3 %collective-permute-start.1 = (bf16[2,64,128]{2,1,0:T(8,128)(2,1)S(1)}, bf16[2,64,128]{2,1,0:T(8,128)(2,1)S(1)}, u32[]{:S(2)}, u32[]{:S(2)}) collective-permute-start(bf16[2,64,128]{2,1,0:T(8,128)(2,1)S(1)} %pad_maximum_fusion.1), channel_id=1, source_target_pairs={{0,12},{4,8},{8,4},{12,0},{1,13},{5,9},{9,5},{13,1},{2,14},{6,10},... | collective-permute-start | bytes 98312 | tf_op jit(solution)/shard_map/ppermute | solution.py:55
  11.7 1.8 %collective-permute-start.3 = (s32[1,6]{1,0:T(1,128)S(1)}, s32[1,6]{1,0:T(1,128)S(1)}, u32[]{:S(2)}, u32[]{:S(2)}) collective-permute-start(s32[1,6]{1,0:T(1,128)S(1)} %copy-done.4), channel_id=1, source_target_pairs={{0,2},{2,0},{1,3},{3,1},{4,6},{6,4},{5,7},{7,5},{8,10},{10,8},{9,1... | collective-permute-start | bytes 80 | tf_op jit(solution)/shard_map/ppermute | solution.py:25
  13.5 0.8 collective-permute-done.3.other_ids
  14.3 1.3 %collective-permute-start.6 = (bf16[4,64,128]{2,1,0:T(8,128)(2,1)S(1)}, bf16[4,64,128]{2,1,0:T(8,128)(2,1)S(1)}, u32[]{:S(2)}, u32[]{:S(2)}) collective-permute-start(bf16[4,64,128]{2,1,0:T(8,128)(2,1)S(1)} %pad_maximum_fusion), channel_id=1, source_target_pairs={{0,16},{2,66},{16,32},{18,82},{32,48},{34,98},{48,0},{50,114},{64,... | collective-permute-start | bytes 196616 | tf_op jit(solution)/shard_map/ppermute | solution.py:50
  15.6 2.6 %collective-permute-start.5 = (bf16[4,64,128]{2,1,0:T(8,128)(2,1)S(1)}, bf16[4,64,128]{2,1,0:T(8,128)(2,1)S(1)}, u32[]{:S(2)}, u32[]{:S(2)}) collective-permute-start(bf16[4,64,128]{2,1,0:T(8,128)(2,1)S(1)} %pad_maximum_fusion), channel_id=1, source_target_pairs={{0,32},{2,130},{16,48},{18,146},{32,0},{34,162},{48,16},{50,178},{... | collective-permute-start | bytes 196616 | tf_op jit(solution)/shard_map/ppermute | solution.py:50
  18.2 1.1 %collective-permute-start.4 = (bf16[4,64,128]{2,1,0:T(8,128)(2,1)S(1)}, bf16[4,64,128]{2,1,0:T(8,128)(2,1)S(1)}, u32[]{:S(2)}, u32[]{:S(2)}) collective-permute-start(bf16[4,64,128]{2,1,0:T(8,128)(2,1)S(1)} %pad_maximum_fusion), channel_id=1, source_target_pairs={{0,48},{2,194},{16,0},{18,210},{32,16},{34,226},{48,32},{50,242},{... | collective-permute-start | bytes 196616 | tf_op jit(solution)/shard_map/ppermute | solution.py:50
  19.3 0.7 collective-permute-start.11
  20.1 1.3 %collective-permute-done.4 = bf16[4,64,128]{2,1,0:T(8,128)(2,1)S(1)} collective-permute-done((bf16[4,64,128]{2,1,0:T(8,128)(2,1)S(1)}, bf16[4,64,128]{2,1,0:T(8,128)(2,1)S(1)}, u32[]{:S(2)}, u32[]{:S(2)}) %collective-permute-start.4) | collective-permute-done | bytes 65568 | tf_op jit(solution)/shard_map/ppermute | solution.py:50
  21.4 1.3 %collective-permute-start.9 = (bf16[16,64,128]{2,1,0:T(8,128)(2,1)S(1)}, bf16[16,64,128]{2,1,0:T(8,128)(2,1)S(1)}, u32[]{:S(2)}, u32[]{:S(2)}) collective-permute-start(bf16[16,64,128]{2,1,0:T(8,128)(2,1)S(1)} %constant_dynamic-update-slice_fusion.p0), channel_id=1, source_target_pairs={{0,64},{2,18},{16,80},{18,34},{32,96},{34,50},{48,112},{50,2},{64,... | collective-permute-start | bytes 786440 | tf_op jit(solution)/shard_map/ppermute | solution.py:50
  22.7 2.7 %collective-permute-start.8 = (bf16[16,64,128]{2,1,0:T(8,128)(2,1)S(1)}, bf16[16,64,128]{2,1,0:T(8,128)(2,1)S(1)}, u32[]{:S(2)}, u32[]{:S(2)}) collective-permute-start(bf16[16,64,128]{2,1,0:T(8,128)(2,1)S(1)} %constant_dynamic-update-slice_fusion.p0), channel_id=1, source_target_pairs={{0,128},{2,34},{16,144},{18,50},{32,160},{34,2},{48,176},{50,18},{... | collective-permute-start | bytes 786440 | tf_op jit(solution)/shard_map/ppermute | solution.py:50
  25.5 0.9 collective-permute-start.7
  26.3 0.7 collective-permute-start.12
  28.0 4.0 %collective-permute-done.8.p2 = bf16[16,64,128]{2,1,0:T(8,128)(2,1)S(1)} collective-permute-done((bf16[16,64,128]{2,1,0:T(8,128)(2,1)S(1)}, bf16[16,64,128]{2,1,0:T(8,128)(2,1)S(1)}, u32[]{:S(2)}, u32[]{:S(2)}) %collective-permute-start.8) | collective-permute-done | bytes 262176 | tf_op jit(solution)/shard_map/ppermute | solution.py:50
  32.0 1.1 %shard_map.82 = (bf16[6,64,128]{2,1,0:T(8,128)(2,1)S(1)}, bf16[6,64,128]{2,1,0:T(8,128)(2,1)S(1)}) custom-call(s32[6]{0:T(128)S(1)} %stack.35.where, s32[1,6]{1,0:T(1,128)S(1)} %copy-done.4, s32[1,6]{1,0:T(1,128)S(1)} %collective-permute-done.3.other_ids, bf16[16,64,128]{2,1,0:T(8,128)(2,1)S(1)} %constant_dynamic-update-slice_fusion.p0, ...), custom_call_target="tpu_custom_call" | custom-call | tf_op jit(solution)/shard_map/pallas_call | solution.py:227
  33.1 4.0 %collective-permute-start.10 = (bf16[6,64,128]{2,1,0:T(8,128)(2,1)S(1)}, bf16[6,64,128]{2,1,0:T(8,128)(2,1)S(1)}, u32[]{:S(2)}, u32[]{:S(2)}) collective-permute-start(bf16[6,64,128]{2,1,0:T(8,128)(2,1)S(1)} %get-tuple-element.29), channel_id=1, source_target_pairs={{0,2},{2,0},{1,3},{3,1},{4,6},{6,4},{5,7},{7,5},{8,10},{10,8},{9,1... | collective-permute-start | bytes 294920 | tf_op jit(solution)/shard_map/ppermute | solution.py:25
  37.1 0.9 collective-permute-done.10.other_picked
  38.1 1.6 %shard_map.83 = (f32[6,64,128]{2,1,0:T(8,128)S(1)}, f32[6,64,128]{2,1,0:T(8,128)S(1)}) custom-call(s32[6]{0:T(128)S(1)} %stack.35.where, bf16[6,64,128]{2,1,0:T(8,128)(2,1)S(1)} %get-tuple-element.28.own_picked, bf16[6,64,128]{2,1,0:T(8,128)(2,1)S(1)} %collective-permute-done.10.other_picked, bf16[256,768]{1,0:T(8,128)(2,1)S(1)} %bitcast.12, ...), custom_call_target="tpu_custom_call" | custom-call | tf_op jit(solution)/shard_map/pallas_call | solution.py:233
  39.6 0.4 collective-permute-start.13
  40.1 1.1 %collective-permute-done.13.arrived = f32[6,64,128]{2,1,0:T(8,128)S(1)} collective-permute-done((f32[6,64,128]{2,1,0:T(8,128)S(1)}, f32[6,64,128]{2,1,0:T(8,128)S(1)}, u32[]{:S(2)}, u32[]{:S(2)}) %collective-permute-start.13) | collective-permute-done | bytes 196640 | tf_op jit(solution)/shard_map/ppermute | solution.py:25
  41.2 1.3 %shard_map.84 = (f32[16,64,128]{2,1,0:T(8,128)S(1)}, bf16[16,64,128]{2,1,0:T(8,128)(2,1)S(1)}, bf16[16,64,128]{2,1,0:T(8,128)(2,1)S(1)}, bf16[16,64,128]{2,1,0:T(8,128)(2,1)S(1)}) custom-call(s32[6]{0:T(128)S(1)} %stack.35.where, s32[1,6]{1,0:T(1,128)S(1)} %copy-done.4, s32[1,6]{1,0:T(1,128)S(1)} %collective-permute-done.3.other_ids, ...), custom_call_target="tpu_custom_call" | custom-call | tf_op jit(solution)/shard_map/pallas_call | solution.py:242
  42.8 3.3 %collective-permute-start.15 = (bf16[16,64,128]{2,1,0:T(8,128)(2,1)S(1)}, bf16[16,64,128]{2,1,0:T(8,128)(2,1)S(1)}, u32[]{:S(2)}, u32[]{:S(2)}) collective-permute-start(bf16[16,64,128]{2,1,0:T(8,128)(2,1)S(1)} %get-tuple-element.36), channel_id=1, source_target_pairs={{0,128},{2,34},{16,144},{18,50},{32,160},{34,2},{48,176},{50,18},{... | collective-permute-start | bytes 786440 | tf_op jit(solution)/shard_map/ppermute | solution.py:50
  46.1 3.2 %collective-permute-done.14 = bf16[16,64,128]{2,1,0:T(8,128)(2,1)S(1)} collective-permute-done((bf16[16,64,128]{2,1,0:T(8,128)(2,1)S(1)}, bf16[16,64,128]{2,1,0:T(8,128)(2,1)S(1)}, u32[]{:S(2)}, u32[]{:S(2)}) %collective-permute-start.14) | collective-permute-done | bytes 262176 | tf_op jit(solution)/shard_map/ppermute | solution.py:50
  49.3 3.7 %collective-permute-done.15 = bf16[16,64,128]{2,1,0:T(8,128)(2,1)S(1)} collective-permute-done((bf16[16,64,128]{2,1,0:T(8,128)(2,1)S(1)}, bf16[16,64,128]{2,1,0:T(8,128)(2,1)S(1)}, u32[]{:S(2)}, u32[]{:S(2)}) %collective-permute-start.15) | collective-permute-done | bytes 262176 | tf_op jit(solution)/shard_map/ppermute | solution.py:50
  53.1 1.6 %collective-permute-start.17 = (bf16[4,64,128]{2,1,0:T(8,128)(2,1)S(1)}, bf16[4,64,128]{2,1,0:T(8,128)(2,1)S(1)}, u32[]{:S(2)}, u32[]{:S(2)}) collective-permute-start(bf16[4,64,128]{2,1,0:T(8,128)(2,1)S(1)} %get-tuple-element.50), channel_id=1, source_target_pairs={{0,16},{2,66},{16,32},{18,82},{32,48},{34,98},{48,0},{50,114},{64,... | collective-permute-start | bytes 196616 | tf_op jit(solution)/shard_map/ppermute | solution.py:50
  54.7 1.2 %collective-permute-start.19 = (bf16[4,64,128]{2,1,0:T(8,128)(2,1)S(1)}, bf16[4,64,128]{2,1,0:T(8,128)(2,1)S(1)}, u32[]{:S(2)}, u32[]{:S(2)}) collective-permute-start(bf16[4,64,128]{2,1,0:T(8,128)(2,1)S(1)} %get-tuple-element.51), channel_id=1, source_target_pairs={{0,48},{2,194},{16,0},{18,210},{32,16},{34,226},{48,32},{50,242},{... | collective-permute-start | bytes 196616 | tf_op jit(solution)/shard_map/ppermute | solution.py:50
  55.9 0.9 collective-permute-start.18
  56.8 0.7 collective-permute-done.17
  57.8 2.7 %collective-permute-done.18 = bf16[4,64,128]{2,1,0:T(8,128)(2,1)S(1)} collective-permute-done((bf16[4,64,128]{2,1,0:T(8,128)(2,1)S(1)}, bf16[4,64,128]{2,1,0:T(8,128)(2,1)S(1)}, u32[]{:S(2)}, u32[]{:S(2)}) %collective-permute-start.18) | collective-permute-done | bytes 65568 | tf_op jit(solution)/shard_map/ppermute | solution.py:50
  60.6 1.1 %collective-permute-start.22 = (bf16[4,64,128]{2,1,0:T(8,128)(2,1)S(1)}, bf16[4,64,128]{2,1,0:T(8,128)(2,1)S(1)}, u32[]{:S(2)}, u32[]{:S(2)}) collective-permute-start(bf16[4,64,128]{2,1,0:T(8,128)(2,1)S(1)} %fusion.3), channel_id=1, source_target_pairs={{0,4},{4,0},{8,12},{12,8},{1,5},{5,1},{9,13},{13,9},{2,6},{6,2},{1... | collective-permute-start | bytes 196616 | tf_op jit(solution)/shard_map/ppermute | solution.py:55
  61.7 3.0 %collective-permute-done.22 = bf16[4,64,128]{2,1,0:T(8,128)(2,1)S(1)} collective-permute-done((bf16[4,64,128]{2,1,0:T(8,128)(2,1)S(1)}, bf16[4,64,128]{2,1,0:T(8,128)(2,1)S(1)}, u32[]{:S(2)}, u32[]{:S(2)}) %collective-permute-start.22) | collective-permute-done | bytes 65568 | tf_op jit(solution)/shard_map/ppermute | solution.py:55
  64.7 4.4 %collective-permute-start.23 = (bf16[4,64,128]{2,1,0:T(8,128)(2,1)S(1)}, bf16[4,64,128]{2,1,0:T(8,128)(2,1)S(1)}, u32[]{:S(2)}, u32[]{:S(2)}) collective-permute-start(bf16[4,64,128]{2,1,0:T(8,128)(2,1)S(1)} %fusion.4), channel_id=1, source_target_pairs={{0,12},{4,8},{8,4},{12,0},{1,13},{5,9},{9,5},{13,1},{2,14},{6,10},... | collective-permute-start | bytes 196616 | tf_op jit(solution)/shard_map/ppermute | solution.py:55
  69.1 0.9 collective-permute-start.20
  70.1 1.7 %collective-permute-start.21 = (bf16[64,2048]{1,0:T(8,128)(2,1)S(1)}, bf16[64,2048]{1,0:T(8,128)(2,1)S(1)}, u32[]{:S(2)}, u32[]{:S(2)}) collective-permute-start(bf16[64,2048]{1,0:T(8,128)(2,1)S(1)} %get-tuple-element.39), channel_id=1, source_target_pairs={{0,192},{64,0},{128,64},{192,128},{1,193},{65,1},{129,65},{193,129... | collective-permute-start | bytes 786440 | tf_op jit(solution)/shard_map/ppermute | solution.py:33
  71.8 6.2 %collective-permute-start.27 = (bf16[4,64,128]{2,1,0:T(8,128)(2,1)S(1)}, bf16[4,64,128]{2,1,0:T(8,128)(2,1)S(1)}, u32[]{:S(2)}, u32[]{:S(2)}) collective-permute-start(bf16[4,64,128]{2,1,0:T(8,128)(2,1)S(1)} %fusion.2.refs_0_), channel_id=1, source_target_pairs={{0,2},{2,0},{1,3},{3,1},{4,6},{6,4},{5,7},{7,5},{8,10},{10,8},{9,1... | collective-permute-start | bytes 196616 | tf_op jit(solution)/shard_map/ppermute | solution.py:25
  78.0 2.3 %collective-permute-start.25 = (bf16[4,64,128]{2,1,0:T(8,128)(2,1)S(1)}, bf16[4,64,128]{2,1,0:T(8,128)(2,1)S(1)}, u32[]{:S(2)}, u32[]{:S(2)}) collective-permute-start(bf16[4,64,128]{2,1,0:T(8,128)(2,1)S(1)} %fusion.2.refs_0_), channel_id=1, source_target_pairs={{0,32},{16,48},{32,0},{48,16},{1,33},{17,49},{33,1},{49,17},{2,34}... | collective-permute-start | bytes 196616 | tf_op jit(solution)/shard_map/ppermute | solution.py:29
  80.7 2.5 %collective-permute-done.26.refs_3_ = bf16[4,64,128]{2,1,0:T(8,128)(2,1)S(1)} collective-permute-done((bf16[4,64,128]{2,1,0:T(8,128)(2,1)S(1)}, bf16[4,64,128]{2,1,0:T(8,128)(2,1)S(1)}, u32[]{:S(2)}, u32[]{:S(2)}) %collective-permute-start.26) | collective-permute-done | bytes 65568 | tf_op jit(solution)/shard_map/ppermute | solution.py:29
  83.2 1.9 %collective-permute-start.30 = (bf16[4,64,128]{2,1,0:T(8,128)(2,1)S(1)}, bf16[4,64,128]{2,1,0:T(8,128)(2,1)S(1)}, u32[]{:S(2)}, u32[]{:S(2)}) collective-permute-start(bf16[4,64,128]{2,1,0:T(8,128)(2,1)S(1)} %collective-permute-done.26.refs_3_), channel_id=1, source_target_pairs={{0,2},{2,0},{1,3},{3,1},{4,6},{6,4},{5,7},{7,5},{8,10},{10,8},{9,1... | collective-permute-start | bytes 196616 | tf_op jit(solution)/shard_map/ppermute | solution.py:25
  85.1 0.6 collective-permute-start.28
  86.6 1.1 %shard_map.85 = (f32[64,128]{1,0:T(8,128)S(1)}, f32[64,128]{1,0:T(8,128)S(1)}, f32[64,128]{1,0:T(8,128)S(1)}, f32[64,128]{1,0:T(8,128)S(1)}) custom-call(s32[6]{0:T(128)S(1)} %stack.35.where, f32[64,128]{1,0:T(8,128)S(1)} %copy-done.3, bf16[64,8192]{1,0:T(8,128)(2,1)S(1)} %copy-done, bf16[64,2048]{1,0:T(8,128)(2,1)S(1)} %collective-permute-done.2.b1, ...), custom_call_target="tpu_custom_call" | custom-call | tf_op jit(solution)/shard_map/pallas_call | solution.py:266
  88.0 1.2 %collective-permute-start.32 = (f32[64,128]{1,0:T(8,128)S(1)}, f32[64,128]{1,0:T(8,128)S(1)}, u32[]{:S(2)}, u32[]{:S(2)}) collective-permute-start(f32[64,128]{1,0:T(8,128)S(1)} %get-tuple-element.43), channel_id=1, source_target_pairs={{0,128},{64,192},{128,0},{192,64},{1,129},{65,193},{129,1},{193,65... | collective-permute-start | bytes 98312 | tf_op jit(solution)/shard_map/ppermute | solution.py:29
  89.5 1.0 %collective-permute-done.31 = f32[64,128]{1,0:T(8,128)S(1)} collective-permute-done((f32[64,128]{1,0:T(8,128)S(1)}, f32[64,128]{1,0:T(8,128)S(1)}, u32[]{:S(2)}, u32[]{:S(2)}) %collective-permute-start.31) | collective-permute-done | bytes 32800 | tf_op jit(solution)/shard_map/ppermute | solution.py:29
  90.5 1.8 %collective-permute-done.32 = f32[64,128]{1,0:T(8,128)S(1)} collective-permute-done((f32[64,128]{1,0:T(8,128)S(1)}, f32[64,128]{1,0:T(8,128)S(1)}, u32[]{:S(2)}, u32[]{:S(2)}) %collective-permute-start.32) | collective-permute-done | bytes 32800 | tf_op jit(solution)/shard_map/ppermute | solution.py:29
  92.3 1.4 %collective-permute-done.33 = f32[64,128]{1,0:T(8,128)S(1)} collective-permute-done((f32[64,128]{1,0:T(8,128)S(1)}, f32[64,128]{1,0:T(8,128)S(1)}, u32[]{:S(2)}, u32[]{:S(2)}) %collective-permute-start.33) | collective-permute-done | bytes 32800 | tf_op jit(solution)/shard_map/ppermute | solution.py:29
  93.7 0.6 add_add_fusion
  (52 shorter events, 3.3 us)
Async XLA Ops:
  0.9 6.5 %collective-permute-start = (bf16[64,128]{1,0:T(8,128)(2,1)S(1)}, bf16[64,128]{1,0:T(8,128)(2,1)S(1)}, u32[]{:S(2)}, u32[]{:S(2)}) collective-permute-start(bf16[64,128]{1,0:T(8,128)(2,1)S(1)} %get-tuple-element.60), channel_id=1, source_target_pairs={{0,4},{4,0},{8,12},{12,8},{1,5},{5,1},{9,13},{13,9},{2,6},{6,2},{1... | collective-permute-start | bytes 49160 | tf_op jit(solution)/shard_map/ppermute | solution.py:55
  4.8 14.5 %copy-start.1 = (bf16[1,256,768]{2,1,0:T(8,128)(2,1)S(1)}, bf16[1,256,768]{2,1,0:T(8,128)(2,1)}, u32[]{:S(2)}) copy-start(bf16[1,256,768]{2,1,0:T(8,128)(2,1)} %param.12) | copy-start | bytes 1179652
  6.0 8.3 %collective-permute-start.2 = (bf16[64,2048]{1,0:T(8,128)(2,1)S(1)}, bf16[64,2048]{1,0:T(8,128)(2,1)S(1)}, u32[]{:S(2)}, u32[]{:S(2)}) collective-permute-start(bf16[64,2048]{1,0:T(8,128)(2,1)S(1)} %get-tuple-element.49), channel_id=1, source_target_pairs={{0,64},{64,128},{128,192},{192,0},{1,65},{65,129},{129,193},{193,1... | collective-permute-start | bytes 786440 | tf_op jit(solution)/shard_map/ppermute | solution.py:33
  7.4 4.3 %copy-start.4 = (s32[1,6]{1,0:T(1,128)S(1)}, s32[1,6]{1,0:T(1,128)}, u32[]{:S(2)}) copy-start(s32[1,6]{1,0:T(1,128)} %own_ids.3) | copy-start | bytes 76
  7.4 6.1 %collective-permute-start.1 = (bf16[2,64,128]{2,1,0:T(8,128)(2,1)S(1)}, bf16[2,64,128]{2,1,0:T(8,128)(2,1)S(1)}, u32[]{:S(2)}, u32[]{:S(2)}) collective-permute-start(bf16[2,64,128]{2,1,0:T(8,128)(2,1)S(1)} %pad_maximum_fusion.1), channel_id=1, source_target_pairs={{0,12},{4,8},{8,4},{12,0},{1,13},{5,9},{9,5},{13,1},{2,14},{6,10},... | collective-permute-start | bytes 98312 | tf_op jit(solution)/shard_map/ppermute | solution.py:55
  11.7 2.6 %collective-permute-start.3 = (s32[1,6]{1,0:T(1,128)S(1)}, s32[1,6]{1,0:T(1,128)S(1)}, u32[]{:S(2)}, u32[]{:S(2)}) collective-permute-start(s32[1,6]{1,0:T(1,128)S(1)} %copy-done.4), channel_id=1, source_target_pairs={{0,2},{2,0},{1,3},{3,1},{4,6},{6,4},{5,7},{7,5},{8,10},{10,8},{9,1... | collective-permute-start | bytes 80 | tf_op jit(solution)/shard_map/ppermute | solution.py:25
  14.3 12.0 %copy-start.2 = (bf16[1,256,512]{2,1,0:T(8,128)(2,1)S(1)}, bf16[1,256,512]{2,1,0:T(8,128)(2,1)}, u32[]{:S(2)}) copy-start(bf16[1,256,512]{2,1,0:T(8,128)(2,1)} %param.13) | copy-start | bytes 786436
  14.3 7.1 %collective-permute-start.6 = (bf16[4,64,128]{2,1,0:T(8,128)(2,1)S(1)}, bf16[4,64,128]{2,1,0:T(8,128)(2,1)S(1)}, u32[]{:S(2)}, u32[]{:S(2)}) collective-permute-start(bf16[4,64,128]{2,1,0:T(8,128)(2,1)S(1)} %pad_maximum_fusion), channel_id=1, source_target_pairs={{0,16},{2,66},{16,32},{18,82},{32,48},{34,98},{48,0},{50,114},{64,... | collective-permute-start | bytes 196616 | tf_op jit(solution)/shard_map/ppermute | solution.py:50
  15.6 5.8 %collective-permute-start.5 = (bf16[4,64,128]{2,1,0:T(8,128)(2,1)S(1)}, bf16[4,64,128]{2,1,0:T(8,128)(2,1)S(1)}, u32[]{:S(2)}, u32[]{:S(2)}) collective-permute-start(bf16[4,64,128]{2,1,0:T(8,128)(2,1)S(1)} %pad_maximum_fusion), channel_id=1, source_target_pairs={{0,32},{2,130},{16,48},{18,146},{32,0},{34,162},{48,16},{50,178},{... | collective-permute-start | bytes 196616 | tf_op jit(solution)/shard_map/ppermute | solution.py:50
  18.2 3.1 %collective-permute-start.4 = (bf16[4,64,128]{2,1,0:T(8,128)(2,1)S(1)}, bf16[4,64,128]{2,1,0:T(8,128)(2,1)S(1)}, u32[]{:S(2)}, u32[]{:S(2)}) collective-permute-start(bf16[4,64,128]{2,1,0:T(8,128)(2,1)S(1)} %pad_maximum_fusion), channel_id=1, source_target_pairs={{0,48},{2,194},{16,0},{18,210},{32,16},{34,226},{48,32},{50,242},{... | collective-permute-start | bytes 196616 | tf_op jit(solution)/shard_map/ppermute | solution.py:50
  19.3 17.8 %collective-permute-start.11 = (bf16[256,768]{1,0:T(8,128)(2,1)S(1)}, bf16[256,768]{1,0:T(8,128)(2,1)S(1)}, u32[]{:S(2)}, u32[]{:S(2)}) collective-permute-start(bf16[256,768]{1,0:T(8,128)(2,1)S(1)} %bitcast.11), channel_id=1, source_target_pairs={{0,1},{1,0},{2,3},{3,2},{4,5},{5,4},{6,7},{7,6},{8,9},{9,8},{10,11... | collective-permute-start | bytes 1179656 | tf_op jit(solution)/shard_map/ppermute | solution.py:25
  21.4 6.6 %collective-permute-start.9 = (bf16[16,64,128]{2,1,0:T(8,128)(2,1)S(1)}, bf16[16,64,128]{2,1,0:T(8,128)(2,1)S(1)}, u32[]{:S(2)}, u32[]{:S(2)}) collective-permute-start(bf16[16,64,128]{2,1,0:T(8,128)(2,1)S(1)} %constant_dynamic-update-slice_fusion.p0), channel_id=1, source_target_pairs={{0,64},{2,18},{16,80},{18,34},{32,96},{34,50},{48,112},{50,2},{64,... | collective-permute-start | bytes 786440 | tf_op jit(solution)/shard_map/ppermute | solution.py:50
  22.7 9.3 %collective-permute-start.8 = (bf16[16,64,128]{2,1,0:T(8,128)(2,1)S(1)}, bf16[16,64,128]{2,1,0:T(8,128)(2,1)S(1)}, u32[]{:S(2)}, u32[]{:S(2)}) collective-permute-start(bf16[16,64,128]{2,1,0:T(8,128)(2,1)S(1)} %constant_dynamic-update-slice_fusion.p0), channel_id=1, source_target_pairs={{0,128},{2,34},{16,144},{18,50},{32,160},{34,2},{48,176},{50,18},{... | collective-permute-start | bytes 786440 | tf_op jit(solution)/shard_map/ppermute | solution.py:50
  25.5 6.6 %collective-permute-start.7 = (bf16[16,64,128]{2,1,0:T(8,128)(2,1)S(1)}, bf16[16,64,128]{2,1,0:T(8,128)(2,1)S(1)}, u32[]{:S(2)}, u32[]{:S(2)}) collective-permute-start(bf16[16,64,128]{2,1,0:T(8,128)(2,1)S(1)} %constant_dynamic-update-slice_fusion.p0), channel_id=1, source_target_pairs={{0,192},{2,50},{16,208},{18,2},{32,224},{34,18},{48,240},{50,34},{... | collective-permute-start | bytes 786440 | tf_op jit(solution)/shard_map/ppermute | solution.py:50
  26.3 10.8 %collective-permute-start.12 = (bf16[256,512]{1,0:T(8,128)(2,1)S(1)}, bf16[256,512]{1,0:T(8,128)(2,1)S(1)}, u32[]{:S(2)}, u32[]{:S(2)}) collective-permute-start(bf16[256,512]{1,0:T(8,128)(2,1)S(1)} %bitcast.13), channel_id=1, source_target_pairs={{0,1},{1,0},{2,3},{3,2},{4,5},{5,4},{6,7},{7,6},{8,9},{9,8},{10,11... | collective-permute-start | bytes 786440 | tf_op jit(solution)/shard_map/ppermute | solution.py:25
  33.1 5.0 %collective-permute-start.10 = (bf16[6,64,128]{2,1,0:T(8,128)(2,1)S(1)}, bf16[6,64,128]{2,1,0:T(8,128)(2,1)S(1)}, u32[]{:S(2)}, u32[]{:S(2)}) collective-permute-start(bf16[6,64,128]{2,1,0:T(8,128)(2,1)S(1)} %get-tuple-element.29), channel_id=1, source_target_pairs={{0,2},{2,0},{1,3},{3,1},{4,6},{6,4},{5,7},{7,5},{8,10},{10,8},{9,1... | collective-permute-start | bytes 294920 | tf_op jit(solution)/shard_map/ppermute | solution.py:25
  39.6 1.5 %collective-permute-start.13 = (f32[6,64,128]{2,1,0:T(8,128)S(1)}, f32[6,64,128]{2,1,0:T(8,128)S(1)}, u32[]{:S(2)}, u32[]{:S(2)}) collective-permute-start(f32[6,64,128]{2,1,0:T(8,128)S(1)} %get-tuple-element.33), channel_id=1, source_target_pairs={{0,2},{2,0},{1,3},{3,1},{4,6},{6,4},{5,7},{7,5},{8,10},{10,8},{9,1... | collective-permute-start | bytes 589832 | tf_op jit(solution)/shard_map/ppermute | solution.py:25
  42.5 6.8 %collective-permute-start.14 = (bf16[16,64,128]{2,1,0:T(8,128)(2,1)S(1)}, bf16[16,64,128]{2,1,0:T(8,128)(2,1)S(1)}, u32[]{:S(2)}, u32[]{:S(2)}) collective-permute-start(bf16[16,64,128]{2,1,0:T(8,128)(2,1)S(1)} %get-tuple-element.35), channel_id=1, source_target_pairs={{0,64},{2,18},{16,80},{18,34},{32,96},{34,50},{48,112},{50,2},{64,... | collective-permute-start | bytes 786440 | tf_op jit(solution)/shard_map/ppermute | solution.py:50
  42.8 10.1 %collective-permute-start.15 = (bf16[16,64,128]{2,1,0:T(8,128)(2,1)S(1)}, bf16[16,64,128]{2,1,0:T(8,128)(2,1)S(1)}, u32[]{:S(2)}, u32[]{:S(2)}) collective-permute-start(bf16[16,64,128]{2,1,0:T(8,128)(2,1)S(1)} %get-tuple-element.36), channel_id=1, source_target_pairs={{0,128},{2,34},{16,144},{18,50},{32,160},{34,2},{48,176},{50,18},{... | collective-permute-start | bytes 786440 | tf_op jit(solution)/shard_map/ppermute | solution.py:50
  46.1 6.9 %collective-permute-start.16 = (bf16[16,64,128]{2,1,0:T(8,128)(2,1)S(1)}, bf16[16,64,128]{2,1,0:T(8,128)(2,1)S(1)}, u32[]{:S(2)}, u32[]{:S(2)}) collective-permute-start(bf16[16,64,128]{2,1,0:T(8,128)(2,1)S(1)} %get-tuple-element.37), channel_id=1, source_target_pairs={{0,192},{2,50},{16,208},{18,2},{32,224},{34,18},{48,240},{50,34},{... | collective-permute-start | bytes 786440 | tf_op jit(solution)/shard_map/ppermute | solution.py:50
  53.1 33.5 %copy-start = (bf16[64,8192]{1,0:T(8,128)(2,1)S(1)}, bf16[64,8192]{1,0:T(8,128)(2,1)}, u32[]{:S(2)}) copy-start(bf16[64,8192]{1,0:T(8,128)(2,1)} %precond.1) | copy-start | bytes 3145732
  53.1 4.4 %collective-permute-start.17 = (bf16[4,64,128]{2,1,0:T(8,128)(2,1)S(1)}, bf16[4,64,128]{2,1,0:T(8,128)(2,1)S(1)}, u32[]{:S(2)}, u32[]{:S(2)}) collective-permute-start(bf16[4,64,128]{2,1,0:T(8,128)(2,1)S(1)} %get-tuple-element.50), channel_id=1, source_target_pairs={{0,16},{2,66},{16,32},{18,82},{32,48},{34,98},{48,0},{50,114},{64,... | collective-permute-start | bytes 196616 | tf_op jit(solution)/shard_map/ppermute | solution.py:50
  54.7 3.1 %collective-permute-start.19 = (bf16[4,64,128]{2,1,0:T(8,128)(2,1)S(1)}, bf16[4,64,128]{2,1,0:T(8,128)(2,1)S(1)}, u32[]{:S(2)}, u32[]{:S(2)}) collective-permute-start(bf16[4,64,128]{2,1,0:T(8,128)(2,1)S(1)} %get-tuple-element.51), channel_id=1, source_target_pairs={{0,48},{2,194},{16,0},{18,210},{32,16},{34,226},{48,32},{50,242},{... | collective-permute-start | bytes 196616 | tf_op jit(solution)/shard_map/ppermute | solution.py:50
  55.9 4.6 %collective-permute-start.18 = (bf16[4,64,128]{2,1,0:T(8,128)(2,1)S(1)}, bf16[4,64,128]{2,1,0:T(8,128)(2,1)S(1)}, u32[]{:S(2)}, u32[]{:S(2)}) collective-permute-start(bf16[4,64,128]{2,1,0:T(8,128)(2,1)S(1)} %get-tuple-element.52), channel_id=1, source_target_pairs={{0,32},{2,130},{16,48},{18,146},{32,0},{34,162},{48,16},{50,178},{... | collective-permute-start | bytes 196616 | tf_op jit(solution)/shard_map/ppermute | solution.py:50
  60.6 4.1 %collective-permute-start.22 = (bf16[4,64,128]{2,1,0:T(8,128)(2,1)S(1)}, bf16[4,64,128]{2,1,0:T(8,128)(2,1)S(1)}, u32[]{:S(2)}, u32[]{:S(2)}) collective-permute-start(bf16[4,64,128]{2,1,0:T(8,128)(2,1)S(1)} %fusion.3), channel_id=1, source_target_pairs={{0,4},{4,0},{8,12},{12,8},{1,5},{5,1},{9,13},{13,9},{2,6},{6,2},{1... | collective-permute-start | bytes 196616 | tf_op jit(solution)/shard_map/ppermute | solution.py:55
  64.7 7.0 %collective-permute-start.23 = (bf16[4,64,128]{2,1,0:T(8,128)(2,1)S(1)}, bf16[4,64,128]{2,1,0:T(8,128)(2,1)S(1)}, u32[]{:S(2)}, u32[]{:S(2)}) collective-permute-start(bf16[4,64,128]{2,1,0:T(8,128)(2,1)S(1)} %fusion.4), channel_id=1, source_target_pairs={{0,12},{4,8},{8,4},{12,0},{1,13},{5,9},{9,5},{13,1},{2,14},{6,10},... | collective-permute-start | bytes 196616 | tf_op jit(solution)/shard_map/ppermute | solution.py:55
  69.1 16.6 %collective-permute-start.20 = (bf16[64,2048]{1,0:T(8,128)(2,1)S(1)}, bf16[64,2048]{1,0:T(8,128)(2,1)S(1)}, u32[]{:S(2)}, u32[]{:S(2)}) collective-permute-start(bf16[64,2048]{1,0:T(8,128)(2,1)S(1)} %get-tuple-element.38), channel_id=1, source_target_pairs={{0,128},{64,192},{128,0},{192,64},{1,129},{65,193},{129,1},{193,65... | collective-permute-start | bytes 786440 | tf_op jit(solution)/shard_map/ppermute | solution.py:33
  70.1 15.6 %collective-permute-start.21 = (bf16[64,2048]{1,0:T(8,128)(2,1)S(1)}, bf16[64,2048]{1,0:T(8,128)(2,1)S(1)}, u32[]{:S(2)}, u32[]{:S(2)}) collective-permute-start(bf16[64,2048]{1,0:T(8,128)(2,1)S(1)} %get-tuple-element.39), channel_id=1, source_target_pairs={{0,192},{64,0},{128,64},{192,128},{1,193},{65,1},{129,65},{193,129... | collective-permute-start | bytes 786440 | tf_op jit(solution)/shard_map/ppermute | solution.py:33
  71.7 14.9 %copy-start.3 = (f32[64,128]{1,0:T(8,128)S(1)}, f32[64,128]{1,0:T(8,128)}, u32[]{:S(2)}) copy-start(f32[64,128]{1,0:T(8,128)} %start.1) | copy-start | bytes 98308
  71.8 8.5 %collective-permute-start.27 = (bf16[4,64,128]{2,1,0:T(8,128)(2,1)S(1)}, bf16[4,64,128]{2,1,0:T(8,128)(2,1)S(1)}, u32[]{:S(2)}, u32[]{:S(2)}) collective-permute-start(bf16[4,64,128]{2,1,0:T(8,128)(2,1)S(1)} %fusion.2.refs_0_), channel_id=1, source_target_pairs={{0,2},{2,0},{1,3},{3,1},{4,6},{6,4},{5,7},{7,5},{8,10},{10,8},{9,1... | collective-permute-start | bytes 196616 | tf_op jit(solution)/shard_map/ppermute | solution.py:25
  78.0 5.2 %collective-permute-start.26 = (bf16[4,64,128]{2,1,0:T(8,128)(2,1)S(1)}, bf16[4,64,128]{2,1,0:T(8,128)(2,1)S(1)}, u32[]{:S(2)}, u32[]{:S(2)}) collective-permute-start(bf16[4,64,128]{2,1,0:T(8,128)(2,1)S(1)} %fusion.2.refs_0_), channel_id=1, source_target_pairs={{0,16},{16,32},{32,48},{48,0},{1,17},{17,33},{33,49},{49,1},{2,18}... | collective-permute-start | bytes 196616 | tf_op jit(solution)/shard_map/ppermute | solution.py:29
  78.0 7.1 %collective-permute-start.25 = (bf16[4,64,128]{2,1,0:T(8,128)(2,1)S(1)}, bf16[4,64,128]{2,1,0:T(8,128)(2,1)S(1)}, u32[]{:S(2)}, u32[]{:S(2)}) collective-permute-start(bf16[4,64,128]{2,1,0:T(8,128)(2,1)S(1)} %fusion.2.refs_0_), channel_id=1, source_target_pairs={{0,32},{16,48},{32,0},{48,16},{1,33},{17,49},{33,1},{49,17},{2,34}... | collective-permute-start | bytes 196616 | tf_op jit(solution)/shard_map/ppermute | solution.py:29
  80.3 4.8 %collective-permute-start.24 = (bf16[4,64,128]{2,1,0:T(8,128)(2,1)S(1)}, bf16[4,64,128]{2,1,0:T(8,128)(2,1)S(1)}, u32[]{:S(2)}, u32[]{:S(2)}) collective-permute-start(bf16[4,64,128]{2,1,0:T(8,128)(2,1)S(1)} %fusion.2.refs_0_), channel_id=1, source_target_pairs={{0,48},{16,0},{32,16},{48,32},{1,49},{17,1},{33,17},{49,33},{2,50}... | collective-permute-start | bytes 196616 | tf_op jit(solution)/shard_map/ppermute | solution.py:29
  83.2 2.8 %collective-permute-start.30 = (bf16[4,64,128]{2,1,0:T(8,128)(2,1)S(1)}, bf16[4,64,128]{2,1,0:T(8,128)(2,1)S(1)}, u32[]{:S(2)}, u32[]{:S(2)}) collective-permute-start(bf16[4,64,128]{2,1,0:T(8,128)(2,1)S(1)} %collective-permute-done.26.refs_3_), channel_id=1, source_target_pairs={{0,2},{2,0},{1,3},{3,1},{4,6},{6,4},{5,7},{7,5},{8,10},{10,8},{9,1... | collective-permute-start | bytes 196616 | tf_op jit(solution)/shard_map/ppermute | solution.py:25
  85.1 1.3 %collective-permute-start.29 = (bf16[4,64,128]{2,1,0:T(8,128)(2,1)S(1)}, bf16[4,64,128]{2,1,0:T(8,128)(2,1)S(1)}, u32[]{:S(2)}, u32[]{:S(2)}) collective-permute-start(bf16[4,64,128]{2,1,0:T(8,128)(2,1)S(1)} %collective-permute-done.25.refs_2_), channel_id=1, source_target_pairs={{0,2},{2,0},{1,3},{3,1},{4,6},{6,4},{5,7},{7,5},{8,10},{10,8},{9,1... | collective-permute-start | bytes 196616 | tf_op jit(solution)/shard_map/ppermute | solution.py:25
  85.1 1.5 %collective-permute-start.28 = (bf16[4,64,128]{2,1,0:T(8,128)(2,1)S(1)}, bf16[4,64,128]{2,1,0:T(8,128)(2,1)S(1)}, u32[]{:S(2)}, u32[]{:S(2)}) collective-permute-start(bf16[4,64,128]{2,1,0:T(8,128)(2,1)S(1)} %collective-permute-done.24.refs_1_), channel_id=1, source_target_pairs={{0,2},{2,0},{1,3},{3,1},{4,6},{6,4},{5,7},{7,5},{8,10},{10,8},{9,1... | collective-permute-start | bytes 196616 | tf_op jit(solution)/shard_map/ppermute | solution.py:25
  87.7 2.8 %collective-permute-start.31 = (f32[64,128]{1,0:T(8,128)S(1)}, f32[64,128]{1,0:T(8,128)S(1)}, u32[]{:S(2)}, u32[]{:S(2)}) collective-permute-start(f32[64,128]{1,0:T(8,128)S(1)} %get-tuple-element.42), channel_id=1, source_target_pairs={{0,192},{64,0},{128,64},{192,128},{1,193},{65,1},{129,65},{193,129... | collective-permute-start | bytes 98312 | tf_op jit(solution)/shard_map/ppermute | solution.py:29
  88.0 4.3 %collective-permute-start.32 = (f32[64,128]{1,0:T(8,128)S(1)}, f32[64,128]{1,0:T(8,128)S(1)}, u32[]{:S(2)}, u32[]{:S(2)}) collective-permute-start(f32[64,128]{1,0:T(8,128)S(1)} %get-tuple-element.43), channel_id=1, source_target_pairs={{0,128},{64,192},{128,0},{192,64},{1,129},{65,193},{129,1},{193,65... | collective-permute-start | bytes 98312 | tf_op jit(solution)/shard_map/ppermute | solution.py:29
  89.2 4.5 %collective-permute-start.33 = (f32[64,128]{1,0:T(8,128)S(1)}, f32[64,128]{1,0:T(8,128)S(1)}, u32[]{:S(2)}, u32[]{:S(2)}) collective-permute-start(f32[64,128]{1,0:T(8,128)S(1)} %get-tuple-element.44), channel_id=1, source_target_pairs={{0,64},{64,128},{128,192},{192,0},{1,65},{65,129},{129,193},{193,1... | collective-permute-start | bytes 98312 | tf_op jit(solution)/shard_map/ppermute | solution.py:29

commit v12 on v11

--- a/solution.py
+++ b/solution.py
@@ -78,11 +78,10 @@
     for ids, out in ((other_ids, other_ref), (own_ids, own_ref)):
         for j in range(ids.shape[1]):
             chunk, rest = spread_place(ids[0, j], where)
-            for k, piece in enumerate((p0, p1, p2, p3)):
-
-                @pl.when(chunk == k)
-                def _():
-                    out[j] = piece[rest]
+            value = p0[rest]
+            for k, piece in enumerate((p1, p2, p3)):
+                value = jnp.where(chunk == k + 1, piece[rest], value)
+            out[j] = value
 
 
 def scenario_kernel(
@@ -114,9 +113,9 @@
     solved_own = masked(jnp.dot(inverse_own[...], operand, preferred_element_type=F32), own_start)
     solved_other = masked(jnp.dot(inverse_other[...], operand, preferred_element_type=F32), other_start)
     numbers = (((0,), (0,)), ((), ()))
-    term = lax.dot_general(border_own[...], solved_own, numbers, preferred_element_type=F32)
-    term += lax.dot_general(border_other[...], solved_other, numbers, preferred_element_type=F32)
-    term = term.reshape(tiles, 2, HALF, term.shape[1])
+    turned = lax.dot_general(solved_own, border_own[...], numbers, preferred_element_type=F32)
+    turned += lax.dot_general(solved_other, border_other[...], numbers, preferred_element_type=F32)
+    term = turned.T.reshape(tiles, 2, HALF, turned.shape[0])
 
     @pl.when(core == 0)
     def _():
@@ -136,24 +135,19 @@
             chunk, rest = spread_place(ids[0, j], where)
             spots.append((chunk, rest, chunk * 16 + rest))
     half = len(spots) // 2
-    near_rows = near.shape[0]
-    total[0:near_rows] = jnp.zeros_like(near)
-    chunks = (c1, c2, c3)
-    for chunk in chunks:
-        chunk[...] = jnp.zeros_like(chunk)
+    outs = (near, c1, c2, c3)
+    for out in outs:
+        out[...] = jnp.zeros_like(out)
     for _, _, spot in spots[half:]:
         total[spot] = jnp.zeros_like(total[spot])
     for j, (_, _, spot) in enumerate(spots[:half]):
         total[spot] = keep[j]
     for j, (_, _, spot) in enumerate(spots[half:]):
         total[spot] += arrived[j]
-    near[...] = total[0:near_rows]
     for chunk, rest, spot in spots:
-        for k, out in enumerate(chunks):
-
-            @pl.when(chunk == k + 1)
-            def _():
-                out[rest] = total[spot].astype(BF16)
+        value = total[spot]
+        for k, out in enumerate(outs):
+            out[rest] = jnp.where(chunk == k, value.astype(out.dtype), out[rest])
 
 
 def update_kernel(where, start, precond, b1, b2, b3, *refs):
@@ -216,8 +210,8 @@
 
     block1 = to_ahead(for_ahead(1), Y, 1)
     other_tiles = swap(column_tiles, CORE)
-    line, block1, other_tiles, border_late, inverse_late = lax.optimization_barrier(
-        (line, block1, other_tiles, border, inverse)
+    line, block1, other_tiles, border_late, inverse_late, right_side = lax.optimization_barrier(
+        (line, block1, other_tiles, border, inverse, right_side)
     )
     border_other = swap(border_late, SIDE)
     inverse_other = swap(inverse_late, SIDE)
@@ -262,6 +256,7 @@
     line = line + jnp.concatenate([met[2:], met[:2]])
 
     mine = ring_pieces(line.astype(BF16), X)
+    mine[0], mine[1] = lax.optimization_barrier((mine[0], mine[1]))
     partners = [swap(piece, CORE) for piece in mine]
     parts = call(
         update_kernel,

time: 94.5 us -> 93 us (0.984)
  starting transfers between devices: 55.8 us -> 50 us
  waiting for transfers between devices: 29.5 us -> 34.3 us
    ppermute x12, waiting for transfers between devices: 16.1 us -> 22.9 us  [across(): return lax.ppermute(value, (Y, X, CORE), pairs)]
    ppermute x12, starting transfers between devices: 17.2 us -> 11 us  [across(): return lax.ppermute(value, (Y, X, CORE), pairs)]
    ppermute x6, waiting for transfers between devices: 6.67 us -> 4.42 us  [from_ahead(): lax.ppermute(value, axis, [(i, (i - distance) % RING) for i in range(RING)])]
  transfers between devices with their start and end apart: 34 -> 34, of which waited for: 19 -> 22; matrix products, arithmetic and copies ran while one was open for 1% -> 2% of each run, Pallas kernels for 1% -> 1%
where the time goes in v12:
time: 93 us; the launch traced here: 92.8 us
  starting transfers between devices  50 us (54%)
  waiting for transfers between devices  34.3 us (37%)
  Pallas kernels  4.62 us (5%)
  other arithmetic  1.73 us (2%)
  local copies, waits for them, and re-layouts  1.42 us (2%)
    ppermute x12, waiting for transfers between devices, across(): return lax.ppermute(value, (Y, X, CORE), pairs)  22.9 us
    ppermute x9, starting transfers between devices, swap(): return lax.ppermute(value, axis, SWAP)  16.4 us
    ppermute x4, starting transfers between devices, pair(): return lax.ppermute(value, axis, list(enumerate(other)))  13.4 us
    ppermute x12, starting transfers between devices, across(): return lax.ppermute(value, (Y, X, CORE), pairs)  11 us
    ppermute x6, starting transfers between devices, from_ahead(): lax.ppermute(value, axis, [(i, (i - distance) % RING) for i in range(RING)])  4.65 us
    ppermute x3, starting transfers between devices, to_ahead(): lax.ppermute(value, axis, [(i, (i + distance) % RING) for i in range(RING)])  4.5 us
    ppermute x6, waiting for transfers between devices, from_ahead(): lax.ppermute(value, axis, [(i, (i - distance) % RING) for i in range(RING)])  4.42 us
    ppermute x9, waiting for transfers between devices, swap(): return lax.ppermute(value, axis, SWAP)  4.09 us
  transfers between devices with their start and end apart: 34, of which 22 were waited for; matrix products, arithmetic and copies ran while one was open for 2% of the time, Pallas kernels for 1%

profile of v12, /device:TPU:1, one launch (start us, length us, event | category | flops | bytes accessed | tf_op | source)
XLA Modules:
  0.0 92.8 jit_solution(17132014527791434009)
XLA Ops:
  0.0 0.8 convert_element_type.39
  0.8 3.8 %collective-permute-start = (bf16[64,128]{1,0:T(8,128)(2,1)S(1)}, bf16[64,128]{1,0:T(8,128)(2,1)S(1)}, u32[]{:S(2)}, u32[]{:S(2)}) collective-permute-start(bf16[64,128]{1,0:T(8,128)(2,1)S(1)} %convert_element_type.39), channel_id=1, source_target_pairs={{0,4},{4,0},{8,12},{12,8},{1,5},{5,1},{9,13},{13,9},{2,6},{6,2},{1... | collective-permute-start | bytes 49160 | tf_op jit(solution)/shard_map/ppermute | solution.py:55
  4.6 1.2 %constant_dynamic-slice_fusion = (bf16[64,2048]{1,0:T(8,128)(2,1)S(1)}, bf16[64,2048]{1,0:T(8,128)(2,1)S(1)}, bf16[64,2048]{1,0:T(8,128)(2,1)S(1)}) fusion(bf16[64,8192]{1,0:T(8,128)(2,1)} %precond.1, s32[]{:T(128)S(6)} %select_n.29, s32[]{:T(128)S(6)} %select_n.27, s32[]{:T(128)S(6)} %select_n.25), kind=kLoop, calls=%fused_computation.17 | loop fusion | bytes 1572876 | tf_op jit(solution)/shard_map/dynamic_slice | solution.py:209
  5.8 1.4 %collective-permute-start.2 = (bf16[64,2048]{1,0:T(8,128)(2,1)S(1)}, bf16[64,2048]{1,0:T(8,128)(2,1)S(1)}, u32[]{:S(2)}, u32[]{:S(2)}) collective-permute-start(bf16[64,2048]{1,0:T(8,128)(2,1)S(1)} %get-tuple-element.55), channel_id=1, source_target_pairs={{0,64},{64,128},{128,192},{192,0},{1,65},{65,129},{129,193},{193,1... | collective-permute-start | bytes 786440 | tf_op jit(solution)/shard_map/ppermute | solution.py:33
  7.2 4.3 %collective-permute-start.1 = (bf16[2,64,128]{2,1,0:T(8,128)(2,1)S(1)}, bf16[2,64,128]{2,1,0:T(8,128)(2,1)S(1)}, u32[]{:S(2)}, u32[]{:S(2)}) collective-permute-start(bf16[2,64,128]{2,1,0:T(8,128)(2,1)S(1)} %pad_maximum_fusion.1), channel_id=1, source_target_pairs={{0,12},{4,8},{8,4},{12,0},{1,13},{5,9},{9,5},{13,1},{2,14},{6,10},... | collective-permute-start | bytes 98312 | tf_op jit(solution)/shard_map/ppermute | solution.py:55
  11.5 1.8 %collective-permute-start.3 = (s32[1,6]{1,0:T(1,128)S(1)}, s32[1,6]{1,0:T(1,128)S(1)}, u32[]{:S(2)}, u32[]{:S(2)}) collective-permute-start(s32[1,6]{1,0:T(1,128)S(1)} %copy-done.4), channel_id=1, source_target_pairs={{0,2},{2,0},{1,3},{3,1},{4,6},{6,4},{5,7},{7,5},{8,10},{10,8},{9,1... | collective-permute-start | bytes 80 | tf_op jit(solution)/shard_map/ppermute | solution.py:25
  13.3 0.8 collective-permute-done.3.other_ids
  14.1 2.7 %collective-permute-start.4 = (bf16[4,64,128]{2,1,0:T(8,128)(2,1)S(1)}, bf16[4,64,128]{2,1,0:T(8,128)(2,1)S(1)}, u32[]{:S(2)}, u32[]{:S(2)}) collective-permute-start(bf16[4,64,128]{2,1,0:T(8,128)(2,1)S(1)} %pad_maximum_fusion), channel_id=1, source_target_pairs={{0,48},{2,194},{16,0},{18,210},{32,16},{34,226},{48,32},{50,242},{... | collective-permute-start | bytes 196616 | tf_op jit(solution)/shard_map/ppermute | solution.py:50
  17.2 0.7 collective-permute-start.6
  17.9 0.7 collective-permute-start.11
  18.7 2.9 %collective-permute-done.5 = bf16[4,64,128]{2,1,0:T(8,128)(2,1)S(1)} collective-permute-done((bf16[4,64,128]{2,1,0:T(8,128)(2,1)S(1)}, bf16[4,64,128]{2,1,0:T(8,128)(2,1)S(1)}, u32[]{:S(2)}, u32[]{:S(2)}) %collective-permute-start.5) | collective-permute-done | bytes 65568 | tf_op jit(solution)/shard_map/ppermute | solution.py:50
  21.6 0.6 collective-permute-done.6
  22.2 2.6 %collective-permute-start.7 = (bf16[16,64,128]{2,1,0:T(8,128)(2,1)S(1)}, bf16[16,64,128]{2,1,0:T(8,128)(2,1)S(1)}, u32[]{:S(2)}, u32[]{:S(2)}) collective-permute-start(bf16[16,64,128]{2,1,0:T(8,128)(2,1)S(1)} %constant_dynamic-update-slice_fusion.p0), channel_id=1, source_target_pairs={{0,192},{2,50},{16,208},{18,2},{32,224},{34,18},{48,240},{50,34},{... | collective-permute-start | bytes 786440 | tf_op jit(solution)/shard_map/ppermute | solution.py:50
  25.3 0.6 collective-permute-start.9
  25.9 0.9 collective-permute-start.12
  27.5 3.4 %collective-permute-done.7.p1 = bf16[16,64,128]{2,1,0:T(8,128)(2,1)S(1)} collective-permute-done((bf16[16,64,128]{2,1,0:T(8,128)(2,1)S(1)}, bf16[16,64,128]{2,1,0:T(8,128)(2,1)S(1)}, u32[]{:S(2)}, u32[]{:S(2)}) %collective-permute-start.7) | collective-permute-done | bytes 262176 | tf_op jit(solution)/shard_map/ppermute | solution.py:50
  30.9 0.7 collective-permute-done.8.p2
  31.6 3.0 %collective-permute-done.9.p3 = bf16[16,64,128]{2,1,0:T(8,128)(2,1)S(1)} collective-permute-done((bf16[16,64,128]{2,1,0:T(8,128)(2,1)S(1)}, bf16[16,64,128]{2,1,0:T(8,128)(2,1)S(1)}, u32[]{:S(2)}, u32[]{:S(2)}) %collective-permute-start.9) | collective-permute-done | bytes 262176 | tf_op jit(solution)/shard_map/ppermute | solution.py:50
  34.6 0.9 shard_map.82
  35.5 3.8 %collective-permute-start.10 = (bf16[6,64,128]{2,1,0:T(8,128)(2,1)S(1)}, bf16[6,64,128]{2,1,0:T(8,128)(2,1)S(1)}, u32[]{:S(2)}, u32[]{:S(2)}) collective-permute-start(bf16[6,64,128]{2,1,0:T(8,128)(2,1)S(1)} %get-tuple-element.32), channel_id=1, source_target_pairs={{0,2},{2,0},{1,3},{3,1},{4,6},{6,4},{5,7},{7,5},{8,10},{10,8},{9,1... | collective-permute-start | bytes 294920 | tf_op jit(solution)/shard_map/ppermute | solution.py:25
  39.3 0.9 %collective-permute-done.10.other_picked = bf16[6,64,128]{2,1,0:T(8,128)(2,1)S(1)} collective-permute-done((bf16[6,64,128]{2,1,0:T(8,128)(2,1)S(1)}, bf16[6,64,128]{2,1,0:T(8,128)(2,1)S(1)}, u32[]{:S(2)}, u32[]{:S(2)}) %collective-permute-start.10) | collective-permute-done | bytes 98336 | tf_op jit(solution)/shard_map/ppermute | solution.py:25
  40.3 1.6 %shard_map.83 = (f32[6,64,128]{2,1,0:T(8,128)S(1)}, f32[6,64,128]{2,1,0:T(8,128)S(1)}) custom-call(s32[6]{0:T(128)S(1)} %stack.35.where, bf16[6,64,128]{2,1,0:T(8,128)(2,1)S(1)} %get-tuple-element.31.own_picked, bf16[6,64,128]{2,1,0:T(8,128)(2,1)S(1)} %collective-permute-done.10.other_picked, bf16[256,768]{1,0:T(8,128)(2,1)S(1)} %bitcast.13, ...), custom_call_target="tpu_custom_call" | custom-call | tf_op jit(solution)/shard_map/pallas_call | solution.py:227
  42.3 1.1 %collective-permute-done.13.arrived = f32[6,64,128]{2,1,0:T(8,128)S(1)} collective-permute-done((f32[6,64,128]{2,1,0:T(8,128)S(1)}, f32[6,64,128]{2,1,0:T(8,128)S(1)}, u32[]{:S(2)}, u32[]{:S(2)}) %collective-permute-start.13) | collective-permute-done | bytes 196640 | tf_op jit(solution)/shard_map/ppermute | solution.py:25
  43.4 1.0 %shard_map.84 = (f32[16,64,128]{2,1,0:T(8,128)S(1)}, bf16[16,64,128]{2,1,0:T(8,128)(2,1)S(1)}, bf16[16,64,128]{2,1,0:T(8,128)(2,1)S(1)}, bf16[16,64,128]{2,1,0:T(8,128)(2,1)S(1)}) custom-call(s32[6]{0:T(128)S(1)} %stack.35.where, s32[1,6]{1,0:T(1,128)S(1)} %copy-done.4, s32[1,6]{1,0:T(1,128)S(1)} %collective-permute-done.3.other_ids, ...), custom_call_target="tpu_custom_call" | custom-call | tf_op jit(solution)/shard_map/pallas_call | solution.py:236
  44.8 0.9 collective-permute-start.15
  45.7 0.8 collective-permute-start.14
  46.5 3.6 %collective-permute-done.16 = bf16[16,64,128]{2,1,0:T(8,128)(2,1)S(1)} collective-permute-done((bf16[16,64,128]{2,1,0:T(8,128)(2,1)S(1)}, bf16[16,64,128]{2,1,0:T(8,128)(2,1)S(1)}, u32[]{:S(2)}, u32[]{:S(2)}) %collective-permute-start.16) | collective-permute-done | bytes 262176 | tf_op jit(solution)/shard_map/ppermute | solution.py:50
  50.1 1.8 %collective-permute-done.15 = bf16[16,64,128]{2,1,0:T(8,128)(2,1)S(1)} collective-permute-done((bf16[16,64,128]{2,1,0:T(8,128)(2,1)S(1)}, bf16[16,64,128]{2,1,0:T(8,128)(2,1)S(1)}, u32[]{:S(2)}, u32[]{:S(2)}) %collective-permute-start.15) | collective-permute-done | bytes 262176 | tf_op jit(solution)/shard_map/ppermute | solution.py:50
  51.9 2.8 %collective-permute-done.14 = bf16[16,64,128]{2,1,0:T(8,128)(2,1)S(1)} collective-permute-done((bf16[16,64,128]{2,1,0:T(8,128)(2,1)S(1)}, bf16[16,64,128]{2,1,0:T(8,128)(2,1)S(1)}, u32[]{:S(2)}, u32[]{:S(2)}) %collective-permute-start.14) | collective-permute-done | bytes 262176 | tf_op jit(solution)/shard_map/ppermute | solution.py:50
  55.5 0.9 collective-permute-start.17
  56.5 1.6 %collective-permute-done.19 = bf16[4,64,128]{2,1,0:T(8,128)(2,1)S(1)} collective-permute-done((bf16[4,64,128]{2,1,0:T(8,128)(2,1)S(1)}, bf16[4,64,128]{2,1,0:T(8,128)(2,1)S(1)}, u32[]{:S(2)}, u32[]{:S(2)}) %collective-permute-start.19) | collective-permute-done | bytes 65568 | tf_op jit(solution)/shard_map/ppermute | solution.py:50
  58.1 1.8 %collective-permute-done.18 = bf16[4,64,128]{2,1,0:T(8,128)(2,1)S(1)} collective-permute-done((bf16[4,64,128]{2,1,0:T(8,128)(2,1)S(1)}, bf16[4,64,128]{2,1,0:T(8,128)(2,1)S(1)}, u32[]{:S(2)}, u32[]{:S(2)}) %collective-permute-start.18) | collective-permute-done | bytes 65568 | tf_op jit(solution)/shard_map/ppermute | solution.py:50
  59.9 0.7 collective-permute-done.17
  60.7 1.3 %collective-permute-start.22 = (bf16[4,64,128]{2,1,0:T(8,128)(2,1)S(1)}, bf16[4,64,128]{2,1,0:T(8,128)(2,1)S(1)}, u32[]{:S(2)}, u32[]{:S(2)}) collective-permute-start(bf16[4,64,128]{2,1,0:T(8,128)(2,1)S(1)} %fusion.3), channel_id=1, source_target_pairs={{0,4},{4,0},{8,12},{12,8},{1,5},{5,1},{9,13},{13,9},{2,6},{6,2},{1... | collective-permute-start | bytes 196616 | tf_op jit(solution)/shard_map/ppermute | solution.py:55
  61.9 2.9 %collective-permute-done.22 = bf16[4,64,128]{2,1,0:T(8,128)(2,1)S(1)} collective-permute-done((bf16[4,64,128]{2,1,0:T(8,128)(2,1)S(1)}, bf16[4,64,128]{2,1,0:T(8,128)(2,1)S(1)}, u32[]{:S(2)}, u32[]{:S(2)}) %collective-permute-start.22) | collective-permute-done | bytes 65568 | tf_op jit(solution)/shard_map/ppermute | solution.py:55
  64.8 4.0 %collective-permute-start.23 = (bf16[4,64,128]{2,1,0:T(8,128)(2,1)S(1)}, bf16[4,64,128]{2,1,0:T(8,128)(2,1)S(1)}, u32[]{:S(2)}, u32[]{:S(2)}) collective-permute-start(bf16[4,64,128]{2,1,0:T(8,128)(2,1)S(1)} %fusion.4), channel_id=1, source_target_pairs={{0,12},{4,8},{8,4},{12,0},{1,13},{5,9},{9,5},{13,1},{2,14},{6,10},... | collective-permute-start | bytes 196616 | tf_op jit(solution)/shard_map/ppermute | solution.py:55
  68.8 0.8 collective-permute-start.20
  69.6 2.4 %collective-permute-start.21 = (bf16[64,2048]{1,0:T(8,128)(2,1)S(1)}, bf16[64,2048]{1,0:T(8,128)(2,1)S(1)}, u32[]{:S(2)}, u32[]{:S(2)}) collective-permute-start(bf16[64,2048]{1,0:T(8,128)(2,1)S(1)} %get-tuple-element.42), channel_id=1, source_target_pairs={{0,192},{64,0},{128,64},{192,128},{1,193},{65,1},{129,65},{193,129... | collective-permute-start | bytes 786440 | tf_op jit(solution)/shard_map/ppermute | solution.py:33
  73.6 1.6 %collective-permute-done.24.refs_1_ = bf16[4,64,128]{2,1,0:T(8,128)(2,1)S(1)} collective-permute-done((bf16[4,64,128]{2,1,0:T(8,128)(2,1)S(1)}, bf16[4,64,128]{2,1,0:T(8,128)(2,1)S(1)}, u32[]{:S(2)}, u32[]{:S(2)}) %collective-permute-start.24) | collective-permute-done | bytes 65568 | tf_op jit(solution)/shard_map/ppermute | solution.py:29
  75.2 4.8 %collective-permute-start.27 = (bf16[4,64,128]{2,1,0:T(8,128)(2,1)S(1)}, bf16[4,64,128]{2,1,0:T(8,128)(2,1)S(1)}, u32[]{:S(2)}, u32[]{:S(2)}) collective-permute-start(bf16[4,64,128]{2,1,0:T(8,128)(2,1)S(1)} %fusion.2.refs_0_), channel_id=1, source_target_pairs={{0,2},{2,0},{1,3},{3,1},{4,6},{6,4},{5,7},{7,5},{8,10},{10,8},{9,1... | collective-permute-start | bytes 196616 | tf_op jit(solution)/shard_map/ppermute | solution.py:25
  80.0 3.3 %collective-permute-start.28 = (bf16[4,64,128]{2,1,0:T(8,128)(2,1)S(1)}, bf16[4,64,128]{2,1,0:T(8,128)(2,1)S(1)}, u32[]{:S(2)}, u32[]{:S(2)}) collective-permute-start(bf16[4,64,128]{2,1,0:T(8,128)(2,1)S(1)} %collective-permute-done.24.refs_1_), channel_id=1, source_target_pairs={{0,2},{2,0},{1,3},{3,1},{4,6},{6,4},{5,7},{7,5},{8,10},{10,8},{9,1... | collective-permute-start | bytes 196616 | tf_op jit(solution)/shard_map/ppermute | solution.py:25
  83.3 0.7 collective-permute-start.29
  84.2 0.7 collective-permute-done.29.refs_6_
  85.2 1.1 %shard_map.85 = (f32[64,128]{1,0:T(8,128)S(1)}, f32[64,128]{1,0:T(8,128)S(1)}, f32[64,128]{1,0:T(8,128)S(1)}, f32[64,128]{1,0:T(8,128)S(1)}) custom-call(s32[6]{0:T(128)S(1)} %stack.35.where, f32[64,128]{1,0:T(8,128)S(1)} %copy-done.1, bf16[64,8192]{1,0:T(8,128)(2,1)S(1)} %copy-done, bf16[64,2048]{1,0:T(8,128)(2,1)S(1)} %collective-permute-done.2.b1, ...), custom_call_target="tpu_custom_call" | custom-call | tf_op jit(solution)/shard_map/pallas_call | solution.py:261
  86.4 2.7 %collective-permute-start.32 = (f32[64,128]{1,0:T(8,128)S(1)}, f32[64,128]{1,0:T(8,128)S(1)}, u32[]{:S(2)}, u32[]{:S(2)}) collective-permute-start(f32[64,128]{1,0:T(8,128)S(1)} %get-tuple-element.49), channel_id=1, source_target_pairs={{0,128},{64,192},{128,0},{192,64},{1,129},{65,193},{129,1},{193,65... | collective-permute-start | bytes 98312 | tf_op jit(solution)/shard_map/ppermute | solution.py:29
  89.4 0.9 %collective-permute-done.33 = f32[64,128]{1,0:T(8,128)S(1)} collective-permute-done((f32[64,128]{1,0:T(8,128)S(1)}, f32[64,128]{1,0:T(8,128)S(1)}, u32[]{:S(2)}, u32[]{:S(2)}) %collective-permute-start.33) | collective-permute-done | bytes 32800 | tf_op jit(solution)/shard_map/ppermute | solution.py:29
  90.9 1.3 %collective-permute-done.31 = f32[64,128]{1,0:T(8,128)S(1)} collective-permute-done((f32[64,128]{1,0:T(8,128)S(1)}, f32[64,128]{1,0:T(8,128)S(1)}, u32[]{:S(2)}, u32[]{:S(2)}) %collective-permute-start.31) | collective-permute-done | bytes 32800 | tf_op jit(solution)/shard_map/ppermute | solution.py:29
  92.2 0.6 add_add_fusion
  (58 shorter events, 5.9 us)
Async XLA Ops:
  0.8 6.4 %collective-permute-start = (bf16[64,128]{1,0:T(8,128)(2,1)S(1)}, bf16[64,128]{1,0:T(8,128)(2,1)S(1)}, u32[]{:S(2)}, u32[]{:S(2)}) collective-permute-start(bf16[64,128]{1,0:T(8,128)(2,1)S(1)} %convert_element_type.39), channel_id=1, source_target_pairs={{0,4},{4,0},{8,12},{12,8},{1,5},{5,1},{9,13},{13,9},{2,6},{6,2},{1... | collective-permute-start | bytes 49160 | tf_op jit(solution)/shard_map/ppermute | solution.py:55
  4.6 2.6 %copy-start.1 = (f32[64,128]{1,0:T(8,128)S(1)}, f32[64,128]{1,0:T(8,128)}, u32[]{:S(2)}) copy-start(f32[64,128]{1,0:T(8,128)} %start.1) | copy-start | bytes 98308
  4.6 13.3 %copy-start.2 = (bf16[1,256,768]{2,1,0:T(8,128)(2,1)S(1)}, bf16[1,256,768]{2,1,0:T(8,128)(2,1)}, u32[]{:S(2)}) copy-start(bf16[1,256,768]{2,1,0:T(8,128)(2,1)} %param.12) | copy-start | bytes 1179652
  5.8 8.3 %collective-permute-start.2 = (bf16[64,2048]{1,0:T(8,128)(2,1)S(1)}, bf16[64,2048]{1,0:T(8,128)(2,1)S(1)}, u32[]{:S(2)}, u32[]{:S(2)}) collective-permute-start(bf16[64,2048]{1,0:T(8,128)(2,1)S(1)} %get-tuple-element.55), channel_id=1, source_target_pairs={{0,64},{64,128},{128,192},{192,0},{1,65},{65,129},{129,193},{193,1... | collective-permute-start | bytes 786440 | tf_op jit(solution)/shard_map/ppermute | solution.py:33
  7.2 4.3 %copy-start.4 = (s32[1,6]{1,0:T(1,128)S(1)}, s32[1,6]{1,0:T(1,128)}, u32[]{:S(2)}) copy-start(s32[1,6]{1,0:T(1,128)} %own_ids.3) | copy-start | bytes 76
  7.2 6.1 %collective-permute-start.1 = (bf16[2,64,128]{2,1,0:T(8,128)(2,1)S(1)}, bf16[2,64,128]{2,1,0:T(8,128)(2,1)S(1)}, u32[]{:S(2)}, u32[]{:S(2)}) collective-permute-start(bf16[2,64,128]{2,1,0:T(8,128)(2,1)S(1)} %pad_maximum_fusion.1), channel_id=1, source_target_pairs={{0,12},{4,8},{8,4},{12,0},{1,13},{5,9},{9,5},{13,1},{2,14},{6,10},... | collective-permute-start | bytes 98312 | tf_op jit(solution)/shard_map/ppermute | solution.py:55
  11.5 2.6 %collective-permute-start.3 = (s32[1,6]{1,0:T(1,128)S(1)}, s32[1,6]{1,0:T(1,128)S(1)}, u32[]{:S(2)}, u32[]{:S(2)}) collective-permute-start(s32[1,6]{1,0:T(1,128)S(1)} %copy-done.4), channel_id=1, source_target_pairs={{0,2},{2,0},{1,3},{3,1},{4,6},{6,4},{5,7},{7,5},{8,10},{10,8},{9,1... | collective-permute-start | bytes 80 | tf_op jit(solution)/shard_map/ppermute | solution.py:25
  14.1 11.8 %copy-start.3 = (bf16[1,256,512]{2,1,0:T(8,128)(2,1)S(1)}, bf16[1,256,512]{2,1,0:T(8,128)(2,1)}, u32[]{:S(2)}) copy-start(bf16[1,256,512]{2,1,0:T(8,128)(2,1)} %param.13) | copy-start | bytes 786436
  14.1 4.5 %collective-permute-start.4 = (bf16[4,64,128]{2,1,0:T(8,128)(2,1)S(1)}, bf16[4,64,128]{2,1,0:T(8,128)(2,1)S(1)}, u32[]{:S(2)}, u32[]{:S(2)}) collective-permute-start(bf16[4,64,128]{2,1,0:T(8,128)(2,1)S(1)} %pad_maximum_fusion), channel_id=1, source_target_pairs={{0,48},{2,194},{16,0},{18,210},{32,16},{34,226},{48,32},{50,242},{... | collective-permute-start | bytes 196616 | tf_op jit(solution)/shard_map/ppermute | solution.py:50
  16.9 4.7 %collective-permute-start.5 = (bf16[4,64,128]{2,1,0:T(8,128)(2,1)S(1)}, bf16[4,64,128]{2,1,0:T(8,128)(2,1)S(1)}, u32[]{:S(2)}, u32[]{:S(2)}) collective-permute-start(bf16[4,64,128]{2,1,0:T(8,128)(2,1)S(1)} %pad_maximum_fusion), channel_id=1, source_target_pairs={{0,32},{2,130},{16,48},{18,146},{32,0},{34,162},{48,16},{50,178},{... | collective-permute-start | bytes 196616 | tf_op jit(solution)/shard_map/ppermute | solution.py:50
  17.2 5.0 %collective-permute-start.6 = (bf16[4,64,128]{2,1,0:T(8,128)(2,1)S(1)}, bf16[4,64,128]{2,1,0:T(8,128)(2,1)S(1)}, u32[]{:S(2)}, u32[]{:S(2)}) collective-permute-start(bf16[4,64,128]{2,1,0:T(8,128)(2,1)S(1)} %pad_maximum_fusion), channel_id=1, source_target_pairs={{0,16},{2,66},{16,32},{18,82},{32,48},{34,98},{48,0},{50,114},{64,... | collective-permute-start | bytes 196616 | tf_op jit(solution)/shard_map/ppermute | solution.py:50
  17.9 21.4 %collective-permute-start.11 = (bf16[256,768]{1,0:T(8,128)(2,1)S(1)}, bf16[256,768]{1,0:T(8,128)(2,1)S(1)}, u32[]{:S(2)}, u32[]{:S(2)}) collective-permute-start(bf16[256,768]{1,0:T(8,128)(2,1)S(1)} %bitcast.12), channel_id=1, source_target_pairs={{0,1},{1,0},{2,3},{3,2},{4,5},{5,4},{6,7},{7,6},{8,9},{9,8},{10,11... | collective-permute-start | bytes 1179656 | tf_op jit(solution)/shard_map/ppermute | solution.py:25
  22.2 8.7 %collective-permute-start.7 = (bf16[16,64,128]{2,1,0:T(8,128)(2,1)S(1)}, bf16[16,64,128]{2,1,0:T(8,128)(2,1)S(1)}, u32[]{:S(2)}, u32[]{:S(2)}) collective-permute-start(bf16[16,64,128]{2,1,0:T(8,128)(2,1)S(1)} %constant_dynamic-update-slice_fusion.p0), channel_id=1, source_target_pairs={{0,192},{2,50},{16,208},{18,2},{32,224},{34,18},{48,240},{50,34},{... | collective-permute-start | bytes 786440 | tf_op jit(solution)/shard_map/ppermute | solution.py:50
  24.8 6.8 %collective-permute-start.8 = (bf16[16,64,128]{2,1,0:T(8,128)(2,1)S(1)}, bf16[16,64,128]{2,1,0:T(8,128)(2,1)S(1)}, u32[]{:S(2)}, u32[]{:S(2)}) collective-permute-start(bf16[16,64,128]{2,1,0:T(8,128)(2,1)S(1)} %constant_dynamic-update-slice_fusion.p0), channel_id=1, source_target_pairs={{0,128},{2,34},{16,144},{18,50},{32,160},{34,2},{48,176},{50,18},{... | collective-permute-start | bytes 786440 | tf_op jit(solution)/shard_map/ppermute | solution.py:50
  25.3 9.3 %collective-permute-start.9 = (bf16[16,64,128]{2,1,0:T(8,128)(2,1)S(1)}, bf16[16,64,128]{2,1,0:T(8,128)(2,1)S(1)}, u32[]{:S(2)}, u32[]{:S(2)}) collective-permute-start(bf16[16,64,128]{2,1,0:T(8,128)(2,1)S(1)} %constant_dynamic-update-slice_fusion.p0), channel_id=1, source_target_pairs={{0,64},{2,18},{16,80},{18,34},{32,96},{34,50},{48,112},{50,2},{64,... | collective-permute-start | bytes 786440 | tf_op jit(solution)/shard_map/ppermute | solution.py:50
  25.9 13.4 %collective-permute-start.12 = (bf16[256,512]{1,0:T(8,128)(2,1)S(1)}, bf16[256,512]{1,0:T(8,128)(2,1)S(1)}, u32[]{:S(2)}, u32[]{:S(2)}) collective-permute-start(bf16[256,512]{1,0:T(8,128)(2,1)S(1)} %bitcast.14), channel_id=1, source_target_pairs={{0,1},{1,0},{2,3},{3,2},{4,5},{5,4},{6,7},{7,6},{8,9},{9,8},{10,11... | collective-permute-start | bytes 786440 | tf_op jit(solution)/shard_map/ppermute | solution.py:25
  35.5 4.8 %collective-permute-start.10 = (bf16[6,64,128]{2,1,0:T(8,128)(2,1)S(1)}, bf16[6,64,128]{2,1,0:T(8,128)(2,1)S(1)}, u32[]{:S(2)}, u32[]{:S(2)}) collective-permute-start(bf16[6,64,128]{2,1,0:T(8,128)(2,1)S(1)} %get-tuple-element.32), channel_id=1, source_target_pairs={{0,2},{2,0},{1,3},{3,1},{4,6},{6,4},{5,7},{7,5},{8,10},{10,8},{9,1... | collective-permute-start | bytes 294920 | tf_op jit(solution)/shard_map/ppermute | solution.py:25
  41.9 1.5 %collective-permute-start.13 = (f32[6,64,128]{2,1,0:T(8,128)S(1)}, f32[6,64,128]{2,1,0:T(8,128)S(1)}, u32[]{:S(2)}, u32[]{:S(2)}) collective-permute-start(f32[6,64,128]{2,1,0:T(8,128)S(1)} %get-tuple-element.36), channel_id=1, source_target_pairs={{0,2},{2,0},{1,3},{3,1},{4,6},{6,4},{5,7},{7,5},{8,10},{10,8},{9,1... | collective-permute-start | bytes 589832 | tf_op jit(solution)/shard_map/ppermute | solution.py:25
  44.5 5.6 %collective-permute-start.16 = (bf16[16,64,128]{2,1,0:T(8,128)(2,1)S(1)}, bf16[16,64,128]{2,1,0:T(8,128)(2,1)S(1)}, u32[]{:S(2)}, u32[]{:S(2)}) collective-permute-start(bf16[16,64,128]{2,1,0:T(8,128)(2,1)S(1)} %get-tuple-element.40), channel_id=1, source_target_pairs={{0,192},{2,50},{16,208},{18,2},{32,224},{34,18},{48,240},{50,34},{... | collective-permute-start | bytes 786440 | tf_op jit(solution)/shard_map/ppermute | solution.py:50
  44.8 7.1 %collective-permute-start.15 = (bf16[16,64,128]{2,1,0:T(8,128)(2,1)S(1)}, bf16[16,64,128]{2,1,0:T(8,128)(2,1)S(1)}, u32[]{:S(2)}, u32[]{:S(2)}) collective-permute-start(bf16[16,64,128]{2,1,0:T(8,128)(2,1)S(1)} %get-tuple-element.39), channel_id=1, source_target_pairs={{0,128},{2,34},{16,144},{18,50},{32,160},{34,2},{48,176},{50,18},{... | collective-permute-start | bytes 786440 | tf_op jit(solution)/shard_map/ppermute | solution.py:50
  45.7 9.0 %collective-permute-start.14 = (bf16[16,64,128]{2,1,0:T(8,128)(2,1)S(1)}, bf16[16,64,128]{2,1,0:T(8,128)(2,1)S(1)}, u32[]{:S(2)}, u32[]{:S(2)}) collective-permute-start(bf16[16,64,128]{2,1,0:T(8,128)(2,1)S(1)} %get-tuple-element.38), channel_id=1, source_target_pairs={{0,64},{2,18},{16,80},{18,34},{32,96},{34,50},{48,112},{50,2},{64,... | collective-permute-start | bytes 786440 | tf_op jit(solution)/shard_map/ppermute | solution.py:50
  54.8 1.6 %copy-start.5 = (f32[64,128]{1,0:T(8,128)S(1)}, f32[64,128]{1,0:T(8,128)}, u32[]{:S(2)}) copy-start(f32[64,128]{1,0:T(8,128)} %param.9) | copy-start | bytes 98308
  54.9 3.2 %collective-permute-start.19 = (bf16[4,64,128]{2,1,0:T(8,128)(2,1)S(1)}, bf16[4,64,128]{2,1,0:T(8,128)(2,1)S(1)}, u32[]{:S(2)}, u32[]{:S(2)}) collective-permute-start(bf16[4,64,128]{2,1,0:T(8,128)(2,1)S(1)} %get-tuple-element.57), channel_id=1, source_target_pairs={{0,48},{2,194},{16,0},{18,210},{32,16},{34,226},{48,32},{50,242},{... | collective-permute-start | bytes 196616 | tf_op jit(solution)/shard_map/ppermute | solution.py:50
  55.3 1.2 %copy-start.6 = (f32[64]{0:T(128)S(1)}, f32[64]{0:T(128)}, u32[]{:S(2)}) copy-start(f32[64]{0:T(128)} %param.10) | copy-start | bytes 772
  55.3 4.6 %collective-permute-start.18 = (bf16[4,64,128]{2,1,0:T(8,128)(2,1)S(1)}, bf16[4,64,128]{2,1,0:T(8,128)(2,1)S(1)}, u32[]{:S(2)}, u32[]{:S(2)}) collective-permute-start(bf16[4,64,128]{2,1,0:T(8,128)(2,1)S(1)} %get-tuple-element.58), channel_id=1, source_target_pairs={{0,32},{2,130},{16,48},{18,146},{32,0},{34,162},{48,16},{50,178},{... | collective-permute-start | bytes 196616 | tf_op jit(solution)/shard_map/ppermute | solution.py:50
  55.5 5.1 %collective-permute-start.17 = (bf16[4,64,128]{2,1,0:T(8,128)(2,1)S(1)}, bf16[4,64,128]{2,1,0:T(8,128)(2,1)S(1)}, u32[]{:S(2)}, u32[]{:S(2)}) collective-permute-start(bf16[4,64,128]{2,1,0:T(8,128)(2,1)S(1)} %get-tuple-element.56), channel_id=1, source_target_pairs={{0,16},{2,66},{16,32},{18,82},{32,48},{34,98},{48,0},{50,114},{64,... | collective-permute-start | bytes 196616 | tf_op jit(solution)/shard_map/ppermute | solution.py:50
  56.5 28.8 %copy-start = (bf16[64,8192]{1,0:T(8,128)(2,1)S(1)}, bf16[64,8192]{1,0:T(8,128)(2,1)}, u32[]{:S(2)}) copy-start(bf16[64,8192]{1,0:T(8,128)(2,1)} %precond.1) | copy-start | bytes 3145732
  60.7 4.1 %collective-permute-start.22 = (bf16[4,64,128]{2,1,0:T(8,128)(2,1)S(1)}, bf16[4,64,128]{2,1,0:T(8,128)(2,1)S(1)}, u32[]{:S(2)}, u32[]{:S(2)}) collective-permute-start(bf16[4,64,128]{2,1,0:T(8,128)(2,1)S(1)} %fusion.3), channel_id=1, source_target_pairs={{0,4},{4,0},{8,12},{12,8},{1,5},{5,1},{9,13},{13,9},{2,6},{6,2},{1... | collective-permute-start | bytes 196616 | tf_op jit(solution)/shard_map/ppermute | solution.py:55
  64.8 7.2 %collective-permute-start.23 = (bf16[4,64,128]{2,1,0:T(8,128)(2,1)S(1)}, bf16[4,64,128]{2,1,0:T(8,128)(2,1)S(1)}, u32[]{:S(2)}, u32[]{:S(2)}) collective-permute-start(bf16[4,64,128]{2,1,0:T(8,128)(2,1)S(1)} %fusion.4), channel_id=1, source_target_pairs={{0,12},{4,8},{8,4},{12,0},{1,13},{5,9},{9,5},{13,1},{2,14},{6,10},... | collective-permute-start | bytes 196616 | tf_op jit(solution)/shard_map/ppermute | solution.py:55
  68.8 15.2 %collective-permute-start.20 = (bf16[64,2048]{1,0:T(8,128)(2,1)S(1)}, bf16[64,2048]{1,0:T(8,128)(2,1)S(1)}, u32[]{:S(2)}, u32[]{:S(2)}) collective-permute-start(bf16[64,2048]{1,0:T(8,128)(2,1)S(1)} %get-tuple-element.41), channel_id=1, source_target_pairs={{0,128},{64,192},{128,0},{192,64},{1,129},{65,193},{129,1},{193,65... | collective-permute-start | bytes 786440 | tf_op jit(solution)/shard_map/ppermute | solution.py:33
  69.6 14.4 %collective-permute-start.21 = (bf16[64,2048]{1,0:T(8,128)(2,1)S(1)}, bf16[64,2048]{1,0:T(8,128)(2,1)S(1)}, u32[]{:S(2)}, u32[]{:S(2)}) collective-permute-start(bf16[64,2048]{1,0:T(8,128)(2,1)S(1)} %get-tuple-element.42), channel_id=1, source_target_pairs={{0,192},{64,0},{128,64},{192,128},{1,193},{65,1},{129,65},{193,129... | collective-permute-start | bytes 786440 | tf_op jit(solution)/shard_map/ppermute | solution.py:33
  72.0 3.2 %collective-permute-start.24 = (bf16[4,64,128]{2,1,0:T(8,128)(2,1)S(1)}, bf16[4,64,128]{2,1,0:T(8,128)(2,1)S(1)}, u32[]{:S(2)}, u32[]{:S(2)}) collective-permute-start(bf16[4,64,128]{2,1,0:T(8,128)(2,1)S(1)} %fusion.2.refs_0_), channel_id=1, source_target_pairs={{0,48},{16,0},{32,16},{48,32},{1,49},{17,1},{33,17},{49,33},{2,50}... | collective-permute-start | bytes 196616 | tf_op jit(solution)/shard_map/ppermute | solution.py:29
  72.4 7.6 %collective-permute-start.25 = (bf16[4,64,128]{2,1,0:T(8,128)(2,1)S(1)}, bf16[4,64,128]{2,1,0:T(8,128)(2,1)S(1)}, u32[]{:S(2)}, u32[]{:S(2)}) collective-permute-start(bf16[4,64,128]{2,1,0:T(8,128)(2,1)S(1)} %fusion.2.refs_0_), channel_id=1, source_target_pairs={{0,32},{16,48},{32,0},{48,16},{1,33},{17,49},{33,1},{49,17},{2,34}... | collective-permute-start | bytes 196616 | tf_op jit(solution)/shard_map/ppermute | solution.py:29
  73.0 10.3 %collective-permute-start.26 = (bf16[4,64,128]{2,1,0:T(8,128)(2,1)S(1)}, bf16[4,64,128]{2,1,0:T(8,128)(2,1)S(1)}, u32[]{:S(2)}, u32[]{:S(2)}) collective-permute-start(bf16[4,64,128]{2,1,0:T(8,128)(2,1)S(1)} %fusion.2.refs_0_), channel_id=1, source_target_pairs={{0,16},{16,32},{32,48},{48,0},{1,17},{17,33},{33,49},{49,1},{2,18}... | collective-permute-start | bytes 196616 | tf_op jit(solution)/shard_map/ppermute | solution.py:29
  75.2 8.8 %collective-permute-start.27 = (bf16[4,64,128]{2,1,0:T(8,128)(2,1)S(1)}, bf16[4,64,128]{2,1,0:T(8,128)(2,1)S(1)}, u32[]{:S(2)}, u32[]{:S(2)}) collective-permute-start(bf16[4,64,128]{2,1,0:T(8,128)(2,1)S(1)} %fusion.2.refs_0_), channel_id=1, source_target_pairs={{0,2},{2,0},{1,3},{3,1},{4,6},{6,4},{5,7},{7,5},{8,10},{10,8},{9,1... | collective-permute-start | bytes 196616 | tf_op jit(solution)/shard_map/ppermute | solution.py:25
  80.0 4.2 %collective-permute-start.28 = (bf16[4,64,128]{2,1,0:T(8,128)(2,1)S(1)}, bf16[4,64,128]{2,1,0:T(8,128)(2,1)S(1)}, u32[]{:S(2)}, u32[]{:S(2)}) collective-permute-start(bf16[4,64,128]{2,1,0:T(8,128)(2,1)S(1)} %collective-permute-done.24.refs_1_), channel_id=1, source_target_pairs={{0,2},{2,0},{1,3},{3,1},{4,6},{6,4},{5,7},{7,5},{8,10},{10,8},{9,1... | collective-permute-start | bytes 196616 | tf_op jit(solution)/shard_map/ppermute | solution.py:25
  83.3 1.6 %collective-permute-start.29 = (bf16[4,64,128]{2,1,0:T(8,128)(2,1)S(1)}, bf16[4,64,128]{2,1,0:T(8,128)(2,1)S(1)}, u32[]{:S(2)}, u32[]{:S(2)}) collective-permute-start(bf16[4,64,128]{2,1,0:T(8,128)(2,1)S(1)} %collective-permute-done.25.refs_2_), channel_id=1, source_target_pairs={{0,2},{2,0},{1,3},{3,1},{4,6},{6,4},{5,7},{7,5},{8,10},{10,8},{9,1... | collective-permute-start | bytes 196616 | tf_op jit(solution)/shard_map/ppermute | solution.py:25
  84.0 1.3 %collective-permute-start.30 = (bf16[4,64,128]{2,1,0:T(8,128)(2,1)S(1)}, bf16[4,64,128]{2,1,0:T(8,128)(2,1)S(1)}, u32[]{:S(2)}, u32[]{:S(2)}) collective-permute-start(bf16[4,64,128]{2,1,0:T(8,128)(2,1)S(1)} %collective-permute-done.26.refs_3_), channel_id=1, source_target_pairs={{0,2},{2,0},{1,3},{3,1},{4,6},{6,4},{5,7},{7,5},{8,10},{10,8},{9,1... | collective-permute-start | bytes 196616 | tf_op jit(solution)/shard_map/ppermute | solution.py:25
  86.3 4.1 %collective-permute-start.33 = (f32[64,128]{1,0:T(8,128)S(1)}, f32[64,128]{1,0:T(8,128)S(1)}, u32[]{:S(2)}, u32[]{:S(2)}) collective-permute-start(f32[64,128]{1,0:T(8,128)S(1)} %get-tuple-element.50), channel_id=1, source_target_pairs={{0,64},{64,128},{128,192},{192,0},{1,65},{65,129},{129,193},{193,1... | collective-permute-start | bytes 98312 | tf_op jit(solution)/shard_map/ppermute | solution.py:29
  86.4 4.4 %collective-permute-start.32 = (f32[64,128]{1,0:T(8,128)S(1)}, f32[64,128]{1,0:T(8,128)S(1)}, u32[]{:S(2)}, u32[]{:S(2)}) collective-permute-start(f32[64,128]{1,0:T(8,128)S(1)} %get-tuple-element.49), channel_id=1, source_target_pairs={{0,128},{64,192},{128,0},{192,64},{1,129},{65,193},{129,1},{193,65... | collective-permute-start | bytes 98312 | tf_op jit(solution)/shard_map/ppermute | solution.py:29
  89.1 3.1 %collective-permute-start.31 = (f32[64,128]{1,0:T(8,128)S(1)}, f32[64,128]{1,0:T(8,128)S(1)}, u32[]{:S(2)}, u32[]{:S(2)}) collective-permute-start(f32[64,128]{1,0:T(8,128)S(1)} %get-tuple-element.48), channel_id=1, source_target_pairs={{0,192},{64,0},{128,64},{192,128},{1,193},{65,1},{129,65},{193,129... | collective-permute-start | bytes 98312 | tf_op jit(solution)/shard_map/ppermute | solution.py:29

commit v13 on v12

--- a/solution.py
+++ b/solution.py
@@ -50,26 +50,32 @@
     return lax.ppermute(value, (Y, X, CORE), pairs)
 
 
-def pair(axis, value, first):
-    other = [1, 0, 3, 2] if first else [3, 2, 1, 0]
-    return lax.ppermute(value, axis, list(enumerate(other)))
+def pair(value, first):
+    pairs = []
+    for z in range(RING):
+        for core in range(2):
+            other = z ^ 1 if (core == 0) == first else RING - 1 - z
+            pairs.append((z * 2 + core, other * 2 + core))
+    return lax.ppermute(value, (Z, CORE), pairs)
 
 
 def line_gather(value):
-    two = jnp.stack([value, pair(Z, value, True)])
-    return jnp.concatenate([two, pair(Z, two, False)])
-
-
-def line_slot(tile_z, z):
+    two = jnp.stack([value, pair(value, True)])
+    return jnp.concatenate([two, pair(two, False)])
+
+
+def line_slot(tile_z, z, core):
+    near, far = z ^ 1, RING - 1 - z
+    near_slot = 1 + core
     return jnp.where(
-        tile_z == z, 0, jnp.where(tile_z == (z ^ 1), 1, jnp.where(tile_z == 3 - z, 2, 3))
+        tile_z == z, 0, jnp.where(tile_z == near, near_slot, jnp.where(tile_z == far, 3 - near_slot, 3))
     )
 
 
 def spread_place(tile, where):
     dy = (tile // 16 - where[0] + RING) % RING
     dx = ((tile // RING) % RING - where[1] + RING) % RING
-    slot = line_slot(tile % RING, where[2])
+    slot = line_slot(tile % RING, where[2], where[3])
     first = where[3] == 0
     return jnp.where(first, dy, dx), jnp.where(first, dx, dy) * RING + slot
 
@@ -113,9 +119,9 @@
     solved_own = masked(jnp.dot(inverse_own[...], operand, preferred_element_type=F32), own_start)
     solved_other = masked(jnp.dot(inverse_other[...], operand, preferred_element_type=F32), other_start)
     numbers = (((0,), (0,)), ((), ()))
-    turned = lax.dot_general(solved_own, border_own[...], numbers, preferred_element_type=F32)
-    turned += lax.dot_general(solved_other, border_other[...], numbers, preferred_element_type=F32)
-    term = turned.T.reshape(tiles, 2, HALF, turned.shape[0])
+    term = lax.dot_general(border_own[...], solved_own, numbers, preferred_element_type=F32)
+    term += lax.dot_general(border_other[...], solved_other, numbers, preferred_element_type=F32)
+    term = term.reshape(tiles, 2, HALF, term.shape[1])
 
     @pl.when(core == 0)
     def _():
@@ -153,9 +159,10 @@
 def update_kernel(where, start, precond, b1, b2, b3, *refs):
     pieces, (o0, o1, o2, o3, whole) = refs[:8], refs[8:]
     y, x, z, core = where[0], where[1], where[2], where[3]
-    slots = (z, z ^ 1, 3 - z, (3 - z) ^ 1)
+    near, far = z ^ 1, RING - 1 - z
     for side in range(2):
         half = core if side == 0 else 1 - core
+        slots = (z, jnp.where(half == 0, near, far), jnp.where(half == 0, far, near), far ^ 1)
         for i in range(RING):
             piece = pieces[side * RING + i]
             base = ((x + i) % RING) * 4
@@ -250,9 +257,9 @@
     block2, block3 = to_ahead(columns2, Y, 2), to_ahead(columns3, Y, 3)
     own_terms = right_side - root_diagonal[:, None] * start_guess
     line = line + jnp.concatenate([own_terms[None], jnp.zeros_like(line[1:])])
-    met = pair(Z, line.astype(BF16), True).astype(F32)
+    met = pair(line.astype(BF16), True).astype(F32)
     line = line + jnp.stack([met[1], met[0], met[3], met[2]])
-    met = pair(Z, line.astype(BF16), False).astype(F32)
+    met = pair(line.astype(BF16), False).astype(F32)
     line = line + jnp.concatenate([met[2:], met[:2]])
 
     mine = ring_pieces(line.astype(BF16), X)

time: 93 us -> 93 us (level)
    ppermute x3, waiting for transfers between devices: 0.01 us -> 2.23 us  [to_ahead(): lax.ppermute(value, axis, [(i, (i + distance) % RING) for i in range(RING)])]
    ppermute x12, starting transfers between devices: 11 us -> 9.48 us  [across(): return lax.ppermute(value, (Y, X, CORE), pairs)]
    ppermute x12, waiting for transfers between devices: 22.9 us -> 21.5 us  [across(): return lax.ppermute(value, (Y, X, CORE), pairs)]
  transfers between devices with their start and end apart: 34 -> 34, of which waited for: 22 -> 23; matrix products, arithmetic and copies ran while one was open for 2% -> 2% of each run, Pallas kernels for 1% -> 1%
where the time goes in v13:
time: 93 us; the launch traced here: 92.8 us
  starting transfers between devices  49.7 us (53%)
  waiting for transfers between devices  34.5 us (37%)
  Pallas kernels  4.6 us (5%)
  other arithmetic  1.73 us (2%)
  local copies, waits for them, and re-layouts  1.42 us (2%)
    ppermute x12, waiting for transfers between devices, across(): return lax.ppermute(value, (Y, X, CORE), pairs)  21.5 us
    ppermute x9, starting transfers between devices, swap(): return lax.ppermute(value, axis, SWAP)  16.8 us
    ppermute x4, starting transfers between devices, pair(): return lax.ppermute(value, (Z, CORE), pairs)  14.2 us
    ppermute x12, starting transfers between devices, across(): return lax.ppermute(value, (Y, X, CORE), pairs)  9.48 us
    ppermute x6, starting transfers between devices, from_ahead(): lax.ppermute(value, axis, [(i, (i - distance) % RING) for i in range(RING)])  4.69 us
    ppermute x6, waiting for transfers between devices, from_ahead(): lax.ppermute(value, axis, [(i, (i - distance) % RING) for i in range(RING)])  4.69 us
    ppermute x3, starting transfers between devices, to_ahead(): lax.ppermute(value, axis, [(i, (i + distance) % RING) for i in range(RING)])  4.6 us
    ppermute x9, waiting for transfers between devices, swap(): return lax.ppermute(value, axis, SWAP)  3.28 us
  transfers between devices with their start and end apart: 34, of which 23 were waited for; matrix products, arithmetic and copies ran while one was open for 2% of the time, Pallas kernels for 1%

profile of v13, /device:TPU:1, one launch (start us, length us, event | category | flops | bytes accessed | tf_op | source)
XLA Modules:
  0.0 92.8 jit_solution(3115987741219940500)
XLA Ops:
  0.0 0.8 convert_element_type.39
  0.8 6.8 %collective-permute-start = (bf16[64,128]{1,0:T(8,128)(2,1)S(1)}, bf16[64,128]{1,0:T(8,128)(2,1)S(1)}, u32[]{:S(2)}, u32[]{:S(2)}) collective-permute-start(bf16[64,128]{1,0:T(8,128)(2,1)S(1)} %convert_element_type.39), channel_id=1, source_target_pairs={{0,4},{2,14},{4,0},{6,10},{8,12},{10,6},{12,8},{14,2},{1,5},{3,15}... | collective-permute-start | bytes 49160 | tf_op jit(solution)/shard_map/ppermute | solution.py:59
  7.6 1.2 %constant_dynamic-slice_fusion = (bf16[64,2048]{1,0:T(8,128)(2,1)S(1)}, bf16[64,2048]{1,0:T(8,128)(2,1)S(1)}, bf16[64,2048]{1,0:T(8,128)(2,1)S(1)}) fusion(bf16[64,8192]{1,0:T(8,128)(2,1)} %precond.1, s32[]{:T(128)S(6)} %select_n.29, s32[]{:T(128)S(6)} %select_n.27, s32[]{:T(128)S(6)} %select_n.25), kind=kLoop, calls=%fused_computation.17 | loop fusion | bytes 1572876 | tf_op jit(solution)/shard_map/dynamic_slice | solution.py:216
  8.8 1.4 %collective-permute-start.2 = (bf16[64,2048]{1,0:T(8,128)(2,1)S(1)}, bf16[64,2048]{1,0:T(8,128)(2,1)S(1)}, u32[]{:S(2)}, u32[]{:S(2)}) collective-permute-start(bf16[64,2048]{1,0:T(8,128)(2,1)S(1)} %get-tuple-element.55), channel_id=1, source_target_pairs={{0,64},{64,128},{128,192},{192,0},{1,65},{65,129},{129,193},{193,1... | collective-permute-start | bytes 786440 | tf_op jit(solution)/shard_map/ppermute | solution.py:33
  10.3 1.3 %collective-permute-start.1 = (bf16[2,64,128]{2,1,0:T(8,128)(2,1)S(1)}, bf16[2,64,128]{2,1,0:T(8,128)(2,1)S(1)}, u32[]{:S(2)}, u32[]{:S(2)}) collective-permute-start(bf16[2,64,128]{2,1,0:T(8,128)(2,1)S(1)} %pad_maximum_fusion.1), channel_id=1, source_target_pairs={{0,12},{2,6},{4,8},{6,2},{8,4},{10,14},{12,0},{14,10},{1,13},{3,7}... | collective-permute-start | bytes 98312 | tf_op jit(solution)/shard_map/ppermute | solution.py:59
  11.5 1.8 %collective-permute-start.3 = (s32[1,6]{1,0:T(1,128)S(1)}, s32[1,6]{1,0:T(1,128)S(1)}, u32[]{:S(2)}, u32[]{:S(2)}) collective-permute-start(s32[1,6]{1,0:T(1,128)S(1)} %copy-done.4), channel_id=1, source_target_pairs={{0,2},{2,0},{1,3},{3,1},{4,6},{6,4},{5,7},{7,5},{8,10},{10,8},{9,1... | collective-permute-start | bytes 80 | tf_op jit(solution)/shard_map/ppermute | solution.py:25
  13.3 1.0 %collective-permute-done.1 = bf16[2,64,128]{2,1,0:T(8,128)(2,1)S(1)} collective-permute-done((bf16[2,64,128]{2,1,0:T(8,128)(2,1)S(1)}, bf16[2,64,128]{2,1,0:T(8,128)(2,1)S(1)}, u32[]{:S(2)}, u32[]{:S(2)}) %collective-permute-start.1) | collective-permute-done | bytes 32800 | tf_op jit(solution)/shard_map/ppermute | solution.py:59
  14.3 2.2 %collective-permute-done.2.b1 = bf16[64,2048]{1,0:T(8,128)(2,1)S(1)} collective-permute-done((bf16[64,2048]{1,0:T(8,128)(2,1)S(1)}, bf16[64,2048]{1,0:T(8,128)(2,1)S(1)}, u32[]{:S(2)}, u32[]{:S(2)}) %collective-permute-start.2) | collective-permute-done | bytes 262176 | tf_op jit(solution)/shard_map/ppermute | solution.py:33
  16.6 1.5 %collective-permute-start.4 = (bf16[4,64,128]{2,1,0:T(8,128)(2,1)S(1)}, bf16[4,64,128]{2,1,0:T(8,128)(2,1)S(1)}, u32[]{:S(2)}, u32[]{:S(2)}) collective-permute-start(bf16[4,64,128]{2,1,0:T(8,128)(2,1)S(1)} %pad_maximum_fusion), channel_id=1, source_target_pairs={{0,48},{2,194},{16,0},{18,210},{32,16},{34,226},{48,32},{50,242},{... | collective-permute-start | bytes 196616 | tf_op jit(solution)/shard_map/ppermute | solution.py:50
  18.4 0.7 collective-permute-start.6
  19.1 1.6 %collective-permute-start.11 = (bf16[256,768]{1,0:T(8,128)(2,1)S(1)}, bf16[256,768]{1,0:T(8,128)(2,1)S(1)}, u32[]{:S(2)}, u32[]{:S(2)}) collective-permute-start(bf16[256,768]{1,0:T(8,128)(2,1)S(1)} %bitcast.12), channel_id=1, source_target_pairs={{0,1},{1,0},{2,3},{3,2},{4,5},{5,4},{6,7},{7,6},{8,9},{9,8},{10,11... | collective-permute-start | bytes 1179656 | tf_op jit(solution)/shard_map/ppermute | solution.py:25
  20.8 2.2 %collective-permute-done.5 = bf16[4,64,128]{2,1,0:T(8,128)(2,1)S(1)} collective-permute-done((bf16[4,64,128]{2,1,0:T(8,128)(2,1)S(1)}, bf16[4,64,128]{2,1,0:T(8,128)(2,1)S(1)}, u32[]{:S(2)}, u32[]{:S(2)}) %collective-permute-start.5) | collective-permute-done | bytes 65568 | tf_op jit(solution)/shard_map/ppermute | solution.py:50
  23.0 0.7 collective-permute-done.6
  23.7 2.3 %collective-permute-start.7 = (bf16[16,64,128]{2,1,0:T(8,128)(2,1)S(1)}, bf16[16,64,128]{2,1,0:T(8,128)(2,1)S(1)}, u32[]{:S(2)}, u32[]{:S(2)}) collective-permute-start(bf16[16,64,128]{2,1,0:T(8,128)(2,1)S(1)} %constant_dynamic-update-slice_fusion.p0), channel_id=1, source_target_pairs={{0,192},{2,50},{16,208},{18,2},{32,224},{34,18},{48,240},{50,34},{... | collective-permute-start | bytes 786440 | tf_op jit(solution)/shard_map/ppermute | solution.py:50
  27.1 1.6 %collective-permute-start.12 = (bf16[256,512]{1,0:T(8,128)(2,1)S(1)}, bf16[256,512]{1,0:T(8,128)(2,1)S(1)}, u32[]{:S(2)}, u32[]{:S(2)}) collective-permute-start(bf16[256,512]{1,0:T(8,128)(2,1)S(1)} %bitcast.14), channel_id=1, source_target_pairs={{0,1},{1,0},{2,3},{3,2},{4,5},{5,4},{6,7},{7,6},{8,9},{9,8},{10,11... | collective-permute-start | bytes 786440 | tf_op jit(solution)/shard_map/ppermute | solution.py:25
  29.5 2.6 %collective-permute-done.7.p1 = bf16[16,64,128]{2,1,0:T(8,128)(2,1)S(1)} collective-permute-done((bf16[16,64,128]{2,1,0:T(8,128)(2,1)S(1)}, bf16[16,64,128]{2,1,0:T(8,128)(2,1)S(1)}, u32[]{:S(2)}, u32[]{:S(2)}) %collective-permute-start.7) | collective-permute-done | bytes 262176 | tf_op jit(solution)/shard_map/ppermute | solution.py:50
  32.1 0.9 %collective-permute-done.8.p2 = bf16[16,64,128]{2,1,0:T(8,128)(2,1)S(1)} collective-permute-done((bf16[16,64,128]{2,1,0:T(8,128)(2,1)S(1)}, bf16[16,64,128]{2,1,0:T(8,128)(2,1)S(1)}, u32[]{:S(2)}, u32[]{:S(2)}) %collective-permute-start.8) | collective-permute-done | bytes 262176 | tf_op jit(solution)/shard_map/ppermute | solution.py:50
  33.0 2.8 %collective-permute-done.9.p3 = bf16[16,64,128]{2,1,0:T(8,128)(2,1)S(1)} collective-permute-done((bf16[16,64,128]{2,1,0:T(8,128)(2,1)S(1)}, bf16[16,64,128]{2,1,0:T(8,128)(2,1)S(1)}, u32[]{:S(2)}, u32[]{:S(2)}) %collective-permute-start.9) | collective-permute-done | bytes 262176 | tf_op jit(solution)/shard_map/ppermute | solution.py:50
  35.8 0.9 shard_map.82
  36.7 2.6 %collective-permute-start.10 = (bf16[6,64,128]{2,1,0:T(8,128)(2,1)S(1)}, bf16[6,64,128]{2,1,0:T(8,128)(2,1)S(1)}, u32[]{:S(2)}, u32[]{:S(2)}) collective-permute-start(bf16[6,64,128]{2,1,0:T(8,128)(2,1)S(1)} %get-tuple-element.32), channel_id=1, source_target_pairs={{0,2},{2,0},{1,3},{3,1},{4,6},{6,4},{5,7},{7,5},{8,10},{10,8},{9,1... | collective-permute-start | bytes 294920 | tf_op jit(solution)/shard_map/ppermute | solution.py:25
  39.3 0.9 %collective-permute-done.10.other_picked = bf16[6,64,128]{2,1,0:T(8,128)(2,1)S(1)} collective-permute-done((bf16[6,64,128]{2,1,0:T(8,128)(2,1)S(1)}, bf16[6,64,128]{2,1,0:T(8,128)(2,1)S(1)}, u32[]{:S(2)}, u32[]{:S(2)}) %collective-permute-start.10) | collective-permute-done | bytes 98336 | tf_op jit(solution)/shard_map/ppermute | solution.py:25
  40.3 1.6 %shard_map.83 = (f32[6,64,128]{2,1,0:T(8,128)S(1)}, f32[6,64,128]{2,1,0:T(8,128)S(1)}) custom-call(s32[6]{0:T(128)S(1)} %stack.35.where, bf16[6,64,128]{2,1,0:T(8,128)(2,1)S(1)} %get-tuple-element.31.own_picked, bf16[6,64,128]{2,1,0:T(8,128)(2,1)S(1)} %collective-permute-done.10.other_picked, bf16[256,768]{1,0:T(8,128)(2,1)S(1)} %bitcast.13, ...), custom_call_target="tpu_custom_call" | custom-call | tf_op jit(solution)/shard_map/pallas_call | solution.py:234
  42.3 1.1 %collective-permute-done.13.arrived = f32[6,64,128]{2,1,0:T(8,128)S(1)} collective-permute-done((f32[6,64,128]{2,1,0:T(8,128)S(1)}, f32[6,64,128]{2,1,0:T(8,128)S(1)}, u32[]{:S(2)}, u32[]{:S(2)}) %collective-permute-start.13) | collective-permute-done | bytes 196640 | tf_op jit(solution)/shard_map/ppermute | solution.py:25
  43.4 1.1 %shard_map.84 = (f32[16,64,128]{2,1,0:T(8,128)S(1)}, bf16[16,64,128]{2,1,0:T(8,128)(2,1)S(1)}, bf16[16,64,128]{2,1,0:T(8,128)(2,1)S(1)}, bf16[16,64,128]{2,1,0:T(8,128)(2,1)S(1)}) custom-call(s32[6]{0:T(128)S(1)} %stack.35.where, s32[1,6]{1,0:T(1,128)S(1)} %copy-done.4, s32[1,6]{1,0:T(1,128)S(1)} %collective-permute-done.3.other_ids, ...), custom_call_target="tpu_custom_call" | custom-call | tf_op jit(solution)/shard_map/pallas_call | solution.py:243
  44.8 1.0 %collective-permute-start.15 = (bf16[16,64,128]{2,1,0:T(8,128)(2,1)S(1)}, bf16[16,64,128]{2,1,0:T(8,128)(2,1)S(1)}, u32[]{:S(2)}, u32[]{:S(2)}) collective-permute-start(bf16[16,64,128]{2,1,0:T(8,128)(2,1)S(1)} %get-tuple-element.39), channel_id=1, source_target_pairs={{0,128},{2,34},{16,144},{18,50},{32,160},{34,2},{48,176},{50,18},{... | collective-permute-start | bytes 786440 | tf_op jit(solution)/shard_map/ppermute | solution.py:50
  46.4 3.6 %collective-permute-done.16 = bf16[16,64,128]{2,1,0:T(8,128)(2,1)S(1)} collective-permute-done((bf16[16,64,128]{2,1,0:T(8,128)(2,1)S(1)}, bf16[16,64,128]{2,1,0:T(8,128)(2,1)S(1)}, u32[]{:S(2)}, u32[]{:S(2)}) %collective-permute-start.16) | collective-permute-done | bytes 262176 | tf_op jit(solution)/shard_map/ppermute | solution.py:50
  50.0 1.8 %collective-permute-done.15 = bf16[16,64,128]{2,1,0:T(8,128)(2,1)S(1)} collective-permute-done((bf16[16,64,128]{2,1,0:T(8,128)(2,1)S(1)}, bf16[16,64,128]{2,1,0:T(8,128)(2,1)S(1)}, u32[]{:S(2)}, u32[]{:S(2)}) %collective-permute-start.15) | collective-permute-done | bytes 262176 | tf_op jit(solution)/shard_map/ppermute | solution.py:50
  51.9 2.8 %collective-permute-done.14 = bf16[16,64,128]{2,1,0:T(8,128)(2,1)S(1)} collective-permute-done((bf16[16,64,128]{2,1,0:T(8,128)(2,1)S(1)}, bf16[16,64,128]{2,1,0:T(8,128)(2,1)S(1)}, u32[]{:S(2)}, u32[]{:S(2)}) %collective-permute-start.14) | collective-permute-done | bytes 262176 | tf_op jit(solution)/shard_map/ppermute | solution.py:50
  55.2 0.9 collective-permute-start.18
  56.5 1.6 %collective-permute-done.19 = bf16[4,64,128]{2,1,0:T(8,128)(2,1)S(1)} collective-permute-done((bf16[4,64,128]{2,1,0:T(8,128)(2,1)S(1)}, bf16[4,64,128]{2,1,0:T(8,128)(2,1)S(1)}, u32[]{:S(2)}, u32[]{:S(2)}) %collective-permute-start.19) | collective-permute-done | bytes 65568 | tf_op jit(solution)/shard_map/ppermute | solution.py:50
  58.0 1.8 %collective-permute-done.18 = bf16[4,64,128]{2,1,0:T(8,128)(2,1)S(1)} collective-permute-done((bf16[4,64,128]{2,1,0:T(8,128)(2,1)S(1)}, bf16[4,64,128]{2,1,0:T(8,128)(2,1)S(1)}, u32[]{:S(2)}, u32[]{:S(2)}) %collective-permute-start.18) | collective-permute-done | bytes 65568 | tf_op jit(solution)/shard_map/ppermute | solution.py:50
  59.9 0.7 collective-permute-done.17
  60.6 4.2 %collective-permute-start.22 = (bf16[4,64,128]{2,1,0:T(8,128)(2,1)S(1)}, bf16[4,64,128]{2,1,0:T(8,128)(2,1)S(1)}, u32[]{:S(2)}, u32[]{:S(2)}) collective-permute-start(bf16[4,64,128]{2,1,0:T(8,128)(2,1)S(1)} %fusion.3), channel_id=1, source_target_pairs={{0,4},{2,14},{4,0},{6,10},{8,12},{10,6},{12,8},{14,2},{1,5},{3,15}... | collective-permute-start | bytes 196616 | tf_op jit(solution)/shard_map/ppermute | solution.py:59
  64.9 1.8 %collective-permute-done.22 = bf16[4,64,128]{2,1,0:T(8,128)(2,1)S(1)} collective-permute-done((bf16[4,64,128]{2,1,0:T(8,128)(2,1)S(1)}, bf16[4,64,128]{2,1,0:T(8,128)(2,1)S(1)}, u32[]{:S(2)}, u32[]{:S(2)}) %collective-permute-start.22) | collective-permute-done | bytes 65568 | tf_op jit(solution)/shard_map/ppermute | solution.py:59
  66.7 1.9 %collective-permute-start.23 = (bf16[4,64,128]{2,1,0:T(8,128)(2,1)S(1)}, bf16[4,64,128]{2,1,0:T(8,128)(2,1)S(1)}, u32[]{:S(2)}, u32[]{:S(2)}) collective-permute-start(bf16[4,64,128]{2,1,0:T(8,128)(2,1)S(1)} %fusion.4), channel_id=1, source_target_pairs={{0,12},{2,6},{4,8},{6,2},{8,4},{10,14},{12,0},{14,10},{1,13},{3,7}... | collective-permute-start | bytes 196616 | tf_op jit(solution)/shard_map/ppermute | solution.py:59
  68.5 0.8 collective-permute-start.20
  69.3 2.5 %collective-permute-start.21 = (bf16[64,2048]{1,0:T(8,128)(2,1)S(1)}, bf16[64,2048]{1,0:T(8,128)(2,1)S(1)}, u32[]{:S(2)}, u32[]{:S(2)}) collective-permute-start(bf16[64,2048]{1,0:T(8,128)(2,1)S(1)} %get-tuple-element.42), channel_id=1, source_target_pairs={{0,192},{64,0},{128,64},{192,128},{1,193},{65,1},{129,65},{193,129... | collective-permute-start | bytes 786440 | tf_op jit(solution)/shard_map/ppermute | solution.py:33
  72.6 0.8 collective-permute-start.26
  73.3 1.9 %collective-permute-done.24.refs_1_ = bf16[4,64,128]{2,1,0:T(8,128)(2,1)S(1)} collective-permute-done((bf16[4,64,128]{2,1,0:T(8,128)(2,1)S(1)}, bf16[4,64,128]{2,1,0:T(8,128)(2,1)S(1)}, u32[]{:S(2)}, u32[]{:S(2)}) %collective-permute-start.24) | collective-permute-done | bytes 65568 | tf_op jit(solution)/shard_map/ppermute | solution.py:29
  75.3 4.9 %collective-permute-start.27 = (bf16[4,64,128]{2,1,0:T(8,128)(2,1)S(1)}, bf16[4,64,128]{2,1,0:T(8,128)(2,1)S(1)}, u32[]{:S(2)}, u32[]{:S(2)}) collective-permute-start(bf16[4,64,128]{2,1,0:T(8,128)(2,1)S(1)} %fusion.2.refs_0_), channel_id=1, source_target_pairs={{0,2},{2,0},{1,3},{3,1},{4,6},{6,4},{5,7},{7,5},{8,10},{10,8},{9,1... | collective-permute-start | bytes 196616 | tf_op jit(solution)/shard_map/ppermute | solution.py:25
  80.2 3.0 %collective-permute-start.28 = (bf16[4,64,128]{2,1,0:T(8,128)(2,1)S(1)}, bf16[4,64,128]{2,1,0:T(8,128)(2,1)S(1)}, u32[]{:S(2)}, u32[]{:S(2)}) collective-permute-start(bf16[4,64,128]{2,1,0:T(8,128)(2,1)S(1)} %collective-permute-done.24.refs_1_), channel_id=1, source_target_pairs={{0,2},{2,0},{1,3},{3,1},{4,6},{6,4},{5,7},{7,5},{8,10},{10,8},{9,1... | collective-permute-start | bytes 196616 | tf_op jit(solution)/shard_map/ppermute | solution.py:25
  83.2 0.7 collective-permute-start.29
  84.1 0.7 collective-permute-done.29.refs_6_
  85.2 1.1 %shard_map.85 = (f32[64,128]{1,0:T(8,128)S(1)}, f32[64,128]{1,0:T(8,128)S(1)}, f32[64,128]{1,0:T(8,128)S(1)}, f32[64,128]{1,0:T(8,128)S(1)}) custom-call(s32[6]{0:T(128)S(1)} %stack.35.where, f32[64,128]{1,0:T(8,128)S(1)} %copy-done.1, bf16[64,8192]{1,0:T(8,128)(2,1)S(1)} %copy-done, bf16[64,2048]{1,0:T(8,128)(2,1)S(1)} %collective-permute-done.2.b1, ...), custom_call_target="tpu_custom_call" | custom-call | tf_op jit(solution)/shard_map/pallas_call | solution.py:268
  86.4 2.7 %collective-permute-start.32 = (f32[64,128]{1,0:T(8,128)S(1)}, f32[64,128]{1,0:T(8,128)S(1)}, u32[]{:S(2)}, u32[]{:S(2)}) collective-permute-start(f32[64,128]{1,0:T(8,128)S(1)} %get-tuple-element.49), channel_id=1, source_target_pairs={{0,128},{64,192},{128,0},{192,64},{1,129},{65,193},{129,1},{193,65... | collective-permute-start | bytes 98312 | tf_op jit(solution)/shard_map/ppermute | solution.py:29
  89.4 0.9 collective-permute-done.33
  90.9 1.3 %collective-permute-done.31 = f32[64,128]{1,0:T(8,128)S(1)} collective-permute-done((f32[64,128]{1,0:T(8,128)S(1)}, f32[64,128]{1,0:T(8,128)S(1)}, u32[]{:S(2)}, u32[]{:S(2)}) %collective-permute-start.31) | collective-permute-done | bytes 32800 | tf_op jit(solution)/shard_map/ppermute | solution.py:29
  92.2 0.6 add_add_fusion
  (58 shorter events, 6.4 us)
Async XLA Ops:
  0.8 9.5 %collective-permute-start = (bf16[64,128]{1,0:T(8,128)(2,1)S(1)}, bf16[64,128]{1,0:T(8,128)(2,1)S(1)}, u32[]{:S(2)}, u32[]{:S(2)}) collective-permute-start(bf16[64,128]{1,0:T(8,128)(2,1)S(1)} %convert_element_type.39), channel_id=1, source_target_pairs={{0,4},{2,14},{4,0},{6,10},{8,12},{10,6},{12,8},{14,2},{1,5},{3,15}... | collective-permute-start | bytes 49160 | tf_op jit(solution)/shard_map/ppermute | solution.py:59
  7.6 2.6 %copy-start.1 = (f32[64,128]{1,0:T(8,128)S(1)}, f32[64,128]{1,0:T(8,128)}, u32[]{:S(2)}) copy-start(f32[64,128]{1,0:T(8,128)} %start.1) | copy-start | bytes 98308
  7.6 11.5 %copy-start.2 = (bf16[1,256,768]{2,1,0:T(8,128)(2,1)S(1)}, bf16[1,256,768]{2,1,0:T(8,128)(2,1)}, u32[]{:S(2)}) copy-start(bf16[1,256,768]{2,1,0:T(8,128)(2,1)} %param.12) | copy-start | bytes 1179652
  8.8 7.7 %collective-permute-start.2 = (bf16[64,2048]{1,0:T(8,128)(2,1)S(1)}, bf16[64,2048]{1,0:T(8,128)(2,1)S(1)}, u32[]{:S(2)}, u32[]{:S(2)}) collective-permute-start(bf16[64,2048]{1,0:T(8,128)(2,1)S(1)} %get-tuple-element.55), channel_id=1, source_target_pairs={{0,64},{64,128},{128,192},{192,0},{1,65},{65,129},{129,193},{193,1... | collective-permute-start | bytes 786440 | tf_op jit(solution)/shard_map/ppermute | solution.py:33
  10.2 1.3 %copy-start.4 = (s32[1,6]{1,0:T(1,128)S(1)}, s32[1,6]{1,0:T(1,128)}, u32[]{:S(2)}) copy-start(s32[1,6]{1,0:T(1,128)} %own_ids.3) | copy-start | bytes 76
  10.3 4.0 %collective-permute-start.1 = (bf16[2,64,128]{2,1,0:T(8,128)(2,1)S(1)}, bf16[2,64,128]{2,1,0:T(8,128)(2,1)S(1)}, u32[]{:S(2)}, u32[]{:S(2)}) collective-permute-start(bf16[2,64,128]{2,1,0:T(8,128)(2,1)S(1)} %pad_maximum_fusion.1), channel_id=1, source_target_pairs={{0,12},{2,6},{4,8},{6,2},{8,4},{10,14},{12,0},{14,10},{1,13},{3,7}... | collective-permute-start | bytes 98312 | tf_op jit(solution)/shard_map/ppermute | solution.py:59
  11.5 2.8 %collective-permute-start.3 = (s32[1,6]{1,0:T(1,128)S(1)}, s32[1,6]{1,0:T(1,128)S(1)}, u32[]{:S(2)}, u32[]{:S(2)}) collective-permute-start(s32[1,6]{1,0:T(1,128)S(1)} %copy-done.4), channel_id=1, source_target_pairs={{0,2},{2,0},{1,3},{3,1},{4,6},{6,4},{5,7},{7,5},{8,10},{10,8},{9,1... | collective-permute-start | bytes 80 | tf_op jit(solution)/shard_map/ppermute | solution.py:25
  16.5 10.5 %copy-start.3 = (bf16[1,256,512]{2,1,0:T(8,128)(2,1)S(1)}, bf16[1,256,512]{2,1,0:T(8,128)(2,1)}, u32[]{:S(2)}) copy-start(bf16[1,256,512]{2,1,0:T(8,128)(2,1)} %param.13) | copy-start | bytes 786436
  16.6 4.2 %collective-permute-start.4 = (bf16[4,64,128]{2,1,0:T(8,128)(2,1)S(1)}, bf16[4,64,128]{2,1,0:T(8,128)(2,1)S(1)}, u32[]{:S(2)}, u32[]{:S(2)}) collective-permute-start(bf16[4,64,128]{2,1,0:T(8,128)(2,1)S(1)} %pad_maximum_fusion), channel_id=1, source_target_pairs={{0,48},{2,194},{16,0},{18,210},{32,16},{34,226},{48,32},{50,242},{... | collective-permute-start | bytes 196616 | tf_op jit(solution)/shard_map/ppermute | solution.py:50
  18.1 4.9 %collective-permute-start.5 = (bf16[4,64,128]{2,1,0:T(8,128)(2,1)S(1)}, bf16[4,64,128]{2,1,0:T(8,128)(2,1)S(1)}, u32[]{:S(2)}, u32[]{:S(2)}) collective-permute-start(bf16[4,64,128]{2,1,0:T(8,128)(2,1)S(1)} %pad_maximum_fusion), channel_id=1, source_target_pairs={{0,32},{2,130},{16,48},{18,146},{32,0},{34,162},{48,16},{50,178},{... | collective-permute-start | bytes 196616 | tf_op jit(solution)/shard_map/ppermute | solution.py:50
  18.4 5.3 %collective-permute-start.6 = (bf16[4,64,128]{2,1,0:T(8,128)(2,1)S(1)}, bf16[4,64,128]{2,1,0:T(8,128)(2,1)S(1)}, u32[]{:S(2)}, u32[]{:S(2)}) collective-permute-start(bf16[4,64,128]{2,1,0:T(8,128)(2,1)S(1)} %pad_maximum_fusion), channel_id=1, source_target_pairs={{0,16},{2,66},{16,32},{18,82},{32,48},{34,98},{48,0},{50,114},{64,... | collective-permute-start | bytes 196616 | tf_op jit(solution)/shard_map/ppermute | solution.py:50
  19.1 20.2 %collective-permute-start.11 = (bf16[256,768]{1,0:T(8,128)(2,1)S(1)}, bf16[256,768]{1,0:T(8,128)(2,1)S(1)}, u32[]{:S(2)}, u32[]{:S(2)}) collective-permute-start(bf16[256,768]{1,0:T(8,128)(2,1)S(1)} %bitcast.12), channel_id=1, source_target_pairs={{0,1},{1,0},{2,3},{3,2},{4,5},{5,4},{6,7},{7,6},{8,9},{9,8},{10,11... | collective-permute-start | bytes 1179656 | tf_op jit(solution)/shard_map/ppermute | solution.py:25
  23.7 8.4 %collective-permute-start.7 = (bf16[16,64,128]{2,1,0:T(8,128)(2,1)S(1)}, bf16[16,64,128]{2,1,0:T(8,128)(2,1)S(1)}, u32[]{:S(2)}, u32[]{:S(2)}) collective-permute-start(bf16[16,64,128]{2,1,0:T(8,128)(2,1)S(1)} %constant_dynamic-update-slice_fusion.p0), channel_id=1, source_target_pairs={{0,192},{2,50},{16,208},{18,2},{32,224},{34,18},{48,240},{50,34},{... | collective-permute-start | bytes 786440 | tf_op jit(solution)/shard_map/ppermute | solution.py:50
  26.0 7.1 %collective-permute-start.8 = (bf16[16,64,128]{2,1,0:T(8,128)(2,1)S(1)}, bf16[16,64,128]{2,1,0:T(8,128)(2,1)S(1)}, u32[]{:S(2)}, u32[]{:S(2)}) collective-permute-start(bf16[16,64,128]{2,1,0:T(8,128)(2,1)S(1)} %constant_dynamic-update-slice_fusion.p0), channel_id=1, source_target_pairs={{0,128},{2,34},{16,144},{18,50},{32,160},{34,2},{48,176},{50,18},{... | collective-permute-start | bytes 786440 | tf_op jit(solution)/shard_map/ppermute | solution.py:50
  26.5 9.3 %collective-permute-start.9 = (bf16[16,64,128]{2,1,0:T(8,128)(2,1)S(1)}, bf16[16,64,128]{2,1,0:T(8,128)(2,1)S(1)}, u32[]{:S(2)}, u32[]{:S(2)}) collective-permute-start(bf16[16,64,128]{2,1,0:T(8,128)(2,1)S(1)} %constant_dynamic-update-slice_fusion.p0), channel_id=1, source_target_pairs={{0,64},{2,18},{16,80},{18,34},{32,96},{34,50},{48,112},{50,2},{64,... | collective-permute-start | bytes 786440 | tf_op jit(solution)/shard_map/ppermute | solution.py:50
  27.1 12.2 %collective-permute-start.12 = (bf16[256,512]{1,0:T(8,128)(2,1)S(1)}, bf16[256,512]{1,0:T(8,128)(2,1)S(1)}, u32[]{:S(2)}, u32[]{:S(2)}) collective-permute-start(bf16[256,512]{1,0:T(8,128)(2,1)S(1)} %bitcast.14), channel_id=1, source_target_pairs={{0,1},{1,0},{2,3},{3,2},{4,5},{5,4},{6,7},{7,6},{8,9},{9,8},{10,11... | collective-permute-start | bytes 786440 | tf_op jit(solution)/shard_map/ppermute | solution.py:25
  36.7 3.6 %collective-permute-start.10 = (bf16[6,64,128]{2,1,0:T(8,128)(2,1)S(1)}, bf16[6,64,128]{2,1,0:T(8,128)(2,1)S(1)}, u32[]{:S(2)}, u32[]{:S(2)}) collective-permute-start(bf16[6,64,128]{2,1,0:T(8,128)(2,1)S(1)} %get-tuple-element.32), channel_id=1, source_target_pairs={{0,2},{2,0},{1,3},{3,1},{4,6},{6,4},{5,7},{7,5},{8,10},{10,8},{9,1... | collective-permute-start | bytes 294920 | tf_op jit(solution)/shard_map/ppermute | solution.py:25
  41.8 1.5 %collective-permute-start.13 = (f32[6,64,128]{2,1,0:T(8,128)S(1)}, f32[6,64,128]{2,1,0:T(8,128)S(1)}, u32[]{:S(2)}, u32[]{:S(2)}) collective-permute-start(f32[6,64,128]{2,1,0:T(8,128)S(1)} %get-tuple-element.36), channel_id=1, source_target_pairs={{0,2},{2,0},{1,3},{3,1},{4,6},{6,4},{5,7},{7,5},{8,10},{10,8},{9,1... | collective-permute-start | bytes 589832 | tf_op jit(solution)/shard_map/ppermute | solution.py:25
  44.4 5.6 %collective-permute-start.16 = (bf16[16,64,128]{2,1,0:T(8,128)(2,1)S(1)}, bf16[16,64,128]{2,1,0:T(8,128)(2,1)S(1)}, u32[]{:S(2)}, u32[]{:S(2)}) collective-permute-start(bf16[16,64,128]{2,1,0:T(8,128)(2,1)S(1)} %get-tuple-element.40), channel_id=1, source_target_pairs={{0,192},{2,50},{16,208},{18,2},{32,224},{34,18},{48,240},{50,34},{... | collective-permute-start | bytes 786440 | tf_op jit(solution)/shard_map/ppermute | solution.py:50
  44.8 7.1 %collective-permute-start.15 = (bf16[16,64,128]{2,1,0:T(8,128)(2,1)S(1)}, bf16[16,64,128]{2,1,0:T(8,128)(2,1)S(1)}, u32[]{:S(2)}, u32[]{:S(2)}) collective-permute-start(bf16[16,64,128]{2,1,0:T(8,128)(2,1)S(1)} %get-tuple-element.39), channel_id=1, source_target_pairs={{0,128},{2,34},{16,144},{18,50},{32,160},{34,2},{48,176},{50,18},{... | collective-permute-start | bytes 786440 | tf_op jit(solution)/shard_map/ppermute | solution.py:50
  45.8 8.8 %collective-permute-start.14 = (bf16[16,64,128]{2,1,0:T(8,128)(2,1)S(1)}, bf16[16,64,128]{2,1,0:T(8,128)(2,1)S(1)}, u32[]{:S(2)}, u32[]{:S(2)}) collective-permute-start(bf16[16,64,128]{2,1,0:T(8,128)(2,1)S(1)} %get-tuple-element.38), channel_id=1, source_target_pairs={{0,64},{2,18},{16,80},{18,34},{32,96},{34,50},{48,112},{50,2},{64,... | collective-permute-start | bytes 786440 | tf_op jit(solution)/shard_map/ppermute | solution.py:50
  54.8 1.6 %copy-start.5 = (f32[64,128]{1,0:T(8,128)S(1)}, f32[64,128]{1,0:T(8,128)}, u32[]{:S(2)}) copy-start(f32[64,128]{1,0:T(8,128)} %param.9) | copy-start | bytes 98308
  54.8 3.2 %collective-permute-start.19 = (bf16[4,64,128]{2,1,0:T(8,128)(2,1)S(1)}, bf16[4,64,128]{2,1,0:T(8,128)(2,1)S(1)}, u32[]{:S(2)}, u32[]{:S(2)}) collective-permute-start(bf16[4,64,128]{2,1,0:T(8,128)(2,1)S(1)} %get-tuple-element.57), channel_id=1, source_target_pairs={{0,48},{2,194},{16,0},{18,210},{32,16},{34,226},{48,32},{50,242},{... | collective-permute-start | bytes 196616 | tf_op jit(solution)/shard_map/ppermute | solution.py:50
  55.2 1.2 %copy-start.6 = (f32[64]{0:T(128)S(1)}, f32[64]{0:T(128)}, u32[]{:S(2)}) copy-start(f32[64]{0:T(128)} %param.10) | copy-start | bytes 772
  55.2 4.6 %collective-permute-start.18 = (bf16[4,64,128]{2,1,0:T(8,128)(2,1)S(1)}, bf16[4,64,128]{2,1,0:T(8,128)(2,1)S(1)}, u32[]{:S(2)}, u32[]{:S(2)}) collective-permute-start(bf16[4,64,128]{2,1,0:T(8,128)(2,1)S(1)} %get-tuple-element.58), channel_id=1, source_target_pairs={{0,32},{2,130},{16,48},{18,146},{32,0},{34,162},{48,16},{50,178},{... | collective-permute-start | bytes 196616 | tf_op jit(solution)/shard_map/ppermute | solution.py:50
  56.1 4.4 %collective-permute-start.17 = (bf16[4,64,128]{2,1,0:T(8,128)(2,1)S(1)}, bf16[4,64,128]{2,1,0:T(8,128)(2,1)S(1)}, u32[]{:S(2)}, u32[]{:S(2)}) collective-permute-start(bf16[4,64,128]{2,1,0:T(8,128)(2,1)S(1)} %get-tuple-element.56), channel_id=1, source_target_pairs={{0,16},{2,66},{16,32},{18,82},{32,48},{34,98},{48,0},{50,114},{64,... | collective-permute-start | bytes 196616 | tf_op jit(solution)/shard_map/ppermute | solution.py:50
  56.5 28.7 %copy-start = (bf16[64,8192]{1,0:T(8,128)(2,1)S(1)}, bf16[64,8192]{1,0:T(8,128)(2,1)}, u32[]{:S(2)}) copy-start(bf16[64,8192]{1,0:T(8,128)(2,1)} %precond.1) | copy-start | bytes 3145732
  60.6 6.0 %collective-permute-start.22 = (bf16[4,64,128]{2,1,0:T(8,128)(2,1)S(1)}, bf16[4,64,128]{2,1,0:T(8,128)(2,1)S(1)}, u32[]{:S(2)}, u32[]{:S(2)}) collective-permute-start(bf16[4,64,128]{2,1,0:T(8,128)(2,1)S(1)} %fusion.3), channel_id=1, source_target_pairs={{0,4},{2,14},{4,0},{6,10},{8,12},{10,6},{12,8},{14,2},{1,5},{3,15}... | collective-permute-start | bytes 196616 | tf_op jit(solution)/shard_map/ppermute | solution.py:59
  66.7 5.1 %collective-permute-start.23 = (bf16[4,64,128]{2,1,0:T(8,128)(2,1)S(1)}, bf16[4,64,128]{2,1,0:T(8,128)(2,1)S(1)}, u32[]{:S(2)}, u32[]{:S(2)}) collective-permute-start(bf16[4,64,128]{2,1,0:T(8,128)(2,1)S(1)} %fusion.4), channel_id=1, source_target_pairs={{0,12},{2,6},{4,8},{6,2},{8,4},{10,14},{12,0},{14,10},{1,13},{3,7}... | collective-permute-start | bytes 196616 | tf_op jit(solution)/shard_map/ppermute | solution.py:59
  68.5 15.4 %collective-permute-start.20 = (bf16[64,2048]{1,0:T(8,128)(2,1)S(1)}, bf16[64,2048]{1,0:T(8,128)(2,1)S(1)}, u32[]{:S(2)}, u32[]{:S(2)}) collective-permute-start(bf16[64,2048]{1,0:T(8,128)(2,1)S(1)} %get-tuple-element.41), channel_id=1, source_target_pairs={{0,128},{64,192},{128,0},{192,64},{1,129},{65,193},{129,1},{193,65... | collective-permute-start | bytes 786440 | tf_op jit(solution)/shard_map/ppermute | solution.py:33
  69.3 14.7 %collective-permute-start.21 = (bf16[64,2048]{1,0:T(8,128)(2,1)S(1)}, bf16[64,2048]{1,0:T(8,128)(2,1)S(1)}, u32[]{:S(2)}, u32[]{:S(2)}) collective-permute-start(bf16[64,2048]{1,0:T(8,128)(2,1)S(1)} %get-tuple-element.42), channel_id=1, source_target_pairs={{0,192},{64,0},{128,64},{192,128},{1,193},{65,1},{129,65},{193,129... | collective-permute-start | bytes 786440 | tf_op jit(solution)/shard_map/ppermute | solution.py:33
  71.8 3.5 %collective-permute-start.24 = (bf16[4,64,128]{2,1,0:T(8,128)(2,1)S(1)}, bf16[4,64,128]{2,1,0:T(8,128)(2,1)S(1)}, u32[]{:S(2)}, u32[]{:S(2)}) collective-permute-start(bf16[4,64,128]{2,1,0:T(8,128)(2,1)S(1)} %fusion.2.refs_0_), channel_id=1, source_target_pairs={{0,48},{16,0},{32,16},{48,32},{1,49},{17,1},{33,17},{49,33},{2,50}... | collective-permute-start | bytes 196616 | tf_op jit(solution)/shard_map/ppermute | solution.py:29
  72.1 8.1 %collective-permute-start.25 = (bf16[4,64,128]{2,1,0:T(8,128)(2,1)S(1)}, bf16[4,64,128]{2,1,0:T(8,128)(2,1)S(1)}, u32[]{:S(2)}, u32[]{:S(2)}) collective-permute-start(bf16[4,64,128]{2,1,0:T(8,128)(2,1)S(1)} %fusion.2.refs_0_), channel_id=1, source_target_pairs={{0,32},{16,48},{32,0},{48,16},{1,33},{17,49},{33,1},{49,17},{2,34}... | collective-permute-start | bytes 196616 | tf_op jit(solution)/shard_map/ppermute | solution.py:29
  72.6 10.7 %collective-permute-start.26 = (bf16[4,64,128]{2,1,0:T(8,128)(2,1)S(1)}, bf16[4,64,128]{2,1,0:T(8,128)(2,1)S(1)}, u32[]{:S(2)}, u32[]{:S(2)}) collective-permute-start(bf16[4,64,128]{2,1,0:T(8,128)(2,1)S(1)} %fusion.2.refs_0_), channel_id=1, source_target_pairs={{0,16},{16,32},{32,48},{48,0},{1,17},{17,33},{33,49},{49,1},{2,18}... | collective-permute-start | bytes 196616 | tf_op jit(solution)/shard_map/ppermute | solution.py:29
  75.3 8.7 %collective-permute-start.27 = (bf16[4,64,128]{2,1,0:T(8,128)(2,1)S(1)}, bf16[4,64,128]{2,1,0:T(8,128)(2,1)S(1)}, u32[]{:S(2)}, u32[]{:S(2)}) collective-permute-start(bf16[4,64,128]{2,1,0:T(8,128)(2,1)S(1)} %fusion.2.refs_0_), channel_id=1, source_target_pairs={{0,2},{2,0},{1,3},{3,1},{4,6},{6,4},{5,7},{7,5},{8,10},{10,8},{9,1... | collective-permute-start | bytes 196616 | tf_op jit(solution)/shard_map/ppermute | solution.py:25
  80.2 4.0 %collective-permute-start.28 = (bf16[4,64,128]{2,1,0:T(8,128)(2,1)S(1)}, bf16[4,64,128]{2,1,0:T(8,128)(2,1)S(1)}, u32[]{:S(2)}, u32[]{:S(2)}) collective-permute-start(bf16[4,64,128]{2,1,0:T(8,128)(2,1)S(1)} %collective-permute-done.24.refs_1_), channel_id=1, source_target_pairs={{0,2},{2,0},{1,3},{3,1},{4,6},{6,4},{5,7},{7,5},{8,10},{10,8},{9,1... | collective-permute-start | bytes 196616 | tf_op jit(solution)/shard_map/ppermute | solution.py:25
  83.2 1.6 %collective-permute-start.29 = (bf16[4,64,128]{2,1,0:T(8,128)(2,1)S(1)}, bf16[4,64,128]{2,1,0:T(8,128)(2,1)S(1)}, u32[]{:S(2)}, u32[]{:S(2)}) collective-permute-start(bf16[4,64,128]{2,1,0:T(8,128)(2,1)S(1)} %collective-permute-done.25.refs_2_), channel_id=1, source_target_pairs={{0,2},{2,0},{1,3},{3,1},{4,6},{6,4},{5,7},{7,5},{8,10},{10,8},{9,1... | collective-permute-start | bytes 196616 | tf_op jit(solution)/shard_map/ppermute | solution.py:25
  83.9 1.3 %collective-permute-start.30 = (bf16[4,64,128]{2,1,0:T(8,128)(2,1)S(1)}, bf16[4,64,128]{2,1,0:T(8,128)(2,1)S(1)}, u32[]{:S(2)}, u32[]{:S(2)}) collective-permute-start(bf16[4,64,128]{2,1,0:T(8,128)(2,1)S(1)} %collective-permute-done.26.refs_3_), channel_id=1, source_target_pairs={{0,2},{2,0},{1,3},{3,1},{4,6},{6,4},{5,7},{7,5},{8,10},{10,8},{9,1... | collective-permute-start | bytes 196616 | tf_op jit(solution)/shard_map/ppermute | solution.py:25
  86.3 4.1 %collective-permute-start.33 = (f32[64,128]{1,0:T(8,128)S(1)}, f32[64,128]{1,0:T(8,128)S(1)}, u32[]{:S(2)}, u32[]{:S(2)}) collective-permute-start(f32[64,128]{1,0:T(8,128)S(1)} %get-tuple-element.50), channel_id=1, source_target_pairs={{0,64},{64,128},{128,192},{192,0},{1,65},{65,129},{129,193},{193,1... | collective-permute-start | bytes 98312 | tf_op jit(solution)/shard_map/ppermute | solution.py:29
  86.4 4.5 %collective-permute-start.32 = (f32[64,128]{1,0:T(8,128)S(1)}, f32[64,128]{1,0:T(8,128)S(1)}, u32[]{:S(2)}, u32[]{:S(2)}) collective-permute-start(f32[64,128]{1,0:T(8,128)S(1)} %get-tuple-element.49), channel_id=1, source_target_pairs={{0,128},{64,192},{128,0},{192,64},{1,129},{65,193},{129,1},{193,65... | collective-permute-start | bytes 98312 | tf_op jit(solution)/shard_map/ppermute | solution.py:29
  89.1 3.1 %collective-permute-start.31 = (f32[64,128]{1,0:T(8,128)S(1)}, f32[64,128]{1,0:T(8,128)S(1)}, u32[]{:S(2)}, u32[]{:S(2)}) collective-permute-start(f32[64,128]{1,0:T(8,128)S(1)} %get-tuple-element.48), channel_id=1, source_target_pairs={{0,192},{64,0},{128,64},{192,128},{1,193},{65,1},{129,65},{193,129... | collective-permute-start | bytes 98312 | tf_op jit(solution)/shard_map/ppermute | solution.py:29

commit v14 on v13

--- a/solution.py
+++ b/solution.py
@@ -157,18 +157,19 @@
 
 
 def update_kernel(where, start, precond, b1, b2, b3, *refs):
-    pieces, (o0, o1, o2, o3, whole) = refs[:8], refs[8:]
+    mine, (early, late), (o0, o1, o2, o3, whole) = refs[:4], refs[4:6], refs[6:]
+    swapped = (early, 0), (late, 0), (late, RING), (early, RING)
     y, x, z, core = where[0], where[1], where[2], where[3]
     near, far = z ^ 1, RING - 1 - z
     for side in range(2):
         half = core if side == 0 else 1 - core
         slots = (z, jnp.where(half == 0, near, far), jnp.where(half == 0, far, near), far ^ 1)
         for i in range(RING):
-            piece = pieces[side * RING + i]
+            piece, skip = (mine[i], 0) if side == 0 else swapped[i]
             base = ((x + i) % RING) * 4
             for j in range(RING):
                 at = pl.multiple_of((base + slots[j]) * TILE + half * HALF, HALF)
-                whole[pl.ds(at, HALF), :] = piece[j]
+                whole[pl.ds(at, HALF), :] = piece[skip + j]
     operand = whole[...]
     span = operand.shape[0]
     own = precond[:, pl.ds(pl.multiple_of(y * span, span), span)]
@@ -263,11 +264,14 @@
     line = line + jnp.concatenate([met[2:], met[:2]])
 
     mine = ring_pieces(line.astype(BF16), X)
-    mine[0], mine[1] = lax.optimization_barrier((mine[0], mine[1]))
-    partners = [swap(piece, CORE) for piece in mine]
+    mine[1], mine[2], block2, block3 = lax.optimization_barrier((mine[1], mine[2], block2, block3))
+    partners = [
+        swap(jnp.concatenate([mine[0], mine[3]]), CORE),
+        swap(jnp.concatenate([mine[1], mine[2]]), CORE),
+    ]
     parts = call(
         update_kernel,
-        [SMEM] + [VMEM] * 13,
+        [SMEM] + [VMEM] * 11,
         [shape((rows, cols), F32)] * RING,
         [pltpu.VMEM((span, cols), BF16)],
     )(where, start_guess, preconditioner, block1, block2, block3, *mine, *partners)

time: 93 us -> 93.8 us (level)
  starting transfers between devices: 49.7 us -> 51 us
    ppermute x6, starting transfers between devices: 4.69 us -> 5.85 us  [from_ahead(): lax.ppermute(value, axis, [(i, (i - distance) % RING) for i in range(RING)])]
    ppermute x9 -> x7, waiting for transfers between devices: 3.28 us -> 3.03 us  [swap(): return lax.ppermute(value, axis, SWAP)]
    ppermute x9 -> x7, starting transfers between devices: 16.8 us -> 16.9 us  [swap(): return lax.ppermute(value, axis, SWAP)]
  transfers between devices with their start and end apart: 34 -> 32, of which waited for: 23 -> 21; matrix products, arithmetic and copies ran while one was open for 2% -> 2% of each run, Pallas kernels for 1% -> 1%
where the time goes in v14:
time: 93.8 us; the launch traced here: 93.6 us
  starting transfers between devices  51 us (54%)
  waiting for transfers between devices  34 us (36%)
  Pallas kernels  4.59 us (5%)
  other arithmetic  1.76 us (2%)
  local copies, waits for them, and re-layouts  1.42 us (2%)
    ppermute x12, waiting for transfers between devices, across(): return lax.ppermute(value, (Y, X, CORE), pairs)  21.5 us
    ppermute x7, starting transfers between devices, swap(): return lax.ppermute(value, axis, SWAP)  16.9 us
    ppermute x4, starting transfers between devices, pair(): return lax.ppermute(value, (Z, CORE), pairs)  14.2 us
    ppermute x12, starting transfers between devices, across(): return lax.ppermute(value, (Y, X, CORE), pairs)  9.48 us
    ppermute x6, starting transfers between devices, from_ahead(): lax.ppermute(value, axis, [(i, (i - distance) % RING) for i in range(RING)])  5.85 us
    ppermute x3, starting transfers between devices, to_ahead(): lax.ppermute(value, axis, [(i, (i + distance) % RING) for i in range(RING)])  4.6 us
    ppermute x6, waiting for transfers between devices, from_ahead(): lax.ppermute(value, axis, [(i, (i - distance) % RING) for i in range(RING)])  4.43 us
    ppermute x7, waiting for transfers between devices, swap(): return lax.ppermute(value, axis, SWAP)  3.03 us
  transfers between devices with their start and end apart: 32, of which 21 were waited for; matrix products, arithmetic and copies ran while one was open for 2% of the time, Pallas kernels for 1%

profile of v14, /device:TPU:1, one launch (start us, length us, event | category | flops | bytes accessed | tf_op | source)
XLA Modules:
  0.0 93.6 jit_solution(768057175922618051)
XLA Ops:
  0.0 0.8 convert_element_type.39
  0.8 6.8 %collective-permute-start = (bf16[64,128]{1,0:T(8,128)(2,1)S(1)}, bf16[64,128]{1,0:T(8,128)(2,1)S(1)}, u32[]{:S(2)}, u32[]{:S(2)}) collective-permute-start(bf16[64,128]{1,0:T(8,128)(2,1)S(1)} %convert_element_type.39), channel_id=1, source_target_pairs={{0,4},{2,14},{4,0},{6,10},{8,12},{10,6},{12,8},{14,2},{1,5},{3,15}... | collective-permute-start | bytes 49160 | tf_op jit(solution)/shard_map/ppermute | solution.py:59
  7.6 1.2 %constant_dynamic-slice_fusion = (bf16[64,2048]{1,0:T(8,128)(2,1)S(1)}, bf16[64,2048]{1,0:T(8,128)(2,1)S(1)}, bf16[64,2048]{1,0:T(8,128)(2,1)S(1)}) fusion(bf16[64,8192]{1,0:T(8,128)(2,1)} %precond.1, s32[]{:T(128)S(6)} %select_n.29, s32[]{:T(128)S(6)} %select_n.27, s32[]{:T(128)S(6)} %select_n.25), kind=kLoop, calls=%fused_computation.19 | loop fusion | bytes 1572876 | tf_op jit(solution)/shard_map/dynamic_slice | solution.py:217
  8.8 1.4 %collective-permute-start.2 = (bf16[64,2048]{1,0:T(8,128)(2,1)S(1)}, bf16[64,2048]{1,0:T(8,128)(2,1)S(1)}, u32[]{:S(2)}, u32[]{:S(2)}) collective-permute-start(bf16[64,2048]{1,0:T(8,128)(2,1)S(1)} %get-tuple-element.59), channel_id=1, source_target_pairs={{0,64},{64,128},{128,192},{192,0},{1,65},{65,129},{129,193},{193,1... | collective-permute-start | bytes 786440 | tf_op jit(solution)/shard_map/ppermute | solution.py:33
  10.3 1.3 %collective-permute-start.1 = (bf16[2,64,128]{2,1,0:T(8,128)(2,1)S(1)}, bf16[2,64,128]{2,1,0:T(8,128)(2,1)S(1)}, u32[]{:S(2)}, u32[]{:S(2)}) collective-permute-start(bf16[2,64,128]{2,1,0:T(8,128)(2,1)S(1)} %pad_maximum_fusion.3), channel_id=1, source_target_pairs={{0,12},{2,6},{4,8},{6,2},{8,4},{10,14},{12,0},{14,10},{1,13},{3,7}... | collective-permute-start | bytes 98312 | tf_op jit(solution)/shard_map/ppermute | solution.py:59
  11.5 1.8 %collective-permute-start.3 = (s32[1,6]{1,0:T(1,128)S(1)}, s32[1,6]{1,0:T(1,128)S(1)}, u32[]{:S(2)}, u32[]{:S(2)}) collective-permute-start(s32[1,6]{1,0:T(1,128)S(1)} %copy-done.4), channel_id=1, source_target_pairs={{0,2},{2,0},{1,3},{3,1},{4,6},{6,4},{5,7},{7,5},{8,10},{10,8},{9,1... | collective-permute-start | bytes 80 | tf_op jit(solution)/shard_map/ppermute | solution.py:25
  13.3 1.0 %collective-permute-done.1 = bf16[2,64,128]{2,1,0:T(8,128)(2,1)S(1)} collective-permute-done((bf16[2,64,128]{2,1,0:T(8,128)(2,1)S(1)}, bf16[2,64,128]{2,1,0:T(8,128)(2,1)S(1)}, u32[]{:S(2)}, u32[]{:S(2)}) %collective-permute-start.1) | collective-permute-done | bytes 32800 | tf_op jit(solution)/shard_map/ppermute | solution.py:59
  14.3 2.2 %collective-permute-done.2.b1 = bf16[64,2048]{1,0:T(8,128)(2,1)S(1)} collective-permute-done((bf16[64,2048]{1,0:T(8,128)(2,1)S(1)}, bf16[64,2048]{1,0:T(8,128)(2,1)S(1)}, u32[]{:S(2)}, u32[]{:S(2)}) %collective-permute-start.2) | collective-permute-done | bytes 262176 | tf_op jit(solution)/shard_map/ppermute | solution.py:33
  16.6 1.5 %collective-permute-start.4 = (bf16[4,64,128]{2,1,0:T(8,128)(2,1)S(1)}, bf16[4,64,128]{2,1,0:T(8,128)(2,1)S(1)}, u32[]{:S(2)}, u32[]{:S(2)}) collective-permute-start(bf16[4,64,128]{2,1,0:T(8,128)(2,1)S(1)} %pad_maximum_fusion.2), channel_id=1, source_target_pairs={{0,48},{2,194},{16,0},{18,210},{32,16},{34,226},{48,32},{50,242},{... | collective-permute-start | bytes 196616 | tf_op jit(solution)/shard_map/ppermute | solution.py:50
  18.4 0.7 collective-permute-start.6
  19.1 1.6 %collective-permute-start.11 = (bf16[256,768]{1,0:T(8,128)(2,1)S(1)}, bf16[256,768]{1,0:T(8,128)(2,1)S(1)}, u32[]{:S(2)}, u32[]{:S(2)}) collective-permute-start(bf16[256,768]{1,0:T(8,128)(2,1)S(1)} %bitcast.12), channel_id=1, source_target_pairs={{0,1},{1,0},{2,3},{3,2},{4,5},{5,4},{6,7},{7,6},{8,9},{9,8},{10,11... | collective-permute-start | bytes 1179656 | tf_op jit(solution)/shard_map/ppermute | solution.py:25
  20.8 2.2 %collective-permute-done.5 = bf16[4,64,128]{2,1,0:T(8,128)(2,1)S(1)} collective-permute-done((bf16[4,64,128]{2,1,0:T(8,128)(2,1)S(1)}, bf16[4,64,128]{2,1,0:T(8,128)(2,1)S(1)}, u32[]{:S(2)}, u32[]{:S(2)}) %collective-permute-start.5) | collective-permute-done | bytes 65568 | tf_op jit(solution)/shard_map/ppermute | solution.py:50
  23.0 0.7 collective-permute-done.6
  23.7 2.3 %collective-permute-start.7 = (bf16[16,64,128]{2,1,0:T(8,128)(2,1)S(1)}, bf16[16,64,128]{2,1,0:T(8,128)(2,1)S(1)}, u32[]{:S(2)}, u32[]{:S(2)}) collective-permute-start(bf16[16,64,128]{2,1,0:T(8,128)(2,1)S(1)} %constant_dynamic-update-slice_fusion.p0), channel_id=1, source_target_pairs={{0,192},{2,50},{16,208},{18,2},{32,224},{34,18},{48,240},{50,34},{... | collective-permute-start | bytes 786440 | tf_op jit(solution)/shard_map/ppermute | solution.py:50
  26.5 0.6 collective-permute-start.9
  27.1 1.6 %collective-permute-start.12 = (bf16[256,512]{1,0:T(8,128)(2,1)S(1)}, bf16[256,512]{1,0:T(8,128)(2,1)S(1)}, u32[]{:S(2)}, u32[]{:S(2)}) collective-permute-start(bf16[256,512]{1,0:T(8,128)(2,1)S(1)} %bitcast.14), channel_id=1, source_target_pairs={{0,1},{1,0},{2,3},{3,2},{4,5},{5,4},{6,7},{7,6},{8,9},{9,8},{10,11... | collective-permute-start | bytes 786440 | tf_op jit(solution)/shard_map/ppermute | solution.py:25
  29.5 2.6 %collective-permute-done.7.p1 = bf16[16,64,128]{2,1,0:T(8,128)(2,1)S(1)} collective-permute-done((bf16[16,64,128]{2,1,0:T(8,128)(2,1)S(1)}, bf16[16,64,128]{2,1,0:T(8,128)(2,1)S(1)}, u32[]{:S(2)}, u32[]{:S(2)}) %collective-permute-start.7) | collective-permute-done | bytes 262176 | tf_op jit(solution)/shard_map/ppermute | solution.py:50
  32.1 0.9 %collective-permute-done.8.p2 = bf16[16,64,128]{2,1,0:T(8,128)(2,1)S(1)} collective-permute-done((bf16[16,64,128]{2,1,0:T(8,128)(2,1)S(1)}, bf16[16,64,128]{2,1,0:T(8,128)(2,1)S(1)}, u32[]{:S(2)}, u32[]{:S(2)}) %collective-permute-start.8) | collective-permute-done | bytes 262176 | tf_op jit(solution)/shard_map/ppermute | solution.py:50
  33.0 2.8 %collective-permute-done.9.p3 = bf16[16,64,128]{2,1,0:T(8,128)(2,1)S(1)} collective-permute-done((bf16[16,64,128]{2,1,0:T(8,128)(2,1)S(1)}, bf16[16,64,128]{2,1,0:T(8,128)(2,1)S(1)}, u32[]{:S(2)}, u32[]{:S(2)}) %collective-permute-start.9) | collective-permute-done | bytes 262176 | tf_op jit(solution)/shard_map/ppermute | solution.py:50
  35.8 0.9 shard_map.82
  36.7 2.6 %collective-permute-start.10 = (bf16[6,64,128]{2,1,0:T(8,128)(2,1)S(1)}, bf16[6,64,128]{2,1,0:T(8,128)(2,1)S(1)}, u32[]{:S(2)}, u32[]{:S(2)}) collective-permute-start(bf16[6,64,128]{2,1,0:T(8,128)(2,1)S(1)} %get-tuple-element.34), channel_id=1, source_target_pairs={{0,2},{2,0},{1,3},{3,1},{4,6},{6,4},{5,7},{7,5},{8,10},{10,8},{9,1... | collective-permute-start | bytes 294920 | tf_op jit(solution)/shard_map/ppermute | solution.py:25
  39.3 0.9 %collective-permute-done.10.other_picked = bf16[6,64,128]{2,1,0:T(8,128)(2,1)S(1)} collective-permute-done((bf16[6,64,128]{2,1,0:T(8,128)(2,1)S(1)}, bf16[6,64,128]{2,1,0:T(8,128)(2,1)S(1)}, u32[]{:S(2)}, u32[]{:S(2)}) %collective-permute-start.10) | collective-permute-done | bytes 98336 | tf_op jit(solution)/shard_map/ppermute | solution.py:25
  40.3 1.6 %shard_map.83 = (f32[6,64,128]{2,1,0:T(8,128)S(1)}, f32[6,64,128]{2,1,0:T(8,128)S(1)}) custom-call(s32[6]{0:T(128)S(1)} %stack.35.where, bf16[6,64,128]{2,1,0:T(8,128)(2,1)S(1)} %get-tuple-element.33.own_picked, bf16[6,64,128]{2,1,0:T(8,128)(2,1)S(1)} %collective-permute-done.10.other_picked, bf16[256,768]{1,0:T(8,128)(2,1)S(1)} %bitcast.13, ...), custom_call_target="tpu_custom_call" | custom-call | tf_op jit(solution)/shard_map/pallas_call | solution.py:235
  42.3 1.1 %collective-permute-done.13.arrived = f32[6,64,128]{2,1,0:T(8,128)S(1)} collective-permute-done((f32[6,64,128]{2,1,0:T(8,128)S(1)}, f32[6,64,128]{2,1,0:T(8,128)S(1)}, u32[]{:S(2)}, u32[]{:S(2)}) %collective-permute-start.13) | collective-permute-done | bytes 196640 | tf_op jit(solution)/shard_map/ppermute | solution.py:25
  43.4 1.1 %shard_map.84 = (f32[16,64,128]{2,1,0:T(8,128)S(1)}, bf16[16,64,128]{2,1,0:T(8,128)(2,1)S(1)}, bf16[16,64,128]{2,1,0:T(8,128)(2,1)S(1)}, bf16[16,64,128]{2,1,0:T(8,128)(2,1)S(1)}) custom-call(s32[6]{0:T(128)S(1)} %stack.35.where, s32[1,6]{1,0:T(1,128)S(1)} %copy-done.4, s32[1,6]{1,0:T(1,128)S(1)} %collective-permute-done.3.other_ids, ...), custom_call_target="tpu_custom_call" | custom-call | tf_op jit(solution)/shard_map/pallas_call | solution.py:244
  44.8 1.0 %collective-permute-start.15 = (bf16[16,64,128]{2,1,0:T(8,128)(2,1)S(1)}, bf16[16,64,128]{2,1,0:T(8,128)(2,1)S(1)}, u32[]{:S(2)}, u32[]{:S(2)}) collective-permute-start(bf16[16,64,128]{2,1,0:T(8,128)(2,1)S(1)} %get-tuple-element.41), channel_id=1, source_target_pairs={{0,128},{2,34},{16,144},{18,50},{32,160},{34,2},{48,176},{50,18},{... | collective-permute-start | bytes 786440 | tf_op jit(solution)/shard_map/ppermute | solution.py:50
  46.4 3.6 %collective-permute-done.16 = bf16[16,64,128]{2,1,0:T(8,128)(2,1)S(1)} collective-permute-done((bf16[16,64,128]{2,1,0:T(8,128)(2,1)S(1)}, bf16[16,64,128]{2,1,0:T(8,128)(2,1)S(1)}, u32[]{:S(2)}, u32[]{:S(2)}) %collective-permute-start.16) | collective-permute-done | bytes 262176 | tf_op jit(solution)/shard_map/ppermute | solution.py:50
  50.0 1.8 %collective-permute-done.15 = bf16[16,64,128]{2,1,0:T(8,128)(2,1)S(1)} collective-permute-done((bf16[16,64,128]{2,1,0:T(8,128)(2,1)S(1)}, bf16[16,64,128]{2,1,0:T(8,128)(2,1)S(1)}, u32[]{:S(2)}, u32[]{:S(2)}) %collective-permute-start.15) | collective-permute-done | bytes 262176 | tf_op jit(solution)/shard_map/ppermute | solution.py:50
  51.9 2.8 %collective-permute-done.14 = bf16[16,64,128]{2,1,0:T(8,128)(2,1)S(1)} collective-permute-done((bf16[16,64,128]{2,1,0:T(8,128)(2,1)S(1)}, bf16[16,64,128]{2,1,0:T(8,128)(2,1)S(1)}, u32[]{:S(2)}, u32[]{:S(2)}) %collective-permute-start.14) | collective-permute-done | bytes 262176 | tf_op jit(solution)/shard_map/ppermute | solution.py:50
  55.2 0.9 collective-permute-start.18
  56.5 1.6 %collective-permute-done.19 = bf16[4,64,128]{2,1,0:T(8,128)(2,1)S(1)} collective-permute-done((bf16[4,64,128]{2,1,0:T(8,128)(2,1)S(1)}, bf16[4,64,128]{2,1,0:T(8,128)(2,1)S(1)}, u32[]{:S(2)}, u32[]{:S(2)}) %collective-permute-start.19) | collective-permute-done | bytes 65568 | tf_op jit(solution)/shard_map/ppermute | solution.py:50
  58.0 1.8 %collective-permute-done.18 = bf16[4,64,128]{2,1,0:T(8,128)(2,1)S(1)} collective-permute-done((bf16[4,64,128]{2,1,0:T(8,128)(2,1)S(1)}, bf16[4,64,128]{2,1,0:T(8,128)(2,1)S(1)}, u32[]{:S(2)}, u32[]{:S(2)}) %collective-permute-start.18) | collective-permute-done | bytes 65568 | tf_op jit(solution)/shard_map/ppermute | solution.py:50
  59.9 0.7 collective-permute-done.17
  60.6 4.2 %collective-permute-start.20 = (bf16[4,64,128]{2,1,0:T(8,128)(2,1)S(1)}, bf16[4,64,128]{2,1,0:T(8,128)(2,1)S(1)}, u32[]{:S(2)}, u32[]{:S(2)}) collective-permute-start(bf16[4,64,128]{2,1,0:T(8,128)(2,1)S(1)} %fusion.3), channel_id=1, source_target_pairs={{0,4},{2,14},{4,0},{6,10},{8,12},{10,6},{12,8},{14,2},{1,5},{3,15}... | collective-permute-start | bytes 196616 | tf_op jit(solution)/shard_map/ppermute | solution.py:59
  64.9 1.8 %collective-permute-done.20 = bf16[4,64,128]{2,1,0:T(8,128)(2,1)S(1)} collective-permute-done((bf16[4,64,128]{2,1,0:T(8,128)(2,1)S(1)}, bf16[4,64,128]{2,1,0:T(8,128)(2,1)S(1)}, u32[]{:S(2)}, u32[]{:S(2)}) %collective-permute-start.20) | collective-permute-done | bytes 65568 | tf_op jit(solution)/shard_map/ppermute | solution.py:59
  66.7 1.9 %collective-permute-start.21 = (bf16[4,64,128]{2,1,0:T(8,128)(2,1)S(1)}, bf16[4,64,128]{2,1,0:T(8,128)(2,1)S(1)}, u32[]{:S(2)}, u32[]{:S(2)}) collective-permute-start(bf16[4,64,128]{2,1,0:T(8,128)(2,1)S(1)} %fusion.4), channel_id=1, source_target_pairs={{0,12},{2,6},{4,8},{6,2},{8,4},{10,14},{12,0},{14,10},{1,13},{3,7}... | collective-permute-start | bytes 196616 | tf_op jit(solution)/shard_map/ppermute | solution.py:59
  68.5 0.8 collective-permute-start.24
  69.3 2.5 %collective-permute-start.25 = (bf16[64,2048]{1,0:T(8,128)(2,1)S(1)}, bf16[64,2048]{1,0:T(8,128)(2,1)S(1)}, u32[]{:S(2)}, u32[]{:S(2)}) collective-permute-start(bf16[64,2048]{1,0:T(8,128)(2,1)S(1)} %get-tuple-element.46), channel_id=1, source_target_pairs={{0,192},{64,0},{128,64},{192,128},{1,193},{65,1},{129,65},{193,129... | collective-permute-start | bytes 786440 | tf_op jit(solution)/shard_map/ppermute | solution.py:33
  71.9 2.7 %collective-permute-start.22 = (bf16[4,64,128]{2,1,0:T(8,128)(2,1)S(1)}, bf16[4,64,128]{2,1,0:T(8,128)(2,1)S(1)}, u32[]{:S(2)}, u32[]{:S(2)}) collective-permute-start(bf16[4,64,128]{2,1,0:T(8,128)(2,1)S(1)} %fusion.2.refs_0_), channel_id=1, source_target_pairs={{0,48},{16,0},{32,16},{48,32},{1,49},{17,1},{33,17},{49,33},{2,50}... | collective-permute-start | bytes 196616 | tf_op jit(solution)/shard_map/ppermute | solution.py:29
  74.6 1.6 %collective-permute-done.26.refs_3_ = bf16[4,64,128]{2,1,0:T(8,128)(2,1)S(1)} collective-permute-done((bf16[4,64,128]{2,1,0:T(8,128)(2,1)S(1)}, bf16[4,64,128]{2,1,0:T(8,128)(2,1)S(1)}, u32[]{:S(2)}, u32[]{:S(2)}) %collective-permute-start.26) | collective-permute-done | bytes 65568 | tf_op jit(solution)/shard_map/ppermute | solution.py:29
  76.2 5.3 %collective-permute-start.27 = (bf16[8,64,128]{2,1,0:T(8,128)(2,1)S(1)}, bf16[8,64,128]{2,1,0:T(8,128)(2,1)S(1)}, u32[]{:S(2)}, u32[]{:S(2)}) collective-permute-start(bf16[8,64,128]{2,1,0:T(8,128)(2,1)S(1)} %pad_maximum_fusion), channel_id=1, source_target_pairs={{0,2},{2,0},{1,3},{3,1},{4,6},{6,4},{5,7},{7,5},{8,10},{10,8},{9,1... | collective-permute-start | bytes 393224 | tf_op jit(solution)/shard_map/ppermute | solution.py:25
  81.6 3.5 %collective-permute-start.28 = (bf16[8,64,128]{2,1,0:T(8,128)(2,1)S(1)}, bf16[8,64,128]{2,1,0:T(8,128)(2,1)S(1)}, u32[]{:S(2)}, u32[]{:S(2)}) collective-permute-start(bf16[8,64,128]{2,1,0:T(8,128)(2,1)S(1)} %pad_maximum_fusion.1), channel_id=1, source_target_pairs={{0,2},{2,0},{1,3},{3,1},{4,6},{6,4},{5,7},{7,5},{8,10},{10,8},{9,1... | collective-permute-start | bytes 393224 | tf_op jit(solution)/shard_map/ppermute | solution.py:25
  85.1 1.0 %collective-permute-done.28.refs_5_ = bf16[8,64,128]{2,1,0:T(8,128)(2,1)S(1)} collective-permute-done((bf16[8,64,128]{2,1,0:T(8,128)(2,1)S(1)}, bf16[8,64,128]{2,1,0:T(8,128)(2,1)S(1)}, u32[]{:S(2)}, u32[]{:S(2)}) %collective-permute-start.28) | collective-permute-done | bytes 131104 | tf_op jit(solution)/shard_map/ppermute | solution.py:25
  86.0 1.1 %shard_map.85 = (f32[64,128]{1,0:T(8,128)S(1)}, f32[64,128]{1,0:T(8,128)S(1)}, f32[64,128]{1,0:T(8,128)S(1)}, f32[64,128]{1,0:T(8,128)S(1)}) custom-call(s32[6]{0:T(128)S(1)} %stack.35.where, f32[64,128]{1,0:T(8,128)S(1)} %copy-done.1, bf16[64,8192]{1,0:T(8,128)(2,1)S(1)} %copy-done, bf16[64,2048]{1,0:T(8,128)(2,1)S(1)} %collective-permute-done.2.b1, ...), custom_call_target="tpu_custom_call" | custom-call | tf_op jit(solution)/shard_map/pallas_call | solution.py:272
  87.4 2.4 %collective-permute-start.30 = (f32[64,128]{1,0:T(8,128)S(1)}, f32[64,128]{1,0:T(8,128)S(1)}, u32[]{:S(2)}, u32[]{:S(2)}) collective-permute-start(f32[64,128]{1,0:T(8,128)S(1)} %get-tuple-element.53), channel_id=1, source_target_pairs={{0,128},{64,192},{128,0},{192,64},{1,129},{65,193},{129,1},{193,65... | collective-permute-start | bytes 98312 | tf_op jit(solution)/shard_map/ppermute | solution.py:29
  90.2 1.0 %collective-permute-done.31 = f32[64,128]{1,0:T(8,128)S(1)} collective-permute-done((f32[64,128]{1,0:T(8,128)S(1)}, f32[64,128]{1,0:T(8,128)S(1)}, u32[]{:S(2)}, u32[]{:S(2)}) %collective-permute-start.31) | collective-permute-done | bytes 32800 | tf_op jit(solution)/shard_map/ppermute | solution.py:29
  91.8 1.2 %collective-permute-done.29 = f32[64,128]{1,0:T(8,128)S(1)} collective-permute-done((f32[64,128]{1,0:T(8,128)S(1)}, f32[64,128]{1,0:T(8,128)S(1)}, u32[]{:S(2)}, u32[]{:S(2)}) %collective-permute-start.29) | collective-permute-done | bytes 32800 | tf_op jit(solution)/shard_map/ppermute | solution.py:29
  93.0 0.6 add_add_fusion
  (56 shorter events, 4.8 us)
Async XLA Ops:
  0.8 9.5 %collective-permute-start = (bf16[64,128]{1,0:T(8,128)(2,1)S(1)}, bf16[64,128]{1,0:T(8,128)(2,1)S(1)}, u32[]{:S(2)}, u32[]{:S(2)}) collective-permute-start(bf16[64,128]{1,0:T(8,128)(2,1)S(1)} %convert_element_type.39), channel_id=1, source_target_pairs={{0,4},{2,14},{4,0},{6,10},{8,12},{10,6},{12,8},{14,2},{1,5},{3,15}... | collective-permute-start | bytes 49160 | tf_op jit(solution)/shard_map/ppermute | solution.py:59
  7.6 2.6 %copy-start.1 = (f32[64,128]{1,0:T(8,128)S(1)}, f32[64,128]{1,0:T(8,128)}, u32[]{:S(2)}) copy-start(f32[64,128]{1,0:T(8,128)} %start.1) | copy-start | bytes 98308
  7.6 11.5 %copy-start.2 = (bf16[1,256,768]{2,1,0:T(8,128)(2,1)S(1)}, bf16[1,256,768]{2,1,0:T(8,128)(2,1)}, u32[]{:S(2)}) copy-start(bf16[1,256,768]{2,1,0:T(8,128)(2,1)} %param.12) | copy-start | bytes 1179652
  8.8 7.7 %collective-permute-start.2 = (bf16[64,2048]{1,0:T(8,128)(2,1)S(1)}, bf16[64,2048]{1,0:T(8,128)(2,1)S(1)}, u32[]{:S(2)}, u32[]{:S(2)}) collective-permute-start(bf16[64,2048]{1,0:T(8,128)(2,1)S(1)} %get-tuple-element.59), channel_id=1, source_target_pairs={{0,64},{64,128},{128,192},{192,0},{1,65},{65,129},{129,193},{193,1... | collective-permute-start | bytes 786440 | tf_op jit(solution)/shard_map/ppermute | solution.py:33
  10.2 1.3 %copy-start.4 = (s32[1,6]{1,0:T(1,128)S(1)}, s32[1,6]{1,0:T(1,128)}, u32[]{:S(2)}) copy-start(s32[1,6]{1,0:T(1,128)} %own_ids.3) | copy-start | bytes 76
  10.3 4.0 %collective-permute-start.1 = (bf16[2,64,128]{2,1,0:T(8,128)(2,1)S(1)}, bf16[2,64,128]{2,1,0:T(8,128)(2,1)S(1)}, u32[]{:S(2)}, u32[]{:S(2)}) collective-permute-start(bf16[2,64,128]{2,1,0:T(8,128)(2,1)S(1)} %pad_maximum_fusion.3), channel_id=1, source_target_pairs={{0,12},{2,6},{4,8},{6,2},{8,4},{10,14},{12,0},{14,10},{1,13},{3,7}... | collective-permute-start | bytes 98312 | tf_op jit(solution)/shard_map/ppermute | solution.py:59
  11.5 2.8 %collective-permute-start.3 = (s32[1,6]{1,0:T(1,128)S(1)}, s32[1,6]{1,0:T(1,128)S(1)}, u32[]{:S(2)}, u32[]{:S(2)}) collective-permute-start(s32[1,6]{1,0:T(1,128)S(1)} %copy-done.4), channel_id=1, source_target_pairs={{0,2},{2,0},{1,3},{3,1},{4,6},{6,4},{5,7},{7,5},{8,10},{10,8},{9,1... | collective-permute-start | bytes 80 | tf_op jit(solution)/shard_map/ppermute | solution.py:25
  16.5 10.5 %copy-start.3 = (bf16[1,256,512]{2,1,0:T(8,128)(2,1)S(1)}, bf16[1,256,512]{2,1,0:T(8,128)(2,1)}, u32[]{:S(2)}) copy-start(bf16[1,256,512]{2,1,0:T(8,128)(2,1)} %param.13) | copy-start | bytes 786436
  16.6 4.2 %collective-permute-start.4 = (bf16[4,64,128]{2,1,0:T(8,128)(2,1)S(1)}, bf16[4,64,128]{2,1,0:T(8,128)(2,1)S(1)}, u32[]{:S(2)}, u32[]{:S(2)}) collective-permute-start(bf16[4,64,128]{2,1,0:T(8,128)(2,1)S(1)} %pad_maximum_fusion.2), channel_id=1, source_target_pairs={{0,48},{2,194},{16,0},{18,210},{32,16},{34,226},{48,32},{50,242},{... | collective-permute-start | bytes 196616 | tf_op jit(solution)/shard_map/ppermute | solution.py:50
  18.1 4.9 %collective-permute-start.5 = (bf16[4,64,128]{2,1,0:T(8,128)(2,1)S(1)}, bf16[4,64,128]{2,1,0:T(8,128)(2,1)S(1)}, u32[]{:S(2)}, u32[]{:S(2)}) collective-permute-start(bf16[4,64,128]{2,1,0:T(8,128)(2,1)S(1)} %pad_maximum_fusion.2), channel_id=1, source_target_pairs={{0,32},{2,130},{16,48},{18,146},{32,0},{34,162},{48,16},{50,178},{... | collective-permute-start | bytes 196616 | tf_op jit(solution)/shard_map/ppermute | solution.py:50
  18.4 5.3 %collective-permute-start.6 = (bf16[4,64,128]{2,1,0:T(8,128)(2,1)S(1)}, bf16[4,64,128]{2,1,0:T(8,128)(2,1)S(1)}, u32[]{:S(2)}, u32[]{:S(2)}) collective-permute-start(bf16[4,64,128]{2,1,0:T(8,128)(2,1)S(1)} %pad_maximum_fusion.2), channel_id=1, source_target_pairs={{0,16},{2,66},{16,32},{18,82},{32,48},{34,98},{48,0},{50,114},{64,... | collective-permute-start | bytes 196616 | tf_op jit(solution)/shard_map/ppermute | solution.py:50
  19.1 20.2 %collective-permute-start.11 = (bf16[256,768]{1,0:T(8,128)(2,1)S(1)}, bf16[256,768]{1,0:T(8,128)(2,1)S(1)}, u32[]{:S(2)}, u32[]{:S(2)}) collective-permute-start(bf16[256,768]{1,0:T(8,128)(2,1)S(1)} %bitcast.12), channel_id=1, source_target_pairs={{0,1},{1,0},{2,3},{3,2},{4,5},{5,4},{6,7},{7,6},{8,9},{9,8},{10,11... | collective-permute-start | bytes 1179656 | tf_op jit(solution)/shard_map/ppermute | solution.py:25
  23.7 8.4 %collective-permute-start.7 = (bf16[16,64,128]{2,1,0:T(8,128)(2,1)S(1)}, bf16[16,64,128]{2,1,0:T(8,128)(2,1)S(1)}, u32[]{:S(2)}, u32[]{:S(2)}) collective-permute-start(bf16[16,64,128]{2,1,0:T(8,128)(2,1)S(1)} %constant_dynamic-update-slice_fusion.p0), channel_id=1, source_target_pairs={{0,192},{2,50},{16,208},{18,2},{32,224},{34,18},{48,240},{50,34},{... | collective-permute-start | bytes 786440 | tf_op jit(solution)/shard_map/ppermute | solution.py:50
  26.0 7.1 %collective-permute-start.8 = (bf16[16,64,128]{2,1,0:T(8,128)(2,1)S(1)}, bf16[16,64,128]{2,1,0:T(8,128)(2,1)S(1)}, u32[]{:S(2)}, u32[]{:S(2)}) collective-permute-start(bf16[16,64,128]{2,1,0:T(8,128)(2,1)S(1)} %constant_dynamic-update-slice_fusion.p0), channel_id=1, source_target_pairs={{0,128},{2,34},{16,144},{18,50},{32,160},{34,2},{48,176},{50,18},{... | collective-permute-start | bytes 786440 | tf_op jit(solution)/shard_map/ppermute | solution.py:50
  26.5 9.3 %collective-permute-start.9 = (bf16[16,64,128]{2,1,0:T(8,128)(2,1)S(1)}, bf16[16,64,128]{2,1,0:T(8,128)(2,1)S(1)}, u32[]{:S(2)}, u32[]{:S(2)}) collective-permute-start(bf16[16,64,128]{2,1,0:T(8,128)(2,1)S(1)} %constant_dynamic-update-slice_fusion.p0), channel_id=1, source_target_pairs={{0,64},{2,18},{16,80},{18,34},{32,96},{34,50},{48,112},{50,2},{64,... | collective-permute-start | bytes 786440 | tf_op jit(solution)/shard_map/ppermute | solution.py:50
  27.1 12.2 %collective-permute-start.12 = (bf16[256,512]{1,0:T(8,128)(2,1)S(1)}, bf16[256,512]{1,0:T(8,128)(2,1)S(1)}, u32[]{:S(2)}, u32[]{:S(2)}) collective-permute-start(bf16[256,512]{1,0:T(8,128)(2,1)S(1)} %bitcast.14), channel_id=1, source_target_pairs={{0,1},{1,0},{2,3},{3,2},{4,5},{5,4},{6,7},{7,6},{8,9},{9,8},{10,11... | collective-permute-start | bytes 786440 | tf_op jit(solution)/shard_map/ppermute | solution.py:25
  36.7 3.6 %collective-permute-start.10 = (bf16[6,64,128]{2,1,0:T(8,128)(2,1)S(1)}, bf16[6,64,128]{2,1,0:T(8,128)(2,1)S(1)}, u32[]{:S(2)}, u32[]{:S(2)}) collective-permute-start(bf16[6,64,128]{2,1,0:T(8,128)(2,1)S(1)} %get-tuple-element.34), channel_id=1, source_target_pairs={{0,2},{2,0},{1,3},{3,1},{4,6},{6,4},{5,7},{7,5},{8,10},{10,8},{9,1... | collective-permute-start | bytes 294920 | tf_op jit(solution)/shard_map/ppermute | solution.py:25
  41.8 1.5 %collective-permute-start.13 = (f32[6,64,128]{2,1,0:T(8,128)S(1)}, f32[6,64,128]{2,1,0:T(8,128)S(1)}, u32[]{:S(2)}, u32[]{:S(2)}) collective-permute-start(f32[6,64,128]{2,1,0:T(8,128)S(1)} %get-tuple-element.38), channel_id=1, source_target_pairs={{0,2},{2,0},{1,3},{3,1},{4,6},{6,4},{5,7},{7,5},{8,10},{10,8},{9,1... | collective-permute-start | bytes 589832 | tf_op jit(solution)/shard_map/ppermute | solution.py:25
  44.4 5.6 %collective-permute-start.16 = (bf16[16,64,128]{2,1,0:T(8,128)(2,1)S(1)}, bf16[16,64,128]{2,1,0:T(8,128)(2,1)S(1)}, u32[]{:S(2)}, u32[]{:S(2)}) collective-permute-start(bf16[16,64,128]{2,1,0:T(8,128)(2,1)S(1)} %get-tuple-element.42), channel_id=1, source_target_pairs={{0,192},{2,50},{16,208},{18,2},{32,224},{34,18},{48,240},{50,34},{... | collective-permute-start | bytes 786440 | tf_op jit(solution)/shard_map/ppermute | solution.py:50
  44.8 7.1 %collective-permute-start.15 = (bf16[16,64,128]{2,1,0:T(8,128)(2,1)S(1)}, bf16[16,64,128]{2,1,0:T(8,128)(2,1)S(1)}, u32[]{:S(2)}, u32[]{:S(2)}) collective-permute-start(bf16[16,64,128]{2,1,0:T(8,128)(2,1)S(1)} %get-tuple-element.41), channel_id=1, source_target_pairs={{0,128},{2,34},{16,144},{18,50},{32,160},{34,2},{48,176},{50,18},{... | collective-permute-start | bytes 786440 | tf_op jit(solution)/shard_map/ppermute | solution.py:50
  45.8 8.8 %collective-permute-start.14 = (bf16[16,64,128]{2,1,0:T(8,128)(2,1)S(1)}, bf16[16,64,128]{2,1,0:T(8,128)(2,1)S(1)}, u32[]{:S(2)}, u32[]{:S(2)}) collective-permute-start(bf16[16,64,128]{2,1,0:T(8,128)(2,1)S(1)} %get-tuple-element.40), channel_id=1, source_target_pairs={{0,64},{2,18},{16,80},{18,34},{32,96},{34,50},{48,112},{50,2},{64,... | collective-permute-start | bytes 786440 | tf_op jit(solution)/shard_map/ppermute | solution.py:50
  54.8 1.6 %copy-start.5 = (f32[64,128]{1,0:T(8,128)S(1)}, f32[64,128]{1,0:T(8,128)}, u32[]{:S(2)}) copy-start(f32[64,128]{1,0:T(8,128)} %param.9) | copy-start | bytes 98308
  54.8 3.2 %collective-permute-start.19 = (bf16[4,64,128]{2,1,0:T(8,128)(2,1)S(1)}, bf16[4,64,128]{2,1,0:T(8,128)(2,1)S(1)}, u32[]{:S(2)}, u32[]{:S(2)}) collective-permute-start(bf16[4,64,128]{2,1,0:T(8,128)(2,1)S(1)} %get-tuple-element.61), channel_id=1, source_target_pairs={{0,48},{2,194},{16,0},{18,210},{32,16},{34,226},{48,32},{50,242},{... | collective-permute-start | bytes 196616 | tf_op jit(solution)/shard_map/ppermute | solution.py:50
  55.2 1.1 %copy-start.6 = (f32[64]{0:T(128)S(1)}, f32[64]{0:T(128)}, u32[]{:S(2)}) copy-start(f32[64]{0:T(128)} %param.10) | copy-start | bytes 772
  55.2 4.6 %collective-permute-start.18 = (bf16[4,64,128]{2,1,0:T(8,128)(2,1)S(1)}, bf16[4,64,128]{2,1,0:T(8,128)(2,1)S(1)}, u32[]{:S(2)}, u32[]{:S(2)}) collective-permute-start(bf16[4,64,128]{2,1,0:T(8,128)(2,1)S(1)} %get-tuple-element.62), channel_id=1, source_target_pairs={{0,32},{2,130},{16,48},{18,146},{32,0},{34,162},{48,16},{50,178},{... | collective-permute-start | bytes 196616 | tf_op jit(solution)/shard_map/ppermute | solution.py:50
  56.2 4.4 %collective-permute-start.17 = (bf16[4,64,128]{2,1,0:T(8,128)(2,1)S(1)}, bf16[4,64,128]{2,1,0:T(8,128)(2,1)S(1)}, u32[]{:S(2)}, u32[]{:S(2)}) collective-permute-start(bf16[4,64,128]{2,1,0:T(8,128)(2,1)S(1)} %get-tuple-element.60), channel_id=1, source_target_pairs={{0,16},{2,66},{16,32},{18,82},{32,48},{34,98},{48,0},{50,114},{64,... | collective-permute-start | bytes 196616 | tf_op jit(solution)/shard_map/ppermute | solution.py:50
  60.6 25.4 %copy-start = (bf16[64,8192]{1,0:T(8,128)(2,1)S(1)}, bf16[64,8192]{1,0:T(8,128)(2,1)}, u32[]{:S(2)}) copy-start(bf16[64,8192]{1,0:T(8,128)(2,1)} %precond.1) | copy-start | bytes 3145732
  60.6 6.0 %collective-permute-start.20 = (bf16[4,64,128]{2,1,0:T(8,128)(2,1)S(1)}, bf16[4,64,128]{2,1,0:T(8,128)(2,1)S(1)}, u32[]{:S(2)}, u32[]{:S(2)}) collective-permute-start(bf16[4,64,128]{2,1,0:T(8,128)(2,1)S(1)} %fusion.3), channel_id=1, source_target_pairs={{0,4},{2,14},{4,0},{6,10},{8,12},{10,6},{12,8},{14,2},{1,5},{3,15}... | collective-permute-start | bytes 196616 | tf_op jit(solution)/shard_map/ppermute | solution.py:59
  66.7 5.1 %collective-permute-start.21 = (bf16[4,64,128]{2,1,0:T(8,128)(2,1)S(1)}, bf16[4,64,128]{2,1,0:T(8,128)(2,1)S(1)}, u32[]{:S(2)}, u32[]{:S(2)}) collective-permute-start(bf16[4,64,128]{2,1,0:T(8,128)(2,1)S(1)} %fusion.4), channel_id=1, source_target_pairs={{0,12},{2,6},{4,8},{6,2},{8,4},{10,14},{12,0},{14,10},{1,13},{3,7}... | collective-permute-start | bytes 196616 | tf_op jit(solution)/shard_map/ppermute | solution.py:59
  68.5 13.0 %collective-permute-start.24 = (bf16[64,2048]{1,0:T(8,128)(2,1)S(1)}, bf16[64,2048]{1,0:T(8,128)(2,1)S(1)}, u32[]{:S(2)}, u32[]{:S(2)}) collective-permute-start(bf16[64,2048]{1,0:T(8,128)(2,1)S(1)} %get-tuple-element.45), channel_id=1, source_target_pairs={{0,128},{64,192},{128,0},{192,64},{1,129},{65,193},{129,1},{193,65... | collective-permute-start | bytes 786440 | tf_op jit(solution)/shard_map/ppermute | solution.py:33
  69.3 12.2 %collective-permute-start.25 = (bf16[64,2048]{1,0:T(8,128)(2,1)S(1)}, bf16[64,2048]{1,0:T(8,128)(2,1)S(1)}, u32[]{:S(2)}, u32[]{:S(2)}) collective-permute-start(bf16[64,2048]{1,0:T(8,128)(2,1)S(1)} %get-tuple-element.46), channel_id=1, source_target_pairs={{0,192},{64,0},{128,64},{192,128},{1,193},{65,1},{129,65},{193,129... | collective-permute-start | bytes 786440 | tf_op jit(solution)/shard_map/ppermute | solution.py:33
  71.8 4.4 %collective-permute-start.26 = (bf16[4,64,128]{2,1,0:T(8,128)(2,1)S(1)}, bf16[4,64,128]{2,1,0:T(8,128)(2,1)S(1)}, u32[]{:S(2)}, u32[]{:S(2)}) collective-permute-start(bf16[4,64,128]{2,1,0:T(8,128)(2,1)S(1)} %fusion.2.refs_0_), channel_id=1, source_target_pairs={{0,16},{16,32},{32,48},{48,0},{1,17},{17,33},{33,49},{49,1},{2,18}... | collective-permute-start | bytes 196616 | tf_op jit(solution)/shard_map/ppermute | solution.py:29
  71.9 9.6 %collective-permute-start.22 = (bf16[4,64,128]{2,1,0:T(8,128)(2,1)S(1)}, bf16[4,64,128]{2,1,0:T(8,128)(2,1)S(1)}, u32[]{:S(2)}, u32[]{:S(2)}) collective-permute-start(bf16[4,64,128]{2,1,0:T(8,128)(2,1)S(1)} %fusion.2.refs_0_), channel_id=1, source_target_pairs={{0,48},{16,0},{32,16},{48,32},{1,49},{17,1},{33,17},{49,33},{2,50}... | collective-permute-start | bytes 196616 | tf_op jit(solution)/shard_map/ppermute | solution.py:29
  74.6 7.0 %collective-permute-start.23 = (bf16[4,64,128]{2,1,0:T(8,128)(2,1)S(1)}, bf16[4,64,128]{2,1,0:T(8,128)(2,1)S(1)}, u32[]{:S(2)}, u32[]{:S(2)}) collective-permute-start(bf16[4,64,128]{2,1,0:T(8,128)(2,1)S(1)} %fusion.2.refs_0_), channel_id=1, source_target_pairs={{0,32},{16,48},{32,0},{48,16},{1,33},{17,49},{33,1},{49,17},{2,34}... | collective-permute-start | bytes 196616 | tf_op jit(solution)/shard_map/ppermute | solution.py:29
  76.2 8.8 %collective-permute-start.27 = (bf16[8,64,128]{2,1,0:T(8,128)(2,1)S(1)}, bf16[8,64,128]{2,1,0:T(8,128)(2,1)S(1)}, u32[]{:S(2)}, u32[]{:S(2)}) collective-permute-start(bf16[8,64,128]{2,1,0:T(8,128)(2,1)S(1)} %pad_maximum_fusion), channel_id=1, source_target_pairs={{0,2},{2,0},{1,3},{3,1},{4,6},{6,4},{5,7},{7,5},{8,10},{10,8},{9,1... | collective-permute-start | bytes 393224 | tf_op jit(solution)/shard_map/ppermute | solution.py:25
  81.6 4.5 %collective-permute-start.28 = (bf16[8,64,128]{2,1,0:T(8,128)(2,1)S(1)}, bf16[8,64,128]{2,1,0:T(8,128)(2,1)S(1)}, u32[]{:S(2)}, u32[]{:S(2)}) collective-permute-start(bf16[8,64,128]{2,1,0:T(8,128)(2,1)S(1)} %pad_maximum_fusion.1), channel_id=1, source_target_pairs={{0,2},{2,0},{1,3},{3,1},{4,6},{6,4},{5,7},{7,5},{8,10},{10,8},{9,1... | collective-permute-start | bytes 393224 | tf_op jit(solution)/shard_map/ppermute | solution.py:25
  87.1 4.1 %collective-permute-start.31 = (f32[64,128]{1,0:T(8,128)S(1)}, f32[64,128]{1,0:T(8,128)S(1)}, u32[]{:S(2)}, u32[]{:S(2)}) collective-permute-start(f32[64,128]{1,0:T(8,128)S(1)} %get-tuple-element.54), channel_id=1, source_target_pairs={{0,64},{64,128},{128,192},{192,0},{1,65},{65,129},{129,193},{193,1... | collective-permute-start | bytes 98312 | tf_op jit(solution)/shard_map/ppermute | solution.py:29
  87.4 4.3 %collective-permute-start.30 = (f32[64,128]{1,0:T(8,128)S(1)}, f32[64,128]{1,0:T(8,128)S(1)}, u32[]{:S(2)}, u32[]{:S(2)}) collective-permute-start(f32[64,128]{1,0:T(8,128)S(1)} %get-tuple-element.53), channel_id=1, source_target_pairs={{0,128},{64,192},{128,0},{192,64},{1,129},{65,193},{129,1},{193,65... | collective-permute-start | bytes 98312 | tf_op jit(solution)/shard_map/ppermute | solution.py:29
  89.8 3.2 %collective-permute-start.29 = (f32[64,128]{1,0:T(8,128)S(1)}, f32[64,128]{1,0:T(8,128)S(1)}, u32[]{:S(2)}, u32[]{:S(2)}) collective-permute-start(f32[64,128]{1,0:T(8,128)S(1)} %get-tuple-element.52), channel_id=1, source_target_pairs={{0,192},{64,0},{128,64},{192,128},{1,193},{65,1},{129,65},{193,129... | collective-permute-start | bytes 98312 | tf_op jit(solution)/shard_map/ppermute | solution.py:29
